TPU v7x, 256 devices: a whole 4x4x8 slice. The times are simulated.
256 devices in a mesh: lat: 8 (over x, y_hi), lon: 32 (over y_lo, z, core).
Axes of the slice: x: 4, y: 4 (y_hi: 2, y_lo: 2; y = y_hi * 2 + y_lo), z: 8, core: 2. Of those that a mesh axis runs over, the one named last changes fastest.
Arguments:
- field: bfloat16 [192, 768, 384], P('lat', 'lon'), may hold values from -6 to 6
- cotangent: bfloat16 [192, 768, 384], P('lat', 'lon'), may hold values from -6 to 6
- mix_weight: bfloat16 [3, 384, 384], replicated, may hold values from -0.1875 to 0.1875
- taps: float32 [192, 3, 3, 8], replicated, may hold values from -1.8 to 1.8
- offsets: int32 [192, 3, 8], replicated, may hold values from -8 to 8, as said below
- counts: int32 [192], replicated, may hold values from 1 to 8, as said below
Outputs:
- grad_field: bfloat16 [192, 768, 384], P('lat', 'lon')
- grad_spectra: float32 [2, 384, 384, 384], P(None, 'lat', 'lon')
- grad_mix: float32 [3, 384, 384], replicated
Inputs may be any that keep to these rules, and one draw needn't show every extreme that they name: For every row and latitude offset the 8 longitude offsets are distinct. Tap slots of a row at or beyond counts are inactive; the polar rows use all 8.
All inputs are finite; a program needn't handle non-finite values.
Results may differ from a plain program's by a relative error of at most 0.0061.
Values may be sent and summed in bfloat16 or wider, within the bound.
No kernel may reach another device: no remote copies, remote signals or barrier semaphores. Data moves between devices by JAX's collectives and lax.ppermute only.
A program may use at most 64 MiB of HBM per device.

v0:
```python
import math

import jax
import jax.numpy as jnp
from jax import lax
from jax.sharding import PartitionSpec as P

M = 384
L = 384
K = 3
R = 8
S = 8
LB = 32
SUBS = 1


def extended(shard, sides, width, wrap):
    for axis, dim in sides:
        devices, length = (lax.axis_size(axis), shard.shape[dim])
        up = [(i, (i + 1) % devices) for i in range(devices if wrap else devices - 1)]
        down = [(j, i) for i, j in up]
        last = lax.slice_in_dim(shard, length - width, length, axis=dim)
        leading = lax.slice_in_dim(shard, 0, width, axis=dim)
        before = lax.ppermute(last, axis, up)
        after = lax.ppermute(leading, axis, down)
        shard = jnp.concatenate([before, shard, after], axis=dim)
    return shard


def live_taps(taps, counts):
    slot_ids = lax.broadcasted_iota(jnp.int32, taps.shape, 3)
    keep_mask = slot_ids < counts[:, None, None, None]
    return jnp.where(keep_mask, taps, jnp.float32(0.0)).astype(jnp.bfloat16)


def band_matrix(weights, shifts, orient, lon_width):
    row_total = weights.shape[0]
    ext_width = lon_width + 2 * R
    out_col = lax.broadcasted_iota(jnp.int32, (lon_width, ext_width), 0)
    in_col = lax.broadcasted_iota(jnp.int32, (lon_width, ext_width), 1)
    summed = jnp.zeros((row_total, 3, weights.shape[1], lon_width, ext_width), jnp.float32)
    for tap_slot in range(S):
        target = out_col[None, None] + R + orient * shifts[:, :, tap_slot, None, None]
        tap_hit = (in_col[None, None] == target).astype(jnp.float32)
        tap_value = jnp.transpose(weights[:, :, :, tap_slot], (0, 2, 1)).astype(jnp.float32)
        summed = summed + tap_value[:, :, :, None, None] * tap_hit[:, :, None]
    return summed.astype(jnp.bfloat16)


def dft_table(lon_total, orders):
    columns = lax.broadcasted_iota(jnp.int32, (lon_total,), 0)
    phases = orders[:, None] * columns[None, :] % lon_total
    angles = 2.0 * math.pi / lon_total * phases.astype(jnp.float32)
    return jnp.stack([jnp.cos(angles), -jnp.sin(angles)]).astype(jnp.bfloat16)


def colatitudes(lat_total):
    angles = (lax.broadcasted_iota(jnp.int32, (lat_total,), 0).astype(jnp.float32) + 0.5) * (
        math.pi / lat_total
    )
    return (jnp.cos(angles), jnp.log(jnp.sin(angles)))


def seed_logs(order_total):
    degrees = lax.broadcasted_iota(jnp.int32, (order_total,), 0).astype(jnp.float32)
    step_logs = jnp.log((2.0 * degrees + 1.0) / (2.0 * degrees + 2.0))
    prefix = jnp.concatenate([jnp.zeros((1,), jnp.float32), jnp.cumsum(step_logs)[:-1]])
    return 0.5 * jnp.log((2.0 * degrees + 1.0) / (4.0 * math.pi)) + 0.5 * prefix


def advance(degree, previous, earlier, orders, cosines):
    deg_f = jnp.asarray(degree).astype(jnp.float32)
    ord_f = orders.astype(jnp.float32)[:, None]
    higher = (degree > orders)[:, None]
    lower_a = jnp.where(higher, deg_f * deg_f - ord_f * ord_f, 1.0)
    factor_a = jnp.sqrt((4.0 * deg_f * deg_f - 1.0) / lower_a)
    upper_b = jnp.maximum((deg_f - 1.0) * (deg_f - 1.0) - ord_f * ord_f, 0.0)
    lower_b = jnp.maximum(4.0 * (deg_f - 1.0) * (deg_f - 1.0) - 1.0, 1.0)
    factor_b = jnp.sqrt(upper_b / lower_b)
    grown = factor_a * (cosines[None, :] * previous - factor_b * earlier)
    seeded = jnp.where((degree == orders)[:, None], jnp.float32(1.0), jnp.float32(0.0))
    return jnp.where(higher, grown, seeded)


def rescale(previous, earlier, scales):
    biggest = jnp.maximum(jnp.abs(previous), jnp.abs(earlier))
    divisor = jnp.where(biggest > 0.0, biggest, jnp.float32(1.0))
    return (previous / divisor, earlier / divisor, scales + jnp.log(divisor))


def legendre_range(
    start_block, orders, cosines, logscale, spec_part, result, row_offset, leg_scale
):
    state_zero = jnp.zeros(logscale.shape, jnp.float32)

    def block_step(block_idx, loop_state):
        previous, earlier, scales, summed = loop_state
        factor = jnp.exp(scales)
        levels = []
        for inner_step in range(LB):
            degree = block_idx * LB + inner_step
            fresh = advance(degree, previous, earlier, orders, cosines)
            levels.append(fresh * factor)
            earlier, previous = (previous, fresh)
        contrib = (
            jnp.einsum(
                "lmt,pmct->pmcl", jnp.stack(levels), spec_part, precision=lax.Precision.HIGHEST
            )
            * leg_scale
        )
        level_start = (block_idx * LB).astype(jnp.int32)
        zero_index = jnp.zeros((), jnp.int32)
        summed = lax.dynamic_update_slice(
            summed,
            contrib,
            (zero_index, jnp.asarray(row_offset).astype(jnp.int32), zero_index, level_start),
        )
        previous, earlier, scales = rescale(previous, earlier, scales)
        return (previous, earlier, scales, summed)

    return lax.fori_loop(
        start_block, L // LB, block_step, (state_zero, state_zero, logscale, result)
    )[3]


def on_device(field, cotangent, mix_weight, taps, offsets, counts):
    lat_dev, lon_dev, channels = field.shape
    lat_count = lax.axis_size("lat")
    lon_count = lax.axis_size("lon")
    total_lat = lat_dev * lat_count
    total_lon = lon_dev * lon_count
    lat_pos = lax.axis_index("lat")
    first_row = lat_pos * lat_dev
    live_table = live_taps(taps, counts)
    taps_padded = jnp.pad(live_table, ((1, 1), (0, 0), (0, 0), (0, 0)))
    shifts_padded = jnp.pad(offsets, ((1, 1), (0, 0), (0, 0)))
    taps_ext = lax.dynamic_slice_in_dim(taps_padded, first_row, lat_dev + 2, 0)
    shifts_ext = lax.dynamic_slice_in_dim(shifts_padded, first_row, lat_dev + 2, 0)
    band_own = band_matrix(taps_ext[1:-1], shifts_ext[1:-1], 1, lon_dev)
    band_back = band_matrix(taps_ext, shifts_ext, -1, lon_dev)
    basis_own = jnp.einsum(
        "tfd,kcd->tfkc", cotangent, mix_weight, preferred_element_type=jnp.float32
    ).astype(jnp.bfloat16)
    stacked = jnp.concatenate([field, basis_own.reshape(lat_dev, lon_dev, K * channels)], axis=2)
    wide_rims = extended(stacked, (("lon", 1),), R, True)
    full_ext = extended(wide_rims, (("lat", 0),), 1, False)
    field_ext = full_ext[:, :, :channels]
    basis_ext = full_ext[:, :, channels:].reshape(lat_dev + 2, lon_dev + 2 * R, K, channels)
    response = jnp.zeros((lat_dev, lon_dev, K, channels), jnp.float32)
    for lat_step in range(3):
        response = response + jnp.einsum(
            "tkfx,txc->tfkc",
            band_own[:, lat_step],
            field_ext[lat_step : lat_step + lat_dev],
            preferred_element_type=jnp.float32,
        )
    response = response.astype(jnp.bfloat16)
    mix_local = jnp.einsum(
        "tfkc,tfd->kcd", response, cotangent, preferred_element_type=jnp.float32
    ) * (1.0 / math.sqrt(total_lat * total_lon))
    grad_mix = lax.psum(mix_local, ("lat", "lon"))
    adjoint = cotangent.astype(jnp.float32)
    for lat_step in range(3):
        row_base = 2 - lat_step
        adjoint = adjoint + jnp.einsum(
            "tkfx,txkc->tfc",
            band_back[row_base : row_base + lat_dev, lat_step],
            basis_ext[row_base : row_base + lat_dev],
            preferred_element_type=jnp.float32,
        )
    grad_field = adjoint.astype(jnp.bfloat16)
    column_set = lax.all_to_all(grad_field, "lon", split_axis=2, concat_axis=1, tiled=True)
    all_orders = lax.broadcasted_iota(jnp.int32, (M,), 0)
    block_rows = M // lat_count
    dft_rows = dft_table(total_lon, all_orders)
    spectra = (
        jnp.einsum("tfc,pmf->pmct", column_set, dft_rows, preferred_element_type=jnp.float32)
        * (1.0 / math.sqrt(total_lon))
    ).astype(jnp.bfloat16)
    mode_block = lax.all_to_all(spectra, "lat", split_axis=1, concat_axis=3, tiled=True)
    spec_full = mode_block.astype(jnp.float32)
    cosines, log_sines = colatitudes(total_lat)
    order_logs = seed_logs(M)
    group_rows = block_rows // SUBS
    chan_block = spec_full.shape[2]
    result = jnp.zeros((2, block_rows, chan_block, L), jnp.float32)
    leg_scale = math.sqrt(4.0 * math.pi / total_lat)
    local_rows = 0 + lax.broadcasted_iota(jnp.int32, (group_rows,), 0)
    orders = lat_pos * block_rows + local_rows
    order_hit = all_orders[None, :] == orders[:, None]
    seed_part = jnp.sum(jnp.where(order_hit, order_logs[None, :], jnp.float32(0.0)), axis=1)
    logscale = seed_part[:, None] + orders.astype(jnp.float32)[:, None] * log_sines[None, :]
    start_block = jnp.min(orders) // LB
    result = legendre_range(start_block, orders, cosines, logscale, spec_full, result, 0, leg_scale)
    return (grad_field, result, grad_mix)


def solution(mesh):
    placed = (P("lat", "lon", None), P("lat", "lon", None), P(), P(), P(), P())
    return jax.shard_map(
        on_device,
        mesh=mesh,
        in_specs=placed,
        out_specs=(P("lat", "lon", None), P(None, "lat", "lon", None), P()),
        check_vma=False,
    )
```

profile of v0, /device:TPU:1, one launch (start us, length us, event | category | flops | bytes accessed | tf_op | source)
XLA Modules:
  0.0 624.6 jit_solution(15827072017148987797)
XLA Ops:
  8.3 2.0 fusion.121
  11.9 3.0 collective-permute-start
  18.5 6.1 negate_convert_fusion
  37.7 3.9 add_convert_fusion.2
  41.6 3.1 add_convert_fusion
  44.8 4.6 collective-permute-start.3
  51.9 4.6 collective-permute-done.2
  60.6 3.6 copy.292
  64.2 5.2 reshape.1991
  69.4 12.0 %all-to-all-start = ((bf16[32,2,3456]{2,1,0:T(2,128)(2,1)}), bf16[32,2,3456]{2,1,0:T(2,128)(2,1)}, u32[]{:S(2)}, u32[]{:S(2)}) async-start(bf16[32,2,3456]{2,1,0:T(2,128)(2,1)} %reshape.1991), calls=%async_computation | async-start | bytes 884736 | tf_op jit(solution)/shard_map/all_to_all | solution.py:172
  84.7 3.2 fusion.185
  87.9 3.1 fusion.190
  91.0 5.3 all-to-all-done
  96.3 5.6 reshape.1992
  101.9 4.0 copy.293
  105.9 4.9 reshape.1984
  110.7 2.7 fusion.148
  113.5 6.2 copy.294
  119.7 8.7 %reshape.1993 = bf16[8,2,13824]{2,1,0:T(2,128)(2,1)} reshape(bf16[384,12,2,24]{3,2,1,0:T(2,128)(2,1)} %bitcast.632) | data formatting | bytes 884736
  128.4 6.8 %all-to-all-start.1 = ((bf16[8,2,13824]{2,1,0:T(2,128)(2,1)}), bf16[8,2,13824]{2,1,0:T(2,128)(2,1)}, u32[]{:S(2)}, u32[]{:S(2)}) async-start(bf16[8,2,13824]{2,1,0:T(2,128)(2,1)} %reshape.1993), calls=%async_computation.1 | async-start | bytes 884736 | tf_op jit(solution)/shard_map/all_to_all | solution.py:180
  135.5 5.4 bitcast_multiply_fusion
  141.0 2.4 all-to-all-done.1
  143.4 9.4 %reshape.1994 = bf16[384,12,2,24]{3,2,1,0:T(2,128)(2,1)} reshape(bf16[8,2,13824]{2,1,0:T(2,128)(2,1)} %all-to-all-done.1) | data formatting | bytes 884736
  152.8 6.6 %copy.295 = f32[2,8,48,12,24]{2,4,1,3,0:T(8,128)} copy(bf16[2,8,48,12,24]{4,0,3,2,1:T(2,128)(2,1)} %bitcast.633) | data formatting | bytes 1327104 | tf_op jit(solution)/shard_map/convert_element_type | solution.py:181
  159.4 2.9 copy.296
  163.6 450.8 %while.22 = (s32[]{:T(128)}, f32[48,192]{1,0:T(8,128)S(1)}, f32[48,192]{1,0:T(8,128)S(1)}, f32[48,192]{1,0:T(8,128)S(1)}, f32[2,48,12,384]{3,1,2,0:T(8,128)}, /*...) while((s32[]{:T(128)}, f32[48,192]{1,0:T(8,128)S(1)}, ...), condition=%wide.region_5.6_spmd.clone.clone.clone, body=%wide.region_4.5_spmd.clone.clone.clone.sunk | while | flops 87389472 | bytes 10750051 | solution.py:121
  185.9 5.8 stack.340
  191.7 1.7 fusion.304
  193.8 5.7 dynamic_update_slice.11
  221.7 5.8 stack.340
  227.5 1.7 fusion.304
  229.5 8.5 %dynamic_update_slice.11 = f32[2,48,12,384]{3,1,2,0:T(8,128)} dynamic-update-slice(f32[2,48,12,384]{3,1,2,0:T(8,128)} %get-tuple-element.1358, f32[2,48,12,32]{3,1,2,0:T(8,128)S(1)} %copy.477, s32[]{:T(128)} %constant.392.clone.1..sunk, s32[]{:T(128)} %constant.392.clone.1..sunk, s32[]{:T(128)} %constant.392.clone.1..sunk, s32[]{:T(128)S(6)} %select_n.1786) | dynamic-update-slice | bytes 294916 | tf_op jit(solution)/shard_map/while/body/dynamic_update_slice | solution.py:113
  239.6 1.6 exponential_multiply_fusion.2
  260.3 5.8 stack.340
  266.1 1.7 fusion.304
  268.1 8.5 %dynamic_update_slice.11 = f32[2,48,12,384]{3,1,2,0:T(8,128)} dynamic-update-slice(f32[2,48,12,384]{3,1,2,0:T(8,128)} %get-tuple-element.1358, f32[2,48,12,32]{3,1,2,0:T(8,128)S(1)} %copy.477, s32[]{:T(128)} %constant.392.clone.1..sunk, s32[]{:T(128)} %constant.392.clone.1..sunk, s32[]{:T(128)} %constant.392.clone.1..sunk, s32[]{:T(128)S(6)} %select_n.1786) | dynamic-update-slice | bytes 294916 | tf_op jit(solution)/shard_map/while/body/dynamic_update_slice | solution.py:113
  298.9 5.8 stack.340
  304.7 1.7 fusion.304
  306.7 8.5 %dynamic_update_slice.11 = f32[2,48,12,384]{3,1,2,0:T(8,128)} dynamic-update-slice(f32[2,48,12,384]{3,1,2,0:T(8,128)} %get-tuple-element.1358, f32[2,48,12,32]{3,1,2,0:T(8,128)S(1)} %copy.477, s32[]{:T(128)} %constant.392.clone.1..sunk, s32[]{:T(128)} %constant.392.clone.1..sunk, s32[]{:T(128)} %constant.392.clone.1..sunk, s32[]{:T(128)S(6)} %select_n.1786) | dynamic-update-slice | bytes 294916 | tf_op jit(solution)/shard_map/while/body/dynamic_update_slice | solution.py:113
  337.5 5.8 stack.340
  343.3 1.7 fusion.304
  345.3 5.7 dynamic_update_slice.11
  373.2 5.8 stack.340
  379.0 1.7 fusion.304
  381.1 8.5 %dynamic_update_slice.11 = f32[2,48,12,384]{3,1,2,0:T(8,128)} dynamic-update-slice(f32[2,48,12,384]{3,1,2,0:T(8,128)} %get-tuple-element.1358, f32[2,48,12,32]{3,1,2,0:T(8,128)S(1)} %copy.477, s32[]{:T(128)} %constant.392.clone.1..sunk, s32[]{:T(128)} %constant.392.clone.1..sunk, s32[]{:T(128)} %constant.392.clone.1..sunk, s32[]{:T(128)S(6)} %select_n.1786) | dynamic-update-slice | bytes 294916 | tf_op jit(solution)/shard_map/while/body/dynamic_update_slice | solution.py:113
  411.8 5.8 stack.340
  417.6 1.7 fusion.304
  419.7 8.5 %dynamic_update_slice.11 = f32[2,48,12,384]{3,1,2,0:T(8,128)} dynamic-update-slice(f32[2,48,12,384]{3,1,2,0:T(8,128)} %get-tuple-element.1358, f32[2,48,12,32]{3,1,2,0:T(8,128)S(1)} %copy.477, s32[]{:T(128)} %constant.392.clone.1..sunk, s32[]{:T(128)} %constant.392.clone.1..sunk, s32[]{:T(128)} %constant.392.clone.1..sunk, s32[]{:T(128)S(6)} %select_n.1786) | dynamic-update-slice | bytes 294916 | tf_op jit(solution)/shard_map/while/body/dynamic_update_slice | solution.py:113
  450.4 5.8 stack.340
  456.2 1.7 fusion.304
  458.3 8.5 %dynamic_update_slice.11 = f32[2,48,12,384]{3,1,2,0:T(8,128)} dynamic-update-slice(f32[2,48,12,384]{3,1,2,0:T(8,128)} %get-tuple-element.1358, f32[2,48,12,32]{3,1,2,0:T(8,128)S(1)} %copy.477, s32[]{:T(128)} %constant.392.clone.1..sunk, s32[]{:T(128)} %constant.392.clone.1..sunk, s32[]{:T(128)} %constant.392.clone.1..sunk, s32[]{:T(128)S(6)} %select_n.1786) | dynamic-update-slice | bytes 294916 | tf_op jit(solution)/shard_map/while/body/dynamic_update_slice | solution.py:113
  489.0 5.8 stack.340
  494.8 1.7 fusion.304
  496.8 4.9 dynamic_update_slice.11
  524.0 5.8 stack.340
  529.7 1.7 fusion.304
  531.8 7.5 %dynamic_update_slice.11 = f32[2,48,12,384]{3,1,2,0:T(8,128)} dynamic-update-slice(f32[2,48,12,384]{3,1,2,0:T(8,128)} %get-tuple-element.1358, f32[2,48,12,32]{3,1,2,0:T(8,128)S(1)} %copy.477, s32[]{:T(128)} %constant.392.clone.1..sunk, s32[]{:T(128)} %constant.392.clone.1..sunk, s32[]{:T(128)} %constant.392.clone.1..sunk, s32[]{:T(128)S(6)} %select_n.1786) | dynamic-update-slice | bytes 294916 | tf_op jit(solution)/shard_map/while/body/dynamic_update_slice | solution.py:113
  561.5 5.8 stack.340
  567.3 1.7 fusion.304
  569.4 7.5 %dynamic_update_slice.11 = f32[2,48,12,384]{3,1,2,0:T(8,128)} dynamic-update-slice(f32[2,48,12,384]{3,1,2,0:T(8,128)} %get-tuple-element.1358, f32[2,48,12,32]{3,1,2,0:T(8,128)S(1)} %copy.477, s32[]{:T(128)} %constant.392.clone.1..sunk, s32[]{:T(128)} %constant.392.clone.1..sunk, s32[]{:T(128)} %constant.392.clone.1..sunk, s32[]{:T(128)S(6)} %select_n.1786) | dynamic-update-slice | bytes 294916 | tf_op jit(solution)/shard_map/while/body/dynamic_update_slice | solution.py:113
  599.1 5.8 stack.340
  604.9 1.7 fusion.304
  606.9 7.5 %dynamic_update_slice.11 = f32[2,48,12,384]{3,1,2,0:T(8,128)} dynamic-update-slice(f32[2,48,12,384]{3,1,2,0:T(8,128)} %get-tuple-element.1358, f32[2,48,12,32]{3,1,2,0:T(8,128)S(1)} %copy.477, s32[]{:T(128)} %constant.392.clone.1..sunk, s32[]{:T(128)} %constant.392.clone.1..sunk, s32[]{:T(128)} %constant.392.clone.1..sunk, s32[]{:T(128)S(6)} %select_n.1786) | dynamic-update-slice | bytes 294916 | tf_op jit(solution)/shard_map/while/body/dynamic_update_slice | solution.py:113
  614.4 2.9 copy.498
  (1241 shorter events, 286.0 us)
Async XLA Ops:
  7.2 1.2 copy-start
  7.2 3.3 copy-start.3
  10.5 4.6 copy-start.8
  10.6 4.6 copy-start.9
  10.6 4.6 copy-start.4
  11.9 32.9 %collective-permute-start = (bf16[24,8,1536]{2,1,0:T(8,128)(2,1)}, bf16[24,8,1536]{2,1,0:T(8,128)(2,1)S(1)}, u32[]{:S(2)}, u32[]{:S(2)}) collective-permute-start(bf16[24,8,1536]{2,1,0:T(8,128)(2,1)} %get-tuple-element.817), channel_id=1, source_target_pairs={{0,1},{1,2},{2,3},{3,4},{4,5},{5,6},{6,7},{7,8},{8,9},{9,10},{10,1... | collective-permute-start | bytes 1769480 | tf_op jit(solution)/shard_map/ppermute | solution.py:24
  14.9 29.8 %collective-permute-start.1 = (bf16[24,8,1536]{2,1,0:T(8,128)(2,1)}, bf16[24,8,1536]{2,1,0:T(8,128)(2,1)S(1)}, u32[]{:S(2)}, u32[]{:S(2)}) collective-permute-start(bf16[24,8,1536]{2,1,0:T(8,128)(2,1)} %get-tuple-element.818), channel_id=1, source_target_pairs={{1,0},{2,1},{3,2},{4,3},{5,4},{6,5},{7,6},{8,7},{9,8},{10,9},{11,1... | collective-permute-start | bytes 1769480 | tf_op jit(solution)/shard_map/ppermute | solution.py:25
  36.7 1.0 copy-start.5
  36.7 1.0 copy-start.6
  36.7 1.0 copy-start.7
  44.8 7.1 %collective-permute-start.3 = (bf16[1,40,1536]{2,1,0:T(8,128)(2,1)S(1)}, bf16[1,40,1536]{2,1,0:T(8,128)(2,1)S(1)}, u32[]{:S(2)}, u32[]{:S(2)}) collective-permute-start(bf16[1,40,1536]{2,1,0:T(8,128)(2,1)S(1)} %get-tuple-element.816), channel_id=1, source_target_pairs={{0,32},{32,64},{64,96},{96,128},{128,160},{160,192},{192,224},{1,3... | collective-permute-start | bytes 368648 | tf_op jit(solution)/shard_map/ppermute | solution.py:24
  49.4 7.1 %collective-permute-start.2 = (bf16[1,40,1536]{2,1,0:T(8,128)(2,1)S(1)}, bf16[1,40,1536]{2,1,0:T(8,128)(2,1)S(1)}, u32[]{:S(2)}, u32[]{:S(2)}) collective-permute-start(bf16[1,40,1536]{2,1,0:T(8,128)(2,1)S(1)} %get-tuple-element.815), channel_id=1, source_target_pairs={{32,0},{64,32},{96,64},{128,96},{160,128},{192,160},{224,192},{33,... | collective-permute-start | bytes 368648 | tf_op jit(solution)/shard_map/ppermute | solution.py:25
  58.1 1.0 copy-start.2
  64.2 20.5 %copy-start.10 = (f32[48]{0:T(128)S(1)}, f32[48]{0:T(128)}, u32[]{:S(2)}) copy-start(f32[48]{0:T(128)} %get-tuple-element.884) | copy-start | bytes 580
  69.4 26.9 %all-to-all-start = ((bf16[32,2,3456]{2,1,0:T(2,128)(2,1)}), bf16[32,2,3456]{2,1,0:T(2,128)(2,1)}, u32[]{:S(2)}, u32[]{:S(2)}) async-start(bf16[32,2,3456]{2,1,0:T(2,128)(2,1)} %reshape.1991), calls=%async_computation | async-start | bytes 884736 | tf_op jit(solution)/shard_map/all_to_all | solution.py:172
  128.4 15.0 %all-to-all-start.1 = ((bf16[8,2,13824]{2,1,0:T(2,128)(2,1)}), bf16[8,2,13824]{2,1,0:T(2,128)(2,1)}, u32[]{:S(2)}, u32[]{:S(2)}) async-start(bf16[8,2,13824]{2,1,0:T(2,128)(2,1)} %reshape.1993), calls=%async_computation.1 | async-start | bytes 884736 | tf_op jit(solution)/shard_map/all_to_all | solution.py:180
  135.2 479.2 %all-reduce.4.cloned.1.call-start = ((), (), s32[]{:S(2)}) async-start(), calls=%async_computation.2 | async-start | bytes 3538944 | tf_op jit(solution)/shard_map/psum | solution.py:161
  614.4 2.9 copy-start.1
Sparse Core Ops, SparseCore 0:
  142.0 257.8 all-reduce.3
where the time goes:
time: 637 us; the launch traced here: 625 us
  local copies, waits for them, and re-layouts  458 us (72%)
  other arithmetic  56.7 us (9%)
  matrix products  39.5 us (6%)
  starting transfers between devices  28.5 us (4%)
  between operations  17.3 us (3%)
  waiting for transfers between devices  12.4 us (2%)
  loops' own time  12.2 us (2%)
    another operation x396, local copies, waits for them, and re-layouts, block_step(): jnp.stack(levels)  288 us
    dynamic_update_slice x24, local copies, waits for them, and re-layouts, block_step(): lax.dynamic_update_slice(summed, contrib, (zero_index, jnp.asarray(row_of...  93.8 us
    unnamed x37, local copies, waits for them, and re-layouts  42.2 us
    dot_general x12, matrix products, block_step(): jnp.einsum('lmt,pmct->pmcl', jnp.stack(levels), spec_part, precision=lax....  20.4 us
    mul x12, other arithmetic, block_step(): levels.append(fresh * factor)  18.6 us
  transfers between devices with their start and end apart: 7, of which 3 were waited for; matrix products, arithmetic and copies ran while one was open for 80% of the time, Pallas kernels for 0%

commit v1 on v0

v1 whole, which is shorter than its diff:
```python
import functools
import math

import jax
import jax.numpy as jnp
import ml_dtypes
import numpy as np
from jax import lax
from jax.experimental import pallas as pl
from jax.experimental.pallas import tpu as pltpu
from jax.sharding import PartitionSpec as P

C = 384
M = 384
L = 384
K = 3
R = 8
S = 8
LB = 32
NLAT = 192
NLON = 768
LATS = 8
LONS = 32
TD = NLAT // LATS
FD = NLON // LONS
CD = C // LONS
MD = M // LATS
XW = FD + 2 * R
TP = 32
QUAD = 4
F32 = jnp.float32
BF16 = jnp.bfloat16
VMEM_BYTES = 56 * 1024 * 1024


def call(kernel, out_shape, **kw):
    return pl.pallas_call(
        kernel,
        out_shape=out_shape,
        compiler_params=pltpu.CompilerParams(vmem_limit_bytes=VMEM_BYTES),
        **kw,
    )


def shape(dims, dtype):
    return jax.ShapeDtypeStruct(dims, dtype)


def swap_blocks(parts):
    lane = lax.broadcasted_iota(jnp.int32, parts[0].shape, 1)
    low = lane < 64
    even = (lane & 32) == 0
    a0, a1, a2, a3 = parts
    b0 = jnp.where(low, a0, pltpu.roll(a2, 64, 1))
    b2 = jnp.where(low, pltpu.roll(a0, 64, 1), a2)
    b1 = jnp.where(low, a1, pltpu.roll(a3, 64, 1))
    b3 = jnp.where(low, pltpu.roll(a1, 64, 1), a3)
    c0 = jnp.where(even, b0, pltpu.roll(b1, 32, 1))
    c1 = jnp.where(even, pltpu.roll(b0, 96, 1), b1)
    c2 = jnp.where(even, b2, pltpu.roll(b3, 32, 1))
    c3 = jnp.where(even, pltpu.roll(b2, 96, 1), b3)
    return c0, c1, c2, c3


def stencil_kernel(tab, cot, left, right, top, bottom, field, g_out, mix_out, ext, band):
    ext[1:TD + 1, 0:R, :] = left[...].astype(F32)
    ext[1:TD + 1, R:R + FD, :] = cot[...].astype(F32)
    ext[1:TD + 1, R + FD:XW, :] = right[...].astype(F32)
    ext[0:1] = top[...].astype(F32)
    ext[TD + 1:TD + 2] = bottom[...].astype(F32)
    lane = lax.broadcasted_iota(jnp.int32, (FD, 256), 1)
    column = lane
    for edge in range(1, QUAD + 2):
        column = column - jnp.where(lane >= edge * XW, XW, 0)
    apart = (column - lax.broadcasted_iota(jnp.int32, (FD, 256), 0)).astype(F32)
    zero = jnp.zeros((FD, 256), F32)
    for quad in range(TD // QUAD):
        for r in range(QUAD):
            t = quad * QUAD + r
            sums = [zero] * K
            for s in range(S):
                hit = apart == tab[t, K * S + s:K * S + s + 1, :]
                for k in range(K):
                    sums[k] = sums[k] + jnp.where(hit, tab[t, k * S + s:k * S + s + 1, :], 0.0)
            for k in range(K):
                row = (k * QUAD + r) * FD
                band[row:row + FD, :] = sums[k]
        slab = ext[quad * QUAD:quad * QUAD + QUAD + 2].reshape((QUAD + 2) * XW, C).astype(BF16)
        weights = band[:, :(QUAD + 2) * XW].astype(BF16)
        got = jnp.dot(weights, slab, preferred_element_type=F32).astype(BF16)
        rows = QUAD * FD
        for k in range(K):
            g_out[quad * rows:(quad + 1) * rows, k * C:(k + 1) * C] = got[k * rows:(k + 1) * rows]
    mix = lax.dot_general(
        field[...], g_out[...], (((0,), (0,)), ((), ())), preferred_element_type=F32
    )
    mix_out[...] = (mix * (1.0 / math.sqrt(NLAT * NLON))).astype(BF16)


def field_kernel(g, cot, mix, gf_out, send_out, flat, turned, send):
    total = cot[...].astype(F32)
    for k in range(K):
        total = total + lax.dot_general(
            g[:, k * C:(k + 1) * C], mix[k], (((1,), (1,)), ((), ())), preferred_element_type=F32
        )
    rounded = total.astype(BF16)
    gf_out[...] = rounded
    for h in range(C // 128):
        flat[h] = rounded[:, h * 128:(h + 1) * 128].astype(F32)
    pad = jnp.zeros((TP - TD, 128), F32)
    for fq in range(FD // 4):
        for h in range(C // 128):
            pieces = []
            for fr in range(4):
                pieces.append(flat[h, pl.ds(fq * 4 + fr, TD, stride=FD), :])
                pieces.append(pad)
            turned[fq, h * 128:(h + 1) * 128, :] = jnp.concatenate(pieces, axis=0).T
    for fq in range(FD // 4):
        for q in range(CD // 4):
            parts = [
                turned[fq, pl.ds(q * 4 + cr, LONS, stride=CD), :] for cr in range(4)
            ]
            for fr, part in enumerate(swap_blocks(parts)):
                send[q, pl.ds(fq * 4 + fr, LONS, stride=FD), :] = part
    for q in range(CD // 4):
        send_out[:, q * 128:(q + 1) * 128] = send[q].astype(BF16)


def legendre_kernel(pos, cosines, logscale, out, coef, prev_s, early_s, scale_s, rows):
    block = pl.program_id(0)
    order = pos[0] * MD + lax.broadcasted_iota(jnp.int32, (MD, 128), 0)
    order_f = order.astype(F32)

    @pl.when(block == 0)
    def _():
        prev_s[...] = jnp.zeros_like(prev_s)
        early_s[...] = jnp.zeros_like(early_s)
        scale_s[...] = logscale[...]

    lane = lax.broadcasted_iota(jnp.int32, (MD, 128), 1)
    degree = block * LB + (lane & (LB - 1))
    deg_f = degree.astype(F32)
    higher = degree > order
    lower_a = jnp.where(higher, deg_f * deg_f - order_f * order_f, 1.0)
    factor_a = jnp.where(higher, jnp.sqrt((4.0 * deg_f * deg_f - 1.0) / lower_a), 0.0)
    before = deg_f - 1.0
    upper_b = jnp.maximum(before * before - order_f * order_f, 0.0)
    lower_b = jnp.maximum(4.0 * before * before - 1.0, 1.0)
    factor_b = jnp.sqrt(upper_b / lower_b)
    coef[...] = jnp.where(lane < LB, factor_a, factor_b)

    x = [jnp.broadcast_to(cosines[0:1, h * 128:(h + 1) * 128], (MD, 128)) for h in range(2)]
    prev = [prev_s[:, h * 128:(h + 1) * 128] for h in range(2)]
    early = [early_s[:, h * 128:(h + 1) * 128] for h in range(2)]
    factor = [jnp.exp(scale_s[:, h * 128:(h + 1) * 128]) for h in range(2)]
    for step in range(LB):
        a = jnp.broadcast_to(coef[:, step:step + 1], (MD, 128))
        b = jnp.broadcast_to(coef[:, LB + step:LB + step + 1], (MD, 128))
        seed = jnp.where(order == block * LB + step, 1.0, 0.0)
        for h in range(2):
            fresh = a * (x[h] * prev[h] - b * early[h]) + seed
            rows[h, step * MD:(step + 1) * MD, :] = fresh * factor[h]
            early[h], prev[h] = prev[h], fresh
    for h in range(2):
        span = slice(h * 128, (h + 1) * 128)
        biggest = jnp.maximum(jnp.abs(prev[h]), jnp.abs(early[h]))
        divisor = jnp.where(biggest > 0.0, biggest, 1.0)
        prev_s[:, span] = prev[h] / divisor
        early_s[:, span] = early[h] / divisor
        scale_s[:, span] = scale_s[:, span] + jnp.log(divisor)
    for m in range(MD):
        for h in range(2):
            span = slice(h * 128, (h + 1) * 128)
            out[m, :, span] = rows[h, pl.ds(m, LB, stride=MD), :].astype(BF16)


MSTEP = 8


def synthesis_kernel(spec, leg, out, lined):
    step = pl.program_id(0)

    @pl.when(step == 0)
    def _():
        for g in range(2):
            for q in range(CD // 4):
                parts = [spec[4 * g + iq, :, q * 128:(q + 1) * 128].astype(F32) for iq in range(4)]
                for cr, part in enumerate(swap_blocks(parts)):
                    for p in range(2):
                        base = (p * CD + q * 4 + cr) * MD
                        lined[g, base:base + MD, :] = part[p * MD:(p + 1) * MD]

    for mm in range(MSTEP):
        halves = [lined[g, pl.ds(step * MSTEP + mm, 2 * CD, stride=MD), :] for g in range(2)]
        lhs = jnp.concatenate(halves, axis=1).astype(BF16)
        got = lax.dot_general(
            lhs, leg[mm], (((1,), (1,)), ((), ())), preferred_element_type=F32
        ) * math.sqrt(4.0 * math.pi / NLAT)
        out[0, mm] = got[:CD]
        out[1, mm] = got[CD:]


TILES = (MD // 8) * (K * C // 128)


def sum_lat_kernel(parts, out):
    total = parts[0].astype(F32)
    for i in range(1, LATS):
        total = total + parts[i].astype(F32)
    lanes = K * C // 128
    for n in range(0, 2 * LONS, 2):
        tiles = []
        for tile in (n, n + 1):
            if tile < TILES:
                row, col = divmod(tile, lanes)
                tiles.append(total[row * 8:(row + 1) * 8, col * 128:(col + 1) * 128])
            else:
                tiles.append(jnp.zeros((8, 128), F32))
        out[n // 2] = jnp.concatenate(tiles, axis=0).astype(BF16)


def sum_lon_kernel(parts, out):
    total = parts[0].astype(F32)
    for j in range(1, LONS):
        total = total + parts[j].astype(F32)
    total = total.astype(BF16)
    for j in range(LONS):
        out[j] = total


def copies_kernel(part, out):
    for i in range(LATS):
        out[i] = part[...]


def mix_kernel(parts, out):
    lanes = K * C // 128
    for i in range(LATS):
        for n in range(0, TILES, 2):
            pair = parts[i, n // 2].astype(F32)
            for half in range(2):
                row, col = divmod(n + half, lanes)
                k, d = divmod(col, C // 128)
                out[k, i * MD + row * 8:i * MD + row * 8 + 8, d * 128:(d + 1) * 128] = pair[half * 8:half * 8 + 8]


def dft_rows():
    order = np.arange(M).reshape(LATS, 1, MD)
    order = np.broadcast_to(order, (LATS, 2, MD)).reshape(-1)
    part = np.broadcast_to(np.arange(2).reshape(1, 2, 1), (LATS, 2, MD)).reshape(-1)
    angle = 2.0 * np.pi / NLON * ((order[:, None] * np.arange(NLON)[None, :]) % NLON)
    angle = angle.astype(np.float32)
    return np.where(part[:, None] == 0, np.cos(angle), -np.sin(angle)).astype(ml_dtypes.bfloat16)


def latitudes():
    angle = ((np.arange(NLAT) + 0.5) * (np.pi / NLAT)).reshape(LATS, TD)
    cosine = np.zeros((LATS, TP), np.float32)
    logsine = np.zeros((LATS, TP), np.float32)
    cosine[:, :TD] = np.cos(angle)
    logsine[:, :TD] = np.log(np.sin(angle))
    return cosine.reshape(1, -1), logsine.reshape(1, -1)


def seed_logs():
    degree = np.arange(M, dtype=np.float64)
    steps = np.log((2.0 * degree + 1.0) / (2.0 * degree + 2.0))
    prefix = np.concatenate([np.zeros(1), np.cumsum(steps)[:-1]])
    return (0.5 * np.log((2.0 * degree + 1.0) / (4.0 * np.pi)) + 0.5 * prefix).astype(np.float32)


def band_lanes():
    mark = np.zeros((TD, 3, 256), np.float32)
    for t in range(TD):
        for rr in range(3):
            start = (t % QUAD + rr) * XW
            mark[t, rr, start:start + XW] = 1.0
    return mark


def tap_table(taps, offsets, counts, first_row):
    slot_ids = lax.broadcasted_iota(jnp.int32, taps.shape, 3)
    live = jnp.where(slot_ids < counts[:, None, None, None], taps, 0.0).astype(BF16).astype(F32)
    shift = (R - offsets).astype(F32)[:, None]
    both = jnp.concatenate([live, shift], axis=1)
    both = jnp.pad(both, ((1, 1), (0, 0), (0, 0), (0, 0)))
    both = lax.dynamic_slice_in_dim(both, first_row, TD + 2, 0)
    marks = band_lanes()
    table = 0.0
    for rr in range(3):
        mine = both[rr:rr + TD, :, 2 - rr, :].reshape(TD, (K + 1) * S)
        table = table + mine[:, :, None] * marks[:, rr][:, None, :]
    return table


def on_device(field, cotangent, mix_weight, taps, offsets, counts):
    lat_pos = lax.axis_index("lat")
    up = [(i, (i + 1) % LONS) for i in range(LONS)]
    down = [(j, i) for i, j in up]
    left = lax.ppermute(cotangent[:, FD - R:], "lon", up)
    right = lax.ppermute(cotangent[:, :R], "lon", down)
    edge_rows = [
        jnp.concatenate([left[t:t + 1], cotangent[t:t + 1], right[t:t + 1]], axis=1) for t in (0, TD - 1)
    ]
    north = [(i, i + 1) for i in range(LATS - 1)]
    south = [(j, i) for i, j in north]
    top = lax.ppermute(edge_rows[1], "lat", north)
    bottom = lax.ppermute(edge_rows[0], "lat", south)

    cosine, logsine = latitudes()
    first_order = lat_pos * MD
    seeds = lax.dynamic_slice_in_dim(jnp.asarray(seed_logs()), first_order, MD, 0)
    orders = (first_order + jnp.arange(MD, dtype=jnp.int32)).astype(F32)
    logscale = seeds[:, None] + orders[:, None] * logsine
    table = call(
        legendre_kernel,
        shape((MD, L, LATS * TP), BF16),
        grid_spec=pltpu.PrefetchScalarGridSpec(
            num_scalar_prefetch=1,
            grid=(L // LB,),
            in_specs=[
                pl.BlockSpec((1, LATS * TP), lambda b, pos: (0, 0)),
                pl.BlockSpec((MD, LATS * TP), lambda b, pos: (0, 0)),
            ],
            out_specs=pl.BlockSpec((MD, LB, LATS * TP), lambda b, pos: (0, b, 0)),
            scratch_shapes=[
                pltpu.VMEM((MD, 128), F32),
                pltpu.VMEM((MD, LATS * TP), F32),
                pltpu.VMEM((MD, LATS * TP), F32),
                pltpu.VMEM((MD, LATS * TP), F32),
                pltpu.VMEM((2, LB * MD, 128), F32),
            ],
        ),
        name="legendre",
    )(jnp.reshape(lat_pos, (1,)).astype(jnp.int32), jnp.asarray(cosine), logscale)

    tab = tap_table(taps, offsets, counts, lat_pos * TD)
    cells = TD * FD
    grown, mix_part = call(
        stencil_kernel,
        (shape((cells, K * C), BF16), shape((C, K * C), BF16)),
        scratch_shapes=[pltpu.VMEM((TD + 2, XW, C), F32), pltpu.VMEM((K * QUAD * FD, 256), F32)],
        name="stencil",
    )(tab, cotangent, left, right, top, bottom, field.reshape(cells, C))
    mix_lat = lax.all_to_all(mix_part.reshape(LATS, MD, K * C), "lat", 0, 0, tiled=True)

    grad_field, send = call(
        field_kernel,
        (shape((cells, C), BF16), shape((LONS * FD, CD * TP), BF16)),
        scratch_shapes=[
            pltpu.VMEM((C // 128, cells, 128), F32),
            pltpu.VMEM((FD // 4, C, 128), F32),
            pltpu.VMEM((CD // 4, LONS * FD, 128), F32),
        ],
        name="grad_field",
    )(grown, cotangent.reshape(cells, C), mix_weight)
    columns = lax.all_to_all(send.reshape(LONS, FD, CD * TP), "lon", 0, 0, tiled=True)

    mix_lon = lax.all_to_all(
        call(sum_lat_kernel, shape((LONS, 16, 128), BF16), name="mix_sum_lat")(mix_lat), "lon", 0, 0, tiled=True
    )
    spectra = jnp.dot(
        jnp.asarray(dft_rows()), columns.reshape(NLON, CD * TP), preferred_element_type=F32
    )
    spectra = (spectra * (1.0 / math.sqrt(NLON))).astype(BF16)
    spec = lax.all_to_all(spectra.reshape(LATS, 2 * MD, CD * TP), "lat", 0, 0, tiled=True)

    mix_mine = call(sum_lon_kernel, shape((LONS, 16, 128), BF16), name="mix_sum_lon")(mix_lon)
    mix_row = lax.all_to_all(mix_mine, "lon", 0, 0, tiled=True)
    mix_copies = call(copies_kernel, shape((LATS, LONS, 16, 128), BF16), name="mix_copies")(mix_row)
    mix_all = lax.all_to_all(mix_copies, "lat", 0, 0, tiled=True)
    grad_mix = call(mix_kernel, shape((K, C, C), F32), name="mix_out")(mix_all)

    grad_spectra = call(
        synthesis_kernel,
        shape((2, MD, CD, L), F32),
        grid_spec=pltpu.PrefetchScalarGridSpec(
            num_scalar_prefetch=0,
            grid=(MD // MSTEP,),
            in_specs=[
                pl.BlockSpec((LATS, 2 * MD, CD * TP), lambda b: (0, 0, 0)),
                pl.BlockSpec((MSTEP, L, LATS * TP), lambda b: (b, 0, 0)),
            ],
            out_specs=pl.BlockSpec((2, MSTEP, CD, L), lambda b: (0, b, 0, 0)),
            scratch_shapes=[pltpu.VMEM((2, 2 * CD * MD, 128), F32)],
        ),
        name="synthesis",
    )(spec, table)
    return (grad_field.reshape(TD, FD, C), grad_spectra, grad_mix)


def solution(mesh):
    placed = (P("lat", "lon", None), P("lat", "lon", None), P(), P(), P(), P())
    return jax.shard_map(
        on_device,
        mesh=mesh,
        in_specs=placed,
        out_specs=(P("lat", "lon", None), P(None, "lat", "lon", None), P()),
        check_vma=False,
    )
```

time: 637 us -> 158 us (0.25); the launches traced: 625 us -> 156 us
  local copies, waits for them, and re-layouts: 458 us -> 8.91 us
  other arithmetic: 56.7 us -> 3.74 us
  Pallas kernels: 0 us -> 41.8 us
  matrix products: 39.5 us -> 0.67 us
  waiting for transfers between devices: 12.4 us -> 40.3 us
  between operations: 17.3 us -> 0.83 us
  blocking collectives: 0 us -> 16.4 us
  starting transfers between devices: 28.5 us -> 43.5 us
  loops' own time: 12.2 us -> 0 us
    another operation x399 -> x0, local copies, waits for them, and re-layouts: 288 us -> none  [the longest x396 288 us: block_step(): jnp.stack(levels)]
    dynamic_update_slice x24 -> x0, local copies, waits for them, and re-layouts: 93.8 us -> none  [block_step(): lax.dynamic_update_slice(summed, contrib, (zero_index, jnp.asarray(row_of...]
    pallas_call x0 -> x8, Pallas kernels: none -> 41.8 us  [the longest x1 15.6 us: on_device(): call(legendre_kernel, shape((MD, L, LATS * TP), BF16), grid_spec=pltpu.Pr...]
    dot_general x20 -> x1, matrix products: 39.5 us -> 0.67 us  [on_device(): jnp.dot(jnp.asarray(dft_rows()), columns.reshape(NLON, CD * TP), preferre...]
    unnamed x37 -> x27, local copies, waits for them, and re-layouts: 42.2 us -> 5.03 us
    all_to_all x2 -> x5, waiting for transfers between devices: 7.77 us -> 35.3 us  [the longest x1 16.3 us: on_device(): lax.all_to_all(send.reshape(LONS, FD, CD * TP), 'lon', 0, 0, tiled=True)]
    mul x14 -> x0, other arithmetic: 20 us -> none  [the longest x12 18.6 us: block_step(): levels.append(fresh * factor)]
    convert_element_type x27 -> x1, local copies, waits for them, and re-layouts: 20 us -> 1.06 us  [on_device(): spectra = (spectra * (1.0 / math.sqrt(NLON))).astype(BF16)]
  transfers between devices with their start and end apart: 7 -> 9, of which waited for: 3 -> 6; matrix products, arithmetic and copies ran while one was open for 80% -> 7% of each run, Pallas kernels for 0% -> 21%
where the time goes in v1:
time: 158 us; the launch traced here: 156 us
  starting transfers between devices  43.5 us (28%)
  Pallas kernels  41.8 us (26%)
  waiting for transfers between devices  40.3 us (26%)
  blocking collectives  16.4 us (10%)
  local copies, waits for them, and re-layouts  8.91 us (6%)
  other arithmetic  3.74 us (2%)
    all_to_all x1, blocking collectives, on_device(): lax.all_to_all(mix_part.reshape(LATS, MD, K * C), 'lat', 0, 0, tiled=True)  16.4 us
    all_to_all x1, waiting for transfers between devices, on_device(): lax.all_to_all(send.reshape(LONS, FD, CD * TP), 'lon', 0, 0, tiled=True)  16.3 us
    pallas_call x1, Pallas kernels, on_device(): call(legendre_kernel, shape((MD, L, LATS * TP), BF16), grid_spec=pltpu.Pr...  15.6 us
    all_to_all x1, starting transfers between devices, on_device(): lax.all_to_all(call(sum_lat_kernel, shape((LONS, 16, 128), BF16), name='m...  14.2 us
    pallas_call x1, Pallas kernels, on_device(): call(synthesis_kernel, shape((2, MD, CD, L), F32), grid_spec=pltpu.Prefet...  8.61 us
    all_to_all x1, waiting for transfers between devices, on_device(): mix_row = lax.all_to_all(mix_mine, 'lon', 0, 0, tiled=True)  7.42 us
    all_to_all x1, waiting for transfers between devices, on_device(): lax.all_to_all(spectra.reshape(LATS, 2 * MD, CD * TP), 'lat', 0, 0, tiled...  7.16 us
    all_to_all x1, starting transfers between devices, on_device(): mix_row = lax.all_to_all(mix_mine, 'lon', 0, 0, tiled=True)  5.64 us
  transfers between devices with their start and end apart: 9, of which 6 were waited for; matrix products, arithmetic and copies ran while one was open for 7% of the time, Pallas kernels for 21%

profile of v1, /device:TPU:1, one launch (start us, length us, event | category | flops | bytes accessed | tf_op | source)
XLA Modules:
  0.0 156.1 jit_solution(15431741038708506129)
XLA Ops:
  0.6 0.0 copy-start.8
  0.6 0.0 copy-start.9
  0.7 0.0 copy-start.10
  0.7 1.0 fusion.10
  1.7 3.1 %collective-permute-start = (bf16[24,8,384]{2,1,0:T(8,128)(2,1)S(1)}, bf16[24,8,384]{2,1,0:T(8,128)(2,1)S(1)}, u32[]{:S(2)}, u32[]{:S(2)}) collective-permute-start(bf16[24,8,384]{2,1,0:T(8,128)(2,1)S(1)} %get-tuple-element.17), channel_id=1, source_target_pairs={{0,1},{1,2},{2,3},{3,4},{4,5},{5,6},{6,7},{7,8},{8,9},{9,10},{10,1... | collective-permute-start | bytes 442376 | tf_op jit(solution)/shard_map/ppermute | solution.py:300
  4.8 0.3 collective-permute-start.1
  5.1 0.7 convert_bitcast_fusion
  5.8 0.9 fusion.8
  6.7 0.1 fusion.3
  6.9 0.1 slice_bitcast_fusion.2
  6.9 0.1 copy.18
  7.0 0.1 copy.17
  7.1 0.1 copy.16
  7.1 0.8 fusion.9
  7.9 1.5 collective-permute-done.1.right
  9.4 0.0 copy-start.5
  9.4 0.0 collective-permute-done.left
  9.4 0.0 copy-start.4
  9.4 4.8 %collective-permute-start.2 = (bf16[1,40,384]{2,1,0:T(8,128)(2,1)S(1)}, bf16[1,40,384]{2,1,0:T(8,128)(2,1)S(1)}, u32[]{:S(2)}, u32[]{:S(2)}) collective-permute-start(bf16[1,40,384]{2,1,0:T(8,128)(2,1)S(1)} %pad_maximum_fusion), channel_id=1, source_target_pairs={{0,32},{32,64},{64,96},{96,128},{128,160},{160,192},{192,224},{1,3... | collective-permute-start | bytes 92168 | tf_op jit(solution)/shard_map/ppermute | solution.py:307
  14.3 1.3 collective-permute-start.3
  15.6 0.0 copy-done.8
  15.6 0.0 copy-done.9
  15.6 0.0 copy-done.10
  15.6 1.3 multiply_add_fusion.tab
  16.9 0.0 collective-permute-done.2.top
  16.9 0.0 copy-start.6
  16.9 3.5 %collective-permute-done.3.bottom = bf16[1,40,384]{2,1,0:T(8,128)(2,1)S(1)} collective-permute-done((bf16[1,40,384]{2,1,0:T(8,128)(2,1)S(1)}, bf16[1,40,384]{2,1,0:T(8,128)(2,1)S(1)}, u32[]{:S(2)}, u32[]{:S(2)}) %collective-permute-start.3) | collective-permute-done | bytes 30752 | tf_op jit(solution)/shard_map/ppermute | solution.py:308
  20.4 0.0 copy-start.7
  20.4 0.0 copy-done.5
  20.4 0.0 copy-done.4
  20.4 0.0 copy-done.6
  20.4 0.6 copy-done.7
  21.0 4.8 %stencil.1 = (bf16[576,1152]{1,0:T(8,128)(2,1)}, bf16[384,1152]{1,0:T(8,128)(2,1)}) custom-call(f32[24,32,256]{2,1,0:T(8,128)} %multiply_add_fusion.tab, bf16[24,24,384]{2,1,0:T(8,128)(2,1)} %cot.1, bf16[24,8,384]{2,1,0:T(8,128)(2,1)} %copy-done.4, bf16[24,8,384]{2,1,0:T(8,128)(2,1)} %copy-done.5, bf16[1,40,384]{2,1,0:T(8,128)(2,1)} %copy-done.6, ...), custom_call_target="tpu_custom_call" | custom-call | tf_op jit(solution)/shard_map/stencil/pallas_call | solution.py:339
  25.9 16.4 %all_to_all.30.parts = bf16[8,48,1152]{2,1,0:T(8,128)(2,1)} all-to-all(bf16[8,48,1152]{2,1,0:T(8,128)(2,1)} %bitcast.21), channel_id=1, replica_groups=mesh['lat'=8,'lon'=32] {'lat'}, dimensions={0} | all-to-all | bytes 1769472 | tf_op jit(solution)/shard_map/all_to_all | solution.py:345
  42.3 1.9 %mix_sum_lat.1 = bf16[32,16,128]{2,1,0:T(8,128)(2,1)} custom-call(bf16[8,48,1152]{2,1,0:T(8,128)(2,1)} %all_to_all.30.parts), custom_call_target="tpu_custom_call" | custom-call | tf_op jit(solution)/shard_map/mix_sum_lat/pallas_call | solution.py:360
  44.2 14.2 %all-to-all-start.3 = ((bf16[32,16,128]{2,1,0:T(8,128)(2,1)}), bf16[32,16,128]{2,1,0:T(8,128)(2,1)S(1)}, u32[]{:S(2)}, u32[]{:S(2)}) async-start(bf16[32,16,128]{2,1,0:T(8,128)(2,1)} %mix_sum_lat.1), calls=%async_computation.3 | async-start | bytes 262144 | tf_op jit(solution)/shard_map/all_to_all | solution.py:359
  58.5 4.6 %grad_field.1 = (bf16[576,384]{1,0:T(8,128)(2,1)}, bf16[768,384]{1,0:T(8,128)(2,1)}) custom-call(bf16[576,1152]{1,0:T(8,128)(2,1)} %get-tuple-element.7.g, bf16[576,384]{1,0:T(8,128)(2,1)} %bitcast.20, bf16[3,384,384]{2,1,0:T(8,128)(2,1)} %mix.1), custom_call_target="tpu_custom_call" | custom-call | tf_op jit(solution)/shard_map/grad_field/pallas_call | solution.py:347
  63.0 0.0 copy-start.12
  63.1 4.5 %all-to-all-done.3.parts = bf16[32,16,128]{2,1,0:T(8,128)(2,1)S(1)} async-done(((bf16[32,16,128]{2,1,0:T(8,128)(2,1)}), bf16[32,16,128]{2,1,0:T(8,128)(2,1)S(1)}, u32[]{:S(2)}, u32[]{:S(2)}) %all-to-all-start.3) | async-done | bytes 131104 | tf_op jit(solution)/shard_map/all_to_all | solution.py:359
  67.5 0.0 copy-start.3
  67.5 5.2 %all-to-all-start = ((bf16[32,24,384]{2,1,0:T(8,128)(2,1)}), bf16[32,24,384]{2,1,0:T(8,128)(2,1)S(1)}, u32[]{:S(2)}, u32[]{:S(2)}) async-start(bf16[32,24,384]{2,1,0:T(8,128)(2,1)} %bitcast.23), calls=%async_computation | async-start | bytes 1179648 | tf_op jit(solution)/shard_map/all_to_all | solution.py:357
  72.7 0.0 copy-done.3
  72.7 1.6 %mix_sum_lon.1 = bf16[32,16,128]{2,1,0:T(8,128)(2,1)} custom-call(bf16[32,16,128]{2,1,0:T(8,128)(2,1)} %copy-done.3), custom_call_target="tpu_custom_call" | custom-call | tf_op jit(solution)/shard_map/mix_sum_lon/pallas_call | solution.py:368
  74.3 16.3 %all-to-all-done = bf16[32,24,384]{2,1,0:T(8,128)(2,1)S(1)} async-done(((bf16[32,24,384]{2,1,0:T(8,128)(2,1)}), bf16[32,24,384]{2,1,0:T(8,128)(2,1)S(1)}, u32[]{:S(2)}, u32[]{:S(2)}) %all-to-all-start) | async-done | bytes 589856 | tf_op jit(solution)/shard_map/all_to_all | solution.py:357
  90.6 5.6 %all-to-all-start.4 = ((bf16[32,16,128]{2,1,0:T(8,128)(2,1)}), bf16[32,16,128]{2,1,0:T(8,128)(2,1)S(1)}, u32[]{:S(2)}, u32[]{:S(2)}) async-start(bf16[32,16,128]{2,1,0:T(8,128)(2,1)} %mix_sum_lon.1), calls=%async_computation.4 | async-start | bytes 262144 | tf_op jit(solution)/shard_map/all_to_all | solution.py:369
  96.2 0.0 copy-done.12
  96.3 0.7 fusion.1
  96.9 1.1 copy.19
  98.0 7.4 %all-to-all-done.4.part = bf16[32,16,128]{2,1,0:T(8,128)(2,1)S(1)} async-done(((bf16[32,16,128]{2,1,0:T(8,128)(2,1)}), bf16[32,16,128]{2,1,0:T(8,128)(2,1)S(1)}, u32[]{:S(2)}, u32[]{:S(2)}) %all-to-all-start.4) | async-done | bytes 131104 | tf_op jit(solution)/shard_map/all_to_all | solution.py:369
  105.4 3.5 %all-to-all-start.1 = ((bf16[8,96,384]{2,1,0:T(8,128)(2,1)}), bf16[8,96,384]{2,1,0:T(8,128)(2,1)S(1)}, u32[]{:S(2)}, u32[]{:S(2)}) async-start(bf16[8,96,384]{2,1,0:T(8,128)(2,1)} %bitcast.10), calls=%async_computation.1 | async-start | bytes 1179648 | tf_op jit(solution)/shard_map/all_to_all | solution.py:366
  109.0 0.0 copy-done.2
  109.0 2.0 %mix_copies.1 = bf16[8,32,16,128]{3,2,1,0:T(8,128)(2,1)} custom-call(bf16[32,16,128]{2,1,0:T(8,128)(2,1)} %copy-done.2), custom_call_target="tpu_custom_call" | custom-call | tf_op jit(solution)/shard_map/mix_copies/pallas_call | solution.py:370
  111.0 7.2 %all-to-all-done.1.spec = bf16[8,96,384]{2,1,0:T(8,128)(2,1)S(1)} async-done(((bf16[8,96,384]{2,1,0:T(8,128)(2,1)}), bf16[8,96,384]{2,1,0:T(8,128)(2,1)S(1)}, u32[]{:S(2)}, u32[]{:S(2)}) %all-to-all-start.1) | async-done | bytes 589856 | tf_op jit(solution)/shard_map/all_to_all | solution.py:366
  118.1 5.3 %all-to-all-start.5 = ((bf16[8,32,16,128]{3,2,1,0:T(8,128)(2,1)}), bf16[8,32,16,128]{3,2,1,0:T(8,128)(2,1)S(1)}, u32[]{:S(2)}, u32[]{:S(2)}) async-start(bf16[8,32,16,128]{3,2,1,0:T(8,128)(2,1)} %mix_copies.1), calls=%async_computation.5 | async-start | bytes 2097152 | tf_op jit(solution)/shard_map/all_to_all | solution.py:371
  123.5 0.8 dynamic_slice.7
  124.2 0.0 copy-done.11
  124.2 0.7 multiply_add_fusion.1.logscale
  124.9 15.6 %legendre.1.leg = bf16[48,384,256]{2,1,0:T(8,128)(2,1)} custom-call(s32[1]{0:T(128)} %bitcast.11.pos, f32[1,256]{1,0:T(1,128)} %constant.39.clone.cosines, f32[48,256]{1,0:T(8,128)} %multiply_add_fusion.1.logscale), custom_call_target="tpu_custom_call" | custom-call | tf_op jit(solution)/shard_map/legendre/pallas_call | solution.py:315
  140.6 0.0 copy-done.1
  140.6 8.6 %synthesis.1 = f32[2,48,12,384]{3,2,1,0:T(8,128)} custom-call(bf16[8,96,384]{2,1,0:T(8,128)(2,1)} %copy-done.1, bf16[48,384,256]{2,1,0:T(8,128)(2,1)} %legendre.1.leg), custom_call_target="tpu_custom_call" | custom-call | tf_op jit(solution)/shard_map/synthesis/pallas_call | solution.py:374
  149.2 3.4 %copy.20 = f32[2,48,12,384]{3,1,2,0:T(8,128)} copy(f32[2,48,12,384]{3,2,1,0:T(8,128)} %synthesis.1) | data formatting | bytes 3538944
  152.6 0.0 all-to-all-done.5.parts
  152.6 1.0 copy-done
  153.5 2.5 %mix_out.1 = f32[3,384,384]{2,1,0:T(8,128)} custom-call(bf16[8,32,16,128]{3,2,1,0:T(8,128)(2,1)} %copy-done), custom_call_target="tpu_custom_call" | custom-call | tf_op jit(solution)/shard_map/mix_out/pallas_call | solution.py:372
  (9 shorter events, 0.0 us)
Async XLA Ops:
  0.6 14.9 %copy-start.8 = (f32[24,256]{1,0:T(8,128)S(1)}, f32[24,256]{1,0:T(8,128)}, u32[]{:S(2)}) copy-start(f32[24,256]{1,0:T(8,128)} %constant.50) | copy-start | bytes 73732
  0.6 14.9 %copy-start.9 = (f32[24,256]{1,0:T(8,128)S(1)}, f32[24,256]{1,0:T(8,128)}, u32[]{:S(2)}) copy-start(f32[24,256]{1,0:T(8,128)} %constant.49) | copy-start | bytes 73732
  0.7 14.9 %copy-start.10 = (f32[24,256]{1,0:T(8,128)S(1)}, f32[24,256]{1,0:T(8,128)}, u32[]{:S(2)}) copy-start(f32[24,256]{1,0:T(8,128)} %constant.48) | copy-start | bytes 73732
  1.7 7.7 %collective-permute-start = (bf16[24,8,384]{2,1,0:T(8,128)(2,1)S(1)}, bf16[24,8,384]{2,1,0:T(8,128)(2,1)S(1)}, u32[]{:S(2)}, u32[]{:S(2)}) collective-permute-start(bf16[24,8,384]{2,1,0:T(8,128)(2,1)S(1)} %get-tuple-element.17), channel_id=1, source_target_pairs={{0,1},{1,2},{2,3},{3,4},{4,5},{5,6},{6,7},{7,8},{8,9},{9,10},{10,1... | collective-permute-start | bytes 442376 | tf_op jit(solution)/shard_map/ppermute | solution.py:300
  4.8 4.6 %collective-permute-start.1 = (bf16[24,8,384]{2,1,0:T(8,128)(2,1)S(1)}, bf16[24,8,384]{2,1,0:T(8,128)(2,1)S(1)}, u32[]{:S(2)}, u32[]{:S(2)}) collective-permute-start(bf16[24,8,384]{2,1,0:T(8,128)(2,1)S(1)} %get-tuple-element.16), channel_id=1, source_target_pairs={{1,0},{2,1},{3,2},{4,3},{5,4},{6,5},{7,6},{8,7},{9,8},{10,9},{11,1... | collective-permute-start | bytes 442376 | tf_op jit(solution)/shard_map/ppermute | solution.py:301
  9.4 11.0 %copy-start.5 = (bf16[24,8,384]{2,1,0:T(8,128)(2,1)}, bf16[24,8,384]{2,1,0:T(8,128)(2,1)S(1)}, u32[]{:S(2)}) copy-start(bf16[24,8,384]{2,1,0:T(8,128)(2,1)S(1)} %collective-permute-done.1.right) | copy-start | bytes 442372
  9.4 11.0 %copy-start.4 = (bf16[24,8,384]{2,1,0:T(8,128)(2,1)}, bf16[24,8,384]{2,1,0:T(8,128)(2,1)S(1)}, u32[]{:S(2)}) copy-start(bf16[24,8,384]{2,1,0:T(8,128)(2,1)S(1)} %collective-permute-done.left) | copy-start | bytes 442372
  9.4 7.5 %collective-permute-start.2 = (bf16[1,40,384]{2,1,0:T(8,128)(2,1)S(1)}, bf16[1,40,384]{2,1,0:T(8,128)(2,1)S(1)}, u32[]{:S(2)}, u32[]{:S(2)}) collective-permute-start(bf16[1,40,384]{2,1,0:T(8,128)(2,1)S(1)} %pad_maximum_fusion), channel_id=1, source_target_pairs={{0,32},{32,64},{64,96},{96,128},{128,160},{160,192},{192,224},{1,3... | collective-permute-start | bytes 92168 | tf_op jit(solution)/shard_map/ppermute | solution.py:307
  14.3 6.1 %collective-permute-start.3 = (bf16[1,40,384]{2,1,0:T(8,128)(2,1)S(1)}, bf16[1,40,384]{2,1,0:T(8,128)(2,1)S(1)}, u32[]{:S(2)}, u32[]{:S(2)}) collective-permute-start(bf16[1,40,384]{2,1,0:T(8,128)(2,1)S(1)} %pad_maximum_fusion.1), channel_id=1, source_target_pairs={{32,0},{64,32},{96,64},{128,96},{160,128},{192,160},{224,192},{33,... | collective-permute-start | bytes 92168 | tf_op jit(solution)/shard_map/ppermute | solution.py:308
  16.9 3.5 %copy-start.6 = (bf16[1,40,384]{2,1,0:T(8,128)(2,1)}, bf16[1,40,384]{2,1,0:T(8,128)(2,1)S(1)}, u32[]{:S(2)}) copy-start(bf16[1,40,384]{2,1,0:T(8,128)(2,1)S(1)} %collective-permute-done.2.top) | copy-start | bytes 92164
  20.4 0.6 copy-start.7
  44.2 23.3 %all-to-all-start.3 = ((bf16[32,16,128]{2,1,0:T(8,128)(2,1)}), bf16[32,16,128]{2,1,0:T(8,128)(2,1)S(1)}, u32[]{:S(2)}, u32[]{:S(2)}) async-start(bf16[32,16,128]{2,1,0:T(8,128)(2,1)} %mix_sum_lat.1), calls=%async_computation.3 | async-start | bytes 262144 | tf_op jit(solution)/shard_map/all_to_all | solution.py:359
  63.0 33.2 %copy-start.12 = (bf16[768,768]{1,0:T(8,128)(2,1)S(1)}, bf16[768,768]{1,0:T(8,128)(2,1)}, u32[]{:S(2)}) copy-start(bf16[768,768]{1,0:T(8,128)(2,1)} %constant.43.clone) | copy-start | bytes 3538948
  67.5 5.2 %copy-start.3 = (bf16[32,16,128]{2,1,0:T(8,128)(2,1)}, bf16[32,16,128]{2,1,0:T(8,128)(2,1)S(1)}, u32[]{:S(2)}) copy-start(bf16[32,16,128]{2,1,0:T(8,128)(2,1)S(1)} %all-to-all-done.3.parts) | copy-start | bytes 393220
  67.5 23.1 %all-to-all-start = ((bf16[32,24,384]{2,1,0:T(8,128)(2,1)}), bf16[32,24,384]{2,1,0:T(8,128)(2,1)S(1)}, u32[]{:S(2)}, u32[]{:S(2)}) async-start(bf16[32,24,384]{2,1,0:T(8,128)(2,1)} %bitcast.23), calls=%async_computation | async-start | bytes 1179648 | tf_op jit(solution)/shard_map/all_to_all | solution.py:357
  90.6 14.8 %all-to-all-start.4 = ((bf16[32,16,128]{2,1,0:T(8,128)(2,1)}), bf16[32,16,128]{2,1,0:T(8,128)(2,1)S(1)}, u32[]{:S(2)}, u32[]{:S(2)}) async-start(bf16[32,16,128]{2,1,0:T(8,128)(2,1)} %mix_sum_lon.1), calls=%async_computation.4 | async-start | bytes 262144 | tf_op jit(solution)/shard_map/all_to_all | solution.py:369
  105.4 3.6 %copy-start.2 = (bf16[32,16,128]{2,1,0:T(8,128)(2,1)}, bf16[32,16,128]{2,1,0:T(8,128)(2,1)S(1)}, u32[]{:S(2)}) copy-start(bf16[32,16,128]{2,1,0:T(8,128)(2,1)S(1)} %all-to-all-done.4.part) | copy-start | bytes 393220
  105.4 12.7 %all-to-all-start.1 = ((bf16[8,96,384]{2,1,0:T(8,128)(2,1)}), bf16[8,96,384]{2,1,0:T(8,128)(2,1)S(1)}, u32[]{:S(2)}, u32[]{:S(2)}) async-start(bf16[8,96,384]{2,1,0:T(8,128)(2,1)} %bitcast.10), calls=%async_computation.1 | async-start | bytes 1179648 | tf_op jit(solution)/shard_map/all_to_all | solution.py:366
  111.0 13.2 %copy-start.11 = (f32[256]{0:T(256)S(1)}, f32[256]{0:T(256)}, u32[]{:S(2)}) copy-start(f32[256]{0:T(256)} %constant.51) | copy-start | bytes 3076
  118.1 22.4 %copy-start.1 = (bf16[8,96,384]{2,1,0:T(8,128)(2,1)}, bf16[8,96,384]{2,1,0:T(8,128)(2,1)S(1)}, u32[]{:S(2)}) copy-start(bf16[8,96,384]{2,1,0:T(8,128)(2,1)S(1)} %all-to-all-done.1.spec) | copy-start | bytes 1769476
  118.1 34.4 %all-to-all-start.5 = ((bf16[8,32,16,128]{3,2,1,0:T(8,128)(2,1)}), bf16[8,32,16,128]{3,2,1,0:T(8,128)(2,1)S(1)}, u32[]{:S(2)}, u32[]{:S(2)}) async-start(bf16[8,32,16,128]{3,2,1,0:T(8,128)(2,1)} %mix_copies.1), calls=%async_computation.5 | async-start | bytes 2097152 | tf_op jit(solution)/shard_map/all_to_all | solution.py:371
  152.6 1.0 copy-start

commit v2 on v1

--- a/solution.py
+++ b/solution.py
@@ -33,10 +33,11 @@
 VMEM_BYTES = 56 * 1024 * 1024
 
 
-def call(kernel, out_shape, **kw):
+def call(kernel, out_shape, us, **kw):
     return pl.pallas_call(
         kernel,
         out_shape=out_shape,
+        cost_estimate=pl.CostEstimate(flops=int(us * 1.1e9), bytes_accessed=int(us * 3.0e6), transcendentals=0),
         compiler_params=pltpu.CompilerParams(vmem_limit_bytes=VMEM_BYTES),
         **kw,
     )
@@ -97,7 +98,7 @@
     mix_out[...] = (mix * (1.0 / math.sqrt(NLAT * NLON))).astype(BF16)
 
 
-def field_kernel(g, cot, mix, gf_out, send_out, flat, turned, send):
+def field_kernel(pos, g, cot, mix, gf_out, send_out, flat, turned, send):
     total = cot[...].astype(F32)
     for k in range(K):
         total = total + lax.dot_general(
@@ -105,8 +106,12 @@
         )
     rounded = total.astype(BF16)
     gf_out[...] = rounded
-    for h in range(C // 128):
-        flat[h] = rounded[:, h * 128:(h + 1) * 128].astype(F32)
+    rounded = rounded.astype(F32)
+    southern = pos[0] >= LATS // 2
+    for t in range(TD):
+        row = pl.multiple_of(jnp.where(southern, TD - 1 - t, t) * FD, FD)
+        for h in range(C // 128):
+            flat[h, pl.ds(row, FD), :] = rounded[t * FD:(t + 1) * FD, h * 128:(h + 1) * 128]
     pad = jnp.zeros((TP - TD, 128), F32)
     for fq in range(FD // 4):
         for h in range(C // 128):
@@ -126,6 +131,14 @@
         send_out[:, q * 128:(q + 1) * 128] = send[q].astype(BF16)
 
 
+def dft_kernel(rows, columns, out):
+    got = jnp.dot(rows[...], columns[...], preferred_element_type=F32)
+    out[...] = (got * (1.0 / math.sqrt(NLON))).astype(BF16)
+
+
+HALF = LATS // 2 * TP
+
+
 def legendre_kernel(pos, cosines, logscale, out, coef, prev_s, early_s, scale_s, rows):
     block = pl.program_id(0)
     order = pos[0] * MD + lax.broadcasted_iota(jnp.int32, (MD, 128), 0)
@@ -149,55 +162,70 @@
     factor_b = jnp.sqrt(upper_b / lower_b)
     coef[...] = jnp.where(lane < LB, factor_a, factor_b)
 
-    x = [jnp.broadcast_to(cosines[0:1, h * 128:(h + 1) * 128], (MD, 128)) for h in range(2)]
-    prev = [prev_s[:, h * 128:(h + 1) * 128] for h in range(2)]
-    early = [early_s[:, h * 128:(h + 1) * 128] for h in range(2)]
-    factor = [jnp.exp(scale_s[:, h * 128:(h + 1) * 128]) for h in range(2)]
+    x = jnp.broadcast_to(cosines[...], (MD, 128))
+    prev = prev_s[...]
+    early = early_s[...]
+    factor = jnp.exp(scale_s[...])
     for step in range(LB):
         a = jnp.broadcast_to(coef[:, step:step + 1], (MD, 128))
         b = jnp.broadcast_to(coef[:, LB + step:LB + step + 1], (MD, 128))
         seed = jnp.where(order == block * LB + step, 1.0, 0.0)
-        for h in range(2):
-            fresh = a * (x[h] * prev[h] - b * early[h]) + seed
-            rows[h, step * MD:(step + 1) * MD, :] = fresh * factor[h]
-            early[h], prev[h] = prev[h], fresh
-    for h in range(2):
-        span = slice(h * 128, (h + 1) * 128)
-        biggest = jnp.maximum(jnp.abs(prev[h]), jnp.abs(early[h]))
-        divisor = jnp.where(biggest > 0.0, biggest, 1.0)
-        prev_s[:, span] = prev[h] / divisor
-        early_s[:, span] = early[h] / divisor
-        scale_s[:, span] = scale_s[:, span] + jnp.log(divisor)
+        fresh = a * (x * prev - b * early) + seed
+        rows[step * MD:(step + 1) * MD, :] = fresh * factor
+        early, prev = prev, fresh
+    biggest = jnp.maximum(jnp.abs(prev), jnp.abs(early))
+    divisor = jnp.where(biggest > 0.0, biggest, 1.0)
+    prev_s[...] = prev / divisor
+    early_s[...] = early / divisor
+    scale_s[...] = scale_s[...] + jnp.log(divisor)
     for m in range(MD):
-        for h in range(2):
-            span = slice(h * 128, (h + 1) * 128)
-            out[m, :, span] = rows[h, pl.ds(m, LB, stride=MD), :].astype(BF16)
+        side = (m % 2) * 128
+        out[m // 2, :, side:side + 128] = rows[pl.ds(m, LB, stride=MD), :].astype(BF16)
 
 
 MSTEP = 8
 
 
-def synthesis_kernel(spec, leg, out, lined):
+def synthesis_kernel(spec, leg, out, lined, rows):
     step = pl.program_id(0)
 
     @pl.when(step == 0)
     def _():
-        for g in range(2):
-            for q in range(CD // 4):
-                parts = [spec[4 * g + iq, :, q * 128:(q + 1) * 128].astype(F32) for iq in range(4)]
+        for q in range(CD // 4):
+            span = slice(q * 128, (q + 1) * 128)
+            north = [spec[i, :, span].astype(F32) for i in range(LATS // 2)]
+            south = [spec[LATS - 1 - i, :, span].astype(F32) for i in range(LATS // 2)]
+            for odd in range(2):
+                parts = [n - s if odd else n + s for n, s in zip(north, south)]
                 for cr, part in enumerate(swap_blocks(parts)):
                     for p in range(2):
-                        base = (p * CD + q * 4 + cr) * MD
-                        lined[g, base:base + MD, :] = part[p * MD:(p + 1) * MD]
-
-    for mm in range(MSTEP):
-        halves = [lined[g, pl.ds(step * MSTEP + mm, 2 * CD, stride=MD), :] for g in range(2)]
-        lhs = jnp.concatenate(halves, axis=1).astype(BF16)
+                        base = ((odd * 2 + p) * CD + q * 4 + cr) * MD
+                        lined[base:base + MD, :] = part[p * MD:(p + 1) * MD]
+
+    wide = 2 * CD
+    odd_lane = (lax.broadcasted_iota(jnp.int32, (wide, L), 1) & 1) == 1
+    zero = jnp.zeros((2 * wide, HALF), F32)
+    for pair in range(MSTEP // 2):
+        first = step * MSTEP + 2 * pair
+        mine = [lined[pl.ds(first + side, 2 * wide, stride=MD), :] for side in range(2)]
+        lhs = jnp.concatenate(
+            [jnp.concatenate([mine[0], zero], axis=1), jnp.concatenate([zero, mine[1]], axis=1)], axis=0
+        ).astype(BF16)
         got = lax.dot_general(
-            lhs, leg[mm], (((1,), (1,)), ((), ())), preferred_element_type=F32
+            lhs, leg[pair], (((1,), (1,)), ((), ())), preferred_element_type=F32
         ) * math.sqrt(4.0 * math.pi / NLAT)
-        out[0, mm] = got[:CD]
-        out[1, mm] = got[CD:]
+        done = [
+            jnp.where(odd_lane, got[wide:2 * wide], got[:wide]),
+            jnp.where(odd_lane, got[2 * wide:3 * wide], got[3 * wide:]),
+        ]
+        for side in range(2):
+            for h in range(L // 128):
+                rows[h, pl.ds(2 * pair + side, wide, stride=MSTEP), :] = done[side][:, h * 128:(h + 1) * 128]
+    for p in range(2):
+        for c in range(CD):
+            base = (p * CD + c) * MSTEP
+            for h in range(L // 128):
+                out[p, c, :, h * 128:(h + 1) * 128] = rows[h, base:base + MSTEP, :]
 
 
 TILES = (MD // 8) * (K * C // 128)
@@ -228,20 +256,22 @@
         out[j] = total
 
 
+PAIRS = TILES // 2
+
+
 def copies_kernel(part, out):
     for i in range(LATS):
-        out[i] = part[...]
+        out[i] = part[:PAIRS]
 
 
 def mix_kernel(parts, out):
     lanes = K * C // 128
-    for i in range(LATS):
-        for n in range(0, TILES, 2):
-            pair = parts[i, n // 2].astype(F32)
-            for half in range(2):
-                row, col = divmod(n + half, lanes)
-                k, d = divmod(col, C // 128)
-                out[k, i * MD + row * 8:i * MD + row * 8 + 8, d * 128:(d + 1) * 128] = pair[half * 8:half * 8 + 8]
+    for n in range(0, TILES, 2):
+        pair = parts[0, n // 2].astype(F32)
+        for half in range(2):
+            row, col = divmod(n + half, lanes)
+            k, d = divmod(col, C // 128)
+            out[k, row * 8:row * 8 + 8, d * 128:(d + 1) * 128] = pair[half * 8:half * 8 + 8]
 
 
 def dft_rows():
@@ -259,7 +289,8 @@
     logsine = np.zeros((LATS, TP), np.float32)
     cosine[:, :TD] = np.cos(angle)
     logsine[:, :TD] = np.log(np.sin(angle))
-    return cosine.reshape(1, -1), logsine.reshape(1, -1)
+    half = LATS // 2
+    return cosine[:half].reshape(1, -1), logsine[:half].reshape(1, -1)
 
 
 def seed_logs():
@@ -307,86 +338,106 @@
     top = lax.ppermute(edge_rows[1], "lat", north)
     bottom = lax.ppermute(edge_rows[0], "lat", south)
 
-    cosine, logsine = latitudes()
-    first_order = lat_pos * MD
-    seeds = lax.dynamic_slice_in_dim(jnp.asarray(seed_logs()), first_order, MD, 0)
-    orders = (first_order + jnp.arange(MD, dtype=jnp.int32)).astype(F32)
-    logscale = seeds[:, None] + orders[:, None] * logsine
-    table = call(
-        legendre_kernel,
-        shape((MD, L, LATS * TP), BF16),
-        grid_spec=pltpu.PrefetchScalarGridSpec(
-            num_scalar_prefetch=1,
-            grid=(L // LB,),
-            in_specs=[
-                pl.BlockSpec((1, LATS * TP), lambda b, pos: (0, 0)),
-                pl.BlockSpec((MD, LATS * TP), lambda b, pos: (0, 0)),
-            ],
-            out_specs=pl.BlockSpec((MD, LB, LATS * TP), lambda b, pos: (0, b, 0)),
-            scratch_shapes=[
-                pltpu.VMEM((MD, 128), F32),
-                pltpu.VMEM((MD, LATS * TP), F32),
-                pltpu.VMEM((MD, LATS * TP), F32),
-                pltpu.VMEM((MD, LATS * TP), F32),
-                pltpu.VMEM((2, LB * MD, 128), F32),
-            ],
-        ),
-        name="legendre",
-    )(jnp.reshape(lat_pos, (1,)).astype(jnp.int32), jnp.asarray(cosine), logscale)
-
     tab = tap_table(taps, offsets, counts, lat_pos * TD)
     cells = TD * FD
     grown, mix_part = call(
         stencil_kernel,
         (shape((cells, K * C), BF16), shape((C, K * C), BF16)),
+        5,
         scratch_shapes=[pltpu.VMEM((TD + 2, XW, C), F32), pltpu.VMEM((K * QUAD * FD, 256), F32)],
         name="stencil",
     )(tab, cotangent, left, right, top, bottom, field.reshape(cells, C))
     mix_lat = lax.all_to_all(mix_part.reshape(LATS, MD, K * C), "lat", 0, 0, tiled=True)
 
+    pos = jnp.reshape(lat_pos, (1,)).astype(jnp.int32)
+    whole = pl.BlockSpec(memory_space=pltpu.VMEM)
     grad_field, send = call(
         field_kernel,
         (shape((cells, C), BF16), shape((LONS * FD, CD * TP), BF16)),
+        5,
+        in_specs=[pl.BlockSpec(memory_space=pltpu.SMEM), whole, whole, whole],
         scratch_shapes=[
             pltpu.VMEM((C // 128, cells, 128), F32),
             pltpu.VMEM((FD // 4, C, 128), F32),
             pltpu.VMEM((CD // 4, LONS * FD, 128), F32),
         ],
         name="grad_field",
-    )(grown, cotangent.reshape(cells, C), mix_weight)
+    )(pos, grown, cotangent.reshape(cells, C), mix_weight)
     columns = lax.all_to_all(send.reshape(LONS, FD, CD * TP), "lon", 0, 0, tiled=True)
 
-    mix_lon = lax.all_to_all(
-        call(sum_lat_kernel, shape((LONS, 16, 128), BF16), name="mix_sum_lat")(mix_lat), "lon", 0, 0, tiled=True
+    mix_sum = call(sum_lat_kernel, shape((LONS, 16, 128), BF16), 2, name="mix_sum_lat")(mix_lat)
+    cosine, logsine = latitudes()
+    first_order = lat_pos * MD
+    seeds = lax.dynamic_slice_in_dim(jnp.asarray(seed_logs()), first_order, MD, 0)
+    orders = (first_order + jnp.arange(MD, dtype=jnp.int32)).astype(F32)
+    logscale = seeds[:, None] + orders[:, None] * logsine
+    logscale, _ = lax.optimization_barrier((logscale, send))
+    table = call(
+        legendre_kernel,
+        shape((MD // 2, L, 2 * HALF), BF16),
+        9,
+        grid_spec=pltpu.PrefetchScalarGridSpec(
+            num_scalar_prefetch=1,
+            grid=(L // LB,),
+            in_specs=[
+                pl.BlockSpec((1, HALF), lambda b, pos: (0, 0)),
+                pl.BlockSpec((MD, HALF), lambda b, pos: (0, 0)),
+            ],
+            out_specs=pl.BlockSpec((MD // 2, LB, 2 * HALF), lambda b, pos: (0, b, 0)),
+            scratch_shapes=[
+                pltpu.VMEM((MD, 128), F32),
+                pltpu.VMEM((MD, HALF), F32),
+                pltpu.VMEM((MD, HALF), F32),
+                pltpu.VMEM((MD, HALF), F32),
+                pltpu.VMEM((LB * MD, HALF), F32),
+            ],
+        ),
+        name="legendre",
+    )(pos, jnp.asarray(cosine), logscale)
+    columns, table, mix_sum = lax.optimization_barrier((columns, table, mix_sum))
+
+    mix_lon = lax.all_to_all(mix_sum, "lon", 0, 0, tiled=True)
+    spectra = call(dft_kernel, shape((NLON, CD * TP), BF16), 2, name="dft")(
+        jnp.asarray(dft_rows()), columns.reshape(NLON, CD * TP)
     )
-    spectra = jnp.dot(
-        jnp.asarray(dft_rows()), columns.reshape(NLON, CD * TP), preferred_element_type=F32
-    )
-    spectra = (spectra * (1.0 / math.sqrt(NLON))).astype(BF16)
+    mix_mine = call(sum_lon_kernel, shape((LONS, 16, 128), BF16), 2, name="mix_sum_lon")(mix_lon)
+    mix_row = lax.all_to_all(mix_mine, "lon", 0, 0, tiled=True)
+    mix_row, spectra = lax.optimization_barrier((mix_row, spectra))
+
     spec = lax.all_to_all(spectra.reshape(LATS, 2 * MD, CD * TP), "lat", 0, 0, tiled=True)
-
-    mix_mine = call(sum_lon_kernel, shape((LONS, 16, 128), BF16), name="mix_sum_lon")(mix_lon)
-    mix_row = lax.all_to_all(mix_mine, "lon", 0, 0, tiled=True)
-    mix_copies = call(copies_kernel, shape((LATS, LONS, 16, 128), BF16), name="mix_copies")(mix_row)
+    mix_copies = call(copies_kernel, shape((LATS, PAIRS, 16, 128), BF16), 2, name="mix_copies")(mix_row)
+    spec, mix_copies = lax.optimization_barrier((spec, mix_copies))
     mix_all = lax.all_to_all(mix_copies, "lat", 0, 0, tiled=True)
-    grad_mix = call(mix_kernel, shape((K, C, C), F32), name="mix_out")(mix_all)
 
     grad_spectra = call(
         synthesis_kernel,
-        shape((2, MD, CD, L), F32),
+        shape((2, CD, MD, L), F32),
+        6,
         grid_spec=pltpu.PrefetchScalarGridSpec(
             num_scalar_prefetch=0,
             grid=(MD // MSTEP,),
             in_specs=[
                 pl.BlockSpec((LATS, 2 * MD, CD * TP), lambda b: (0, 0, 0)),
-                pl.BlockSpec((MSTEP, L, LATS * TP), lambda b: (b, 0, 0)),
+                pl.BlockSpec((MSTEP // 2, L, 2 * HALF), lambda b: (b, 0, 0)),
             ],
-            out_specs=pl.BlockSpec((2, MSTEP, CD, L), lambda b: (0, b, 0, 0)),
-            scratch_shapes=[pltpu.VMEM((2, 2 * CD * MD, 128), F32)],
+            out_specs=pl.BlockSpec((2, CD, MSTEP, L), lambda b: (0, 0, b, 0)),
+            scratch_shapes=[
+                pltpu.VMEM((4 * CD * MD, HALF), F32),
+                pltpu.VMEM((L // 128, 2 * CD * MSTEP, 128), F32),
+            ],
         ),
         name="synthesis",
     )(spec, table)
-    return (grad_field.reshape(TD, FD, C), grad_spectra, grad_mix)
+    grad_mix = call(
+        mix_kernel,
+        shape((K, C, C), F32),
+        2,
+        grid=(LATS,),
+        in_specs=[pl.BlockSpec((1, PAIRS, 16, 128), lambda i: (i, 0, 0, 0))],
+        out_specs=pl.BlockSpec((K, MD, C), lambda i: (0, i, 0)),
+        name="mix_out",
+    )(mix_all)
+    return (grad_field.reshape(TD, FD, C), jnp.transpose(grad_spectra, (0, 2, 1, 3)), grad_mix)
 
 
 def solution(mesh):

time: 158 us -> 144 us (0.911)
  waiting for transfers between devices: 40.3 us -> 33.6 us
  local copies, waits for them, and re-layouts: 8.91 us -> 4.38 us
  starting transfers between devices: 43.5 us -> 41.8 us
    all_to_all x1, waiting for transfers between devices: 16.3 us -> 4.03 us  [on_device(): lax.all_to_all(send.reshape(LONS, FD, CD * TP), 'lon', 0, 0, tiled=True)]
    all_to_all x1, starting transfers between devices: 14.2 us -> 5.62 us  [on_device(): lax.all_to_all(mix_part.reshape(LATS, MD, K * C), 'lat', 0, 0, tiled=True)]
    all_to_all x1, starting transfers between devices: 5.18 us -> 12.2 us  [on_device(): lax.all_to_all(send.reshape(LONS, FD, CD * TP), 'lon', 0, 0, tiled=True)]
    all_to_all x1, waiting for transfers between devices: 0.01 us -> 6.18 us  [on_device(): mix_all = lax.all_to_all(mix_copies, 'lat', 0, 0, tiled=True)]
    unnamed x27 -> x20, local copies, waits for them, and re-layouts: 5.03 us -> 1.56 us
    ppermute x1, starting transfers between devices: 3.1 us -> 0.01 us  [on_device(): left = lax.ppermute(cotangent[:, FD - R:], 'lon', up)]
    ppermute x1, starting transfers between devices: 0.3 us -> 3.32 us  [on_device(): right = lax.ppermute(cotangent[:, :R], 'lon', down)]
    ppermute x1, waiting for transfers between devices: 0.01 us -> 2.62 us  [on_device(): left = lax.ppermute(cotangent[:, FD - R:], 'lon', up)]
  transfers between devices with their start and end apart: 9 -> 9, of which waited for: 6 -> 7; matrix products, arithmetic and copies ran while one was open for 7% -> 4% of each run, Pallas kernels for 21% -> 21%
where the time goes in v2:
time: 144 us; the launch traced here: 142 us
  starting transfers between devices  41.8 us (29%)
  Pallas kernels  41.8 us (29%)
  waiting for transfers between devices  33.6 us (23%)
  blocking collectives  15.5 us (11%)
  other arithmetic  4.51 us (3%)
  local copies, waits for them, and re-layouts  4.38 us (3%)
    all_to_all x1, blocking collectives, on_device(): mix_lon = lax.all_to_all(mix_sum, 'lon', 0, 0, tiled=True)  15.5 us
    all_to_all x1, starting transfers between devices, on_device(): lax.all_to_all(send.reshape(LONS, FD, CD * TP), 'lon', 0, 0, tiled=True)  12.2 us
    pallas_call x1, Pallas kernels, on_device(): call(legendre_kernel, shape((MD // 2, L, 2 * HALF), BF16), 9, grid_spec=p...  11.2 us
    pallas_call x1, Pallas kernels, on_device(): call(synthesis_kernel, shape((2, CD, MD, L), F32), 6, grid_spec=pltpu.Pre...  7.33 us
    all_to_all x1, waiting for transfers between devices, on_device(): lax.all_to_all(spectra.reshape(LATS, 2 * MD, CD * TP), 'lat', 0, 0, tiled...  7.06 us
    all_to_all x1, waiting for transfers between devices, on_device(): mix_all = lax.all_to_all(mix_copies, 'lat', 0, 0, tiled=True)  6.18 us
    all_to_all x1, waiting for transfers between devices, on_device(): mix_row = lax.all_to_all(mix_mine, 'lon', 0, 0, tiled=True)  6.14 us
    all_to_all x1, starting transfers between devices, on_device(): lax.all_to_all(mix_part.reshape(LATS, MD, K * C), 'lat', 0, 0, tiled=True)  5.62 us
  transfers between devices with their start and end apart: 9, of which 7 were waited for; matrix products, arithmetic and copies ran while one was open for 4% of the time, Pallas kernels for 21%

profile of v2, /device:TPU:1, one launch (start us, length us, event | category | flops | bytes accessed | tf_op | source)
XLA Modules:
  0.0 142.3 jit_solution(2266570041595993441)
XLA Ops:
  0.6 1.0 fusion.8
  1.6 3.3 %collective-permute-start.1 = (bf16[24,8,384]{2,1,0:T(8,128)(2,1)S(1)}, bf16[24,8,384]{2,1,0:T(8,128)(2,1)S(1)}, u32[]{:S(2)}, u32[]{:S(2)}) collective-permute-start(bf16[24,8,384]{2,1,0:T(8,128)(2,1)S(1)} %get-tuple-element.29), channel_id=1, source_target_pairs={{1,0},{2,1},{3,2},{4,3},{5,4},{6,5},{7,6},{8,7},{9,8},{10,9},{11,1... | collective-permute-start | bytes 442376 | tf_op jit(solution)/shard_map/ppermute | solution.py:332
  5.0 0.0 collective-permute-start
  5.0 0.7 convert_bitcast_fusion
  5.7 0.9 fusion.6
  6.6 0.1 fusion.1
  6.7 0.1 slice_bitcast_fusion.2
  6.8 0.1 copy.16
  6.9 0.1 copy.17
  6.9 0.1 copy.18
  7.0 0.8 fusion.7
  7.8 0.0 collective-permute-done.1.right
  7.8 0.0 copy-start.5
  7.8 2.6 %collective-permute-done.left = bf16[24,8,384]{2,1,0:T(8,128)(2,1)S(1)} collective-permute-done((bf16[24,8,384]{2,1,0:T(8,128)(2,1)S(1)}, bf16[24,8,384]{2,1,0:T(8,128)(2,1)S(1)}, u32[]{:S(2)}, u32[]{:S(2)}) %collective-permute-start) | collective-permute-done | bytes 147488 | tf_op jit(solution)/shard_map/ppermute | solution.py:331
  10.4 0.0 copy-start.6
  10.4 4.5 %collective-permute-start.2 = (bf16[1,40,384]{2,1,0:T(8,128)(2,1)S(1)}, bf16[1,40,384]{2,1,0:T(8,128)(2,1)S(1)}, u32[]{:S(2)}, u32[]{:S(2)}) collective-permute-start(bf16[1,40,384]{2,1,0:T(8,128)(2,1)S(1)} %pad_maximum_fusion), channel_id=1, source_target_pairs={{0,32},{32,64},{64,96},{96,128},{128,160},{160,192},{192,224},{1,3... | collective-permute-start | bytes 92168 | tf_op jit(solution)/shard_map/ppermute | solution.py:338
  15.0 1.3 collective-permute-start.3
  16.3 2.1 %multiply_add_fusion.tab = f32[24,32,256]{2,1,0:T(8,128)} fusion(f32[24,256]{1,0:T(8,128)} %constant.48, f32[24,32]{1,0:T(8,128)S(1)} %copy.18, f32[24,256]{1,0:T(8,128)} %constant.47, f32[24,32]{1,0:T(8,128)S(1)} %copy.17, f32[24,256]{1,0:T(8,128)} %constant.46, f32[24,32]{1,0:T(8,128)S(1)} %copy.16), kind=kLoop, calls=%fused_computation | loop fusion | flops 983040 | bytes 869376 | tf_op jit(solution)/shard_map/add | solution.py:323
  18.3 0.0 collective-permute-done.2.top
  18.3 0.0 copy-start.8
  18.3 2.8 %collective-permute-done.3.bottom = bf16[1,40,384]{2,1,0:T(8,128)(2,1)S(1)} collective-permute-done((bf16[1,40,384]{2,1,0:T(8,128)(2,1)S(1)}, bf16[1,40,384]{2,1,0:T(8,128)(2,1)S(1)}, u32[]{:S(2)}, u32[]{:S(2)}) %collective-permute-start.3) | collective-permute-done | bytes 30752 | tf_op jit(solution)/shard_map/ppermute | solution.py:339
  21.1 0.0 copy-start.9
  21.1 0.0 copy-done.5
  21.1 0.0 copy-done.6
  21.1 0.0 copy-done.8
  21.1 0.6 copy-done.9
  21.7 4.8 %stencil.1 = (bf16[576,1152]{1,0:T(8,128)(2,1)}, bf16[384,1152]{1,0:T(8,128)(2,1)}) custom-call(f32[24,32,256]{2,1,0:T(8,128)} %multiply_add_fusion.tab, bf16[24,24,384]{2,1,0:T(8,128)(2,1)} %cot.1, bf16[24,8,384]{2,1,0:T(8,128)(2,1)} %copy-done.6, bf16[24,8,384]{2,1,0:T(8,128)(2,1)} %copy-done.5, bf16[1,40,384]{2,1,0:T(8,128)(2,1)} %copy-done.8, ...), custom_call_target="tpu_custom_call" | custom-call | flops 5500000256 | bytes 15000000 | tf_op jit(solution)/shard_map/stencil/pallas_call | solution.py:343
  26.6 5.6 %all-to-all-start.1 = ((bf16[8,48,1152]{2,1,0:T(8,128)(2,1)}), bf16[8,48,1152]{2,1,0:T(8,128)(2,1)S(1)}, u32[]{:S(2)}, u32[]{:S(2)}) async-start(bf16[8,48,1152]{2,1,0:T(8,128)(2,1)} %bitcast.17), calls=%async_computation.1 | async-start | bytes 1769472 | tf_op jit(solution)/shard_map/all_to_all | solution.py:350
  32.2 0.8 dynamic_slice.7
  32.9 0.0 copy-start.7
  32.9 4.6 %grad_field.1 = (bf16[576,384]{1,0:T(8,128)(2,1)}, bf16[768,384]{1,0:T(8,128)(2,1)}) custom-call(s32[1]{0:T(128)} %bitcast.pos, bf16[576,1152]{1,0:T(8,128)(2,1)} %get-tuple-element.15.g, bf16[576,384]{1,0:T(8,128)(2,1)} %bitcast.21, bf16[3,384,384]{2,1,0:T(8,128)(2,1)} %mix.1), custom_call_target="tpu_custom_call" | custom-call | flops 5500000256 | bytes 15000000 | tf_op jit(solution)/shard_map/grad_field/pallas_call | solution.py:354
  37.6 4.8 %all-to-all-done.1.parts = bf16[8,48,1152]{2,1,0:T(8,128)(2,1)S(1)} async-done(((bf16[8,48,1152]{2,1,0:T(8,128)(2,1)}), bf16[8,48,1152]{2,1,0:T(8,128)(2,1)S(1)}, u32[]{:S(2)}, u32[]{:S(2)}) %all-to-all-start.1) | async-done | bytes 884768 | tf_op jit(solution)/shard_map/all_to_all | solution.py:350
  42.4 0.0 copy-start
  42.4 12.2 %all-to-all-start = ((bf16[32,24,384]{2,1,0:T(8,128)(2,1)}), bf16[32,24,384]{2,1,0:T(8,128)(2,1)S(1)}, u32[]{:S(2)}, u32[]{:S(2)}) async-start(bf16[32,24,384]{2,1,0:T(8,128)(2,1)} %bitcast.19), calls=%async_computation | async-start | bytes 1179648 | tf_op jit(solution)/shard_map/all_to_all | solution.py:366
  54.6 0.0 copy-done.7
  54.6 0.7 multiply_add_fusion.1.logscale
  55.3 11.2 %legendre.1.leg = bf16[24,384,256]{2,1,0:T(8,128)(2,1)} custom-call(s32[1]{0:T(128)} %bitcast.pos, f32[1,128]{1,0:T(1,128)} %constant.40.clone.cosines, f32[48,128]{1,0:T(8,128)} %multiply_add_fusion.1.logscale), custom_call_target="tpu_custom_call" | custom-call | flops 9900000256 | bytes 27000000 | tf_op jit(solution)/shard_map/legendre/pallas_call | solution.py:375
  66.5 0.0 copy-done
  66.5 1.9 %mix_sum_lat.1 = bf16[32,16,128]{2,1,0:T(8,128)(2,1)} custom-call(bf16[8,48,1152]{2,1,0:T(8,128)(2,1)} %copy-done), custom_call_target="tpu_custom_call" | custom-call | flops 2200000000 | bytes 6000000 | tf_op jit(solution)/shard_map/mix_sum_lat/pallas_call | solution.py:368
  68.5 4.0 %all-to-all-done = bf16[32,24,384]{2,1,0:T(8,128)(2,1)S(1)} async-done(((bf16[32,24,384]{2,1,0:T(8,128)(2,1)}), bf16[32,24,384]{2,1,0:T(8,128)(2,1)S(1)}, u32[]{:S(2)}, u32[]{:S(2)}) %all-to-all-start) | async-done | bytes 589856 | tf_op jit(solution)/shard_map/all_to_all | solution.py:366
  72.5 0.0 copy-start.2
  72.5 15.5 %all_to_all.30.parts = bf16[32,16,128]{2,1,0:T(8,128)(2,1)} all-to-all(bf16[32,16,128]{2,1,0:T(8,128)(2,1)} %mix_sum_lat.1), channel_id=1, replica_groups=mesh['lat'=8,'lon'=32] {'lon'}, dimensions={0} | all-to-all | bytes 262144 | tf_op jit(solution)/shard_map/all_to_all | solution.py:399
  88.0 1.6 %mix_sum_lon.1 = bf16[32,16,128]{2,1,0:T(8,128)(2,1)} custom-call(bf16[32,16,128]{2,1,0:T(8,128)(2,1)} %all_to_all.30.parts), custom_call_target="tpu_custom_call" | custom-call | flops 2200000000 | bytes 6000000 | tf_op jit(solution)/shard_map/mix_sum_lon/pallas_call | solution.py:403
  89.6 0.0 copy-done.2
  89.6 5.1 %all-to-all-start.3 = ((bf16[32,16,128]{2,1,0:T(8,128)(2,1)}), bf16[32,16,128]{2,1,0:T(8,128)(2,1)S(1)}, u32[]{:S(2)}, u32[]{:S(2)}) async-start(bf16[32,16,128]{2,1,0:T(8,128)(2,1)} %mix_sum_lon.1), calls=%async_computation.3 | async-start | bytes 262144 | tf_op jit(solution)/shard_map/all_to_all | solution.py:404
  94.7 3.0 %dft.1 = bf16[768,384]{1,0:T(8,128)(2,1)} custom-call(bf16[768,768]{1,0:T(8,128)(2,1)} %constant.41.clone.rows, bf16[768,384]{1,0:T(8,128)(2,1)} %bitcast.18), custom_call_target="tpu_custom_call" | custom-call | flops 2200000000 | bytes 6000000 | tf_op jit(solution)/shard_map/dft/pallas_call | solution.py:400
  97.7 6.1 %all-to-all-done.3.part = bf16[32,16,128]{2,1,0:T(8,128)(2,1)S(1)} async-done(((bf16[32,16,128]{2,1,0:T(8,128)(2,1)}), bf16[32,16,128]{2,1,0:T(8,128)(2,1)S(1)}, u32[]{:S(2)}, u32[]{:S(2)}) %all-to-all-start.3) | async-done | bytes 131104 | tf_op jit(solution)/shard_map/all_to_all | solution.py:404
  103.9 0.0 copy-start.4
  103.9 4.1 %all-to-all-start.4 = ((bf16[8,96,384]{2,1,0:T(8,128)(2,1)}), bf16[8,96,384]{2,1,0:T(8,128)(2,1)S(1)}, u32[]{:S(2)}, u32[]{:S(2)}) async-start(bf16[8,96,384]{2,1,0:T(8,128)(2,1)} %bitcast.20), calls=%async_computation.4 | async-start | bytes 1179648 | tf_op jit(solution)/shard_map/all_to_all | solution.py:407
  107.9 0.0 copy-done.4
  108.0 1.9 %mix_copies.1 = bf16[8,27,16,128]{3,2,1,0:T(8,128)(2,1)} custom-call(bf16[32,16,128]{2,1,0:T(8,128)(2,1)} %copy-done.4), custom_call_target="tpu_custom_call" | custom-call | flops 2200000000 | bytes 6000000 | tf_op jit(solution)/shard_map/mix_copies/pallas_call | solution.py:408
  109.9 7.1 %all-to-all-done.4.spec = bf16[8,96,384]{2,1,0:T(8,128)(2,1)S(1)} async-done(((bf16[8,96,384]{2,1,0:T(8,128)(2,1)}), bf16[8,96,384]{2,1,0:T(8,128)(2,1)S(1)}, u32[]{:S(2)}, u32[]{:S(2)}) %all-to-all-start.4) | async-done | bytes 589856 | tf_op jit(solution)/shard_map/all_to_all | solution.py:407
  116.9 0.0 copy-start.3
  116.9 5.6 %all-to-all-start.5 = ((bf16[8,27,16,128]{3,2,1,0:T(8,128)(2,1)}), bf16[8,27,16,128]{3,2,1,0:T(8,128)(2,1)S(1)}, u32[]{:S(2)}, u32[]{:S(2)}) async-start(bf16[8,27,16,128]{3,2,1,0:T(8,128)(2,1)} %mix_copies.1), calls=%async_computation.5 | async-start | bytes 1769472 | tf_op jit(solution)/shard_map/all_to_all | solution.py:410
  122.5 0.0 copy-done.3
  122.6 7.3 %synthesis.1 = f32[2,12,48,384]{3,2,1,0:T(8,128)} custom-call(bf16[8,96,384]{2,1,0:T(8,128)(2,1)} %copy-done.3, bf16[24,384,256]{2,1,0:T(8,128)(2,1)} %legendre.1.leg), custom_call_target="tpu_custom_call" | custom-call | flops 6600000000 | bytes 18000000 | tf_op jit(solution)/shard_map/synthesis/pallas_call | solution.py:412
  129.9 6.2 %all-to-all-done.5.parts = bf16[8,27,16,128]{3,2,1,0:T(8,128)(2,1)S(1)} async-done(((bf16[8,27,16,128]{3,2,1,0:T(8,128)(2,1)}), bf16[8,27,16,128]{3,2,1,0:T(8,128)(2,1)S(1)}, u32[]{:S(2)}, u32[]{:S(2)}) %all-to-all-start.5) | async-done | bytes 884768 | tf_op jit(solution)/shard_map/all_to_all | solution.py:410
  136.1 0.0 copy-start.1
  136.1 0.9 copy-done.1
  137.0 5.3 %mix_out.1 = f32[3,384,384]{2,1,0:T(8,128)} custom-call(bf16[8,27,16,128]{3,2,1,0:T(8,128)(2,1)} %copy-done.1), custom_call_target="tpu_custom_call" | custom-call | flops 2200000000 | bytes 6000000 | tf_op jit(solution)/shard_map/mix_out/pallas_call | solution.py:431
  (5 shorter events, 0.0 us)
Async XLA Ops:
  1.6 6.1 %collective-permute-start.1 = (bf16[24,8,384]{2,1,0:T(8,128)(2,1)S(1)}, bf16[24,8,384]{2,1,0:T(8,128)(2,1)S(1)}, u32[]{:S(2)}, u32[]{:S(2)}) collective-permute-start(bf16[24,8,384]{2,1,0:T(8,128)(2,1)S(1)} %get-tuple-element.29), channel_id=1, source_target_pairs={{1,0},{2,1},{3,2},{4,3},{5,4},{6,5},{7,6},{8,7},{9,8},{10,9},{11,1... | collective-permute-start | bytes 442376 | tf_op jit(solution)/shard_map/ppermute | solution.py:332
  5.0 5.4 %collective-permute-start = (bf16[24,8,384]{2,1,0:T(8,128)(2,1)S(1)}, bf16[24,8,384]{2,1,0:T(8,128)(2,1)S(1)}, u32[]{:S(2)}, u32[]{:S(2)}) collective-permute-start(bf16[24,8,384]{2,1,0:T(8,128)(2,1)S(1)} %get-tuple-element.30), channel_id=1, source_target_pairs={{0,1},{1,2},{2,3},{3,4},{4,5},{5,6},{6,7},{7,8},{8,9},{9,10},{10,1... | collective-permute-start | bytes 442376 | tf_op jit(solution)/shard_map/ppermute | solution.py:331
  7.8 13.3 %copy-start.5 = (bf16[24,8,384]{2,1,0:T(8,128)(2,1)}, bf16[24,8,384]{2,1,0:T(8,128)(2,1)S(1)}, u32[]{:S(2)}) copy-start(bf16[24,8,384]{2,1,0:T(8,128)(2,1)S(1)} %collective-permute-done.1.right) | copy-start | bytes 442372
  10.4 10.7 %copy-start.6 = (bf16[24,8,384]{2,1,0:T(8,128)(2,1)}, bf16[24,8,384]{2,1,0:T(8,128)(2,1)S(1)}, u32[]{:S(2)}) copy-start(bf16[24,8,384]{2,1,0:T(8,128)(2,1)S(1)} %collective-permute-done.left) | copy-start | bytes 442372
  10.4 7.9 %collective-permute-start.2 = (bf16[1,40,384]{2,1,0:T(8,128)(2,1)S(1)}, bf16[1,40,384]{2,1,0:T(8,128)(2,1)S(1)}, u32[]{:S(2)}, u32[]{:S(2)}) collective-permute-start(bf16[1,40,384]{2,1,0:T(8,128)(2,1)S(1)} %pad_maximum_fusion), channel_id=1, source_target_pairs={{0,32},{32,64},{64,96},{96,128},{128,160},{160,192},{192,224},{1,3... | collective-permute-start | bytes 92168 | tf_op jit(solution)/shard_map/ppermute | solution.py:338
  15.0 6.1 %collective-permute-start.3 = (bf16[1,40,384]{2,1,0:T(8,128)(2,1)S(1)}, bf16[1,40,384]{2,1,0:T(8,128)(2,1)S(1)}, u32[]{:S(2)}, u32[]{:S(2)}) collective-permute-start(bf16[1,40,384]{2,1,0:T(8,128)(2,1)S(1)} %pad_maximum_fusion.1), channel_id=1, source_target_pairs={{32,0},{64,32},{96,64},{128,96},{160,128},{192,160},{224,192},{33,... | collective-permute-start | bytes 92168 | tf_op jit(solution)/shard_map/ppermute | solution.py:339
  18.3 2.8 %copy-start.8 = (bf16[1,40,384]{2,1,0:T(8,128)(2,1)}, bf16[1,40,384]{2,1,0:T(8,128)(2,1)S(1)}, u32[]{:S(2)}) copy-start(bf16[1,40,384]{2,1,0:T(8,128)(2,1)S(1)} %collective-permute-done.2.top) | copy-start | bytes 92164
  21.1 0.6 copy-start.9
  26.6 15.8 %all-to-all-start.1 = ((bf16[8,48,1152]{2,1,0:T(8,128)(2,1)}), bf16[8,48,1152]{2,1,0:T(8,128)(2,1)S(1)}, u32[]{:S(2)}, u32[]{:S(2)}) async-start(bf16[8,48,1152]{2,1,0:T(8,128)(2,1)} %bitcast.17), calls=%async_computation.1 | async-start | bytes 1769472 | tf_op jit(solution)/shard_map/all_to_all | solution.py:350
  32.9 21.7 %copy-start.7 = (f32[128]{0:T(128)S(1)}, f32[128]{0:T(128)}, u32[]{:S(2)}) copy-start(f32[128]{0:T(128)} %constant.49) | copy-start | bytes 1540
  42.4 24.2 %copy-start = (bf16[8,48,1152]{2,1,0:T(8,128)(2,1)}, bf16[8,48,1152]{2,1,0:T(8,128)(2,1)S(1)}, u32[]{:S(2)}) copy-start(bf16[8,48,1152]{2,1,0:T(8,128)(2,1)S(1)} %all-to-all-done.1.parts) | copy-start | bytes 2654212
  42.4 30.1 %all-to-all-start = ((bf16[32,24,384]{2,1,0:T(8,128)(2,1)}), bf16[32,24,384]{2,1,0:T(8,128)(2,1)S(1)}, u32[]{:S(2)}, u32[]{:S(2)}) async-start(bf16[32,24,384]{2,1,0:T(8,128)(2,1)} %bitcast.19), calls=%async_computation | async-start | bytes 1179648 | tf_op jit(solution)/shard_map/all_to_all | solution.py:366
  72.5 17.1 %copy-start.2 = (bf16[32,24,384]{2,1,0:T(8,128)(2,1)}, bf16[32,24,384]{2,1,0:T(8,128)(2,1)S(1)}, u32[]{:S(2)}) copy-start(bf16[32,24,384]{2,1,0:T(8,128)(2,1)S(1)} %all-to-all-done) | copy-start | bytes 1769476
  89.6 14.3 %all-to-all-start.3 = ((bf16[32,16,128]{2,1,0:T(8,128)(2,1)}), bf16[32,16,128]{2,1,0:T(8,128)(2,1)S(1)}, u32[]{:S(2)}, u32[]{:S(2)}) async-start(bf16[32,16,128]{2,1,0:T(8,128)(2,1)} %mix_sum_lon.1), calls=%async_computation.3 | async-start | bytes 262144 | tf_op jit(solution)/shard_map/all_to_all | solution.py:404
  103.9 4.1 %copy-start.4 = (bf16[32,16,128]{2,1,0:T(8,128)(2,1)}, bf16[32,16,128]{2,1,0:T(8,128)(2,1)S(1)}, u32[]{:S(2)}) copy-start(bf16[32,16,128]{2,1,0:T(8,128)(2,1)S(1)} %all-to-all-done.3.part) | copy-start | bytes 393220
  103.9 13.1 %all-to-all-start.4 = ((bf16[8,96,384]{2,1,0:T(8,128)(2,1)}), bf16[8,96,384]{2,1,0:T(8,128)(2,1)S(1)}, u32[]{:S(2)}, u32[]{:S(2)}) async-start(bf16[8,96,384]{2,1,0:T(8,128)(2,1)} %bitcast.20), calls=%async_computation.4 | async-start | bytes 1179648 | tf_op jit(solution)/shard_map/all_to_all | solution.py:407
  116.9 5.6 %copy-start.3 = (bf16[8,96,384]{2,1,0:T(8,128)(2,1)}, bf16[8,96,384]{2,1,0:T(8,128)(2,1)S(1)}, u32[]{:S(2)}) copy-start(bf16[8,96,384]{2,1,0:T(8,128)(2,1)S(1)} %all-to-all-done.4.spec) | copy-start | bytes 1769476
  116.9 19.1 %all-to-all-start.5 = ((bf16[8,27,16,128]{3,2,1,0:T(8,128)(2,1)}), bf16[8,27,16,128]{3,2,1,0:T(8,128)(2,1)S(1)}, u32[]{:S(2)}, u32[]{:S(2)}) async-start(bf16[8,27,16,128]{3,2,1,0:T(8,128)(2,1)} %mix_copies.1), calls=%async_computation.5 | async-start | bytes 1769472 | tf_op jit(solution)/shard_map/all_to_all | solution.py:410
  136.1 0.9 copy-start.1

commit v3 on v2

--- a/solution.py
+++ b/solution.py
@@ -27,6 +27,7 @@
 MD = M // LATS
 XW = FD + 2 * R
 TP = 32
+FP = FD + 8
 QUAD = 4
 F32 = jnp.float32
 BF16 = jnp.bfloat16
@@ -41,6 +42,10 @@
         compiler_params=pltpu.CompilerParams(vmem_limit_bytes=VMEM_BYTES),
         **kw,
     )
+
+
+def near(array):
+    return pltpu.with_memory_space_constraint(array, pltpu.VMEM)
 
 
 def shape(dims, dtype):
@@ -127,13 +132,21 @@
             ]
             for fr, part in enumerate(swap_blocks(parts)):
                 send[q, pl.ds(fq * 4 + fr, LONS, stride=FD), :] = part
+    send_out[:, FD:, :] = jnp.zeros((LONS, FP - FD, CD * TP), BF16)
     for q in range(CD // 4):
-        send_out[:, q * 128:(q + 1) * 128] = send[q].astype(BF16)
+        send_out[:, :FD, q * 128:(q + 1) * 128] = send[q].reshape(LONS, FD, 128).astype(BF16)
 
 
 def dft_kernel(rows, columns, out):
     got = jnp.dot(rows[...], columns[...], preferred_element_type=F32)
-    out[...] = (got * (1.0 / math.sqrt(NLON))).astype(BF16)
+    got = (got * (1.0 / math.sqrt(NLON))).astype(BF16)
+    total = jnp.zeros((FP - FD, 2 * 128), F32)
+    for j in range(LONS):
+        total = total + columns[j * FP + 16:(j + 1) * FP, :256].astype(F32)[8:]
+    total = jnp.concatenate([total, jnp.zeros((FP - FD, CD * TP - 256), F32)], axis=1).astype(BF16)
+    for i in range(LATS):
+        out[i, :2 * MD, :] = got[i * 2 * MD:(i + 1) * 2 * MD]
+        out[i, 2 * MD:, :] = total
 
 
 HALF = LATS // 2 * TP
@@ -193,8 +206,8 @@
     def _():
         for q in range(CD // 4):
             span = slice(q * 128, (q + 1) * 128)
-            north = [spec[i, :, span].astype(F32) for i in range(LATS // 2)]
-            south = [spec[LATS - 1 - i, :, span].astype(F32) for i in range(LATS // 2)]
+            north = [spec[i, :2 * MD, span].astype(F32) for i in range(LATS // 2)]
+            south = [spec[LATS - 1 - i, :2 * MD, span].astype(F32) for i in range(LATS // 2)]
             for odd in range(2):
                 parts = [n - s if odd else n + s for n, s in zip(north, south)]
                 for cr, part in enumerate(swap_blocks(parts)):
@@ -229,49 +242,47 @@
 
 
 TILES = (MD // 8) * (K * C // 128)
-
-
-def sum_lat_kernel(parts, out):
+PAIRS = TILES // 2
+
+
+def sum_lat_kernel(parts, send, out, rows, sem):
     total = parts[0].astype(F32)
     for i in range(1, LATS):
         total = total + parts[i].astype(F32)
+    total = total.astype(BF16)
     lanes = K * C // 128
-    for n in range(0, 2 * LONS, 2):
-        tiles = []
-        for tile in (n, n + 1):
-            if tile < TILES:
-                row, col = divmod(tile, lanes)
-                tiles.append(total[row * 8:(row + 1) * 8, col * 128:(col + 1) * 128])
-            else:
-                tiles.append(jnp.zeros((8, 128), F32))
-        out[n // 2] = jnp.concatenate(tiles, axis=0).astype(BF16)
-
-
-def sum_lon_kernel(parts, out):
-    total = parts[0].astype(F32)
-    for j in range(1, LONS):
-        total = total + parts[j].astype(F32)
-    total = total.astype(BF16)
+    rows[...] = jnp.zeros_like(rows)
+    for tile in range(TILES):
+        row, col = divmod(tile, lanes)
+        side = (tile % 2) * 128
+        rows[tile // 2, :, side:side + 128] = total[row * 8:(row + 1) * 8, col * 128:(col + 1) * 128]
+    copy = pltpu.make_async_copy(rows, out.at[:, FD:, :], sem)
+    copy.start()
+    copy.wait()
+
+
+def copies_kernel(spec, out):
+    part = spec[:, 2 * MD:, :256]
     for j in range(LONS):
-        out[j] = total
-
-
-PAIRS = TILES // 2
-
-
-def copies_kernel(part, out):
+        out[j] = part
+
+
+def mix_kernel(parts, out, rows, sems):
+    lanes = K * C // 128
+    copies = []
     for i in range(LATS):
-        out[i] = part[:PAIRS]
-
-
-def mix_kernel(parts, out):
-    lanes = K * C // 128
-    for n in range(0, TILES, 2):
-        pair = parts[0, n // 2].astype(F32)
-        for half in range(2):
-            row, col = divmod(n + half, lanes)
+        for tile in range(TILES):
+            row, col = divmod(tile, lanes)
             k, d = divmod(col, C // 128)
-            out[k, row * 8:row * 8 + 8, d * 128:(d + 1) * 128] = pair[half * 8:half * 8 + 8]
+            side = (tile % 2) * 128
+            rows[k, i * MD + row * 8:i * MD + row * 8 + 8, d * 128:(d + 1) * 128] = parts[
+                tile // 2, i, :, side:side + 128
+            ].astype(F32)
+        span = pl.ds(i * MD, MD)
+        copies.append(pltpu.make_async_copy(rows.at[:, span], out.at[:, span], sems.at[i]))
+        copies[-1].start()
+    for copy in copies:
+        copy.wait()
 
 
 def dft_rows():
@@ -280,7 +291,10 @@
     part = np.broadcast_to(np.arange(2).reshape(1, 2, 1), (LATS, 2, MD)).reshape(-1)
     angle = 2.0 * np.pi / NLON * ((order[:, None] * np.arange(NLON)[None, :]) % NLON)
     angle = angle.astype(np.float32)
-    return np.where(part[:, None] == 0, np.cos(angle), -np.sin(angle)).astype(ml_dtypes.bfloat16)
+    rows = np.where(part[:, None] == 0, np.cos(angle), -np.sin(angle))
+    padded = np.zeros((2 * M, LONS, FP), np.float32)
+    padded[:, :, :FD] = rows.reshape(2 * M, LONS, FD)
+    return padded.reshape(2 * M, LONS * FP).astype(ml_dtypes.bfloat16)
 
 
 def latitudes():
@@ -338,22 +352,23 @@
     top = lax.ppermute(edge_rows[1], "lat", north)
     bottom = lax.ppermute(edge_rows[0], "lat", south)
 
+    whole = pl.BlockSpec(memory_space=pltpu.VMEM)
     tab = tap_table(taps, offsets, counts, lat_pos * TD)
     cells = TD * FD
     grown, mix_part = call(
         stencil_kernel,
         (shape((cells, K * C), BF16), shape((C, K * C), BF16)),
         5,
+        in_specs=[whole] * 7,
         scratch_shapes=[pltpu.VMEM((TD + 2, XW, C), F32), pltpu.VMEM((K * QUAD * FD, 256), F32)],
         name="stencil",
-    )(tab, cotangent, left, right, top, bottom, field.reshape(cells, C))
+    )(near(tab), cotangent, near(left), near(right), near(top), near(bottom), field.reshape(cells, C))
     mix_lat = lax.all_to_all(mix_part.reshape(LATS, MD, K * C), "lat", 0, 0, tiled=True)
 
     pos = jnp.reshape(lat_pos, (1,)).astype(jnp.int32)
-    whole = pl.BlockSpec(memory_space=pltpu.VMEM)
     grad_field, send = call(
         field_kernel,
-        (shape((cells, C), BF16), shape((LONS * FD, CD * TP), BF16)),
+        (shape((cells, C), BF16), shape((LONS, FP, CD * TP), BF16)),
         5,
         in_specs=[pl.BlockSpec(memory_space=pltpu.SMEM), whole, whole, whole],
         scratch_shapes=[
@@ -363,9 +378,19 @@
         ],
         name="grad_field",
     )(pos, grown, cotangent.reshape(cells, C), mix_weight)
-    columns = lax.all_to_all(send.reshape(LONS, FD, CD * TP), "lon", 0, 0, tiled=True)
-
-    mix_sum = call(sum_lat_kernel, shape((LONS, 16, 128), BF16), 2, name="mix_sum_lat")(mix_lat)
+    anywhere = pl.BlockSpec(memory_space=pl.ANY)
+    send = call(
+        sum_lat_kernel,
+        shape((LONS, FP, CD * TP), BF16),
+        2,
+        in_specs=[whole, anywhere],
+        out_specs=anywhere,
+        scratch_shapes=[pltpu.VMEM((LONS, FP - FD, CD * TP), BF16), pltpu.SemaphoreType.DMA],
+        input_output_aliases={1: 0},
+        name="mix_sum_lat",
+    )(near(mix_lat), send)
+    columns = lax.all_to_all(send, "lon", 0, 0, tiled=True)
+
     cosine, logsine = latitudes()
     first_order = lat_pos * MD
     seeds = lax.dynamic_slice_in_dim(jnp.asarray(seed_logs()), first_order, MD, 0)
@@ -394,20 +419,14 @@
         ),
         name="legendre",
     )(pos, jnp.asarray(cosine), logscale)
-    columns, table, mix_sum = lax.optimization_barrier((columns, table, mix_sum))
-
-    mix_lon = lax.all_to_all(mix_sum, "lon", 0, 0, tiled=True)
-    spectra = call(dft_kernel, shape((NLON, CD * TP), BF16), 2, name="dft")(
-        jnp.asarray(dft_rows()), columns.reshape(NLON, CD * TP)
+    columns, table = lax.optimization_barrier((columns, table))
+
+    spectra = call(dft_kernel, shape((LATS, 2 * MD + FP - FD, CD * TP), BF16), 2, in_specs=[whole, whole], name="dft")(
+        near(jnp.asarray(dft_rows())), near(columns.reshape(LONS * FP, CD * TP))
     )
-    mix_mine = call(sum_lon_kernel, shape((LONS, 16, 128), BF16), 2, name="mix_sum_lon")(mix_lon)
-    mix_row = lax.all_to_all(mix_mine, "lon", 0, 0, tiled=True)
-    mix_row, spectra = lax.optimization_barrier((mix_row, spectra))
-
-    spec = lax.all_to_all(spectra.reshape(LATS, 2 * MD, CD * TP), "lat", 0, 0, tiled=True)
-    mix_copies = call(copies_kernel, shape((LATS, PAIRS, 16, 128), BF16), 2, name="mix_copies")(mix_row)
-    spec, mix_copies = lax.optimization_barrier((spec, mix_copies))
-    mix_all = lax.all_to_all(mix_copies, "lat", 0, 0, tiled=True)
+    spec = lax.all_to_all(spectra, "lat", 0, 0, tiled=True)
+    mix_copies = call(copies_kernel, shape((LONS, LATS, 8, 256), BF16), 2, name="mix_copies")(spec)
+    mix_all = lax.all_to_all(mix_copies, "lon", 0, 0, tiled=True)
 
     grad_spectra = call(
         synthesis_kernel,
@@ -417,7 +436,7 @@
             num_scalar_prefetch=0,
             grid=(MD // MSTEP,),
             in_specs=[
-                pl.BlockSpec((LATS, 2 * MD, CD * TP), lambda b: (0, 0, 0)),
+                pl.BlockSpec((LATS, 2 * MD + FP - FD, CD * TP), lambda b: (0, 0, 0)),
                 pl.BlockSpec((MSTEP // 2, L, 2 * HALF), lambda b: (b, 0, 0)),
             ],
             out_specs=pl.BlockSpec((2, CD, MSTEP, L), lambda b: (0, 0, b, 0)),
@@ -432,11 +451,11 @@
         mix_kernel,
         shape((K, C, C), F32),
         2,
-        grid=(LATS,),
-        in_specs=[pl.BlockSpec((1, PAIRS, 16, 128), lambda i: (i, 0, 0, 0))],
-        out_specs=pl.BlockSpec((K, MD, C), lambda i: (0, i, 0)),
+        in_specs=[whole],
+        out_specs=anywhere,
+        scratch_shapes=[pltpu.VMEM((K, C, C), F32), pltpu.SemaphoreType.DMA((LATS,))],
         name="mix_out",
-    )(mix_all)
+    )(near(mix_all))
     return (grad_field.reshape(TD, FD, C), jnp.transpose(grad_spectra, (0, 2, 1, 3)), grad_mix)
 
 

time: 144 us -> 133 us (0.924)
  Pallas kernels: 41.8 us -> 33.9 us
  waiting for transfers between devices: 33.6 us -> 39.5 us
  starting transfers between devices: 41.8 us -> 36 us
  blocking collectives: 15.5 us -> 13.9 us
  local copies, waits for them, and re-layouts: 4.38 us -> 2.83 us
    pallas_call x6 -> x5, Pallas kernels: 18.4 us -> 10.8 us  [the longest x1 4.72 us: on_device(): call(field_kernel, (shape((cells, C), BF16), shape((LONS, FP, CD * TP), B...]
    all_to_all x4 -> x2, starting transfers between devices: 27 us -> 21.2 us  [the longest x1 12.2 us: on_device(): columns = lax.all_to_all(send, 'lon', 0, 0, tiled=True)]
    all_to_all x4 -> x2, waiting for transfers between devices: 23.4 us -> 27.7 us  [the longest x1 19.1 us: on_device(): mix_all = lax.all_to_all(mix_copies, 'lon', 0, 0, tiled=True)]
    unnamed x20 -> x4, local copies, waits for them, and re-layouts: 1.56 us -> 0.01 us
    all_to_all x1, blocking collectives: 15.5 us -> 13.9 us  [on_device(): spec = lax.all_to_all(spectra, 'lat', 0, 0, tiled=True)]
  transfers between devices with their start and end apart: 9 -> 7, of which waited for: 7 -> 5; matrix products, arithmetic and copies ran while one was open for 4% -> 4% of each run, Pallas kernels for 21% -> 18%
where the time goes in v3:
time: 133 us; the launch traced here: 130 us
  waiting for transfers between devices  39.5 us (30%)
  starting transfers between devices  36 us (27%)
  Pallas kernels  33.9 us (25%)
  blocking collectives  13.9 us (10%)
  other arithmetic  3.6 us (3%)
  local copies, waits for them, and re-layouts  2.83 us (2%)
    all_to_all x1, waiting for transfers between devices, on_device(): mix_all = lax.all_to_all(mix_copies, 'lon', 0, 0, tiled=True)  19.1 us
    all_to_all x1, blocking collectives, on_device(): spec = lax.all_to_all(spectra, 'lat', 0, 0, tiled=True)  13.9 us
    all_to_all x1, starting transfers between devices, on_device(): columns = lax.all_to_all(send, 'lon', 0, 0, tiled=True)  12.2 us
    pallas_call x1, Pallas kernels, on_device(): call(legendre_kernel, shape((MD // 2, L, 2 * HALF), BF16), 9, grid_spec=p...  11.3 us
    all_to_all x1, starting transfers between devices, on_device(): mix_all = lax.all_to_all(mix_copies, 'lon', 0, 0, tiled=True)  8.97 us
    all_to_all x1, waiting for transfers between devices, on_device(): columns = lax.all_to_all(send, 'lon', 0, 0, tiled=True)  8.6 us
    pallas_call x1, Pallas kernels, on_device(): call(synthesis_kernel, shape((2, CD, MD, L), F32), 6, grid_spec=pltpu.Pre...  7.35 us
    all_to_all x1, starting transfers between devices, on_device(): lax.all_to_all(mix_part.reshape(LATS, MD, K * C), 'lat', 0, 0, tiled=True)  5.62 us
  transfers between devices with their start and end apart: 7, of which 5 were waited for; matrix products, arithmetic and copies ran while one was open for 4% of the time, Pallas kernels for 18%

profile of v3, /device:TPU:1, one launch (start us, length us, event | category | flops | bytes accessed | tf_op | source)
XLA Modules:
  0.0 130.5 jit_solution(11446223193575416267)
XLA Ops:
  0.6 1.0 fusion.8
  1.6 3.3 %collective-permute-start.1 = (bf16[24,8,384]{2,1,0:T(8,128)(2,1)S(1)}, bf16[24,8,384]{2,1,0:T(8,128)(2,1)S(1)}, u32[]{:S(2)}, u32[]{:S(2)}) collective-permute-start(bf16[24,8,384]{2,1,0:T(8,128)(2,1)S(1)} %get-tuple-element.19), channel_id=1, source_target_pairs={{1,0},{2,1},{3,2},{4,3},{5,4},{6,5},{7,6},{8,7},{9,8},{10,9},{11,1... | collective-permute-start | bytes 442376 | tf_op jit(solution)/shard_map/ppermute | solution.py:346
  5.0 0.0 collective-permute-start
  5.0 0.7 convert_bitcast_fusion
  5.7 0.9 fusion.6
  6.6 0.1 fusion.1
  6.7 0.1 slice_bitcast_fusion.2
  6.8 0.1 copy.17
  6.9 0.1 copy.18
  6.9 0.1 copy.19
  7.0 0.8 fusion.7
  7.8 0.0 collective-permute-done.1.right
  7.8 2.6 %collective-permute-done.left = bf16[24,8,384]{2,1,0:T(8,128)(2,1)S(1)} collective-permute-done((bf16[24,8,384]{2,1,0:T(8,128)(2,1)S(1)}, bf16[24,8,384]{2,1,0:T(8,128)(2,1)S(1)}, u32[]{:S(2)}, u32[]{:S(2)}) %collective-permute-start) | collective-permute-done | bytes 147488 | tf_op jit(solution)/shard_map/ppermute | solution.py:345
  10.4 4.5 %collective-permute-start.2 = (bf16[1,40,384]{2,1,0:T(8,128)(2,1)S(1)}, bf16[1,40,384]{2,1,0:T(8,128)(2,1)S(1)}, u32[]{:S(2)}, u32[]{:S(2)}) collective-permute-start(bf16[1,40,384]{2,1,0:T(8,128)(2,1)S(1)} %pad_maximum_fusion), channel_id=1, source_target_pairs={{0,32},{32,64},{64,96},{96,128},{128,160},{160,192},{192,224},{1,3... | collective-permute-start | bytes 92168 | tf_op jit(solution)/shard_map/ppermute | solution.py:352
  15.0 1.3 collective-permute-start.3
  16.3 1.2 multiply_add_fusion.tab
  17.4 0.0 collective-permute-done.2.top
  17.4 3.7 %collective-permute-done.3.bottom = bf16[1,40,384]{2,1,0:T(8,128)(2,1)S(1)} collective-permute-done((bf16[1,40,384]{2,1,0:T(8,128)(2,1)S(1)}, bf16[1,40,384]{2,1,0:T(8,128)(2,1)S(1)}, u32[]{:S(2)}, u32[]{:S(2)}) %collective-permute-start.3) | collective-permute-done | bytes 30752 | tf_op jit(solution)/shard_map/ppermute | solution.py:353
  21.1 4.4 %stencil.1 = (bf16[576,1152]{1,0:T(8,128)(2,1)}, bf16[384,1152]{1,0:T(8,128)(2,1)}) custom-call(f32[24,32,256]{2,1,0:T(8,128)S(1)} %multiply_add_fusion.tab, bf16[24,24,384]{2,1,0:T(8,128)(2,1)} %cot.1, bf16[24,8,384]{2,1,0:T(8,128)(2,1)S(1)} %collective-permute-done.left, bf16[24,8,384]{2,1,0:T(8,128)(2,1)S(1)} %collective-permute-done.1.right, ...), custom_call_target="tpu_custom_call" | custom-call | flops 5500000256 | bytes 15000000 | tf_op jit(solution)/shard_map/stencil/pallas_call | solution.py:358
  25.5 5.6 %all-to-all-start = ((bf16[8,48,1152]{2,1,0:T(8,128)(2,1)}), bf16[8,48,1152]{2,1,0:T(8,128)(2,1)S(1)}, u32[]{:S(2)}, u32[]{:S(2)}) async-start(bf16[8,48,1152]{2,1,0:T(8,128)(2,1)} %bitcast.16), calls=%async_computation | async-start | bytes 1769472 | tf_op jit(solution)/shard_map/all_to_all | solution.py:366
  31.2 4.7 %grad_field.1 = (bf16[576,384]{1,0:T(8,128)(2,1)}, bf16[32,32,384]{2,1,0:T(8,128)(2,1)}) custom-call(s32[1]{0:T(128)} %bitcast.pos, bf16[576,1152]{1,0:T(8,128)(2,1)} %get-tuple-element.10.g, bf16[576,384]{1,0:T(8,128)(2,1)} %bitcast.17, bf16[3,384,384]{2,1,0:T(8,128)(2,1)} %mix.1), custom_call_target="tpu_custom_call" | custom-call | flops 5500000256 | bytes 15000000 | tf_op jit(solution)/shard_map/grad_field/pallas_call | solution.py:369
  35.9 5.5 %all-to-all-done.parts = bf16[8,48,1152]{2,1,0:T(8,128)(2,1)S(1)} async-done(((bf16[8,48,1152]{2,1,0:T(8,128)(2,1)}), bf16[8,48,1152]{2,1,0:T(8,128)(2,1)S(1)}, u32[]{:S(2)}, u32[]{:S(2)}) %all-to-all-start) | async-done | bytes 884768 | tf_op jit(solution)/shard_map/all_to_all | solution.py:366
  41.3 0.0 copy-start.1
  41.3 0.8 mix_sum_lat.1
  42.2 12.2 %all-to-all-start.1 = ((bf16[32,32,384]{2,1,0:T(8,128)(2,1)}), bf16[32,32,384]{2,1,0:T(8,128)(2,1)S(1)}, u32[]{:S(2)}, u32[]{:S(2)}) async-start(bf16[32,32,384]{2,1,0:T(8,128)(2,1)} %mix_sum_lat.1), calls=%async_computation.1 | async-start | bytes 1572864 | tf_op jit(solution)/shard_map/all_to_all | solution.py:392
  54.4 0.8 dynamic_slice.7
  55.2 0.0 copy-done.1
  55.2 0.7 multiply_add_fusion.1.logscale
  55.9 0.0 copy-start
  55.9 11.3 %legendre.1.leg = bf16[24,384,256]{2,1,0:T(8,128)(2,1)} custom-call(s32[1]{0:T(128)} %bitcast.pos, f32[1,128]{1,0:T(1,128)} %constant.40.clone.cosines, f32[48,128]{1,0:T(8,128)} %multiply_add_fusion.1.logscale), custom_call_target="tpu_custom_call" | custom-call | flops 9900000256 | bytes 27000000 | tf_op jit(solution)/shard_map/legendre/pallas_call | solution.py:400
  67.2 8.6 %all-to-all-done.1 = bf16[32,32,384]{2,1,0:T(8,128)(2,1)S(1)} async-done(((bf16[32,32,384]{2,1,0:T(8,128)(2,1)}), bf16[32,32,384]{2,1,0:T(8,128)(2,1)S(1)}, u32[]{:S(2)}, u32[]{:S(2)}) %all-to-all-start.1) | async-done | bytes 786464 | tf_op jit(solution)/shard_map/all_to_all | solution.py:392
  75.8 0.0 copy-done
  75.8 1.8 %dft.1 = bf16[8,104,384]{2,1,0:T(8,128)(2,1)} custom-call(bf16[768,1024]{1,0:T(8,128)(2,1)S(1)} %copy-done, bf16[1024,384]{1,0:T(8,128)(2,1)S(1)} %bitcast.15), custom_call_target="tpu_custom_call" | custom-call | flops 2200000000 | bytes 6000000 | tf_op jit(solution)/shard_map/dft/pallas_call | solution.py:424
  77.6 13.9 %all_to_all.20.spec = bf16[8,104,384]{2,1,0:T(8,128)(2,1)} all-to-all(bf16[8,104,384]{2,1,0:T(8,128)(2,1)} %dft.1), channel_id=1, replica_groups=mesh['lat'=8,'lon'=32] {'lat'}, dimensions={0} | all-to-all | bytes 1277952 | tf_op jit(solution)/shard_map/all_to_all | solution.py:427
  91.6 2.2 %mix_copies.1 = bf16[32,8,8,256]{3,2,1,0:T(8,128)(2,1)} custom-call(bf16[8,104,384]{2,1,0:T(8,128)(2,1)} %all_to_all.20.spec), custom_call_target="tpu_custom_call" | custom-call | flops 2200000000 | bytes 6000000 | tf_op jit(solution)/shard_map/mix_copies/pallas_call | solution.py:428
  93.8 9.0 %all-to-all-start.3 = ((bf16[32,8,8,256]{3,2,1,0:T(8,128)(2,1)}), bf16[32,8,8,256]{3,2,1,0:T(8,128)(2,1)S(1)}, u32[]{:S(2)}, u32[]{:S(2)}) async-start(bf16[32,8,8,256]{3,2,1,0:T(8,128)(2,1)} %mix_copies.1), calls=%async_computation.3 | async-start | bytes 2097152 | tf_op jit(solution)/shard_map/all_to_all | solution.py:429
  102.7 7.3 %synthesis.1 = f32[2,12,48,384]{3,2,1,0:T(8,128)} custom-call(bf16[8,104,384]{2,1,0:T(8,128)(2,1)} %all_to_all.20.spec, bf16[24,384,256]{2,1,0:T(8,128)(2,1)} %legendre.1.leg), custom_call_target="tpu_custom_call" | custom-call | flops 6600000000 | bytes 18000000 | tf_op jit(solution)/shard_map/synthesis/pallas_call | solution.py:431
  110.1 19.1 %all-to-all-done.3.parts = bf16[32,8,8,256]{3,2,1,0:T(8,128)(2,1)S(1)} async-done(((bf16[32,8,8,256]{3,2,1,0:T(8,128)(2,1)}), bf16[32,8,8,256]{3,2,1,0:T(8,128)(2,1)S(1)}, u32[]{:S(2)}, u32[]{:S(2)}) %all-to-all-start.3) | async-done | bytes 1048608 | tf_op jit(solution)/shard_map/all_to_all | solution.py:429
  129.2 1.3 mix_out.1
  (5 shorter events, 0.0 us)
Async XLA Ops:
  1.6 6.1 %collective-permute-start.1 = (bf16[24,8,384]{2,1,0:T(8,128)(2,1)S(1)}, bf16[24,8,384]{2,1,0:T(8,128)(2,1)S(1)}, u32[]{:S(2)}, u32[]{:S(2)}) collective-permute-start(bf16[24,8,384]{2,1,0:T(8,128)(2,1)S(1)} %get-tuple-element.19), channel_id=1, source_target_pairs={{1,0},{2,1},{3,2},{4,3},{5,4},{6,5},{7,6},{8,7},{9,8},{10,9},{11,1... | collective-permute-start | bytes 442376 | tf_op jit(solution)/shard_map/ppermute | solution.py:346
  5.0 5.4 %collective-permute-start = (bf16[24,8,384]{2,1,0:T(8,128)(2,1)S(1)}, bf16[24,8,384]{2,1,0:T(8,128)(2,1)S(1)}, u32[]{:S(2)}, u32[]{:S(2)}) collective-permute-start(bf16[24,8,384]{2,1,0:T(8,128)(2,1)S(1)} %get-tuple-element.20), channel_id=1, source_target_pairs={{0,1},{1,2},{2,3},{3,4},{4,5},{5,6},{6,7},{7,8},{8,9},{9,10},{10,1... | collective-permute-start | bytes 442376 | tf_op jit(solution)/shard_map/ppermute | solution.py:345
  10.4 7.0 %collective-permute-start.2 = (bf16[1,40,384]{2,1,0:T(8,128)(2,1)S(1)}, bf16[1,40,384]{2,1,0:T(8,128)(2,1)S(1)}, u32[]{:S(2)}, u32[]{:S(2)}) collective-permute-start(bf16[1,40,384]{2,1,0:T(8,128)(2,1)S(1)} %pad_maximum_fusion), channel_id=1, source_target_pairs={{0,32},{32,64},{64,96},{96,128},{128,160},{160,192},{192,224},{1,3... | collective-permute-start | bytes 92168 | tf_op jit(solution)/shard_map/ppermute | solution.py:352
  15.0 6.1 %collective-permute-start.3 = (bf16[1,40,384]{2,1,0:T(8,128)(2,1)S(1)}, bf16[1,40,384]{2,1,0:T(8,128)(2,1)S(1)}, u32[]{:S(2)}, u32[]{:S(2)}) collective-permute-start(bf16[1,40,384]{2,1,0:T(8,128)(2,1)S(1)} %pad_maximum_fusion.1), channel_id=1, source_target_pairs={{32,0},{64,32},{96,64},{128,96},{160,128},{192,160},{224,192},{33,... | collective-permute-start | bytes 92168 | tf_op jit(solution)/shard_map/ppermute | solution.py:353
  25.5 15.8 %all-to-all-start = ((bf16[8,48,1152]{2,1,0:T(8,128)(2,1)}), bf16[8,48,1152]{2,1,0:T(8,128)(2,1)S(1)}, u32[]{:S(2)}, u32[]{:S(2)}) async-start(bf16[8,48,1152]{2,1,0:T(8,128)(2,1)} %bitcast.16), calls=%async_computation | async-start | bytes 1769472 | tf_op jit(solution)/shard_map/all_to_all | solution.py:366
  41.3 13.9 %copy-start.1 = (f32[128]{0:T(128)S(1)}, f32[128]{0:T(128)}, u32[]{:S(2)}) copy-start(f32[128]{0:T(128)} %constant.49) | copy-start | bytes 1540
  42.2 33.6 %all-to-all-start.1 = ((bf16[32,32,384]{2,1,0:T(8,128)(2,1)}), bf16[32,32,384]{2,1,0:T(8,128)(2,1)S(1)}, u32[]{:S(2)}, u32[]{:S(2)}) async-start(bf16[32,32,384]{2,1,0:T(8,128)(2,1)} %mix_sum_lat.1), calls=%async_computation.1 | async-start | bytes 1572864 | tf_op jit(solution)/shard_map/all_to_all | solution.py:392
  55.9 19.9 %copy-start = (bf16[768,1024]{1,0:T(8,128)(2,1)S(1)}, bf16[768,1024]{1,0:T(8,128)(2,1)}, u32[]{:S(2)}) copy-start(bf16[768,1024]{1,0:T(8,128)(2,1)} %constant.41.clone.rows) | copy-start | bytes 4718596
  93.8 35.4 %all-to-all-start.3 = ((bf16[32,8,8,256]{3,2,1,0:T(8,128)(2,1)}), bf16[32,8,8,256]{3,2,1,0:T(8,128)(2,1)S(1)}, u32[]{:S(2)}, u32[]{:S(2)}) async-start(bf16[32,8,8,256]{3,2,1,0:T(8,128)(2,1)} %mix_copies.1), calls=%async_computation.3 | async-start | bytes 2097152 | tf_op jit(solution)/shard_map/all_to_all | solution.py:429

commit v4 on v3

--- a/solution.py
+++ b/solution.py
@@ -8,7 +8,7 @@
 from jax import lax
 from jax.experimental import pallas as pl
 from jax.experimental.pallas import tpu as pltpu
-from jax.sharding import PartitionSpec as P
+from jax.sharding import Mesh, PartitionSpec as P
 
 C = 384
 M = 384
@@ -29,6 +29,11 @@
 TP = 32
 FP = FD + 8
 QUAD = 4
+CHIPS = LONS // 2
+LAT = "lat"
+CHIP = "chip"
+CORE = "core"
+LON = (CHIP, CORE)
 F32 = jnp.float32
 BF16 = jnp.bfloat16
 VMEM_BYTES = 56 * 1024 * 1024
@@ -241,8 +246,11 @@
                 out[p, c, :, h * 128:(h + 1) * 128] = rows[h, base:base + MSTEP, :]
 
 
-TILES = (MD // 8) * (K * C // 128)
-PAIRS = TILES // 2
+HALF_TILES = MD // 16 * (K * C // 128)
+
+
+def tiles_of(chip):
+    return [(side, *divmod(2 * chip + side, K * C // 128)) for side in range(2) if 2 * chip + side < HALF_TILES]
 
 
 def sum_lat_kernel(parts, send, out, rows, sem):
@@ -250,12 +258,12 @@
     for i in range(1, LATS):
         total = total + parts[i].astype(F32)
     total = total.astype(BF16)
-    lanes = K * C // 128
     rows[...] = jnp.zeros_like(rows)
-    for tile in range(TILES):
-        row, col = divmod(tile, lanes)
-        side = (tile % 2) * 128
-        rows[tile // 2, :, side:side + 128] = total[row * 8:(row + 1) * 8, col * 128:(col + 1) * 128]
+    for chip in range(CHIPS):
+        for side, row, col in tiles_of(chip):
+            for core in range(2):
+                first = core * (MD // 2) + row * 8
+                rows[2 * chip + core, :, side * 128:(side + 1) * 128] = total[first:first + 8, col * 128:(col + 1) * 128]
     copy = pltpu.make_async_copy(rows, out.at[:, FD:, :], sem)
     copy.start()
     copy.wait()
@@ -263,21 +271,21 @@
 
 def copies_kernel(spec, out):
     part = spec[:, 2 * MD:, :256]
-    for j in range(LONS):
-        out[j] = part
-
-
-def mix_kernel(parts, out, rows, sems):
-    lanes = K * C // 128
+    for chip in range(CHIPS):
+        out[chip] = part
+
+
+def mix_kernel(core, mine, other, out, rows, sems):
     copies = []
     for i in range(LATS):
-        for tile in range(TILES):
-            row, col = divmod(tile, lanes)
-            k, d = divmod(col, C // 128)
-            side = (tile % 2) * 128
-            rows[k, i * MD + row * 8:i * MD + row * 8 + 8, d * 128:(d + 1) * 128] = parts[
-                tile // 2, i, :, side:side + 128
-            ].astype(F32)
+        for parts, half in ((mine, core[0]), (other, 1 - core[0])):
+            base = pl.multiple_of(i * MD + half * (MD // 2), 8)
+            for chip in range(CHIPS):
+                for side, row, col in tiles_of(chip):
+                    k, d = divmod(col, C // 128)
+                    rows[k, pl.ds(base + row * 8, 8), d * 128:(d + 1) * 128] = parts[
+                        chip, i, :, side * 128:(side + 1) * 128
+                    ].astype(F32)
         span = pl.ds(i * MD, MD)
         copies.append(pltpu.make_async_copy(rows.at[:, span], out.at[:, span], sems.at[i]))
         copies[-1].start()
@@ -339,18 +347,18 @@
 
 
 def on_device(field, cotangent, mix_weight, taps, offsets, counts):
-    lat_pos = lax.axis_index("lat")
+    lat_pos = lax.axis_index(LAT)
     up = [(i, (i + 1) % LONS) for i in range(LONS)]
     down = [(j, i) for i, j in up]
-    left = lax.ppermute(cotangent[:, FD - R:], "lon", up)
-    right = lax.ppermute(cotangent[:, :R], "lon", down)
+    left = lax.ppermute(cotangent[:, FD - R:], LON, up)
+    right = lax.ppermute(cotangent[:, :R], LON, down)
     edge_rows = [
         jnp.concatenate([left[t:t + 1], cotangent[t:t + 1], right[t:t + 1]], axis=1) for t in (0, TD - 1)
     ]
     north = [(i, i + 1) for i in range(LATS - 1)]
     south = [(j, i) for i, j in north]
-    top = lax.ppermute(edge_rows[1], "lat", north)
-    bottom = lax.ppermute(edge_rows[0], "lat", south)
+    top = lax.ppermute(edge_rows[1], LAT, north)
+    bottom = lax.ppermute(edge_rows[0], LAT, south)
 
     whole = pl.BlockSpec(memory_space=pltpu.VMEM)
     tab = tap_table(taps, offsets, counts, lat_pos * TD)
@@ -363,7 +371,7 @@
         scratch_shapes=[pltpu.VMEM((TD + 2, XW, C), F32), pltpu.VMEM((K * QUAD * FD, 256), F32)],
         name="stencil",
     )(near(tab), cotangent, near(left), near(right), near(top), near(bottom), field.reshape(cells, C))
-    mix_lat = lax.all_to_all(mix_part.reshape(LATS, MD, K * C), "lat", 0, 0, tiled=True)
+    mix_lat = lax.all_to_all(mix_part.reshape(LATS, MD, K * C), LAT, 0, 0, tiled=True)
 
     pos = jnp.reshape(lat_pos, (1,)).astype(jnp.int32)
     grad_field, send = call(
@@ -389,7 +397,7 @@
         input_output_aliases={1: 0},
         name="mix_sum_lat",
     )(near(mix_lat), send)
-    columns = lax.all_to_all(send, "lon", 0, 0, tiled=True)
+    columns = lax.all_to_all(send, LON, 0, 0, tiled=True)
 
     cosine, logsine = latitudes()
     first_order = lat_pos * MD
@@ -424,9 +432,9 @@
     spectra = call(dft_kernel, shape((LATS, 2 * MD + FP - FD, CD * TP), BF16), 2, in_specs=[whole, whole], name="dft")(
         near(jnp.asarray(dft_rows())), near(columns.reshape(LONS * FP, CD * TP))
     )
-    spec = lax.all_to_all(spectra, "lat", 0, 0, tiled=True)
-    mix_copies = call(copies_kernel, shape((LONS, LATS, 8, 256), BF16), 2, name="mix_copies")(spec)
-    mix_all = lax.all_to_all(mix_copies, "lon", 0, 0, tiled=True)
+    spec = lax.all_to_all(spectra, LAT, 0, 0, tiled=True)
+    mix_copies = call(copies_kernel, shape((CHIPS, LATS, 8, 256), BF16), 2, in_specs=[whole], name="mix_copies")(near(spec))
+    mix_mine = lax.all_to_all(mix_copies, CHIP, 0, 0, tiled=True)
 
     grad_spectra = call(
         synthesis_kernel,
@@ -436,7 +444,7 @@
             num_scalar_prefetch=0,
             grid=(MD // MSTEP,),
             in_specs=[
-                pl.BlockSpec((LATS, 2 * MD + FP - FD, CD * TP), lambda b: (0, 0, 0)),
+                whole,
                 pl.BlockSpec((MSTEP // 2, L, 2 * HALF), lambda b: (b, 0, 0)),
             ],
             out_specs=pl.BlockSpec((2, CD, MSTEP, L), lambda b: (0, 0, b, 0)),
@@ -446,25 +454,28 @@
             ],
         ),
         name="synthesis",
-    )(spec, table)
+    )(near(spec), table)
+    mix_mine, grad_spectra = lax.optimization_barrier((mix_mine, grad_spectra))
+    mix_other = lax.ppermute(mix_mine, CORE, [(0, 1), (1, 0)])
     grad_mix = call(
         mix_kernel,
         shape((K, C, C), F32),
         2,
-        in_specs=[whole],
+        in_specs=[pl.BlockSpec(memory_space=pltpu.SMEM), whole, whole],
         out_specs=anywhere,
         scratch_shapes=[pltpu.VMEM((K, C, C), F32), pltpu.SemaphoreType.DMA((LATS,))],
         name="mix_out",
-    )(near(mix_all))
+    )(jnp.reshape(lax.axis_index(CORE), (1,)).astype(jnp.int32), near(mix_mine), near(mix_other))
     return (grad_field.reshape(TD, FD, C), jnp.transpose(grad_spectra, (0, 2, 1, 3)), grad_mix)
 
 
 def solution(mesh):
-    placed = (P("lat", "lon", None), P("lat", "lon", None), P(), P(), P(), P())
+    chips = Mesh(mesh.devices.reshape(LATS, CHIPS, 2), (LAT, CHIP, CORE))
+    placed = (P(LAT, LON, None), P(LAT, LON, None), P(), P(), P(), P())
     return jax.shard_map(
         on_device,
-        mesh=mesh,
+        mesh=chips,
         in_specs=placed,
-        out_specs=(P("lat", "lon", None), P(None, "lat", "lon", None), P()),
+        out_specs=(P(LAT, LON, None), P(None, LAT, LON, None), P()),
         check_vma=False,
     )

time: 133 us -> 119 us (0.89); the launches traced: 130 us -> 118 us
  waiting for transfers between devices: 39.5 us -> 27.9 us
  Pallas kernels: 33.9 us -> 32.5 us
    all_to_all x3, waiting for transfers between devices: 33.2 us -> 20.1 us  [the longest x1 8.58 us: on_device(): columns = lax.all_to_all(send, LON, 0, 0, tiled=True)]
    ppermute x4 -> x5, starting transfers between devices: 9.13 us -> 12 us  [the longest x1 4.52 us: on_device(): top = lax.ppermute(edge_rows[1], LAT, north)]
    all_to_all x3, starting transfers between devices: 26.8 us -> 24.6 us  [the longest x1 12.2 us: on_device(): columns = lax.all_to_all(send, LON, 0, 0, tiled=True)]
    ppermute x4 -> x5, waiting for transfers between devices: 6.3 us -> 7.84 us  [the longest x1 3.67 us: on_device(): bottom = lax.ppermute(edge_rows[0], LAT, south)]
  transfers between devices with their start and end apart: 7 -> 8, of which waited for: 5 -> 6; matrix products, arithmetic and copies ran while one was open for 4% -> 5% of each run, Pallas kernels for 18% -> 20%
where the time goes in v4:
time: 119 us; the launch traced here: 118 us
  starting transfers between devices  36.6 us (31%)
  Pallas kernels  32.5 us (27%)
  waiting for transfers between devices  27.9 us (23%)
  blocking collectives  13.8 us (12%)
  other arithmetic  3.6 us (3%)
  local copies, waits for them, and re-layouts  2.83 us (2%)
    all_to_all x1, blocking collectives, on_device(): spec = lax.all_to_all(spectra, LAT, 0, 0, tiled=True)  13.8 us
    all_to_all x1, starting transfers between devices, on_device(): columns = lax.all_to_all(send, LON, 0, 0, tiled=True)  12.2 us
    pallas_call x1, Pallas kernels, on_device(): call(legendre_kernel, shape((MD // 2, L, 2 * HALF), BF16), 9, grid_spec=p...  11.4 us
    all_to_all x1, waiting for transfers between devices, on_device(): columns = lax.all_to_all(send, LON, 0, 0, tiled=True)  8.58 us
    pallas_call x1, Pallas kernels, on_device(): call(synthesis_kernel, shape((2, CD, MD, L), F32), 6, grid_spec=pltpu.Pre...  7.15 us
    all_to_all x1, starting transfers between devices, on_device(): mix_mine = lax.all_to_all(mix_copies, CHIP, 0, 0, tiled=True)  6.76 us
    all_to_all x1, waiting for transfers between devices, on_device(): mix_mine = lax.all_to_all(mix_copies, CHIP, 0, 0, tiled=True)  6.03 us
    all_to_all x1, starting transfers between devices, on_device(): lax.all_to_all(mix_part.reshape(LATS, MD, K * C), LAT, 0, 0, tiled=True)  5.62 us
  transfers between devices with their start and end apart: 8, of which 6 were waited for; matrix products, arithmetic and copies ran while one was open for 5% of the time, Pallas kernels for 20%

profile of v4, /device:TPU:1, one launch (start us, length us, event | category | flops | bytes accessed | tf_op | source)
XLA Modules:
  0.0 118.0 jit_solution(6590594374179725629)
XLA Ops:
  0.6 1.0 fusion.8
  1.6 3.3 %collective-permute-start.1 = (bf16[24,8,384]{2,1,0:T(8,128)(2,1)S(1)}, bf16[24,8,384]{2,1,0:T(8,128)(2,1)S(1)}, u32[]{:S(2)}, u32[]{:S(2)}) collective-permute-start(bf16[24,8,384]{2,1,0:T(8,128)(2,1)S(1)} %get-tuple-element.23), channel_id=1, source_target_pairs={{1,0},{2,1},{3,2},{4,3},{5,4},{6,5},{7,6},{8,7},{9,8},{10,9},{11,1... | collective-permute-start | bytes 442376 | tf_op jit(solution)/shard_map/ppermute | solution.py:354
  5.0 0.0 collective-permute-start
  5.0 0.7 convert_bitcast_fusion
  5.7 0.9 fusion.6
  6.6 0.1 fusion.1
  6.7 0.1 slice_bitcast_fusion.2
  6.8 0.1 copy.17
  6.9 0.1 copy.18
  6.9 0.1 copy.19
  7.0 0.8 fusion.7
  7.8 0.0 collective-permute-done.1.right
  7.8 2.6 %collective-permute-done.left = bf16[24,8,384]{2,1,0:T(8,128)(2,1)S(1)} collective-permute-done((bf16[24,8,384]{2,1,0:T(8,128)(2,1)S(1)}, bf16[24,8,384]{2,1,0:T(8,128)(2,1)S(1)}, u32[]{:S(2)}, u32[]{:S(2)}) %collective-permute-start) | collective-permute-done | bytes 147488 | tf_op jit(solution)/shard_map/ppermute | solution.py:353
  10.4 4.5 %collective-permute-start.2 = (bf16[1,40,384]{2,1,0:T(8,128)(2,1)S(1)}, bf16[1,40,384]{2,1,0:T(8,128)(2,1)S(1)}, u32[]{:S(2)}, u32[]{:S(2)}) collective-permute-start(bf16[1,40,384]{2,1,0:T(8,128)(2,1)S(1)} %pad_maximum_fusion), channel_id=1, source_target_pairs={{0,32},{32,64},{64,96},{96,128},{128,160},{160,192},{192,224},{1,3... | collective-permute-start | bytes 92168 | tf_op jit(solution)/shard_map/ppermute | solution.py:360
  15.0 1.3 %collective-permute-start.3 = (bf16[1,40,384]{2,1,0:T(8,128)(2,1)S(1)}, bf16[1,40,384]{2,1,0:T(8,128)(2,1)S(1)}, u32[]{:S(2)}, u32[]{:S(2)}) collective-permute-start(bf16[1,40,384]{2,1,0:T(8,128)(2,1)S(1)} %pad_maximum_fusion.1), channel_id=1, source_target_pairs={{32,0},{64,32},{96,64},{128,96},{160,128},{192,160},{224,192},{33,... | collective-permute-start | bytes 92168 | tf_op jit(solution)/shard_map/ppermute | solution.py:361
  16.3 1.2 multiply_add_fusion.tab
  17.4 0.0 collective-permute-done.2.top
  17.4 3.7 %collective-permute-done.3.bottom = bf16[1,40,384]{2,1,0:T(8,128)(2,1)S(1)} collective-permute-done((bf16[1,40,384]{2,1,0:T(8,128)(2,1)S(1)}, bf16[1,40,384]{2,1,0:T(8,128)(2,1)S(1)}, u32[]{:S(2)}, u32[]{:S(2)}) %collective-permute-start.3) | collective-permute-done | bytes 30752 | tf_op jit(solution)/shard_map/ppermute | solution.py:361
  21.1 4.4 %stencil.1 = (bf16[576,1152]{1,0:T(8,128)(2,1)}, bf16[384,1152]{1,0:T(8,128)(2,1)}) custom-call(f32[24,32,256]{2,1,0:T(8,128)S(1)} %multiply_add_fusion.tab, bf16[24,24,384]{2,1,0:T(8,128)(2,1)} %cot.1, bf16[24,8,384]{2,1,0:T(8,128)(2,1)S(1)} %collective-permute-done.left, bf16[24,8,384]{2,1,0:T(8,128)(2,1)S(1)} %collective-permute-done.1.right, ...), custom_call_target="tpu_custom_call" | custom-call | flops 5500000256 | bytes 15000000 | tf_op jit(solution)/shard_map/stencil/pallas_call | solution.py:366
  25.5 5.6 %all-to-all-start = ((bf16[8,48,1152]{2,1,0:T(8,128)(2,1)}), bf16[8,48,1152]{2,1,0:T(8,128)(2,1)S(1)}, u32[]{:S(2)}, u32[]{:S(2)}) async-start(bf16[8,48,1152]{2,1,0:T(8,128)(2,1)} %bitcast.17), calls=%async_computation | async-start | bytes 1769472 | tf_op jit(solution)/shard_map/all_to_all | solution.py:374
  31.2 4.7 %grad_field.1 = (bf16[576,384]{1,0:T(8,128)(2,1)}, bf16[32,32,384]{2,1,0:T(8,128)(2,1)}) custom-call(s32[1]{0:T(128)} %bitcast.pos, bf16[576,1152]{1,0:T(8,128)(2,1)} %get-tuple-element.12.g, bf16[576,384]{1,0:T(8,128)(2,1)} %bitcast.18, bf16[3,384,384]{2,1,0:T(8,128)(2,1)} %mix.1), custom_call_target="tpu_custom_call" | custom-call | flops 5500000256 | bytes 15000000 | tf_op jit(solution)/shard_map/grad_field/pallas_call | solution.py:377
  35.9 5.5 %all-to-all-done.parts = bf16[8,48,1152]{2,1,0:T(8,128)(2,1)S(1)} async-done(((bf16[8,48,1152]{2,1,0:T(8,128)(2,1)}), bf16[8,48,1152]{2,1,0:T(8,128)(2,1)S(1)}, u32[]{:S(2)}, u32[]{:S(2)}) %all-to-all-start) | async-done | bytes 884768 | tf_op jit(solution)/shard_map/all_to_all | solution.py:374
  41.3 0.0 copy-start.1
  41.3 0.9 mix_sum_lat.1
  42.2 12.2 %all-to-all-start.1 = ((bf16[32,32,384]{2,1,0:T(8,128)(2,1)}), bf16[32,32,384]{2,1,0:T(8,128)(2,1)S(1)}, u32[]{:S(2)}, u32[]{:S(2)}) async-start(bf16[32,32,384]{2,1,0:T(8,128)(2,1)} %mix_sum_lat.1), calls=%async_computation.1 | async-start | bytes 1572864 | tf_op jit(solution)/shard_map/all_to_all | solution.py:400
  54.5 0.8 dynamic_slice.7
  55.2 0.0 copy-done.1
  55.2 0.7 multiply_add_fusion.1.logscale
  55.9 0.0 copy-start
  55.9 11.4 %legendre.1.leg = bf16[24,384,256]{2,1,0:T(8,128)(2,1)} custom-call(s32[1]{0:T(128)} %bitcast.pos, f32[1,128]{1,0:T(1,128)} %constant.44.clone.cosines, f32[48,128]{1,0:T(8,128)} %multiply_add_fusion.1.logscale), custom_call_target="tpu_custom_call" | custom-call | flops 9900000256 | bytes 27000000 | tf_op jit(solution)/shard_map/legendre/pallas_call | solution.py:408
  67.3 8.6 %all-to-all-done.1 = bf16[32,32,384]{2,1,0:T(8,128)(2,1)S(1)} async-done(((bf16[32,32,384]{2,1,0:T(8,128)(2,1)}), bf16[32,32,384]{2,1,0:T(8,128)(2,1)S(1)}, u32[]{:S(2)}, u32[]{:S(2)}) %all-to-all-start.1) | async-done | bytes 786464 | tf_op jit(solution)/shard_map/all_to_all | solution.py:400
  75.9 0.0 copy-done
  75.9 1.8 %dft.1 = bf16[8,104,384]{2,1,0:T(8,128)(2,1)} custom-call(bf16[768,1024]{1,0:T(8,128)(2,1)S(1)} %copy-done, bf16[1024,384]{1,0:T(8,128)(2,1)S(1)} %bitcast.16), custom_call_target="tpu_custom_call" | custom-call | flops 2200000000 | bytes 6000000 | tf_op jit(solution)/shard_map/dft/pallas_call | solution.py:432
  77.7 13.8 %all_to_all.20.spec = bf16[8,104,384]{2,1,0:T(8,128)(2,1)S(1)} all-to-all(bf16[8,104,384]{2,1,0:T(8,128)(2,1)} %dft.1), channel_id=1, replica_groups=mesh['lat'=8,'chip'=16,'core'=2] {'lat'}, dimensions={0} | all-to-all | bytes 1277952 | tf_op jit(solution)/shard_map/all_to_all | solution.py:435
  91.5 0.8 mix_copies.1
  92.4 6.8 %all-to-all-start.3 = ((bf16[16,8,8,256]{3,2,1,0:T(8,128)(2,1)}), bf16[16,8,8,256]{3,2,1,0:T(8,128)(2,1)S(1)}, u32[]{:S(2)}, u32[]{:S(2)}) async-start(bf16[16,8,8,256]{3,2,1,0:T(8,128)(2,1)} %mix_copies.1), calls=%async_computation.3 | async-start | bytes 1048576 | tf_op jit(solution)/shard_map/all_to_all | solution.py:437
  99.1 7.2 %synthesis.1 = f32[2,12,48,384]{3,2,1,0:T(8,128)} custom-call(bf16[8,104,384]{2,1,0:T(8,128)(2,1)S(1)} %all_to_all.20.spec, bf16[24,384,256]{2,1,0:T(8,128)(2,1)} %legendre.1.leg), custom_call_target="tpu_custom_call" | custom-call | flops 6600000000 | bytes 18000000 | tf_op jit(solution)/shard_map/synthesis/pallas_call | solution.py:439
  106.3 6.0 %all-to-all-done.3.mine = bf16[16,8,8,256]{3,2,1,0:T(8,128)(2,1)S(1)} async-done(((bf16[16,8,8,256]{3,2,1,0:T(8,128)(2,1)}), bf16[16,8,8,256]{3,2,1,0:T(8,128)(2,1)S(1)}, u32[]{:S(2)}, u32[]{:S(2)}) %all-to-all-start.3) | async-done | bytes 524320 | tf_op jit(solution)/shard_map/all_to_all | solution.py:437
  112.3 2.9 %collective-permute-start.4 = (bf16[16,8,8,256]{3,2,1,0:T(8,128)(2,1)S(1)}, bf16[16,8,8,256]{3,2,1,0:T(8,128)(2,1)S(1)}, u32[]{:S(2)}, u32[]{:S(2)}) collective-permute-start(bf16[16,8,8,256]{3,2,1,0:T(8,128)(2,1)S(1)} %all-to-all-done.3.mine), channel_id=1, source_target_pairs={{0,1},{1,0},{2,3},{3,2},{4,5},{5,4},{6,7},{7,6},{8,9},{9,8},{10,11... | collective-permute-start | bytes 1572872 | tf_op jit(solution)/shard_map/ppermute | solution.py:459
  115.2 1.5 %collective-permute-done.4.other = bf16[16,8,8,256]{3,2,1,0:T(8,128)(2,1)S(1)} collective-permute-done((bf16[16,8,8,256]{3,2,1,0:T(8,128)(2,1)S(1)}, bf16[16,8,8,256]{3,2,1,0:T(8,128)(2,1)S(1)}, u32[]{:S(2)}, u32[]{:S(2)}) %collective-permute-start.4) | collective-permute-done | bytes 524320 | tf_op jit(solution)/shard_map/ppermute | solution.py:459
  116.7 1.3 %mix_out.1 = f32[3,384,384]{2,1,0:T(8,128)} custom-call(s32[1]{0:T(128)} %bitcast.11.core, bf16[16,8,8,256]{3,2,1,0:T(8,128)(2,1)S(1)} %all-to-all-done.3.mine, bf16[16,8,8,256]{3,2,1,0:T(8,128)(2,1)S(1)} %collective-permute-done.4.other), custom_call_target="tpu_custom_call" | custom-call | flops 2200000000 | bytes 6000000 | tf_op jit(solution)/shard_map/mix_out/pallas_call | solution.py:460
  (5 shorter events, 0.0 us)
Async XLA Ops:
  1.6 6.1 %collective-permute-start.1 = (bf16[24,8,384]{2,1,0:T(8,128)(2,1)S(1)}, bf16[24,8,384]{2,1,0:T(8,128)(2,1)S(1)}, u32[]{:S(2)}, u32[]{:S(2)}) collective-permute-start(bf16[24,8,384]{2,1,0:T(8,128)(2,1)S(1)} %get-tuple-element.23), channel_id=1, source_target_pairs={{1,0},{2,1},{3,2},{4,3},{5,4},{6,5},{7,6},{8,7},{9,8},{10,9},{11,1... | collective-permute-start | bytes 442376 | tf_op jit(solution)/shard_map/ppermute | solution.py:354
  5.0 5.4 %collective-permute-start = (bf16[24,8,384]{2,1,0:T(8,128)(2,1)S(1)}, bf16[24,8,384]{2,1,0:T(8,128)(2,1)S(1)}, u32[]{:S(2)}, u32[]{:S(2)}) collective-permute-start(bf16[24,8,384]{2,1,0:T(8,128)(2,1)S(1)} %get-tuple-element.24), channel_id=1, source_target_pairs={{0,1},{1,2},{2,3},{3,4},{4,5},{5,6},{6,7},{7,8},{8,9},{9,10},{10,1... | collective-permute-start | bytes 442376 | tf_op jit(solution)/shard_map/ppermute | solution.py:353
  10.4 7.0 %collective-permute-start.2 = (bf16[1,40,384]{2,1,0:T(8,128)(2,1)S(1)}, bf16[1,40,384]{2,1,0:T(8,128)(2,1)S(1)}, u32[]{:S(2)}, u32[]{:S(2)}) collective-permute-start(bf16[1,40,384]{2,1,0:T(8,128)(2,1)S(1)} %pad_maximum_fusion), channel_id=1, source_target_pairs={{0,32},{32,64},{64,96},{96,128},{128,160},{160,192},{192,224},{1,3... | collective-permute-start | bytes 92168 | tf_op jit(solution)/shard_map/ppermute | solution.py:360
  15.0 6.1 %collective-permute-start.3 = (bf16[1,40,384]{2,1,0:T(8,128)(2,1)S(1)}, bf16[1,40,384]{2,1,0:T(8,128)(2,1)S(1)}, u32[]{:S(2)}, u32[]{:S(2)}) collective-permute-start(bf16[1,40,384]{2,1,0:T(8,128)(2,1)S(1)} %pad_maximum_fusion.1), channel_id=1, source_target_pairs={{32,0},{64,32},{96,64},{128,96},{160,128},{192,160},{224,192},{33,... | collective-permute-start | bytes 92168 | tf_op jit(solution)/shard_map/ppermute | solution.py:361
  25.5 15.8 %all-to-all-start = ((bf16[8,48,1152]{2,1,0:T(8,128)(2,1)}), bf16[8,48,1152]{2,1,0:T(8,128)(2,1)S(1)}, u32[]{:S(2)}, u32[]{:S(2)}) async-start(bf16[8,48,1152]{2,1,0:T(8,128)(2,1)} %bitcast.17), calls=%async_computation | async-start | bytes 1769472 | tf_op jit(solution)/shard_map/all_to_all | solution.py:374
  41.3 13.9 %copy-start.1 = (f32[128]{0:T(128)S(1)}, f32[128]{0:T(128)}, u32[]{:S(2)}) copy-start(f32[128]{0:T(128)} %constant.53) | copy-start | bytes 1540
  42.2 33.6 %all-to-all-start.1 = ((bf16[32,32,384]{2,1,0:T(8,128)(2,1)}), bf16[32,32,384]{2,1,0:T(8,128)(2,1)S(1)}, u32[]{:S(2)}, u32[]{:S(2)}) async-start(bf16[32,32,384]{2,1,0:T(8,128)(2,1)} %mix_sum_lat.1), calls=%async_computation.1 | async-start | bytes 1572864 | tf_op jit(solution)/shard_map/all_to_all | solution.py:400
  55.9 19.9 %copy-start = (bf16[768,1024]{1,0:T(8,128)(2,1)S(1)}, bf16[768,1024]{1,0:T(8,128)(2,1)}, u32[]{:S(2)}) copy-start(bf16[768,1024]{1,0:T(8,128)(2,1)} %constant.45.clone.rows) | copy-start | bytes 4718596
  92.4 20.0 %all-to-all-start.3 = ((bf16[16,8,8,256]{3,2,1,0:T(8,128)(2,1)}), bf16[16,8,8,256]{3,2,1,0:T(8,128)(2,1)S(1)}, u32[]{:S(2)}, u32[]{:S(2)}) async-start(bf16[16,8,8,256]{3,2,1,0:T(8,128)(2,1)} %mix_copies.1), calls=%async_computation.3 | async-start | bytes 1048576 | tf_op jit(solution)/shard_map/all_to_all | solution.py:437
  112.3 4.4 %collective-permute-start.4 = (bf16[16,8,8,256]{3,2,1,0:T(8,128)(2,1)S(1)}, bf16[16,8,8,256]{3,2,1,0:T(8,128)(2,1)S(1)}, u32[]{:S(2)}, u32[]{:S(2)}) collective-permute-start(bf16[16,8,8,256]{3,2,1,0:T(8,128)(2,1)S(1)} %all-to-all-done.3.mine), channel_id=1, source_target_pairs={{0,1},{1,0},{2,3},{3,2},{4,5},{5,4},{6,7},{7,6},{8,9},{9,8},{10,11... | collective-permute-start | bytes 1572872 | tf_op jit(solution)/shard_map/ppermute | solution.py:459

commit v5 on v4

--- a/solution.py
+++ b/solution.py
@@ -28,6 +28,10 @@
 XW = FD + 2 * R
 TP = 32
 FP = FD + 8
+GROUPS = CD * TP // 128
+SLOTS = 7
+SENT = GROUPS * FP + (SLOTS - GROUPS) * 8
+SPREAD = 40
 QUAD = 4
 CHIPS = LONS // 2
 LAT = "lat"
@@ -73,7 +77,7 @@
     return c0, c1, c2, c3
 
 
-def stencil_kernel(tab, cot, left, right, top, bottom, field, g_out, mix_out, ext, band):
+def stencil_kernel(core, tab, cot, left, right, top, bottom, field, g_out, mine_out, other_out, ext, band):
     ext[1:TD + 1, 0:R, :] = left[...].astype(F32)
     ext[1:TD + 1, R:R + FD, :] = cot[...].astype(F32)
     ext[1:TD + 1, R + FD:XW, :] = right[...].astype(F32)
@@ -105,7 +109,11 @@
     mix = lax.dot_general(
         field[...], g_out[...], (((0,), (0,)), ((), ())), preferred_element_type=F32
     )
-    mix_out[...] = (mix * (1.0 / math.sqrt(NLAT * NLON))).astype(BF16)
+    mix = mix * (1.0 / math.sqrt(NLAT * NLON))
+    first = core[0] == 0
+    low, high = mix[:C // 2], mix[C // 2:]
+    mine_out[...] = jnp.where(first, low, high)
+    other_out[...] = jnp.where(first, high, low).astype(BF16)
 
 
 def field_kernel(pos, g, cot, mix, gf_out, send_out, flat, turned, send):
@@ -137,21 +145,37 @@
             ]
             for fr, part in enumerate(swap_blocks(parts)):
                 send[q, pl.ds(fq * 4 + fr, LONS, stride=FD), :] = part
-    send_out[:, FD:, :] = jnp.zeros((LONS, FP - FD, CD * TP), BF16)
-    for q in range(CD // 4):
-        send_out[:, :FD, q * 128:(q + 1) * 128] = send[q].reshape(LONS, FD, 128).astype(BF16)
+    for q in range(GROUPS):
+        send_out[:, q * FP:q * FP + FD, :] = send[q].reshape(LONS, FD, 128).astype(BF16)
+
+
+def slot_row(slot):
+    return slot * FP + FD if slot < GROUPS else GROUPS * FP + (slot - GROUPS) * 8
+
+
+def piece_place(piece):
+    return 2 * MD + piece // GROUPS * 8, piece % GROUPS * 128
 
 
 def dft_kernel(rows, columns, out):
-    got = jnp.dot(rows[...], columns[...], preferred_element_type=F32)
+    wide = jnp.concatenate(
+        [columns[:, q * FP:(q + 1) * FP, :].reshape(LONS * FP, 128) for q in range(GROUPS)], axis=1
+    )
+    got = jnp.dot(rows[...], wide, preferred_element_type=F32)
     got = (got * (1.0 / math.sqrt(NLON))).astype(BF16)
-    total = jnp.zeros((FP - FD, 2 * 128), F32)
-    for j in range(LONS):
-        total = total + columns[j * FP + 16:(j + 1) * FP, :256].astype(F32)[8:]
-    total = jnp.concatenate([total, jnp.zeros((FP - FD, CD * TP - 256), F32)], axis=1).astype(BF16)
     for i in range(LATS):
         out[i, :2 * MD, :] = got[i * 2 * MD:(i + 1) * 2 * MD]
-        out[i, 2 * MD:, :] = total
+    for half in range(2):
+        for slot in range(SLOTS):
+            first = slot_row(slot) // 16 * 16
+            start = slot_row(slot) - first
+            total = columns[half, first:first + 16, :].astype(F32)
+            for chip in range(1, CHIPS):
+                total = total + columns[2 * chip + half, first:first + 16, :].astype(F32)
+            total = total[start:start + 8].astype(BF16)
+            row, lane = piece_place(half * SLOTS + slot)
+            for i in range(LATS):
+                out[i, row:row + 8, lane:lane + 128] = total
 
 
 HALF = LATS // 2 * TP
@@ -246,48 +270,63 @@
                 out[p, c, :, h * 128:(h + 1) * 128] = rows[h, base:base + MSTEP, :]
 
 
-HALF_TILES = MD // 16 * (K * C // 128)
+HALF_TILES = C // 32 * (K * C // 128)
 
 
 def tiles_of(chip):
-    return [(side, *divmod(2 * chip + side, K * C // 128)) for side in range(2) if 2 * chip + side < HALF_TILES]
-
-
-def sum_lat_kernel(parts, send, out, rows, sem):
-    total = parts[0].astype(F32)
-    for i in range(1, LATS):
-        total = total + parts[i].astype(F32)
-    total = total.astype(BF16)
-    rows[...] = jnp.zeros_like(rows)
+    return [(slot, *divmod(SLOTS * chip + slot, K * C // 128)) for slot in range(SLOTS) if SLOTS * chip + slot < HALF_TILES]
+
+
+def chip_sum_kernel(mine, other, send, out, near_rows, far_rows, sems):
+    total = (mine[...] + other[...].astype(F32)).astype(BF16)
+    near_rows[...] = jnp.zeros_like(near_rows)
+    far_rows[...] = jnp.zeros_like(far_rows)
     for chip in range(CHIPS):
-        for side, row, col in tiles_of(chip):
+        for slot, row, col in tiles_of(chip):
             for core in range(2):
-                first = core * (MD // 2) + row * 8
-                rows[2 * chip + core, :, side * 128:(side + 1) * 128] = total[first:first + 8, col * 128:(col + 1) * 128]
-    copy = pltpu.make_async_copy(rows, out.at[:, FD:, :], sem)
-    copy.start()
-    copy.wait()
+                first = core * (C // 4) + row * 8
+                tile = total[first:first + 8, col * 128:(col + 1) * 128]
+                if slot < GROUPS:
+                    near_rows[slot, 2 * chip + core] = tile
+                else:
+                    far = (slot - GROUPS) * 8
+                    far_rows[2 * chip + core, far:far + 8, :] = tile
+    copies = [
+        pltpu.make_async_copy(near_rows.at[q], out.at[:, q * FP + FD:(q + 1) * FP, :], sems.at[q]) for q in range(GROUPS)
+    ]
+    copies.append(pltpu.make_async_copy(far_rows, out.at[:, GROUPS * FP:, :], sems.at[GROUPS]))
+    for copy in copies:
+        copy.start()
+    for copy in copies:
+        copy.wait()
 
 
 def copies_kernel(spec, out):
-    part = spec[:, 2 * MD:, :256]
-    for chip in range(CHIPS):
-        out[chip] = part
+    for piece in range(2 * SLOTS):
+        row, lane = piece_place(piece)
+        first = row // 16 * 16
+        total = spec[0, first:first + 16, lane:lane + 128].astype(F32)
+        for i in range(1, LATS):
+            total = total + spec[i, first:first + 16, lane:lane + 128].astype(F32)
+        total = total[row - first:row - first + 8].astype(BF16)
+        for chip in range(CHIPS):
+            out[chip, piece * 8:(piece + 1) * 8, :] = total
 
 
 def mix_kernel(core, mine, other, out, rows, sems):
     copies = []
-    for i in range(LATS):
-        for parts, half in ((mine, core[0]), (other, 1 - core[0])):
-            base = pl.multiple_of(i * MD + half * (MD // 2), 8)
+    for half in range(2):
+        for parts, held in ((mine, core[0]), (other, 1 - core[0])):
+            base = pl.multiple_of(half * (C // 2) + held * (C // 4), 8)
             for chip in range(CHIPS):
-                for side, row, col in tiles_of(chip):
+                for slot, row, col in tiles_of(chip):
                     k, d = divmod(col, C // 128)
+                    piece = (half * SLOTS + slot) * 8
                     rows[k, pl.ds(base + row * 8, 8), d * 128:(d + 1) * 128] = parts[
-                        chip, i, :, side * 128:(side + 1) * 128
+                        chip, piece:piece + 8, :
                     ].astype(F32)
-        span = pl.ds(i * MD, MD)
-        copies.append(pltpu.make_async_copy(rows.at[:, span], out.at[:, span], sems.at[i]))
+        span = pl.ds(half * (C // 2), C // 2)
+        copies.append(pltpu.make_async_copy(rows.at[:, span], out.at[:, span], sems.at[half]))
         copies[-1].start()
     for copy in copies:
         copy.wait()
@@ -363,22 +402,27 @@
     whole = pl.BlockSpec(memory_space=pltpu.VMEM)
     tab = tap_table(taps, offsets, counts, lat_pos * TD)
     cells = TD * FD
-    grown, mix_part = call(
+    core = jnp.reshape(lax.axis_index(CORE), (1,)).astype(jnp.int32)
+    scalar = pl.BlockSpec(memory_space=pltpu.SMEM)
+    anywhere = pl.BlockSpec(memory_space=pl.ANY)
+    half = (C // 2, K * C)
+    grown, mix_mine, mix_other = call(
         stencil_kernel,
-        (shape((cells, K * C), BF16), shape((C, K * C), BF16)),
+        (shape((cells, K * C), BF16), shape(half, F32), shape(half, BF16)),
         5,
-        in_specs=[whole] * 7,
+        in_specs=[scalar] + [whole] * 7,
         scratch_shapes=[pltpu.VMEM((TD + 2, XW, C), F32), pltpu.VMEM((K * QUAD * FD, 256), F32)],
         name="stencil",
-    )(near(tab), cotangent, near(left), near(right), near(top), near(bottom), field.reshape(cells, C))
-    mix_lat = lax.all_to_all(mix_part.reshape(LATS, MD, K * C), LAT, 0, 0, tiled=True)
+    )(core, near(tab), cotangent, near(left), near(right), near(top), near(bottom), field.reshape(cells, C))
+    swap = [(0, 1), (1, 0)]
+    mix_other = lax.ppermute(mix_other, CORE, swap)
 
     pos = jnp.reshape(lat_pos, (1,)).astype(jnp.int32)
     grad_field, send = call(
         field_kernel,
-        (shape((cells, C), BF16), shape((LONS, FP, CD * TP), BF16)),
+        (shape((cells, C), BF16), shape((LONS, SENT, 128), BF16)),
         5,
-        in_specs=[pl.BlockSpec(memory_space=pltpu.SMEM), whole, whole, whole],
+        in_specs=[scalar, whole, whole, whole],
         scratch_shapes=[
             pltpu.VMEM((C // 128, cells, 128), F32),
             pltpu.VMEM((FD // 4, C, 128), F32),
@@ -386,17 +430,20 @@
         ],
         name="grad_field",
     )(pos, grown, cotangent.reshape(cells, C), mix_weight)
-    anywhere = pl.BlockSpec(memory_space=pl.ANY)
     send = call(
-        sum_lat_kernel,
-        shape((LONS, FP, CD * TP), BF16),
+        chip_sum_kernel,
+        shape((LONS, SENT, 128), BF16),
         2,
-        in_specs=[whole, anywhere],
+        in_specs=[whole, whole, anywhere],
         out_specs=anywhere,
-        scratch_shapes=[pltpu.VMEM((LONS, FP - FD, CD * TP), BF16), pltpu.SemaphoreType.DMA],
-        input_output_aliases={1: 0},
-        name="mix_sum_lat",
-    )(near(mix_lat), send)
+        scratch_shapes=[
+            pltpu.VMEM((GROUPS, LONS, FP - FD, 128), BF16),
+            pltpu.VMEM((LONS, SENT - GROUPS * FP, 128), BF16),
+            pltpu.SemaphoreType.DMA((GROUPS + 1,)),
+        ],
+        input_output_aliases={2: 0},
+        name="mix_chip_sum",
+    )(near(mix_mine), near(mix_other), send)
     columns = lax.all_to_all(send, LON, 0, 0, tiled=True)
 
     cosine, logsine = latitudes()
@@ -429,11 +476,11 @@
     )(pos, jnp.asarray(cosine), logscale)
     columns, table = lax.optimization_barrier((columns, table))
 
-    spectra = call(dft_kernel, shape((LATS, 2 * MD + FP - FD, CD * TP), BF16), 2, in_specs=[whole, whole], name="dft")(
-        near(jnp.asarray(dft_rows())), near(columns.reshape(LONS * FP, CD * TP))
+    spectra = call(dft_kernel, shape((LATS, 2 * MD + SPREAD, CD * TP), BF16), 2, in_specs=[whole, whole], name="dft")(
+        near(jnp.asarray(dft_rows())), near(columns)
     )
     spec = lax.all_to_all(spectra, LAT, 0, 0, tiled=True)
-    mix_copies = call(copies_kernel, shape((CHIPS, LATS, 8, 256), BF16), 2, in_specs=[whole], name="mix_copies")(near(spec))
+    mix_copies = call(copies_kernel, shape((CHIPS, 2 * SLOTS * 8, 128), BF16), 2, in_specs=[whole], name="mix_copies")(near(spec))
     mix_mine = lax.all_to_all(mix_copies, CHIP, 0, 0, tiled=True)
 
     grad_spectra = call(
@@ -456,16 +503,16 @@
         name="synthesis",
     )(near(spec), table)
     mix_mine, grad_spectra = lax.optimization_barrier((mix_mine, grad_spectra))
-    mix_other = lax.ppermute(mix_mine, CORE, [(0, 1), (1, 0)])
+    mix_other = lax.ppermute(mix_mine, CORE, swap)
     grad_mix = call(
         mix_kernel,
         shape((K, C, C), F32),
         2,
-        in_specs=[pl.BlockSpec(memory_space=pltpu.SMEM), whole, whole],
+        in_specs=[scalar, whole, whole],
         out_specs=anywhere,
-        scratch_shapes=[pltpu.VMEM((K, C, C), F32), pltpu.SemaphoreType.DMA((LATS,))],
+        scratch_shapes=[pltpu.VMEM((K, C, C), F32), pltpu.SemaphoreType.DMA((2,))],
         name="mix_out",
-    )(jnp.reshape(lax.axis_index(CORE), (1,)).astype(jnp.int32), near(mix_mine), near(mix_other))
+    )(core, near(mix_mine), near(mix_other))
     return (grad_field.reshape(TD, FD, C), jnp.transpose(grad_spectra, (0, 2, 1, 3)), grad_mix)
 
 

time: 119 us -> 115 us (0.966)
  starting transfers between devices: 36.6 us -> 29.9 us
  blocking collectives: 13.8 us -> 17.7 us
  waiting for transfers between devices: 27.9 us -> 26.1 us
    all_to_all x1, starting transfers between devices: 12.2 us -> 3.73 us  [on_device(): columns = lax.all_to_all(send, LON, 0, 0, tiled=True)]
    ppermute x1 -> x2, starting transfers between devices: 2.87 us -> 10.2 us  [the longest x1 7.24 us: on_device(): mix_other = lax.ppermute(mix_other, CORE, swap)]
    all_to_all x1 -> x0, starting transfers between devices: 5.62 us -> none  [on_device(): lax.all_to_all(mix_part.reshape(LATS, MD, K * C), LAT, 0, 0, tiled=True)]
    all_to_all x1 -> x0, waiting for transfers between devices: 5.49 us -> none  [on_device(): lax.all_to_all(mix_part.reshape(LATS, MD, K * C), LAT, 0, 0, tiled=True)]
    all_to_all x1, waiting for transfers between devices: 8.58 us -> 13.6 us  [on_device(): columns = lax.all_to_all(send, LON, 0, 0, tiled=True)]
    all_to_all x1, blocking collectives: 13.8 us -> 17.7 us  [on_device(): spec = lax.all_to_all(spectra, LAT, 0, 0, tiled=True)]
    all_to_all x1, waiting for transfers between devices: 6.03 us -> 4.76 us  [on_device(): mix_mine = lax.all_to_all(mix_copies, CHIP, 0, 0, tiled=True)]
  transfers between devices with their start and end apart: 8 -> 8, of which waited for: 6 -> 5; matrix products, arithmetic and copies ran while one was open for 5% -> 5% of each run, Pallas kernels for 20% -> 21%
where the time goes in v5:
time: 115 us; the launch traced here: 114 us
  Pallas kernels  32.9 us (29%)
  starting transfers between devices  29.9 us (26%)
  waiting for transfers between devices  26.1 us (23%)
  blocking collectives  17.7 us (15%)
  other arithmetic  3.6 us (3%)
  local copies, waits for them, and re-layouts  2.84 us (2%)
    all_to_all x1, blocking collectives, on_device(): spec = lax.all_to_all(spectra, LAT, 0, 0, tiled=True)  17.7 us
    all_to_all x1, waiting for transfers between devices, on_device(): columns = lax.all_to_all(send, LON, 0, 0, tiled=True)  13.6 us
    pallas_call x1, Pallas kernels, on_device(): call(legendre_kernel, shape((MD // 2, L, 2 * HALF), BF16), 9, grid_spec=p...  11.4 us
    ppermute x1, starting transfers between devices, on_device(): mix_other = lax.ppermute(mix_other, CORE, swap)  7.24 us
    pallas_call x1, Pallas kernels, on_device(): call(synthesis_kernel, shape((2, CD, MD, L), F32), 6, grid_spec=pltpu.Pre...  7.15 us
    all_to_all x1, starting transfers between devices, on_device(): mix_mine = lax.all_to_all(mix_copies, CHIP, 0, 0, tiled=True)  6.89 us
    pallas_call x1, Pallas kernels, on_device(): call(field_kernel, (shape((cells, C), BF16), shape((LONS, SENT, 128), BF1...  4.84 us
    all_to_all x1, waiting for transfers between devices, on_device(): mix_mine = lax.all_to_all(mix_copies, CHIP, 0, 0, tiled=True)  4.76 us
  transfers between devices with their start and end apart: 8, of which 5 were waited for; matrix products, arithmetic and copies ran while one was open for 5% of the time, Pallas kernels for 21%

profile of v5, /device:TPU:1, one launch (start us, length us, event | category | flops | bytes accessed | tf_op | source)
XLA Modules:
  0.0 113.8 jit_solution(10136101351766425583)
XLA Ops:
  0.6 1.0 fusion.8
  1.6 3.3 %collective-permute-start.1 = (bf16[24,8,384]{2,1,0:T(8,128)(2,1)S(1)}, bf16[24,8,384]{2,1,0:T(8,128)(2,1)S(1)}, u32[]{:S(2)}, u32[]{:S(2)}) collective-permute-start(bf16[24,8,384]{2,1,0:T(8,128)(2,1)S(1)} %get-tuple-element.25), channel_id=1, source_target_pairs={{1,0},{2,1},{3,2},{4,3},{5,4},{6,5},{7,6},{8,7},{9,8},{10,9},{11,1... | collective-permute-start | bytes 442376 | tf_op jit(solution)/shard_map/ppermute | solution.py:393
  5.0 0.0 collective-permute-start
  5.0 0.7 convert_bitcast_fusion
  5.7 0.9 fusion.6
  6.6 0.1 fusion.1
  6.7 0.1 slice_bitcast_fusion.2
  6.8 0.1 copy.17
  6.9 0.1 copy.18
  6.9 0.1 copy.19
  7.0 0.8 fusion.7
  7.8 0.0 collective-permute-done.1.right
  7.8 2.6 %collective-permute-done.left = bf16[24,8,384]{2,1,0:T(8,128)(2,1)S(1)} collective-permute-done((bf16[24,8,384]{2,1,0:T(8,128)(2,1)S(1)}, bf16[24,8,384]{2,1,0:T(8,128)(2,1)S(1)}, u32[]{:S(2)}, u32[]{:S(2)}) %collective-permute-start) | collective-permute-done | bytes 147488 | tf_op jit(solution)/shard_map/ppermute | solution.py:392
  10.4 4.5 %collective-permute-start.2 = (bf16[1,40,384]{2,1,0:T(8,128)(2,1)S(1)}, bf16[1,40,384]{2,1,0:T(8,128)(2,1)S(1)}, u32[]{:S(2)}, u32[]{:S(2)}) collective-permute-start(bf16[1,40,384]{2,1,0:T(8,128)(2,1)S(1)} %pad_maximum_fusion), channel_id=1, source_target_pairs={{0,32},{32,64},{64,96},{96,128},{128,160},{160,192},{192,224},{1,3... | collective-permute-start | bytes 92168 | tf_op jit(solution)/shard_map/ppermute | solution.py:399
  15.0 1.3 %collective-permute-start.3 = (bf16[1,40,384]{2,1,0:T(8,128)(2,1)S(1)}, bf16[1,40,384]{2,1,0:T(8,128)(2,1)S(1)}, u32[]{:S(2)}, u32[]{:S(2)}) collective-permute-start(bf16[1,40,384]{2,1,0:T(8,128)(2,1)S(1)} %pad_maximum_fusion.1), channel_id=1, source_target_pairs={{32,0},{64,32},{96,64},{128,96},{160,128},{192,160},{224,192},{33,... | collective-permute-start | bytes 92168 | tf_op jit(solution)/shard_map/ppermute | solution.py:400
  16.3 1.2 %multiply_add_fusion.tab = f32[24,32,256]{2,1,0:T(8,128)S(1)} fusion(f32[24,256]{1,0:T(8,128)} %constant.52, f32[24,32]{1,0:T(8,128)S(1)} %copy.19, f32[24,256]{1,0:T(8,128)} %constant.51, f32[24,32]{1,0:T(8,128)S(1)} %copy.18, f32[24,256]{1,0:T(8,128)} %constant.50, f32[24,32]{1,0:T(8,128)S(1)} %copy.17), kind=kLoop, calls=%fused_computation | loop fusion | flops 983040 | bytes 869376 | tf_op jit(solution)/shard_map/add | solution.py:384
  17.4 0.0 collective-permute-done.2.top
  17.4 3.7 %collective-permute-done.3.bottom = bf16[1,40,384]{2,1,0:T(8,128)(2,1)S(1)} collective-permute-done((bf16[1,40,384]{2,1,0:T(8,128)(2,1)S(1)}, bf16[1,40,384]{2,1,0:T(8,128)(2,1)S(1)}, u32[]{:S(2)}, u32[]{:S(2)}) %collective-permute-start.3) | collective-permute-done | bytes 30752 | tf_op jit(solution)/shard_map/ppermute | solution.py:400
  21.1 4.6 %stencil.1 = (bf16[576,1152]{1,0:T(8,128)(2,1)}, f32[192,1152]{1,0:T(8,128)}, bf16[192,1152]{1,0:T(8,128)(2,1)}) custom-call(s32[1]{0:T(128)} %bitcast.1.core, f32[24,32,256]{2,1,0:T(8,128)S(1)} %multiply_add_fusion.tab, bf16[24,24,384]{2,1,0:T(8,128)(2,1)} %cot.1, bf16[24,8,384]{2,1,0:T(8,128)(2,1)S(1)} %collective-permute-done.left, ...), custom_call_target="tpu_custom_call" | custom-call | flops 5500000256 | bytes 15000000 | tf_op jit(solution)/shard_map/stencil/pallas_call | solution.py:409
  25.7 7.2 %collective-permute-start.4 = (bf16[192,1152]{1,0:T(8,128)(2,1)}, bf16[192,1152]{1,0:T(8,128)(2,1)S(1)}, u32[]{:S(2)}, u32[]{:S(2)}) collective-permute-start(bf16[192,1152]{1,0:T(8,128)(2,1)} %get-tuple-element.16), channel_id=1, source_target_pairs={{0,1},{1,0},{2,3},{3,2},{4,5},{5,4},{6,7},{7,6},{8,9},{9,8},{10,11... | collective-permute-start | bytes 1327112 | tf_op jit(solution)/shard_map/ppermute | solution.py:418
  32.9 0.0 copy-start.1
  32.9 4.8 %grad_field.1 = (bf16[576,384]{1,0:T(8,128)(2,1)}, bf16[32,128,128]{2,1,0:T(8,128)(2,1)}) custom-call(s32[1]{0:T(128)} %bitcast.pos, bf16[576,1152]{1,0:T(8,128)(2,1)} %get-tuple-element.13.g, bf16[576,384]{1,0:T(8,128)(2,1)} %bitcast.14, bf16[3,384,384]{2,1,0:T(8,128)(2,1)} %mix.1), custom_call_target="tpu_custom_call" | custom-call | flops 5500000256 | bytes 15000000 | tf_op jit(solution)/shard_map/grad_field/pallas_call | solution.py:421
  37.8 0.0 collective-permute-done.4.other
  37.8 0.0 copy-done.1
  37.8 0.9 mix_chip_sum.1
  38.7 0.0 copy-start.2
  38.7 3.7 %all-to-all-start = ((bf16[32,128,128]{2,1,0:T(8,128)(2,1)}), bf16[32,128,128]{2,1,0:T(8,128)(2,1)S(1)}, u32[]{:S(2)}, u32[]{:S(2)}) async-start(bf16[32,128,128]{2,1,0:T(8,128)(2,1)} %mix_chip_sum.1), calls=%async_computation | async-start | bytes 2097152 | tf_op jit(solution)/shard_map/all_to_all | solution.py:447
  42.4 0.8 dynamic_slice.7
  43.2 0.0 copy-done.2
  43.2 0.7 multiply_add_fusion.1.logscale
  43.9 0.0 copy-start
  43.9 11.4 %legendre.1.leg = bf16[24,384,256]{2,1,0:T(8,128)(2,1)} custom-call(s32[1]{0:T(128)} %bitcast.pos, f32[1,128]{1,0:T(1,128)} %constant.44.clone.cosines, f32[48,128]{1,0:T(8,128)} %multiply_add_fusion.1.logscale), custom_call_target="tpu_custom_call" | custom-call | flops 9900000256 | bytes 27000000 | tf_op jit(solution)/shard_map/legendre/pallas_call | solution.py:455
  55.3 13.6 %all-to-all-done.columns = bf16[32,128,128]{2,1,0:T(8,128)(2,1)S(1)} async-done(((bf16[32,128,128]{2,1,0:T(8,128)(2,1)}), bf16[32,128,128]{2,1,0:T(8,128)(2,1)S(1)}, u32[]{:S(2)}, u32[]{:S(2)}) %all-to-all-start) | async-done | bytes 1048608 | tf_op jit(solution)/shard_map/all_to_all | solution.py:447
  68.8 0.0 copy-done
  68.8 1.9 %dft.1 = bf16[8,136,384]{2,1,0:T(8,128)(2,1)} custom-call(bf16[768,1024]{1,0:T(8,128)(2,1)S(1)} %copy-done, bf16[32,128,128]{2,1,0:T(8,128)(2,1)S(1)} %all-to-all-done.columns), custom_call_target="tpu_custom_call" | custom-call | flops 2200000000 | bytes 6000000 | tf_op jit(solution)/shard_map/dft/pallas_call | solution.py:479
  70.7 17.7 %all_to_all.15.spec = bf16[8,136,384]{2,1,0:T(8,128)(2,1)S(1)} all-to-all(bf16[8,136,384]{2,1,0:T(8,128)(2,1)} %dft.1), channel_id=1, replica_groups=mesh['lat'=8,'chip'=16,'core'=2] {'lat'}, dimensions={0} | all-to-all | bytes 1671168 | tf_op jit(solution)/shard_map/all_to_all | solution.py:482
  88.5 0.8 mix_copies.1
  89.3 6.9 %all-to-all-start.2 = ((bf16[16,112,128]{2,1,0:T(8,128)(2,1)}), bf16[16,112,128]{2,1,0:T(8,128)(2,1)S(1)}, u32[]{:S(2)}, u32[]{:S(2)}) async-start(bf16[16,112,128]{2,1,0:T(8,128)(2,1)} %mix_copies.1), calls=%async_computation.2 | async-start | bytes 917504 | tf_op jit(solution)/shard_map/all_to_all | solution.py:484
  96.2 7.2 %synthesis.1 = f32[2,12,48,384]{3,2,1,0:T(8,128)} custom-call(bf16[8,136,384]{2,1,0:T(8,128)(2,1)S(1)} %all_to_all.15.spec, bf16[24,384,256]{2,1,0:T(8,128)(2,1)} %legendre.1.leg), custom_call_target="tpu_custom_call" | custom-call | flops 6600000000 | bytes 18000000 | tf_op jit(solution)/shard_map/synthesis/pallas_call | solution.py:486
  103.4 4.8 %all-to-all-done.2.mine = bf16[16,112,128]{2,1,0:T(8,128)(2,1)S(1)} async-done(((bf16[16,112,128]{2,1,0:T(8,128)(2,1)}), bf16[16,112,128]{2,1,0:T(8,128)(2,1)S(1)}, u32[]{:S(2)}, u32[]{:S(2)}) %all-to-all-start.2) | async-done | bytes 458784 | tf_op jit(solution)/shard_map/all_to_all | solution.py:484
  108.1 2.9 %collective-permute-start.5 = (bf16[16,112,128]{2,1,0:T(8,128)(2,1)S(1)}, bf16[16,112,128]{2,1,0:T(8,128)(2,1)S(1)}, u32[]{:S(2)}, u32[]{:S(2)}) collective-permute-start(bf16[16,112,128]{2,1,0:T(8,128)(2,1)S(1)} %all-to-all-done.2.mine), channel_id=1, source_target_pairs={{0,1},{1,0},{2,3},{3,2},{4,5},{5,4},{6,7},{7,6},{8,9},{9,8},{10,11... | collective-permute-start | bytes 1376264 | tf_op jit(solution)/shard_map/ppermute | solution.py:506
  111.0 1.4 %collective-permute-done.5.other = bf16[16,112,128]{2,1,0:T(8,128)(2,1)S(1)} collective-permute-done((bf16[16,112,128]{2,1,0:T(8,128)(2,1)S(1)}, bf16[16,112,128]{2,1,0:T(8,128)(2,1)S(1)}, u32[]{:S(2)}, u32[]{:S(2)}) %collective-permute-start.5) | collective-permute-done | bytes 458784 | tf_op jit(solution)/shard_map/ppermute | solution.py:506
  112.5 1.3 %mix_out.1 = f32[3,384,384]{2,1,0:T(8,128)} custom-call(s32[1]{0:T(128)} %bitcast.1.core, bf16[16,112,128]{2,1,0:T(8,128)(2,1)S(1)} %all-to-all-done.2.mine, bf16[16,112,128]{2,1,0:T(8,128)(2,1)S(1)} %collective-permute-done.5.other), custom_call_target="tpu_custom_call" | custom-call | flops 2200000000 | bytes 6000000 | tf_op jit(solution)/shard_map/mix_out/pallas_call | solution.py:507
  (5 shorter events, 0.0 us)
Async XLA Ops:
  1.6 6.1 %collective-permute-start.1 = (bf16[24,8,384]{2,1,0:T(8,128)(2,1)S(1)}, bf16[24,8,384]{2,1,0:T(8,128)(2,1)S(1)}, u32[]{:S(2)}, u32[]{:S(2)}) collective-permute-start(bf16[24,8,384]{2,1,0:T(8,128)(2,1)S(1)} %get-tuple-element.25), channel_id=1, source_target_pairs={{1,0},{2,1},{3,2},{4,3},{5,4},{6,5},{7,6},{8,7},{9,8},{10,9},{11,1... | collective-permute-start | bytes 442376 | tf_op jit(solution)/shard_map/ppermute | solution.py:393
  5.0 5.4 %collective-permute-start = (bf16[24,8,384]{2,1,0:T(8,128)(2,1)S(1)}, bf16[24,8,384]{2,1,0:T(8,128)(2,1)S(1)}, u32[]{:S(2)}, u32[]{:S(2)}) collective-permute-start(bf16[24,8,384]{2,1,0:T(8,128)(2,1)S(1)} %get-tuple-element.26), channel_id=1, source_target_pairs={{0,1},{1,2},{2,3},{3,4},{4,5},{5,6},{6,7},{7,8},{8,9},{9,10},{10,1... | collective-permute-start | bytes 442376 | tf_op jit(solution)/shard_map/ppermute | solution.py:392
  10.4 7.0 %collective-permute-start.2 = (bf16[1,40,384]{2,1,0:T(8,128)(2,1)S(1)}, bf16[1,40,384]{2,1,0:T(8,128)(2,1)S(1)}, u32[]{:S(2)}, u32[]{:S(2)}) collective-permute-start(bf16[1,40,384]{2,1,0:T(8,128)(2,1)S(1)} %pad_maximum_fusion), channel_id=1, source_target_pairs={{0,32},{32,64},{64,96},{96,128},{128,160},{160,192},{192,224},{1,3... | collective-permute-start | bytes 92168 | tf_op jit(solution)/shard_map/ppermute | solution.py:399
  15.0 6.1 %collective-permute-start.3 = (bf16[1,40,384]{2,1,0:T(8,128)(2,1)S(1)}, bf16[1,40,384]{2,1,0:T(8,128)(2,1)S(1)}, u32[]{:S(2)}, u32[]{:S(2)}) collective-permute-start(bf16[1,40,384]{2,1,0:T(8,128)(2,1)S(1)} %pad_maximum_fusion.1), channel_id=1, source_target_pairs={{32,0},{64,32},{96,64},{128,96},{160,128},{192,160},{224,192},{33,... | collective-permute-start | bytes 92168 | tf_op jit(solution)/shard_map/ppermute | solution.py:400
  25.7 12.1 %collective-permute-start.4 = (bf16[192,1152]{1,0:T(8,128)(2,1)}, bf16[192,1152]{1,0:T(8,128)(2,1)S(1)}, u32[]{:S(2)}, u32[]{:S(2)}) collective-permute-start(bf16[192,1152]{1,0:T(8,128)(2,1)} %get-tuple-element.16), channel_id=1, source_target_pairs={{0,1},{1,0},{2,3},{3,2},{4,5},{5,4},{6,7},{7,6},{8,9},{9,8},{10,11... | collective-permute-start | bytes 1327112 | tf_op jit(solution)/shard_map/ppermute | solution.py:418
  32.9 4.9 %copy-start.1 = (f32[192,1152]{1,0:T(8,128)S(1)}, f32[192,1152]{1,0:T(8,128)}, u32[]{:S(2)}) copy-start(f32[192,1152]{1,0:T(8,128)} %get-tuple-element.15.mine) | copy-start | bytes 2654212
  38.7 4.5 %copy-start.2 = (f32[128]{0:T(128)S(1)}, f32[128]{0:T(128)}, u32[]{:S(2)}) copy-start(f32[128]{0:T(128)} %constant.53) | copy-start | bytes 1540
  38.7 30.1 %all-to-all-start = ((bf16[32,128,128]{2,1,0:T(8,128)(2,1)}), bf16[32,128,128]{2,1,0:T(8,128)(2,1)S(1)}, u32[]{:S(2)}, u32[]{:S(2)}) async-start(bf16[32,128,128]{2,1,0:T(8,128)(2,1)} %mix_chip_sum.1), calls=%async_computation | async-start | bytes 2097152 | tf_op jit(solution)/shard_map/all_to_all | solution.py:447
  43.9 24.9 %copy-start = (bf16[768,1024]{1,0:T(8,128)(2,1)S(1)}, bf16[768,1024]{1,0:T(8,128)(2,1)}, u32[]{:S(2)}) copy-start(bf16[768,1024]{1,0:T(8,128)(2,1)} %constant.45.clone.rows) | copy-start | bytes 4718596
  89.3 18.8 %all-to-all-start.2 = ((bf16[16,112,128]{2,1,0:T(8,128)(2,1)}), bf16[16,112,128]{2,1,0:T(8,128)(2,1)S(1)}, u32[]{:S(2)}, u32[]{:S(2)}) async-start(bf16[16,112,128]{2,1,0:T(8,128)(2,1)} %mix_copies.1), calls=%async_computation.2 | async-start | bytes 917504 | tf_op jit(solution)/shard_map/all_to_all | solution.py:484
  108.1 4.4 %collective-permute-start.5 = (bf16[16,112,128]{2,1,0:T(8,128)(2,1)S(1)}, bf16[16,112,128]{2,1,0:T(8,128)(2,1)S(1)}, u32[]{:S(2)}, u32[]{:S(2)}) collective-permute-start(bf16[16,112,128]{2,1,0:T(8,128)(2,1)S(1)} %all-to-all-done.2.mine), channel_id=1, source_target_pairs={{0,1},{1,0},{2,3},{3,2},{4,5},{5,4},{6,7},{7,6},{8,9},{9,8},{10,11... | collective-permute-start | bytes 1376264 | tf_op jit(solution)/shard_map/ppermute | solution.py:506

commit v6 on v5

--- a/solution.py
+++ b/solution.py
@@ -59,6 +59,10 @@
 
 def shape(dims, dtype):
     return jax.ShapeDtypeStruct(dims, dtype)
+
+
+def near_shape(dims, dtype):
+    return pltpu.VMEM(dims, dtype)
 
 
 def swap_blocks(parts):
@@ -400,6 +404,7 @@
     bottom = lax.ppermute(edge_rows[0], LAT, south)
 
     whole = pl.BlockSpec(memory_space=pltpu.VMEM)
+    taps, offsets, counts, _ = lax.optimization_barrier((taps, offsets, counts, edge_rows))
     tab = tap_table(taps, offsets, counts, lat_pos * TD)
     cells = TD * FD
     core = jnp.reshape(lax.axis_index(CORE), (1,)).astype(jnp.int32)
@@ -408,12 +413,12 @@
     half = (C // 2, K * C)
     grown, mix_mine, mix_other = call(
         stencil_kernel,
-        (shape((cells, K * C), BF16), shape(half, F32), shape(half, BF16)),
+        (near_shape((cells, K * C), BF16), near_shape(half, F32), near_shape(half, BF16)),
         5,
         in_specs=[scalar] + [whole] * 7,
         scratch_shapes=[pltpu.VMEM((TD + 2, XW, C), F32), pltpu.VMEM((K * QUAD * FD, 256), F32)],
         name="stencil",
-    )(core, near(tab), cotangent, near(left), near(right), near(top), near(bottom), field.reshape(cells, C))
+    )(core, near(tab), near(cotangent), near(left), near(right), near(top), near(bottom), near(field.reshape(cells, C)))
     swap = [(0, 1), (1, 0)]
     mix_other = lax.ppermute(mix_other, CORE, swap)
 
@@ -429,7 +434,7 @@
             pltpu.VMEM((CD // 4, LONS * FD, 128), F32),
         ],
         name="grad_field",
-    )(pos, grown, cotangent.reshape(cells, C), mix_weight)
+    )(pos, near(grown), near(cotangent.reshape(cells, C)), near(mix_weight))
     send = call(
         chip_sum_kernel,
         shape((LONS, SENT, 128), BF16),
@@ -476,11 +481,11 @@
     )(pos, jnp.asarray(cosine), logscale)
     columns, table = lax.optimization_barrier((columns, table))
 
-    spectra = call(dft_kernel, shape((LATS, 2 * MD + SPREAD, CD * TP), BF16), 2, in_specs=[whole, whole], name="dft")(
+    spectra = call(dft_kernel, near_shape((LATS, 2 * MD + SPREAD, CD * TP), BF16), 2, in_specs=[whole, whole], name="dft")(
         near(jnp.asarray(dft_rows())), near(columns)
     )
     spec = lax.all_to_all(spectra, LAT, 0, 0, tiled=True)
-    mix_copies = call(copies_kernel, shape((CHIPS, 2 * SLOTS * 8, 128), BF16), 2, in_specs=[whole], name="mix_copies")(near(spec))
+    mix_copies = call(copies_kernel, near_shape((CHIPS, 2 * SLOTS * 8, 128), BF16), 2, in_specs=[whole], name="mix_copies")(near(spec))
     mix_mine = lax.all_to_all(mix_copies, CHIP, 0, 0, tiled=True)
 
     grad_spectra = call(

time: 115 us -> 109 us (0.948)
  Pallas kernels: 32.9 us -> 28 us
  waiting for transfers between devices: 26.1 us -> 23.4 us
  blocking collectives: 17.7 us -> 19.3 us
    ppermute x1, waiting for transfers between devices: 3.66 us -> 0.01 us  [on_device(): bottom = lax.ppermute(edge_rows[0], LAT, south)]
    ppermute x1, starting transfers between devices: 7.24 us -> 3.71 us  [on_device(): mix_other = lax.ppermute(mix_other, CORE, swap)]
    pallas_call x3, Pallas kernels: 7.33 us -> 4.23 us  [the longest x1 2.41 us: on_device(): call(stencil_kernel, (near_shape((cells, K * C), BF16), near_shape(half,...]
    ppermute x1, starting transfers between devices: 0.01 us -> 3.1 us  [on_device(): left = lax.ppermute(cotangent[:, FD - R:], LON, up)]
    ppermute x1, starting transfers between devices: 3.32 us -> 0.3 us  [on_device(): right = lax.ppermute(cotangent[:, :R], LON, down)]
    all_to_all x1, starting transfers between devices: 3.73 us -> 6.4 us  [on_device(): columns = lax.all_to_all(send, LON, 0, 0, tiled=True)]
    ppermute x1, waiting for transfers between devices: 0.01 us -> 2.46 us  [on_device(): right = lax.ppermute(cotangent[:, :R], LON, down)]
    pallas_call x1, Pallas kernels: 4.84 us -> 3.06 us  [on_device(): call(field_kernel, (shape((cells, C), BF16), shape((LONS, SENT, 128), BF1...]
  transfers between devices with their start and end apart: 8 -> 8, of which waited for: 5 -> 5; matrix products, arithmetic and copies ran while one was open for 5% -> 5% of each run, Pallas kernels for 21% -> 20%
where the time goes in v6:
time: 109 us; the launch traced here: 108 us
  starting transfers between devices  29.9 us (27%)
  Pallas kernels  28 us (26%)
  waiting for transfers between devices  23.4 us (21%)
  blocking collectives  19.3 us (18%)
  other arithmetic  3.62 us (3%)
  local copies, waits for them, and re-layouts  2.91 us (3%)
    all_to_all x1, blocking collectives, on_device(): spec = lax.all_to_all(spectra, LAT, 0, 0, tiled=True)  19.3 us
    all_to_all x1, waiting for transfers between devices, on_device(): columns = lax.all_to_all(send, LON, 0, 0, tiled=True)  13.7 us
    pallas_call x1, Pallas kernels, on_device(): call(legendre_kernel, shape((MD // 2, L, 2 * HALF), BF16), 9, grid_spec=p...  11.3 us
    pallas_call x1, Pallas kernels, on_device(): call(synthesis_kernel, shape((2, CD, MD, L), F32), 6, grid_spec=pltpu.Pre...  7.15 us
    all_to_all x1, starting transfers between devices, on_device(): mix_mine = lax.all_to_all(mix_copies, CHIP, 0, 0, tiled=True)  6.71 us
    all_to_all x1, starting transfers between devices, on_device(): columns = lax.all_to_all(send, LON, 0, 0, tiled=True)  6.4 us
    ppermute x1, starting transfers between devices, on_device(): top = lax.ppermute(edge_rows[1], LAT, north)  5.49 us
    all_to_all x1, waiting for transfers between devices, on_device(): mix_mine = lax.all_to_all(mix_copies, CHIP, 0, 0, tiled=True)  4.74 us
  transfers between devices with their start and end apart: 8, of which 5 were waited for; matrix products, arithmetic and copies ran while one was open for 5% of the time, Pallas kernels for 20%

profile of v6, /device:TPU:1, one launch (start us, length us, event | category | flops | bytes accessed | tf_op | source)
XLA Modules:
  0.0 107.9 jit_solution(15420431441733686353)
XLA Ops:
  0.6 0.0 copy-start
  0.6 0.0 copy-start.2
  0.7 1.1 %fusion.8 = (bf16[24,8,384]{2,1,0:T(8,128)(2,1)S(1)}, bf16[24,8,384]{2,1,0:T(8,128)(2,1)S(1)}) fusion(bf16[24,24,384]{2,1,0:T(8,128)(2,1)} %cot.1), kind=kLoop, calls=%fused_computation.22 | loop fusion | bytes 589824 | tf_op jit(solution)/shard_map/slice | solution.py:396
  1.7 3.1 %collective-permute-start = (bf16[24,8,384]{2,1,0:T(8,128)(2,1)S(1)}, bf16[24,8,384]{2,1,0:T(8,128)(2,1)S(1)}, u32[]{:S(2)}, u32[]{:S(2)}) collective-permute-start(bf16[24,8,384]{2,1,0:T(8,128)(2,1)S(1)} %get-tuple-element.31), channel_id=1, source_target_pairs={{0,1},{1,2},{2,3},{3,4},{4,5},{5,6},{6,7},{7,8},{8,9},{9,10},{10,1... | collective-permute-start | bytes 442376 | tf_op jit(solution)/shard_map/ppermute | solution.py:396
  4.8 0.3 collective-permute-start.1
  5.2 0.7 fusion.7
  5.9 1.1 collective-permute-done.left
  7.0 2.5 %collective-permute-done.1.right = bf16[24,8,384]{2,1,0:T(8,128)(2,1)S(1)} collective-permute-done((bf16[24,8,384]{2,1,0:T(8,128)(2,1)S(1)}, bf16[24,8,384]{2,1,0:T(8,128)(2,1)S(1)}, u32[]{:S(2)}, u32[]{:S(2)}) %collective-permute-start.1) | collective-permute-done | bytes 147488 | tf_op jit(solution)/shard_map/ppermute | solution.py:397
  9.4 1.3 %collective-permute-start.3 = (bf16[1,40,384]{2,1,0:T(8,128)(2,1)S(1)}, bf16[1,40,384]{2,1,0:T(8,128)(2,1)S(1)}, u32[]{:S(2)}, u32[]{:S(2)}) collective-permute-start(bf16[1,40,384]{2,1,0:T(8,128)(2,1)S(1)} %pad_maximum_fusion), channel_id=1, source_target_pairs={{32,0},{64,32},{96,64},{128,96},{160,128},{192,160},{224,192},{33,... | collective-permute-start | bytes 92168 | tf_op jit(solution)/shard_map/ppermute | solution.py:404
  10.7 5.5 %collective-permute-start.2 = (bf16[1,40,384]{2,1,0:T(8,128)(2,1)S(1)}, bf16[1,40,384]{2,1,0:T(8,128)(2,1)S(1)}, u32[]{:S(2)}, u32[]{:S(2)}) collective-permute-start(bf16[1,40,384]{2,1,0:T(8,128)(2,1)S(1)} %pad_maximum_fusion.1), channel_id=1, source_target_pairs={{0,32},{32,64},{64,96},{96,128},{128,160},{160,192},{192,224},{1,3... | collective-permute-start | bytes 92168 | tf_op jit(solution)/shard_map/ppermute | solution.py:403
  16.2 0.7 convert_bitcast_fusion
  17.0 0.9 fusion.6
  17.9 0.1 fusion.1
  18.0 0.1 slice_bitcast_fusion.2
  18.1 0.1 copy.17
  18.1 0.1 copy.18
  18.2 0.1 copy.19
  18.3 1.2 %multiply_add_fusion.tab = f32[24,32,256]{2,1,0:T(8,128)S(1)} fusion(f32[24,256]{1,0:T(8,128)} %constant.52, f32[24,32]{1,0:T(8,128)S(1)} %copy.19, f32[24,256]{1,0:T(8,128)} %constant.51, f32[24,32]{1,0:T(8,128)S(1)} %copy.18, f32[24,256]{1,0:T(8,128)} %constant.50, f32[24,32]{1,0:T(8,128)S(1)} %copy.17), kind=kLoop, calls=%fused_computation | loop fusion | flops 983040 | bytes 869376 | tf_op jit(solution)/shard_map/add | solution.py:388
  19.4 0.0 collective-permute-done.3.bottom
  19.5 0.0 collective-permute-done.2.top
  19.5 0.0 copy-done
  19.5 0.0 copy-done.2
  19.5 0.0 copy-start.1
  19.5 2.4 %stencil.1 = (bf16[576,1152]{1,0:T(8,128)(2,1)S(1)}, f32[192,1152]{1,0:T(8,128)S(1)}, bf16[192,1152]{1,0:T(8,128)(2,1)S(1)}) custom-call(s32[1]{0:T(128)} %bitcast.1.core, f32[24,32,256]{2,1,0:T(8,128)S(1)} %multiply_add_fusion.tab, bf16[24,24,384]{2,1,0:T(8,128)(2,1)S(1)} %copy-done, bf16[24,8,384]{2,1,0:T(8,128)(2,1)S(1)} %collective-permute-done.left, ...), custom_call_target="tpu_custom_call" | custom-call | flops 5500000256 | bytes 15000000 | tf_op jit(solution)/shard_map/stencil/pallas_call | solution.py:414
  21.9 3.7 %collective-permute-start.4 = (bf16[192,1152]{1,0:T(8,128)(2,1)S(1)}, bf16[192,1152]{1,0:T(8,128)(2,1)S(1)}, u32[]{:S(2)}, u32[]{:S(2)}) collective-permute-start(bf16[192,1152]{1,0:T(8,128)(2,1)S(1)} %get-tuple-element.22), channel_id=1, source_target_pairs={{0,1},{1,0},{2,3},{3,2},{4,5},{5,4},{6,7},{7,6},{8,9},{9,8},{10,11... | collective-permute-start | bytes 1327112 | tf_op jit(solution)/shard_map/ppermute | solution.py:423
  25.6 0.0 copy-done.1
  25.6 3.1 %grad_field.1 = (bf16[576,384]{1,0:T(8,128)(2,1)}, bf16[32,128,128]{2,1,0:T(8,128)(2,1)}) custom-call(s32[1]{0:T(128)} %bitcast.pos, bf16[576,1152]{1,0:T(8,128)(2,1)S(1)} %get-tuple-element.19.g, bf16[576,384]{1,0:T(8,128)(2,1)S(1)} %bitcast.14, bf16[3,384,384]{2,1,0:T(8,128)(2,1)S(1)} %copy-done.1), custom_call_target="tpu_custom_call" | custom-call | flops 5500000256 | bytes 15000000 | tf_op jit(solution)/shard_map/grad_field/pallas_call | solution.py:426
  28.7 0.0 collective-permute-done.4.other
  28.7 0.9 mix_chip_sum.1
  29.6 0.0 copy-start.4
  29.6 6.4 %all-to-all-start = ((bf16[32,128,128]{2,1,0:T(8,128)(2,1)}), bf16[32,128,128]{2,1,0:T(8,128)(2,1)S(1)}, u32[]{:S(2)}, u32[]{:S(2)}) async-start(bf16[32,128,128]{2,1,0:T(8,128)(2,1)} %mix_chip_sum.1), calls=%async_computation | async-start | bytes 2097152 | tf_op jit(solution)/shard_map/all_to_all | solution.py:452
  36.0 0.8 dynamic_slice.7
  36.8 0.0 copy-done.4
  36.8 0.7 multiply_add_fusion.1.logscale
  37.5 0.0 copy-start.3
  37.5 11.3 %legendre.1.leg = bf16[24,384,256]{2,1,0:T(8,128)(2,1)} custom-call(s32[1]{0:T(128)} %bitcast.pos, f32[1,128]{1,0:T(1,128)} %constant.44.clone.cosines, f32[48,128]{1,0:T(8,128)} %multiply_add_fusion.1.logscale), custom_call_target="tpu_custom_call" | custom-call | flops 9900000256 | bytes 27000000 | tf_op jit(solution)/shard_map/legendre/pallas_call | solution.py:460
  48.8 13.7 %all-to-all-done.columns = bf16[32,128,128]{2,1,0:T(8,128)(2,1)S(1)} async-done(((bf16[32,128,128]{2,1,0:T(8,128)(2,1)}), bf16[32,128,128]{2,1,0:T(8,128)(2,1)S(1)}, u32[]{:S(2)}, u32[]{:S(2)}) %all-to-all-start) | async-done | bytes 1048608 | tf_op jit(solution)/shard_map/all_to_all | solution.py:452
  62.5 0.0 copy-done.3
  62.5 1.0 dft.1
  63.5 19.3 %all_to_all.15.spec = bf16[8,136,384]{2,1,0:T(8,128)(2,1)S(1)} all-to-all(bf16[8,136,384]{2,1,0:T(8,128)(2,1)S(1)} %dft.1), channel_id=1, replica_groups=mesh['lat'=8,'chip'=16,'core'=2] {'lat'}, dimensions={0} | all-to-all | bytes 1671168 | tf_op jit(solution)/shard_map/all_to_all | solution.py:487
  82.7 0.8 mix_copies.1
  83.6 6.7 %all-to-all-start.2 = ((bf16[16,112,128]{2,1,0:T(8,128)(2,1)}), bf16[16,112,128]{2,1,0:T(8,128)(2,1)S(1)}, u32[]{:S(2)}, u32[]{:S(2)}) async-start(bf16[16,112,128]{2,1,0:T(8,128)(2,1)} %mix_copies.1), calls=%async_computation.2 | async-start | bytes 917504 | tf_op jit(solution)/shard_map/all_to_all | solution.py:489
  90.3 7.2 %synthesis.1 = f32[2,12,48,384]{3,2,1,0:T(8,128)} custom-call(bf16[8,136,384]{2,1,0:T(8,128)(2,1)S(1)} %all_to_all.15.spec, bf16[24,384,256]{2,1,0:T(8,128)(2,1)} %legendre.1.leg), custom_call_target="tpu_custom_call" | custom-call | flops 6600000000 | bytes 18000000 | tf_op jit(solution)/shard_map/synthesis/pallas_call | solution.py:491
  97.5 4.7 %all-to-all-done.2.mine = bf16[16,112,128]{2,1,0:T(8,128)(2,1)S(1)} async-done(((bf16[16,112,128]{2,1,0:T(8,128)(2,1)}), bf16[16,112,128]{2,1,0:T(8,128)(2,1)S(1)}, u32[]{:S(2)}, u32[]{:S(2)}) %all-to-all-start.2) | async-done | bytes 458784 | tf_op jit(solution)/shard_map/all_to_all | solution.py:489
  102.2 2.9 %collective-permute-start.5 = (bf16[16,112,128]{2,1,0:T(8,128)(2,1)S(1)}, bf16[16,112,128]{2,1,0:T(8,128)(2,1)S(1)}, u32[]{:S(2)}, u32[]{:S(2)}) collective-permute-start(bf16[16,112,128]{2,1,0:T(8,128)(2,1)S(1)} %all-to-all-done.2.mine), channel_id=1, source_target_pairs={{0,1},{1,0},{2,3},{3,2},{4,5},{5,4},{6,7},{7,6},{8,9},{9,8},{10,11... | collective-permute-start | bytes 1376264 | tf_op jit(solution)/shard_map/ppermute | solution.py:511
  105.1 1.4 %collective-permute-done.5.other = bf16[16,112,128]{2,1,0:T(8,128)(2,1)S(1)} collective-permute-done((bf16[16,112,128]{2,1,0:T(8,128)(2,1)S(1)}, bf16[16,112,128]{2,1,0:T(8,128)(2,1)S(1)}, u32[]{:S(2)}, u32[]{:S(2)}) %collective-permute-start.5) | collective-permute-done | bytes 458784 | tf_op jit(solution)/shard_map/ppermute | solution.py:511
  106.6 1.3 %mix_out.1 = f32[3,384,384]{2,1,0:T(8,128)} custom-call(s32[1]{0:T(128)} %bitcast.1.core, bf16[16,112,128]{2,1,0:T(8,128)(2,1)S(1)} %all-to-all-done.2.mine, bf16[16,112,128]{2,1,0:T(8,128)(2,1)S(1)} %collective-permute-done.5.other), custom_call_target="tpu_custom_call" | custom-call | flops 2200000000 | bytes 6000000 | tf_op jit(solution)/shard_map/mix_out/pallas_call | solution.py:512
  (5 shorter events, 0.0 us)
Async XLA Ops:
  0.6 18.8 %copy-start = (bf16[24,24,384]{2,1,0:T(8,128)(2,1)S(1)}, bf16[24,24,384]{2,1,0:T(8,128)(2,1)}, u32[]{:S(2)}) copy-start(bf16[24,24,384]{2,1,0:T(8,128)(2,1)} %cot.1) | copy-start | bytes 1327108
  0.6 18.8 %copy-start.2 = (bf16[24,24,384]{2,1,0:T(8,128)(2,1)S(1)}, bf16[24,24,384]{2,1,0:T(8,128)(2,1)}, u32[]{:S(2)}) copy-start(bf16[24,24,384]{2,1,0:T(8,128)(2,1)} %param.13) | copy-start | bytes 1327108
  1.7 5.2 %collective-permute-start = (bf16[24,8,384]{2,1,0:T(8,128)(2,1)S(1)}, bf16[24,8,384]{2,1,0:T(8,128)(2,1)S(1)}, u32[]{:S(2)}, u32[]{:S(2)}) collective-permute-start(bf16[24,8,384]{2,1,0:T(8,128)(2,1)S(1)} %get-tuple-element.31), channel_id=1, source_target_pairs={{0,1},{1,2},{2,3},{3,4},{4,5},{5,6},{6,7},{7,8},{8,9},{9,10},{10,1... | collective-permute-start | bytes 442376 | tf_op jit(solution)/shard_map/ppermute | solution.py:396
  4.8 4.6 %collective-permute-start.1 = (bf16[24,8,384]{2,1,0:T(8,128)(2,1)S(1)}, bf16[24,8,384]{2,1,0:T(8,128)(2,1)S(1)}, u32[]{:S(2)}, u32[]{:S(2)}) collective-permute-start(bf16[24,8,384]{2,1,0:T(8,128)(2,1)S(1)} %get-tuple-element.32), channel_id=1, source_target_pairs={{1,0},{2,1},{3,2},{4,3},{5,4},{6,5},{7,6},{8,7},{9,8},{10,9},{11,1... | collective-permute-start | bytes 442376 | tf_op jit(solution)/shard_map/ppermute | solution.py:397
  9.4 10.0 %collective-permute-start.3 = (bf16[1,40,384]{2,1,0:T(8,128)(2,1)S(1)}, bf16[1,40,384]{2,1,0:T(8,128)(2,1)S(1)}, u32[]{:S(2)}, u32[]{:S(2)}) collective-permute-start(bf16[1,40,384]{2,1,0:T(8,128)(2,1)S(1)} %pad_maximum_fusion), channel_id=1, source_target_pairs={{32,0},{64,32},{96,64},{128,96},{160,128},{192,160},{224,192},{33,... | collective-permute-start | bytes 92168 | tf_op jit(solution)/shard_map/ppermute | solution.py:404
  10.7 8.7 %collective-permute-start.2 = (bf16[1,40,384]{2,1,0:T(8,128)(2,1)S(1)}, bf16[1,40,384]{2,1,0:T(8,128)(2,1)S(1)}, u32[]{:S(2)}, u32[]{:S(2)}) collective-permute-start(bf16[1,40,384]{2,1,0:T(8,128)(2,1)S(1)} %pad_maximum_fusion.1), channel_id=1, source_target_pairs={{0,32},{32,64},{64,96},{96,128},{128,160},{160,192},{192,224},{1,3... | collective-permute-start | bytes 92168 | tf_op jit(solution)/shard_map/ppermute | solution.py:403
  19.5 6.1 %copy-start.1 = (bf16[3,384,384]{2,1,0:T(8,128)(2,1)S(1)}, bf16[3,384,384]{2,1,0:T(8,128)(2,1)}, u32[]{:S(2)}) copy-start(bf16[3,384,384]{2,1,0:T(8,128)(2,1)} %mix.1) | copy-start | bytes 2654212
  21.9 6.8 %collective-permute-start.4 = (bf16[192,1152]{1,0:T(8,128)(2,1)S(1)}, bf16[192,1152]{1,0:T(8,128)(2,1)S(1)}, u32[]{:S(2)}, u32[]{:S(2)}) collective-permute-start(bf16[192,1152]{1,0:T(8,128)(2,1)S(1)} %get-tuple-element.22), channel_id=1, source_target_pairs={{0,1},{1,0},{2,3},{3,2},{4,5},{5,4},{6,7},{7,6},{8,9},{9,8},{10,11... | collective-permute-start | bytes 1327112 | tf_op jit(solution)/shard_map/ppermute | solution.py:423
  29.6 7.2 %copy-start.4 = (f32[128]{0:T(128)S(1)}, f32[128]{0:T(128)}, u32[]{:S(2)}) copy-start(f32[128]{0:T(128)} %constant.53) | copy-start | bytes 1540
  29.6 32.9 %all-to-all-start = ((bf16[32,128,128]{2,1,0:T(8,128)(2,1)}), bf16[32,128,128]{2,1,0:T(8,128)(2,1)S(1)}, u32[]{:S(2)}, u32[]{:S(2)}) async-start(bf16[32,128,128]{2,1,0:T(8,128)(2,1)} %mix_chip_sum.1), calls=%async_computation | async-start | bytes 2097152 | tf_op jit(solution)/shard_map/all_to_all | solution.py:452
  37.5 25.0 %copy-start.3 = (bf16[768,1024]{1,0:T(8,128)(2,1)S(1)}, bf16[768,1024]{1,0:T(8,128)(2,1)}, u32[]{:S(2)}) copy-start(bf16[768,1024]{1,0:T(8,128)(2,1)} %constant.45.clone.rows) | copy-start | bytes 4718596
  83.6 18.6 %all-to-all-start.2 = ((bf16[16,112,128]{2,1,0:T(8,128)(2,1)}), bf16[16,112,128]{2,1,0:T(8,128)(2,1)S(1)}, u32[]{:S(2)}, u32[]{:S(2)}) async-start(bf16[16,112,128]{2,1,0:T(8,128)(2,1)} %mix_copies.1), calls=%async_computation.2 | async-start | bytes 917504 | tf_op jit(solution)/shard_map/all_to_all | solution.py:489
  102.2 4.4 %collective-permute-start.5 = (bf16[16,112,128]{2,1,0:T(8,128)(2,1)S(1)}, bf16[16,112,128]{2,1,0:T(8,128)(2,1)S(1)}, u32[]{:S(2)}, u32[]{:S(2)}) collective-permute-start(bf16[16,112,128]{2,1,0:T(8,128)(2,1)S(1)} %all-to-all-done.2.mine), channel_id=1, source_target_pairs={{0,1},{1,0},{2,3},{3,2},{4,5},{5,4},{6,7},{7,6},{8,9},{9,8},{10,11... | collective-permute-start | bytes 1376264 | tf_op jit(solution)/shard_map/ppermute | solution.py:511

commit v7 on v6

--- a/solution.py
+++ b/solution.py
@@ -28,10 +28,14 @@
 XW = FD + 2 * R
 TP = 32
 FP = FD + 8
-GROUPS = CD * TP // 128
+COLS = CD * TD
+GROUPS = COLS // 128
+REST = COLS - GROUPS * 128
 SLOTS = 7
-SENT = GROUPS * FP + (SLOTS - GROUPS) * 8
-SPREAD = 40
+REST_ROW = GROUPS * FP + (SLOTS - GROUPS) * 8
+SENT = REST_ROW + 8
+TAIL_ROW = GROUPS * 2 * MD + 2 * MD * REST // 128
+SPREAD = TAIL_ROW + 2 * SLOTS * 8
 QUAD = 4
 CHIPS = LONS // 2
 LAT = "lat"
@@ -120,7 +124,7 @@
     other_out[...] = jnp.where(first, high, low).astype(BF16)
 
 
-def field_kernel(pos, g, cot, mix, gf_out, send_out, flat, turned, send):
+def field_kernel(pos, g, cot, mix, pack, gf_out, send_out, flat, turned, send):
     total = cot[...].astype(F32)
     for k in range(K):
         total = total + lax.dot_general(
@@ -149,26 +153,34 @@
             ]
             for fr, part in enumerate(swap_blocks(parts)):
                 send[q, pl.ds(fq * 4 + fr, LONS, stride=FD), :] = part
+    padded = jnp.concatenate([send[q] for q in range(CD // 4)], axis=1).astype(BF16)
+    packed = jnp.dot(padded, pack[...], preferred_element_type=F32)
     for q in range(GROUPS):
-        send_out[:, q * FP:q * FP + FD, :] = send[q].reshape(LONS, FD, 128).astype(BF16)
+        send_out[:, q * FP:q * FP + FD, :] = packed[:, q * 128:(q + 1) * 128].reshape(LONS, FD, 128).astype(BF16)
+    last = packed[:, GROUPS * 128:].reshape(LONS, FD // 8, 8, 128)
+    rest = last[:, 0]
+    for b in range(1, FD // 8):
+        rest = rest + pltpu.roll(last[:, b], b * REST, 2)
+    send_out[:, REST_ROW - 8:, :] = jnp.concatenate([jnp.zeros_like(rest), rest], axis=1).astype(BF16)
 
 
 def slot_row(slot):
     return slot * FP + FD if slot < GROUPS else GROUPS * FP + (slot - GROUPS) * 8
 
 
-def piece_place(piece):
-    return 2 * MD + piece // GROUPS * 8, piece % GROUPS * 128
+def piece_row(piece):
+    return TAIL_ROW + piece * 8
 
 
 def dft_kernel(rows, columns, out):
-    wide = jnp.concatenate(
-        [columns[:, q * FP:(q + 1) * FP, :].reshape(LONS * FP, 128) for q in range(GROUPS)], axis=1
-    )
-    got = jnp.dot(rows[...], wide, preferred_element_type=F32)
-    got = (got * (1.0 / math.sqrt(NLON))).astype(BF16)
-    for i in range(LATS):
-        out[i, :2 * MD, :] = got[i * 2 * MD:(i + 1) * 2 * MD]
+    parts = [columns[:, q * FP:(q + 1) * FP, :].reshape(LONS * FP, 128) for q in range(GROUPS)]
+    rest = columns[:, REST_ROW - 8:, :].astype(F32)[:, 8:]
+    blocks = [rest if b == 0 else pltpu.roll(rest, 128 - b * REST, 2) for b in range(FD // 8)]
+    blocks.append(jnp.zeros_like(rest))
+    parts.append(jnp.concatenate(blocks, axis=1).reshape(LONS * FP, 128).astype(BF16))
+    got = jnp.dot(rows[...], jnp.concatenate(parts, axis=1), preferred_element_type=F32)
+    got = got * (1.0 / math.sqrt(NLON))
+    pieces = []
     for half in range(2):
         for slot in range(SLOTS):
             first = slot_row(slot) // 16 * 16
@@ -176,10 +188,20 @@
             total = columns[half, first:first + 16, :].astype(F32)
             for chip in range(1, CHIPS):
                 total = total + columns[2 * chip + half, first:first + 16, :].astype(F32)
-            total = total[start:start + 8].astype(BF16)
-            row, lane = piece_place(half * SLOTS + slot)
-            for i in range(LATS):
-                out[i, row:row + 8, lane:lane + 128] = total
+            pieces.append(total[start:start + 8])
+    step = 2 * MD * REST // 128
+    inside = lax.broadcasted_iota(jnp.int32, (step, 128), 1) < REST
+    for i in range(LATS):
+        mine = got[i * 2 * MD:(i + 1) * 2 * MD]
+        for q in range(GROUPS):
+            out[i, q * 2 * MD:(q + 1) * 2 * MD, :] = mine[:, q * 128:(q + 1) * 128].astype(BF16)
+        quarters = [
+            jnp.where(inside, mine[b * step:(b + 1) * step, GROUPS * 128:], 0.0) for b in range(128 // REST)
+        ]
+        rest = quarters[0]
+        for b in range(1, 128 // REST):
+            rest = rest + pltpu.roll(quarters[b], b * REST, 1)
+        out[i, GROUPS * 2 * MD:, :] = jnp.concatenate([rest] + pieces, axis=0).astype(BF16)
 
 
 HALF = LATS // 2 * TP
@@ -232,15 +254,26 @@
 MSTEP = 8
 
 
-def synthesis_kernel(spec, leg, out, lined, rows):
+def synthesis_kernel(spec, pack, leg, out, lined, rows):
     step = pl.program_id(0)
 
     @pl.when(step == 0)
     def _():
+        packed = []
+        for i in range(LATS):
+            groups = [spec[i, q * 2 * MD:(q + 1) * 2 * MD, :] for q in range(GROUPS)]
+            rest = spec[i, GROUPS * 2 * MD:GROUPS * 2 * MD + 32, :].astype(F32)[:2 * MD * REST // 128]
+            blocks = [rest if b == 0 else pltpu.roll(rest, 128 - b * REST, 1) for b in range(128 // REST)]
+            groups.append(jnp.concatenate(blocks, axis=0).astype(BF16))
+            packed.append(jnp.concatenate(groups, axis=1))
+        padded = lax.dot_general(
+            jnp.concatenate(packed, axis=0), pack[...], (((1,), (1,)), ((), ())), preferred_element_type=F32
+        )
+        padded = [padded[i * 2 * MD:(i + 1) * 2 * MD] for i in range(LATS)]
         for q in range(CD // 4):
             span = slice(q * 128, (q + 1) * 128)
-            north = [spec[i, :2 * MD, span].astype(F32) for i in range(LATS // 2)]
-            south = [spec[LATS - 1 - i, :2 * MD, span].astype(F32) for i in range(LATS // 2)]
+            north = [padded[i][:, span] for i in range(LATS // 2)]
+            south = [padded[LATS - 1 - i][:, span] for i in range(LATS // 2)]
             for odd in range(2):
                 parts = [n - s if odd else n + s for n, s in zip(north, south)]
                 for cr, part in enumerate(swap_blocks(parts)):
@@ -298,7 +331,7 @@
     copies = [
         pltpu.make_async_copy(near_rows.at[q], out.at[:, q * FP + FD:(q + 1) * FP, :], sems.at[q]) for q in range(GROUPS)
     ]
-    copies.append(pltpu.make_async_copy(far_rows, out.at[:, GROUPS * FP:, :], sems.at[GROUPS]))
+    copies.append(pltpu.make_async_copy(far_rows, out.at[:, GROUPS * FP:REST_ROW, :], sems.at[GROUPS]))
     for copy in copies:
         copy.start()
     for copy in copies:
@@ -307,11 +340,11 @@
 
 def copies_kernel(spec, out):
     for piece in range(2 * SLOTS):
-        row, lane = piece_place(piece)
+        row = piece_row(piece)
         first = row // 16 * 16
-        total = spec[0, first:first + 16, lane:lane + 128].astype(F32)
+        total = spec[0, first:first + 16, :].astype(F32)
         for i in range(1, LATS):
-            total = total + spec[i, first:first + 16, lane:lane + 128].astype(F32)
+            total = total + spec[i, first:first + 16, :].astype(F32)
         total = total[row - first:row - first + 8].astype(BF16)
         for chip in range(CHIPS):
             out[chip, piece * 8:(piece + 1) * 8, :] = total
@@ -346,6 +379,14 @@
     padded = np.zeros((2 * M, LONS, FP), np.float32)
     padded[:, :, :FD] = rows.reshape(2 * M, LONS, FD)
     return padded.reshape(2 * M, LONS * FP).astype(ml_dtypes.bfloat16)
+
+
+def packing():
+    pack = np.zeros((CD * TP, CD * TP), np.float32)
+    for c in range(CD):
+        for t in range(TD):
+            pack[c * TP + t, c * TD + t] = 1.0
+    return pack.astype(ml_dtypes.bfloat16)
 
 
 def latitudes():
@@ -423,18 +464,19 @@
     mix_other = lax.ppermute(mix_other, CORE, swap)
 
     pos = jnp.reshape(lat_pos, (1,)).astype(jnp.int32)
+    pack = jnp.asarray(packing())
     grad_field, send = call(
         field_kernel,
         (shape((cells, C), BF16), shape((LONS, SENT, 128), BF16)),
         5,
-        in_specs=[scalar, whole, whole, whole],
+        in_specs=[scalar, whole, whole, whole, whole],
         scratch_shapes=[
             pltpu.VMEM((C // 128, cells, 128), F32),
             pltpu.VMEM((FD // 4, C, 128), F32),
             pltpu.VMEM((CD // 4, LONS * FD, 128), F32),
         ],
         name="grad_field",
-    )(pos, near(grown), near(cotangent.reshape(cells, C)), near(mix_weight))
+    )(pos, near(grown), near(cotangent.reshape(cells, C)), near(mix_weight), near(pack))
     send = call(
         chip_sum_kernel,
         shape((LONS, SENT, 128), BF16),
@@ -443,7 +485,7 @@
         out_specs=anywhere,
         scratch_shapes=[
             pltpu.VMEM((GROUPS, LONS, FP - FD, 128), BF16),
-            pltpu.VMEM((LONS, SENT - GROUPS * FP, 128), BF16),
+            pltpu.VMEM((LONS, REST_ROW - GROUPS * FP, 128), BF16),
             pltpu.SemaphoreType.DMA((GROUPS + 1,)),
         ],
         input_output_aliases={2: 0},
@@ -481,7 +523,7 @@
     )(pos, jnp.asarray(cosine), logscale)
     columns, table = lax.optimization_barrier((columns, table))
 
-    spectra = call(dft_kernel, near_shape((LATS, 2 * MD + SPREAD, CD * TP), BF16), 2, in_specs=[whole, whole], name="dft")(
+    spectra = call(dft_kernel, near_shape((LATS, SPREAD, 128), BF16), 2, in_specs=[whole, whole], name="dft")(
         near(jnp.asarray(dft_rows())), near(columns)
     )
     spec = lax.all_to_all(spectra, LAT, 0, 0, tiled=True)
@@ -496,6 +538,7 @@
             num_scalar_prefetch=0,
             grid=(MD // MSTEP,),
             in_specs=[
+                whole,
                 whole,
                 pl.BlockSpec((MSTEP // 2, L, 2 * HALF), lambda b: (b, 0, 0)),
             ],
@@ -506,7 +549,7 @@
             ],
         ),
         name="synthesis",
-    )(near(spec), table)
+    )(near(spec), near(pack), table)
     mix_mine, grad_spectra = lax.optimization_barrier((mix_mine, grad_spectra))
     mix_other = lax.ppermute(mix_mine, CORE, swap)
     grad_mix = call(

time: 109 us -> 107 us (0.982)
  waiting for transfers between devices: 23.4 us -> 20.6 us
  local copies, waits for them, and re-layouts: 2.91 us -> 5.29 us
  blocking collectives: 19.3 us -> 17 us
    all_to_all x1, waiting for transfers between devices: 13.7 us -> 11 us  [on_device(): columns = lax.all_to_all(send, LON, 0, 0, tiled=True)]
    unnamed x10 -> x16, local copies, waits for them, and re-layouts: 0.03 us -> 2.41 us
    all_to_all x1, blocking collectives: 19.3 us -> 17 us  [on_device(): spec = lax.all_to_all(spectra, LAT, 0, 0, tiled=True)]
  transfers between devices with their start and end apart: 8 -> 8, of which waited for: 5 -> 5; matrix products, arithmetic and copies ran while one was open for 5% -> 5% of each run, Pallas kernels for 20% -> 21%
where the time goes in v7:
time: 107 us
  starting transfers between devices  30.4 us (28%)
  Pallas kernels  28.7 us (27%)
  waiting for transfers between devices  20.6 us (19%)
  blocking collectives  17 us (16%)
  local copies, waits for them, and re-layouts  5.29 us (5%)
  other arithmetic  3.61 us (3%)
    all_to_all x1, blocking collectives, on_device(): spec = lax.all_to_all(spectra, LAT, 0, 0, tiled=True)  17 us
    pallas_call x1, Pallas kernels, on_device(): call(legendre_kernel, shape((MD // 2, L, 2 * HALF), BF16), 9, grid_spec=p...  11.3 us
    all_to_all x1, waiting for transfers between devices, on_device(): columns = lax.all_to_all(send, LON, 0, 0, tiled=True)  11 us
    all_to_all x1, starting transfers between devices, on_device(): mix_mine = lax.all_to_all(mix_copies, CHIP, 0, 0, tiled=True)  7.39 us
    pallas_call x1, Pallas kernels, on_device(): call(synthesis_kernel, shape((2, CD, MD, L), F32), 6, grid_spec=pltpu.Pre...  7.3 us
    all_to_all x1, starting transfers between devices, on_device(): columns = lax.all_to_all(send, LON, 0, 0, tiled=True)  6.39 us
    ppermute x1, starting transfers between devices, on_device(): top = lax.ppermute(edge_rows[1], LAT, north)  5.49 us
    all_to_all x1, waiting for transfers between devices, on_device(): mix_mine = lax.all_to_all(mix_copies, CHIP, 0, 0, tiled=True)  4.72 us
  transfers between devices with their start and end apart: 8, of which 5 were waited for; matrix products, arithmetic and copies ran while one was open for 5% of the time, Pallas kernels for 21%

profile of v7, /device:TPU:1, one launch (start us, length us, event | category | flops | bytes accessed | tf_op | source)
XLA Modules:
  0.0 106.5 jit_solution(17345172359659521763)
XLA Ops:
  0.6 0.0 copy-start
  0.6 0.0 copy-start.2
  0.7 1.1 %fusion.8 = (bf16[24,8,384]{2,1,0:T(8,128)(2,1)S(1)}, bf16[24,8,384]{2,1,0:T(8,128)(2,1)S(1)}) fusion(bf16[24,24,384]{2,1,0:T(8,128)(2,1)} %cot.1), kind=kLoop, calls=%fused_computation.22 | loop fusion | bytes 589824 | tf_op jit(solution)/shard_map/slice | solution.py:437
  1.7 3.1 %collective-permute-start = (bf16[24,8,384]{2,1,0:T(8,128)(2,1)S(1)}, bf16[24,8,384]{2,1,0:T(8,128)(2,1)S(1)}, u32[]{:S(2)}, u32[]{:S(2)}) collective-permute-start(bf16[24,8,384]{2,1,0:T(8,128)(2,1)S(1)} %get-tuple-element.31), channel_id=1, source_target_pairs={{0,1},{1,2},{2,3},{3,4},{4,5},{5,6},{6,7},{7,8},{8,9},{9,10},{10,1... | collective-permute-start | bytes 442376 | tf_op jit(solution)/shard_map/ppermute | solution.py:437
  4.8 0.3 collective-permute-start.1
  5.2 0.7 fusion.7
  5.9 1.1 collective-permute-done.left
  7.0 2.5 %collective-permute-done.1.right = bf16[24,8,384]{2,1,0:T(8,128)(2,1)S(1)} collective-permute-done((bf16[24,8,384]{2,1,0:T(8,128)(2,1)S(1)}, bf16[24,8,384]{2,1,0:T(8,128)(2,1)S(1)}, u32[]{:S(2)}, u32[]{:S(2)}) %collective-permute-start.1) | collective-permute-done | bytes 147488 | tf_op jit(solution)/shard_map/ppermute | solution.py:438
  9.4 1.3 %collective-permute-start.3 = (bf16[1,40,384]{2,1,0:T(8,128)(2,1)S(1)}, bf16[1,40,384]{2,1,0:T(8,128)(2,1)S(1)}, u32[]{:S(2)}, u32[]{:S(2)}) collective-permute-start(bf16[1,40,384]{2,1,0:T(8,128)(2,1)S(1)} %pad_maximum_fusion), channel_id=1, source_target_pairs={{32,0},{64,32},{96,64},{128,96},{160,128},{192,160},{224,192},{33,... | collective-permute-start | bytes 92168 | tf_op jit(solution)/shard_map/ppermute | solution.py:445
  10.7 5.5 %collective-permute-start.2 = (bf16[1,40,384]{2,1,0:T(8,128)(2,1)S(1)}, bf16[1,40,384]{2,1,0:T(8,128)(2,1)S(1)}, u32[]{:S(2)}, u32[]{:S(2)}) collective-permute-start(bf16[1,40,384]{2,1,0:T(8,128)(2,1)S(1)} %pad_maximum_fusion.1), channel_id=1, source_target_pairs={{0,32},{32,64},{64,96},{96,128},{128,160},{160,192},{192,224},{1,3... | collective-permute-start | bytes 92168 | tf_op jit(solution)/shard_map/ppermute | solution.py:444
  16.2 0.7 convert_bitcast_fusion
  17.0 0.9 fusion.6
  17.9 0.1 fusion.1
  18.0 0.1 slice_bitcast_fusion.2
  18.1 0.1 copy.18
  18.1 0.1 copy.19
  18.2 0.1 copy.20
  18.3 1.2 %multiply_add_fusion.tab = f32[24,32,256]{2,1,0:T(8,128)S(1)} fusion(f32[24,256]{1,0:T(8,128)} %constant.55, f32[24,32]{1,0:T(8,128)S(1)} %copy.20, f32[24,256]{1,0:T(8,128)} %constant.54, f32[24,32]{1,0:T(8,128)S(1)} %copy.19, f32[24,256]{1,0:T(8,128)} %constant.53, f32[24,32]{1,0:T(8,128)S(1)} %copy.18), kind=kLoop, calls=%fused_computation | loop fusion | flops 983040 | bytes 869376 | tf_op jit(solution)/shard_map/add | solution.py:429
  19.4 0.0 collective-permute-done.3.bottom
  19.5 0.0 collective-permute-done.2.top
  19.5 0.0 copy-done
  19.5 0.0 copy-done.2
  19.5 0.0 copy-start.1
  19.5 0.0 copy-start.4
  19.5 2.4 %stencil.1 = (bf16[576,1152]{1,0:T(8,128)(2,1)S(1)}, f32[192,1152]{1,0:T(8,128)S(1)}, bf16[192,1152]{1,0:T(8,128)(2,1)S(1)}) custom-call(s32[1]{0:T(128)} %bitcast.1.core, f32[24,32,256]{2,1,0:T(8,128)S(1)} %multiply_add_fusion.tab, bf16[24,24,384]{2,1,0:T(8,128)(2,1)S(1)} %copy-done, bf16[24,8,384]{2,1,0:T(8,128)(2,1)S(1)} %collective-permute-done.left, ...), custom_call_target="tpu_custom_call" | custom-call | flops 5500000256 | bytes 15000000 | tf_op jit(solution)/shard_map/stencil/pallas_call | solution.py:455
  21.9 0.0 copy-start.5
  21.9 1.1 copy-done.5
  23.0 3.6 %collective-permute-start.4 = (bf16[192,1152]{1,0:T(8,128)(2,1)S(1)}, bf16[192,1152]{1,0:T(8,128)(2,1)S(1)}, u32[]{:S(2)}, u32[]{:S(2)}) collective-permute-start(bf16[192,1152]{1,0:T(8,128)(2,1)S(1)} %get-tuple-element.22), channel_id=1, source_target_pairs={{0,1},{1,0},{2,3},{3,2},{4,5},{5,4},{6,7},{7,6},{8,9},{9,8},{10,11... | collective-permute-start | bytes 1327112 | tf_op jit(solution)/shard_map/ppermute | solution.py:464
  26.6 0.0 copy-done.1
  26.6 0.0 copy-done.4
  26.6 0.0 copy-start.6
  26.6 1.3 %copy-done.6 = bf16[576,1152]{1,0:T(8,128)(2,1)S(1)} copy-done((bf16[576,1152]{1,0:T(8,128)(2,1)S(1)}, bf16[576,1152]{1,0:T(8,128)(2,1)}, u32[]{:S(2)}) %copy-start.6) | copy-done | bytes 1327128
  27.9 3.6 %grad_field.1 = (bf16[576,384]{1,0:T(8,128)(2,1)}, bf16[32,112,128]{2,1,0:T(8,128)(2,1)}) custom-call(s32[1]{0:T(128)} %bitcast.pos, bf16[576,1152]{1,0:T(8,128)(2,1)S(1)} %copy-done.6, bf16[576,384]{1,0:T(8,128)(2,1)S(1)} %bitcast.14, bf16[3,384,384]{2,1,0:T(8,128)(2,1)S(1)} %copy-done.1, bf16[384,384]{1,0:T(8,128)(2,1)S(1)} %copy-done.4), custom_call_target="tpu_custom_call" | custom-call | flops 5500000256 | bytes 15000000 | tf_op jit(solution)/shard_map/grad_field/pallas_call | solution.py:468
  31.6 0.0 collective-permute-done.4.other
  31.6 0.9 mix_chip_sum.1
  32.4 0.0 copy-start.7
  32.5 6.4 %all-to-all-start = ((bf16[32,112,128]{2,1,0:T(8,128)(2,1)}), bf16[32,112,128]{2,1,0:T(8,128)(2,1)S(1)}, u32[]{:S(2)}, u32[]{:S(2)}) async-start(bf16[32,112,128]{2,1,0:T(8,128)(2,1)} %mix_chip_sum.1), calls=%async_computation | async-start | bytes 1835008 | tf_op jit(solution)/shard_map/all_to_all | solution.py:494
  38.9 0.8 dynamic_slice.7
  39.6 0.0 copy-done.7
  39.6 0.7 multiply_add_fusion.1.logscale
  40.3 0.0 copy-start.3
  40.3 11.3 %legendre.1.leg = bf16[24,384,256]{2,1,0:T(8,128)(2,1)} custom-call(s32[1]{0:T(128)} %bitcast.pos, f32[1,128]{1,0:T(1,128)} %constant.47.clone.cosines, f32[48,128]{1,0:T(8,128)} %multiply_add_fusion.1.logscale), custom_call_target="tpu_custom_call" | custom-call | flops 9900000256 | bytes 27000000 | tf_op jit(solution)/shard_map/legendre/pallas_call | solution.py:502
  51.6 11.0 %all-to-all-done.columns = bf16[32,112,128]{2,1,0:T(8,128)(2,1)S(1)} async-done(((bf16[32,112,128]{2,1,0:T(8,128)(2,1)}), bf16[32,112,128]{2,1,0:T(8,128)(2,1)S(1)}, u32[]{:S(2)}, u32[]{:S(2)}) %all-to-all-start) | async-done | bytes 917536 | tf_op jit(solution)/shard_map/all_to_all | solution.py:494
  62.6 0.0 copy-done.3
  62.6 1.1 %dft.1 = bf16[8,328,128]{2,1,0:T(8,128)(2,1)S(1)} custom-call(bf16[768,1024]{1,0:T(8,128)(2,1)S(1)} %copy-done.3, bf16[32,112,128]{2,1,0:T(8,128)(2,1)S(1)} %all-to-all-done.columns), custom_call_target="tpu_custom_call" | custom-call | flops 2200000000 | bytes 6000000 | tf_op jit(solution)/shard_map/dft/pallas_call | solution.py:526
  63.7 17.0 %all_to_all.15.spec = bf16[8,328,128]{2,1,0:T(8,128)(2,1)S(1)} all-to-all(bf16[8,328,128]{2,1,0:T(8,128)(2,1)S(1)} %dft.1), channel_id=1, replica_groups=mesh['lat'=8,'chip'=16,'core'=2] {'lat'}, dimensions={0} | all-to-all | bytes 1343488 | tf_op jit(solution)/shard_map/all_to_all | solution.py:529
  80.7 0.8 mix_copies.1
  81.6 7.4 %all-to-all-start.2 = ((bf16[16,112,128]{2,1,0:T(8,128)(2,1)}), bf16[16,112,128]{2,1,0:T(8,128)(2,1)S(1)}, u32[]{:S(2)}, u32[]{:S(2)}) async-start(bf16[16,112,128]{2,1,0:T(8,128)(2,1)} %mix_copies.1), calls=%async_computation.2 | async-start | bytes 917504 | tf_op jit(solution)/shard_map/all_to_all | solution.py:531
  89.0 7.3 %synthesis.1 = f32[2,12,48,384]{3,2,1,0:T(8,128)} custom-call(bf16[8,328,128]{2,1,0:T(8,128)(2,1)S(1)} %all_to_all.15.spec, bf16[384,384]{1,0:T(8,128)(2,1)S(1)} %copy-done.4, bf16[24,384,256]{2,1,0:T(8,128)(2,1)} %legendre.1.leg), custom_call_target="tpu_custom_call" | custom-call | flops 6600000000 | bytes 18000000 | tf_op jit(solution)/shard_map/synthesis/pallas_call | solution.py:533
  96.3 4.7 %all-to-all-done.2.mine = bf16[16,112,128]{2,1,0:T(8,128)(2,1)S(1)} async-done(((bf16[16,112,128]{2,1,0:T(8,128)(2,1)}), bf16[16,112,128]{2,1,0:T(8,128)(2,1)S(1)}, u32[]{:S(2)}, u32[]{:S(2)}) %all-to-all-start.2) | async-done | bytes 458784 | tf_op jit(solution)/shard_map/all_to_all | solution.py:531
  101.0 2.8 %collective-permute-start.5 = (bf16[16,112,128]{2,1,0:T(8,128)(2,1)S(1)}, bf16[16,112,128]{2,1,0:T(8,128)(2,1)S(1)}, u32[]{:S(2)}, u32[]{:S(2)}) collective-permute-start(bf16[16,112,128]{2,1,0:T(8,128)(2,1)S(1)} %all-to-all-done.2.mine), channel_id=1, source_target_pairs={{0,1},{1,0},{2,3},{3,2},{4,5},{5,4},{6,7},{7,6},{8,9},{9,8},{10,11... | collective-permute-start | bytes 1376264 | tf_op jit(solution)/shard_map/ppermute | solution.py:554
  103.8 1.4 %collective-permute-done.5.other = bf16[16,112,128]{2,1,0:T(8,128)(2,1)S(1)} collective-permute-done((bf16[16,112,128]{2,1,0:T(8,128)(2,1)S(1)}, bf16[16,112,128]{2,1,0:T(8,128)(2,1)S(1)}, u32[]{:S(2)}, u32[]{:S(2)}) %collective-permute-start.5) | collective-permute-done | bytes 458784 | tf_op jit(solution)/shard_map/ppermute | solution.py:554
  105.2 1.3 %mix_out.1 = f32[3,384,384]{2,1,0:T(8,128)} custom-call(s32[1]{0:T(128)} %bitcast.1.core, bf16[16,112,128]{2,1,0:T(8,128)(2,1)S(1)} %all-to-all-done.2.mine, bf16[16,112,128]{2,1,0:T(8,128)(2,1)S(1)} %collective-permute-done.5.other), custom_call_target="tpu_custom_call" | custom-call | flops 2200000000 | bytes 6000000 | tf_op jit(solution)/shard_map/mix_out/pallas_call | solution.py:555
  (5 shorter events, 0.0 us)
Async XLA Ops:
  0.6 18.8 %copy-start = (bf16[24,24,384]{2,1,0:T(8,128)(2,1)S(1)}, bf16[24,24,384]{2,1,0:T(8,128)(2,1)}, u32[]{:S(2)}) copy-start(bf16[24,24,384]{2,1,0:T(8,128)(2,1)} %cot.1) | copy-start | bytes 1327108
  0.6 18.8 %copy-start.2 = (bf16[24,24,384]{2,1,0:T(8,128)(2,1)S(1)}, bf16[24,24,384]{2,1,0:T(8,128)(2,1)}, u32[]{:S(2)}) copy-start(bf16[24,24,384]{2,1,0:T(8,128)(2,1)} %param.14) | copy-start | bytes 1327108
  1.7 5.2 %collective-permute-start = (bf16[24,8,384]{2,1,0:T(8,128)(2,1)S(1)}, bf16[24,8,384]{2,1,0:T(8,128)(2,1)S(1)}, u32[]{:S(2)}, u32[]{:S(2)}) collective-permute-start(bf16[24,8,384]{2,1,0:T(8,128)(2,1)S(1)} %get-tuple-element.31), channel_id=1, source_target_pairs={{0,1},{1,2},{2,3},{3,4},{4,5},{5,6},{6,7},{7,8},{8,9},{9,10},{10,1... | collective-permute-start | bytes 442376 | tf_op jit(solution)/shard_map/ppermute | solution.py:437
  4.8 4.6 %collective-permute-start.1 = (bf16[24,8,384]{2,1,0:T(8,128)(2,1)S(1)}, bf16[24,8,384]{2,1,0:T(8,128)(2,1)S(1)}, u32[]{:S(2)}, u32[]{:S(2)}) collective-permute-start(bf16[24,8,384]{2,1,0:T(8,128)(2,1)S(1)} %get-tuple-element.32), channel_id=1, source_target_pairs={{1,0},{2,1},{3,2},{4,3},{5,4},{6,5},{7,6},{8,7},{9,8},{10,9},{11,1... | collective-permute-start | bytes 442376 | tf_op jit(solution)/shard_map/ppermute | solution.py:438
  9.4 10.0 %collective-permute-start.3 = (bf16[1,40,384]{2,1,0:T(8,128)(2,1)S(1)}, bf16[1,40,384]{2,1,0:T(8,128)(2,1)S(1)}, u32[]{:S(2)}, u32[]{:S(2)}) collective-permute-start(bf16[1,40,384]{2,1,0:T(8,128)(2,1)S(1)} %pad_maximum_fusion), channel_id=1, source_target_pairs={{32,0},{64,32},{96,64},{128,96},{160,128},{192,160},{224,192},{33,... | collective-permute-start | bytes 92168 | tf_op jit(solution)/shard_map/ppermute | solution.py:445
  10.7 8.7 %collective-permute-start.2 = (bf16[1,40,384]{2,1,0:T(8,128)(2,1)S(1)}, bf16[1,40,384]{2,1,0:T(8,128)(2,1)S(1)}, u32[]{:S(2)}, u32[]{:S(2)}) collective-permute-start(bf16[1,40,384]{2,1,0:T(8,128)(2,1)S(1)} %pad_maximum_fusion.1), channel_id=1, source_target_pairs={{0,32},{32,64},{64,96},{96,128},{128,160},{160,192},{192,224},{1,3... | collective-permute-start | bytes 92168 | tf_op jit(solution)/shard_map/ppermute | solution.py:444
  19.5 7.1 %copy-start.1 = (bf16[3,384,384]{2,1,0:T(8,128)(2,1)S(1)}, bf16[3,384,384]{2,1,0:T(8,128)(2,1)}, u32[]{:S(2)}) copy-start(bf16[3,384,384]{2,1,0:T(8,128)(2,1)} %mix.1) | copy-start | bytes 2654212
  19.5 7.1 %copy-start.4 = (bf16[384,384]{1,0:T(8,128)(2,1)S(1)}, bf16[384,384]{1,0:T(8,128)(2,1)}, u32[]{:S(2)}) copy-start(bf16[384,384]{1,0:T(8,128)(2,1)} %constant.44.clone.pack) | copy-start | bytes 884740
  21.9 1.1 copy-start.5
  23.0 8.6 %collective-permute-start.4 = (bf16[192,1152]{1,0:T(8,128)(2,1)S(1)}, bf16[192,1152]{1,0:T(8,128)(2,1)S(1)}, u32[]{:S(2)}, u32[]{:S(2)}) collective-permute-start(bf16[192,1152]{1,0:T(8,128)(2,1)S(1)} %get-tuple-element.22), channel_id=1, source_target_pairs={{0,1},{1,0},{2,3},{3,2},{4,5},{5,4},{6,7},{7,6},{8,9},{9,8},{10,11... | collective-permute-start | bytes 1327112 | tf_op jit(solution)/shard_map/ppermute | solution.py:464
  26.6 1.3 %copy-start.6 = (bf16[576,1152]{1,0:T(8,128)(2,1)S(1)}, bf16[576,1152]{1,0:T(8,128)(2,1)}, u32[]{:S(2)}) copy-start(bf16[576,1152]{1,0:T(8,128)(2,1)} %copy-done.5) | copy-start | bytes 3981316
  32.4 7.2 %copy-start.7 = (f32[128]{0:T(128)S(1)}, f32[128]{0:T(128)}, u32[]{:S(2)}) copy-start(f32[128]{0:T(128)} %constant.56) | copy-start | bytes 1540
  32.5 30.1 %all-to-all-start = ((bf16[32,112,128]{2,1,0:T(8,128)(2,1)}), bf16[32,112,128]{2,1,0:T(8,128)(2,1)S(1)}, u32[]{:S(2)}, u32[]{:S(2)}) async-start(bf16[32,112,128]{2,1,0:T(8,128)(2,1)} %mix_chip_sum.1), calls=%async_computation | async-start | bytes 1835008 | tf_op jit(solution)/shard_map/all_to_all | solution.py:494
  40.3 22.3 %copy-start.3 = (bf16[768,1024]{1,0:T(8,128)(2,1)S(1)}, bf16[768,1024]{1,0:T(8,128)(2,1)}, u32[]{:S(2)}) copy-start(bf16[768,1024]{1,0:T(8,128)(2,1)} %constant.48.clone.rows) | copy-start | bytes 4718596
  81.6 19.4 %all-to-all-start.2 = ((bf16[16,112,128]{2,1,0:T(8,128)(2,1)}), bf16[16,112,128]{2,1,0:T(8,128)(2,1)S(1)}, u32[]{:S(2)}, u32[]{:S(2)}) async-start(bf16[16,112,128]{2,1,0:T(8,128)(2,1)} %mix_copies.1), calls=%async_computation.2 | async-start | bytes 917504 | tf_op jit(solution)/shard_map/all_to_all | solution.py:531
  101.0 4.3 %collective-permute-start.5 = (bf16[16,112,128]{2,1,0:T(8,128)(2,1)S(1)}, bf16[16,112,128]{2,1,0:T(8,128)(2,1)S(1)}, u32[]{:S(2)}, u32[]{:S(2)}) collective-permute-start(bf16[16,112,128]{2,1,0:T(8,128)(2,1)S(1)} %all-to-all-done.2.mine), channel_id=1, source_target_pairs={{0,1},{1,0},{2,3},{3,2},{4,5},{5,4},{6,7},{7,6},{8,9},{9,8},{10,11... | collective-permute-start | bytes 1376264 | tf_op jit(solution)/shard_map/ppermute | solution.py:554

commit v8 on v7

--- a/solution.py
+++ b/solution.py
@@ -44,7 +44,7 @@
 LON = (CHIP, CORE)
 F32 = jnp.float32
 BF16 = jnp.bfloat16
-VMEM_BYTES = 56 * 1024 * 1024
+VMEM_BYTES = 18 * 1024 * 1024
 
 
 def call(kernel, out_shape, us, **kw):
@@ -85,51 +85,86 @@
     return c0, c1, c2, c3
 
 
-def stencil_kernel(core, tab, cot, left, right, top, bottom, field, g_out, mine_out, other_out, ext, band):
-    ext[1:TD + 1, 0:R, :] = left[...].astype(F32)
-    ext[1:TD + 1, R:R + FD, :] = cot[...].astype(F32)
-    ext[1:TD + 1, R + FD:XW, :] = right[...].astype(F32)
-    ext[0:1] = top[...].astype(F32)
-    ext[TD + 1:TD + 2] = bottom[...].astype(F32)
+ROWS = QUAD * FD
+INNER = TD // QUAD - 2
+
+
+def widen(ext, rows, cot, left, right):
+    there = slice(rows.start + 1, rows.stop + 1)
+    ext[there, 0:R, :] = left[rows].astype(F32)
+    ext[there, R:R + FD, :] = cot[rows].astype(F32)
+    ext[there, R + FD:XW, :] = right[rows].astype(F32)
+
+
+def offsets_in_band():
     lane = lax.broadcasted_iota(jnp.int32, (FD, 256), 1)
     column = lane
     for edge in range(1, QUAD + 2):
         column = column - jnp.where(lane >= edge * XW, XW, 0)
-    apart = (column - lax.broadcasted_iota(jnp.int32, (FD, 256), 0)).astype(F32)
+    return (column - lax.broadcasted_iota(jnp.int32, (FD, 256), 0)).astype(F32)
+
+
+def stencil_quad(quad, apart, tab, ext, band):
     zero = jnp.zeros((FD, 256), F32)
-    for quad in range(TD // QUAD):
-        for r in range(QUAD):
-            t = quad * QUAD + r
-            sums = [zero] * K
-            for s in range(S):
-                hit = apart == tab[t, K * S + s:K * S + s + 1, :]
-                for k in range(K):
-                    sums[k] = sums[k] + jnp.where(hit, tab[t, k * S + s:k * S + s + 1, :], 0.0)
+    for r in range(QUAD):
+        t = quad * QUAD + r
+        sums = [zero] * K
+        for s in range(S):
+            hit = apart == tab[t, K * S + s:K * S + s + 1, :]
             for k in range(K):
-                row = (k * QUAD + r) * FD
-                band[row:row + FD, :] = sums[k]
-        slab = ext[quad * QUAD:quad * QUAD + QUAD + 2].reshape((QUAD + 2) * XW, C).astype(BF16)
-        weights = band[:, :(QUAD + 2) * XW].astype(BF16)
-        got = jnp.dot(weights, slab, preferred_element_type=F32).astype(BF16)
-        rows = QUAD * FD
+                sums[k] = sums[k] + jnp.where(hit, tab[t, k * S + s:k * S + s + 1, :], 0.0)
         for k in range(K):
-            g_out[quad * rows:(quad + 1) * rows, k * C:(k + 1) * C] = got[k * rows:(k + 1) * rows]
-    mix = lax.dot_general(
-        field[...], g_out[...], (((0,), (0,)), ((), ())), preferred_element_type=F32
-    )
-    mix = mix * (1.0 / math.sqrt(NLAT * NLON))
+            row = (k * QUAD + r) * FD
+            band[row:row + FD, :] = sums[k]
+    slab = ext[quad * QUAD:quad * QUAD + QUAD + 2].reshape((QUAD + 2) * XW, C).astype(BF16)
+    weights = band[:, :(QUAD + 2) * XW].astype(BF16)
+    return jnp.dot(weights, slab, preferred_element_type=F32).astype(BF16)
+
+
+def cells_dot(field, g):
+    return lax.dot_general(field, g, (((0,), (0,)), ((), ())), preferred_element_type=F32)
+
+
+def inner_kernel(tab, cot, left, right, field, g_out, mix_out, ext, band):
+    widen(ext, slice(QUAD - 1, TD - QUAD + 1), cot, left, right)
+    apart = offsets_in_band()
+    for n in range(INNER):
+        got = stencil_quad(n + 1, apart, tab, ext, band)
+        for k in range(K):
+            g_out[n * ROWS:(n + 1) * ROWS, k * C:(k + 1) * C] = got[k * ROWS:(k + 1) * ROWS]
+    mix_out[...] = cells_dot(field[ROWS:(INNER + 1) * ROWS, :], g_out[...])
+
+
+def outer_kernel(core, tab, cot, left, right, top, bottom, field, mix_inner, g_out, mine_out, other_out, ext, band):
+    widen(ext, slice(0, QUAD + 1), cot, left, right)
+    widen(ext, slice(TD - QUAD - 1, TD), cot, left, right)
+    ext[0:1] = top[...].astype(F32)
+    ext[TD + 1:TD + 2] = bottom[...].astype(F32)
+    apart = offsets_in_band()
+    for n in range(2):
+        got = stencil_quad(n * (INNER + 1), apart, tab, ext, band)
+        for k in range(K):
+            g_out[n * ROWS:(n + 1) * ROWS, k * C:(k + 1) * C] = got[k * ROWS:(k + 1) * ROWS]
+    mine = jnp.concatenate([field[:ROWS, :], field[(INNER + 1) * ROWS:, :]], axis=0)
+    mix = (mix_inner[...] + cells_dot(mine, g_out[...])) * (1.0 / math.sqrt(NLAT * NLON))
     first = core[0] == 0
     low, high = mix[:C // 2], mix[C // 2:]
     mine_out[...] = jnp.where(first, low, high)
     other_out[...] = jnp.where(first, high, low).astype(BF16)
 
 
-def field_kernel(pos, g, cot, mix, pack, gf_out, send_out, flat, turned, send):
-    total = cot[...].astype(F32)
+def field_kernel(pos, g_inner, g_outer, cot, mix, pack, gf_out, send_out, flat, turned, send):
+    inner = jnp.zeros((INNER * ROWS, C), F32)
+    outer = jnp.zeros((2 * ROWS, C), F32)
     for k in range(K):
-        total = total + lax.dot_general(
-            g[:, k * C:(k + 1) * C], mix[k], (((1,), (1,)), ((), ())), preferred_element_type=F32
+        span = slice(k * C, (k + 1) * C)
+        inner = inner + lax.dot_general(
+            g_inner[:, span], mix[k], (((1,), (1,)), ((), ())), preferred_element_type=F32
         )
+        outer = outer + lax.dot_general(
+            g_outer[:, span], mix[k], (((1,), (1,)), ((), ())), preferred_element_type=F32
+        )
+    total = cot[...].astype(F32) + jnp.concatenate([outer[:ROWS], inner, outer[ROWS:]], axis=0)
     rounded = total.astype(BF16)
     gf_out[...] = rounded
     rounded = rounded.astype(F32)
@@ -452,31 +487,44 @@
     scalar = pl.BlockSpec(memory_space=pltpu.SMEM)
     anywhere = pl.BlockSpec(memory_space=pl.ANY)
     half = (C // 2, K * C)
-    grown, mix_mine, mix_other = call(
-        stencil_kernel,
-        (near_shape((cells, K * C), BF16), near_shape(half, F32), near_shape(half, BF16)),
-        5,
-        in_specs=[scalar] + [whole] * 7,
-        scratch_shapes=[pltpu.VMEM((TD + 2, XW, C), F32), pltpu.VMEM((K * QUAD * FD, 256), F32)],
-        name="stencil",
-    )(core, near(tab), near(cotangent), near(left), near(right), near(top), near(bottom), near(field.reshape(cells, C)))
+    rims = (near(left), near(right))
+    near_cot, near_field = near(cotangent), near(field.reshape(cells, C))
+    scratch = [pltpu.VMEM((TD + 2, XW, C), F32), pltpu.VMEM((K * ROWS, 256), F32)]
+    g_inner, mix_inner = call(
+        inner_kernel,
+        (near_shape((INNER * ROWS, K * C), BF16), near_shape((C, K * C), F32)),
+        2,
+        in_specs=[whole] * 5,
+        scratch_shapes=scratch,
+        name="stencil_inner",
+    )(near(tab), near_cot, *rims, near_field)
+    pack = near(jnp.asarray(packing()))
+    mix_near = near(mix_weight)
+    top, bottom, pack, mix_near = lax.optimization_barrier((top, bottom, pack, mix_near))
+    g_outer, mix_mine, mix_other = call(
+        outer_kernel,
+        (near_shape((2 * ROWS, K * C), BF16), near_shape(half, F32), near_shape(half, BF16)),
+        2,
+        in_specs=[scalar] + [whole] * 8,
+        scratch_shapes=scratch,
+        name="stencil_outer",
+    )(core, near(tab), near_cot, *rims, near(top), near(bottom), near_field, near(mix_inner))
     swap = [(0, 1), (1, 0)]
     mix_other = lax.ppermute(mix_other, CORE, swap)
 
     pos = jnp.reshape(lat_pos, (1,)).astype(jnp.int32)
-    pack = jnp.asarray(packing())
     grad_field, send = call(
         field_kernel,
         (shape((cells, C), BF16), shape((LONS, SENT, 128), BF16)),
         5,
-        in_specs=[scalar, whole, whole, whole, whole],
+        in_specs=[scalar] + [whole] * 5,
         scratch_shapes=[
             pltpu.VMEM((C // 128, cells, 128), F32),
             pltpu.VMEM((FD // 4, C, 128), F32),
             pltpu.VMEM((CD // 4, LONS * FD, 128), F32),
         ],
         name="grad_field",
-    )(pos, near(grown), near(cotangent.reshape(cells, C)), near(mix_weight), near(pack))
+    )(pos, near(g_inner), near(g_outer), near(cotangent.reshape(cells, C)), near(mix_near), near(pack))
     send = call(
         chip_sum_kernel,
         shape((LONS, SENT, 128), BF16),

time: 107 us -> 105 us (0.981)
  Pallas kernels: 28.7 us -> 24.9 us
  local copies, waits for them, and re-layouts: 5.29 us -> 7.39 us
    pallas_call x1, Pallas kernels: 7.3 us -> 4.76 us  [on_device(): call(synthesis_kernel, shape((2, CD, MD, L), F32), 6, grid_spec=pltpu.Pre...]
    unnamed x16 -> x18, local copies, waits for them, and re-layouts: 2.41 us -> 4.51 us
    pallas_call x1, Pallas kernels: 11.3 us -> 9.85 us  [on_device(): call(legendre_kernel, shape((MD // 2, L, 2 * HALF), BF16), 9, grid_spec=p...]
    pallas_call x1 -> x2, Pallas kernels: 2.41 us -> 2.62 us  [the longest x1 1.62 us: on_device(): call(inner_kernel, (near_shape((INNER * ROWS, K * C), BF16), near_shape((...]
  transfers between devices with their start and end apart: 8 -> 8, of which waited for: 5 -> 5; matrix products, arithmetic and copies ran while one was open for 5% -> 5% of each run, Pallas kernels for 21% -> 19%
where the time goes in v8:
time: 105 us; the launch traced here: 104 us
  starting transfers between devices  30.2 us (29%)
  Pallas kernels  24.9 us (24%)
  waiting for transfers between devices  20.8 us (20%)
  blocking collectives  17 us (16%)
  local copies, waits for them, and re-layouts  7.39 us (7%)
  other arithmetic  3 us (3%)
    all_to_all x1, blocking collectives, on_device(): spec = lax.all_to_all(spectra, LAT, 0, 0, tiled=True)  17 us
    all_to_all x1, waiting for transfers between devices, on_device(): columns = lax.all_to_all(send, LON, 0, 0, tiled=True)  10.9 us
    pallas_call x1, Pallas kernels, on_device(): call(legendre_kernel, shape((MD // 2, L, 2 * HALF), BF16), 9, grid_spec=p...  9.85 us
    all_to_all x1, starting transfers between devices, on_device(): mix_mine = lax.all_to_all(mix_copies, CHIP, 0, 0, tiled=True)  7.09 us
    all_to_all x1, starting transfers between devices, on_device(): columns = lax.all_to_all(send, LON, 0, 0, tiled=True)  6.42 us
    ppermute x1, starting transfers between devices, on_device(): top = lax.ppermute(edge_rows[1], LAT, north)  5.49 us
    all_to_all x1, waiting for transfers between devices, on_device(): mix_mine = lax.all_to_all(mix_copies, CHIP, 0, 0, tiled=True)  4.95 us
    pallas_call x1, Pallas kernels, on_device(): call(synthesis_kernel, shape((2, CD, MD, L), F32), 6, grid_spec=pltpu.Pre...  4.76 us
  transfers between devices with their start and end apart: 8, of which 5 were waited for; matrix products, arithmetic and copies ran while one was open for 5% of the time, Pallas kernels for 19%

profile of v8, /device:TPU:1, one launch (start us, length us, event | category | flops | bytes accessed | tf_op | source)
XLA Modules:
  0.0 104.1 jit_solution(15501584306601729083)
XLA Ops:
  0.6 0.0 copy-start
  0.6 0.0 copy-start.2
  0.7 1.1 %fusion.8 = (bf16[24,8,384]{2,1,0:T(8,128)(2,1)S(1)}, bf16[24,8,384]{2,1,0:T(8,128)(2,1)S(1)}) fusion(bf16[24,24,384]{2,1,0:T(8,128)(2,1)} %cot.3), kind=kLoop, calls=%fused_computation.22 | loop fusion | bytes 589824 | tf_op jit(solution)/shard_map/slice | solution.py:472
  1.7 3.1 %collective-permute-start = (bf16[24,8,384]{2,1,0:T(8,128)(2,1)S(1)}, bf16[24,8,384]{2,1,0:T(8,128)(2,1)S(1)}, u32[]{:S(2)}, u32[]{:S(2)}) collective-permute-start(bf16[24,8,384]{2,1,0:T(8,128)(2,1)S(1)} %get-tuple-element.43), channel_id=1, source_target_pairs={{0,1},{1,2},{2,3},{3,4},{4,5},{5,6},{6,7},{7,8},{8,9},{9,10},{10,1... | collective-permute-start | bytes 442376 | tf_op jit(solution)/shard_map/ppermute | solution.py:472
  4.8 0.3 collective-permute-start.1
  5.2 0.7 fusion.7
  5.9 1.1 %collective-permute-done.left = bf16[24,8,384]{2,1,0:T(8,128)(2,1)S(1)} collective-permute-done((bf16[24,8,384]{2,1,0:T(8,128)(2,1)S(1)}, bf16[24,8,384]{2,1,0:T(8,128)(2,1)S(1)}, u32[]{:S(2)}, u32[]{:S(2)}) %collective-permute-start) | collective-permute-done | bytes 147488 | tf_op jit(solution)/shard_map/ppermute | solution.py:472
  7.0 2.5 %collective-permute-done.1.right = bf16[24,8,384]{2,1,0:T(8,128)(2,1)S(1)} collective-permute-done((bf16[24,8,384]{2,1,0:T(8,128)(2,1)S(1)}, bf16[24,8,384]{2,1,0:T(8,128)(2,1)S(1)}, u32[]{:S(2)}, u32[]{:S(2)}) %collective-permute-start.1) | collective-permute-done | bytes 147488 | tf_op jit(solution)/shard_map/ppermute | solution.py:473
  9.4 1.3 %collective-permute-start.3 = (bf16[1,40,384]{2,1,0:T(8,128)(2,1)S(1)}, bf16[1,40,384]{2,1,0:T(8,128)(2,1)S(1)}, u32[]{:S(2)}, u32[]{:S(2)}) collective-permute-start(bf16[1,40,384]{2,1,0:T(8,128)(2,1)S(1)} %pad_maximum_fusion), channel_id=1, source_target_pairs={{32,0},{64,32},{96,64},{128,96},{160,128},{192,160},{224,192},{33,... | collective-permute-start | bytes 92168 | tf_op jit(solution)/shard_map/ppermute | solution.py:480
  10.7 5.5 %collective-permute-start.2 = (bf16[1,40,384]{2,1,0:T(8,128)(2,1)S(1)}, bf16[1,40,384]{2,1,0:T(8,128)(2,1)S(1)}, u32[]{:S(2)}, u32[]{:S(2)}) collective-permute-start(bf16[1,40,384]{2,1,0:T(8,128)(2,1)S(1)} %pad_maximum_fusion.1), channel_id=1, source_target_pairs={{0,32},{32,64},{64,96},{96,128},{128,160},{160,192},{192,224},{1,3... | collective-permute-start | bytes 92168 | tf_op jit(solution)/shard_map/ppermute | solution.py:479
  16.2 0.7 convert_bitcast_fusion
  17.0 0.9 fusion.6
  17.9 0.1 fusion.1
  18.0 0.1 slice_bitcast_fusion.2
  18.1 0.1 copy.18
  18.1 0.1 copy.19
  18.2 0.1 copy.20
  18.3 1.2 %multiply_add_fusion.tab = f32[24,32,256]{2,1,0:T(8,128)S(1)} fusion(f32[24,256]{1,0:T(8,128)} %constant.55, f32[24,32]{1,0:T(8,128)S(1)} %copy.20, f32[24,256]{1,0:T(8,128)} %constant.54, f32[24,32]{1,0:T(8,128)S(1)} %copy.19, f32[24,256]{1,0:T(8,128)} %constant.53, f32[24,32]{1,0:T(8,128)S(1)} %copy.18), kind=kLoop, calls=%fused_computation | loop fusion | flops 983040 | bytes 869376 | tf_op jit(solution)/shard_map/add | solution.py:464
  19.4 0.0 copy-done
  19.5 0.0 copy-done.2
  19.5 1.6 %stencil_inner.1 = (bf16[384,1152]{1,0:T(8,128)(2,1)S(1)}, f32[384,1152]{1,0:T(8,128)S(1)}) custom-call(f32[24,32,256]{2,1,0:T(8,128)S(1)} %multiply_add_fusion.tab, bf16[24,24,384]{2,1,0:T(8,128)(2,1)S(1)} %copy-done, bf16[24,8,384]{2,1,0:T(8,128)(2,1)S(1)} %collective-permute-done.left, bf16[24,8,384]{2,1,0:T(8,128)(2,1)S(1)} %collective-permute-done.1.right, ...), custom_call_target="tpu_custom_call" | custom-call | flops 2200000000 | bytes 6000000 | tf_op jit(solution)/shard_map/stencil_inner/pallas_call | solution.py:493
  21.1 0.0 collective-permute-done.3.bottom
  21.1 0.0 collective-permute-done.2.top
  21.1 0.0 copy-start.1
  21.1 0.0 copy-start.4
  21.1 1.0 stencil_outer.1
  22.1 3.7 %collective-permute-start.4 = (bf16[192,1152]{1,0:T(8,128)(2,1)S(1)}, bf16[192,1152]{1,0:T(8,128)(2,1)S(1)}, u32[]{:S(2)}, u32[]{:S(2)}) collective-permute-start(bf16[192,1152]{1,0:T(8,128)(2,1)S(1)} %get-tuple-element.34), channel_id=1, source_target_pairs={{0,1},{1,0},{2,3},{3,2},{4,5},{5,4},{6,7},{7,6},{8,9},{9,8},{10,11... | collective-permute-start | bytes 1327112 | tf_op jit(solution)/shard_map/ppermute | solution.py:513
  25.9 0.0 copy-done.1
  25.9 0.0 copy-done.4
  25.9 3.5 %grad_field.1 = (bf16[576,384]{1,0:T(8,128)(2,1)}, bf16[32,112,128]{2,1,0:T(8,128)(2,1)}) custom-call(s32[1]{0:T(128)} %bitcast.pos, bf16[384,1152]{1,0:T(8,128)(2,1)S(1)} %get-tuple-element.25.g_inner, bf16[192,1152]{1,0:T(8,128)(2,1)S(1)} %get-tuple-element.29.g_outer, bf16[576,384]{1,0:T(8,128)(2,1)S(1)} %bitcast.14, bf16[3,384,384]{2,1,0:T(8,128)(2,1)S(1)} %copy-done.1, ...), custom_call_target="tpu_custom_call" | custom-call | flops 5500000256 | bytes 15000000 | tf_op jit(solution)/shard_map/grad_field/pallas_call | solution.py:516
  29.4 0.0 collective-permute-done.4.other
  29.4 0.9 mix_chip_sum.1
  30.3 0.0 copy-start.8
  30.3 0.0 copy-start.5
  30.3 6.4 %all-to-all-start = ((bf16[32,112,128]{2,1,0:T(8,128)(2,1)}), bf16[32,112,128]{2,1,0:T(8,128)(2,1)S(1)}, u32[]{:S(2)}, u32[]{:S(2)}) async-start(bf16[32,112,128]{2,1,0:T(8,128)(2,1)} %mix_chip_sum.1), calls=%async_computation | async-start | bytes 1835008 | tf_op jit(solution)/shard_map/all_to_all | solution.py:542
  36.8 0.8 dynamic_slice.7
  37.5 0.0 copy-done.8
  37.5 0.1 multiply_add_fusion.1.logscale
  37.6 0.0 copy-done.5
  37.6 0.0 copy-start.3
  37.6 9.8 %legendre.1.leg = bf16[24,384,256]{2,1,0:T(8,128)(2,1)S(1)} custom-call(s32[1]{0:T(128)} %bitcast.pos, f32[1,128]{1,0:T(1,128)S(1)} %copy-done.5, f32[48,128]{1,0:T(8,128)S(1)} %multiply_add_fusion.1.logscale), custom_call_target="tpu_custom_call" | custom-call | flops 9900000256 | bytes 27000000 | tf_op jit(solution)/shard_map/legendre/pallas_call | solution.py:550
  47.5 0.0 copy-start.6
  47.5 2.1 %copy-done.6 = bf16[24,384,256]{2,1,0:T(8,128)(2,1)} copy-done((bf16[24,384,256]{2,1,0:T(8,128)(2,1)}, bf16[24,384,256]{2,1,0:T(8,128)(2,1)S(1)}, u32[]{:S(2)}) %copy-start.6) | copy-done | bytes 4718616
  49.6 10.9 %all-to-all-done.columns = bf16[32,112,128]{2,1,0:T(8,128)(2,1)S(1)} async-done(((bf16[32,112,128]{2,1,0:T(8,128)(2,1)}), bf16[32,112,128]{2,1,0:T(8,128)(2,1)S(1)}, u32[]{:S(2)}, u32[]{:S(2)}) %all-to-all-start) | async-done | bytes 917536 | tf_op jit(solution)/shard_map/all_to_all | solution.py:542
  60.5 0.0 copy-done.3
  60.5 1.1 %dft.1 = bf16[8,328,128]{2,1,0:T(8,128)(2,1)S(1)} custom-call(bf16[768,1024]{1,0:T(8,128)(2,1)S(1)} %copy-done.3, bf16[32,112,128]{2,1,0:T(8,128)(2,1)S(1)} %all-to-all-done.columns), custom_call_target="tpu_custom_call" | custom-call | flops 2200000000 | bytes 6000000 | tf_op jit(solution)/shard_map/dft/pallas_call | solution.py:574
  61.6 17.0 %all_to_all.15.spec = bf16[8,328,128]{2,1,0:T(8,128)(2,1)S(1)} all-to-all(bf16[8,328,128]{2,1,0:T(8,128)(2,1)S(1)} %dft.1), channel_id=1, replica_groups=mesh['lat'=8,'chip'=16,'core'=2] {'lat'}, dimensions={0} | all-to-all | bytes 1343488 | tf_op jit(solution)/shard_map/all_to_all | solution.py:577
  78.6 0.8 mix_copies.1
  79.5 7.1 %all-to-all-start.2 = ((bf16[16,112,128]{2,1,0:T(8,128)(2,1)}), bf16[16,112,128]{2,1,0:T(8,128)(2,1)S(1)}, u32[]{:S(2)}, u32[]{:S(2)}) async-start(bf16[16,112,128]{2,1,0:T(8,128)(2,1)} %mix_copies.1), calls=%async_computation.2 | async-start | bytes 917504 | tf_op jit(solution)/shard_map/all_to_all | solution.py:579
  86.5 0.0 copy-start.7
  86.6 2.3 %copy-done.7 = bf16[24,384,256]{2,1,0:T(8,128)(2,1)S(1)} copy-done((bf16[24,384,256]{2,1,0:T(8,128)(2,1)S(1)}, bf16[24,384,256]{2,1,0:T(8,128)(2,1)}, u32[]{:S(2)}) %copy-start.7) | copy-done | bytes 4718616
  88.9 4.8 %synthesis.1 = f32[2,12,48,384]{3,2,1,0:T(8,128)} custom-call(bf16[8,328,128]{2,1,0:T(8,128)(2,1)S(1)} %all_to_all.15.spec, bf16[384,384]{1,0:T(8,128)(2,1)S(1)} %copy-done.4, bf16[24,384,256]{2,1,0:T(8,128)(2,1)S(1)} %copy-done.7), custom_call_target="tpu_custom_call" | custom-call | flops 6600000000 | bytes 18000000 | tf_op jit(solution)/shard_map/synthesis/pallas_call | solution.py:581
  93.6 5.0 %all-to-all-done.2.mine = bf16[16,112,128]{2,1,0:T(8,128)(2,1)S(1)} async-done(((bf16[16,112,128]{2,1,0:T(8,128)(2,1)}), bf16[16,112,128]{2,1,0:T(8,128)(2,1)S(1)}, u32[]{:S(2)}, u32[]{:S(2)}) %all-to-all-start.2) | async-done | bytes 458784 | tf_op jit(solution)/shard_map/all_to_all | solution.py:579
  98.6 2.8 %collective-permute-start.5 = (bf16[16,112,128]{2,1,0:T(8,128)(2,1)S(1)}, bf16[16,112,128]{2,1,0:T(8,128)(2,1)S(1)}, u32[]{:S(2)}, u32[]{:S(2)}) collective-permute-start(bf16[16,112,128]{2,1,0:T(8,128)(2,1)S(1)} %all-to-all-done.2.mine), channel_id=1, source_target_pairs={{0,1},{1,0},{2,3},{3,2},{4,5},{5,4},{6,7},{7,6},{8,9},{9,8},{10,11... | collective-permute-start | bytes 1376264 | tf_op jit(solution)/shard_map/ppermute | solution.py:602
  101.4 1.4 %collective-permute-done.5.other = bf16[16,112,128]{2,1,0:T(8,128)(2,1)S(1)} collective-permute-done((bf16[16,112,128]{2,1,0:T(8,128)(2,1)S(1)}, bf16[16,112,128]{2,1,0:T(8,128)(2,1)S(1)}, u32[]{:S(2)}, u32[]{:S(2)}) %collective-permute-start.5) | collective-permute-done | bytes 458784 | tf_op jit(solution)/shard_map/ppermute | solution.py:602
  102.8 1.3 %mix_out.1 = f32[3,384,384]{2,1,0:T(8,128)} custom-call(s32[1]{0:T(128)} %bitcast.6.core, bf16[16,112,128]{2,1,0:T(8,128)(2,1)S(1)} %all-to-all-done.2.mine, bf16[16,112,128]{2,1,0:T(8,128)(2,1)S(1)} %collective-permute-done.5.other), custom_call_target="tpu_custom_call" | custom-call | flops 2200000000 | bytes 6000000 | tf_op jit(solution)/shard_map/mix_out/pallas_call | solution.py:603
  (5 shorter events, 0.0 us)
Async XLA Ops:
  0.6 18.8 %copy-start = (bf16[24,24,384]{2,1,0:T(8,128)(2,1)S(1)}, bf16[24,24,384]{2,1,0:T(8,128)(2,1)}, u32[]{:S(2)}) copy-start(bf16[24,24,384]{2,1,0:T(8,128)(2,1)} %cot.3) | copy-start | bytes 1327108
  0.6 18.8 %copy-start.2 = (bf16[24,24,384]{2,1,0:T(8,128)(2,1)S(1)}, bf16[24,24,384]{2,1,0:T(8,128)(2,1)}, u32[]{:S(2)}) copy-start(bf16[24,24,384]{2,1,0:T(8,128)(2,1)} %param.14) | copy-start | bytes 1327108
  1.7 5.2 %collective-permute-start = (bf16[24,8,384]{2,1,0:T(8,128)(2,1)S(1)}, bf16[24,8,384]{2,1,0:T(8,128)(2,1)S(1)}, u32[]{:S(2)}, u32[]{:S(2)}) collective-permute-start(bf16[24,8,384]{2,1,0:T(8,128)(2,1)S(1)} %get-tuple-element.43), channel_id=1, source_target_pairs={{0,1},{1,2},{2,3},{3,4},{4,5},{5,6},{6,7},{7,8},{8,9},{9,10},{10,1... | collective-permute-start | bytes 442376 | tf_op jit(solution)/shard_map/ppermute | solution.py:472
  4.8 4.6 %collective-permute-start.1 = (bf16[24,8,384]{2,1,0:T(8,128)(2,1)S(1)}, bf16[24,8,384]{2,1,0:T(8,128)(2,1)S(1)}, u32[]{:S(2)}, u32[]{:S(2)}) collective-permute-start(bf16[24,8,384]{2,1,0:T(8,128)(2,1)S(1)} %get-tuple-element.44), channel_id=1, source_target_pairs={{1,0},{2,1},{3,2},{4,3},{5,4},{6,5},{7,6},{8,7},{9,8},{10,9},{11,1... | collective-permute-start | bytes 442376 | tf_op jit(solution)/shard_map/ppermute | solution.py:473
  9.4 11.7 %collective-permute-start.3 = (bf16[1,40,384]{2,1,0:T(8,128)(2,1)S(1)}, bf16[1,40,384]{2,1,0:T(8,128)(2,1)S(1)}, u32[]{:S(2)}, u32[]{:S(2)}) collective-permute-start(bf16[1,40,384]{2,1,0:T(8,128)(2,1)S(1)} %pad_maximum_fusion), channel_id=1, source_target_pairs={{32,0},{64,32},{96,64},{128,96},{160,128},{192,160},{224,192},{33,... | collective-permute-start | bytes 92168 | tf_op jit(solution)/shard_map/ppermute | solution.py:480
  10.7 10.4 %collective-permute-start.2 = (bf16[1,40,384]{2,1,0:T(8,128)(2,1)S(1)}, bf16[1,40,384]{2,1,0:T(8,128)(2,1)S(1)}, u32[]{:S(2)}, u32[]{:S(2)}) collective-permute-start(bf16[1,40,384]{2,1,0:T(8,128)(2,1)S(1)} %pad_maximum_fusion.1), channel_id=1, source_target_pairs={{0,32},{32,64},{64,96},{96,128},{128,160},{160,192},{192,224},{1,3... | collective-permute-start | bytes 92168 | tf_op jit(solution)/shard_map/ppermute | solution.py:479
  21.1 4.8 %copy-start.1 = (bf16[3,384,384]{2,1,0:T(8,128)(2,1)S(1)}, bf16[3,384,384]{2,1,0:T(8,128)(2,1)}, u32[]{:S(2)}) copy-start(bf16[3,384,384]{2,1,0:T(8,128)(2,1)} %mix) | copy-start | bytes 2654212
  21.1 4.7 %copy-start.4 = (bf16[384,384]{1,0:T(8,128)(2,1)S(1)}, bf16[384,384]{1,0:T(8,128)(2,1)}, u32[]{:S(2)}) copy-start(bf16[384,384]{1,0:T(8,128)(2,1)} %constant.44.clone.pack) | copy-start | bytes 884740
  22.1 7.2 %collective-permute-start.4 = (bf16[192,1152]{1,0:T(8,128)(2,1)S(1)}, bf16[192,1152]{1,0:T(8,128)(2,1)S(1)}, u32[]{:S(2)}, u32[]{:S(2)}) collective-permute-start(bf16[192,1152]{1,0:T(8,128)(2,1)S(1)} %get-tuple-element.34), channel_id=1, source_target_pairs={{0,1},{1,0},{2,3},{3,2},{4,5},{5,4},{6,7},{7,6},{8,9},{9,8},{10,11... | collective-permute-start | bytes 1327112 | tf_op jit(solution)/shard_map/ppermute | solution.py:513
  30.3 7.2 %copy-start.8 = (f32[128]{0:T(128)S(1)}, f32[128]{0:T(128)}, u32[]{:S(2)}) copy-start(f32[128]{0:T(128)} %constant.56) | copy-start | bytes 1540
  30.3 7.3 %copy-start.5 = (f32[1,128]{1,0:T(1,128)S(1)}, f32[1,128]{1,0:T(1,128)}, u32[]{:S(2)}) copy-start(f32[1,128]{1,0:T(1,128)} %constant.47.clone.cosines) | copy-start | bytes 1540
  30.3 30.2 %all-to-all-start = ((bf16[32,112,128]{2,1,0:T(8,128)(2,1)}), bf16[32,112,128]{2,1,0:T(8,128)(2,1)S(1)}, u32[]{:S(2)}, u32[]{:S(2)}) async-start(bf16[32,112,128]{2,1,0:T(8,128)(2,1)} %mix_chip_sum.1), calls=%async_computation | async-start | bytes 1835008 | tf_op jit(solution)/shard_map/all_to_all | solution.py:542
  37.6 22.9 %copy-start.3 = (bf16[768,1024]{1,0:T(8,128)(2,1)S(1)}, bf16[768,1024]{1,0:T(8,128)(2,1)}, u32[]{:S(2)}) copy-start(bf16[768,1024]{1,0:T(8,128)(2,1)} %constant.48.clone.rows) | copy-start | bytes 4718596
  47.5 2.1 %copy-start.6 = (bf16[24,384,256]{2,1,0:T(8,128)(2,1)}, bf16[24,384,256]{2,1,0:T(8,128)(2,1)S(1)}, u32[]{:S(2)}) copy-start(bf16[24,384,256]{2,1,0:T(8,128)(2,1)S(1)} %legendre.1.leg) | copy-start | bytes 14155780
  79.5 19.1 %all-to-all-start.2 = ((bf16[16,112,128]{2,1,0:T(8,128)(2,1)}), bf16[16,112,128]{2,1,0:T(8,128)(2,1)S(1)}, u32[]{:S(2)}, u32[]{:S(2)}) async-start(bf16[16,112,128]{2,1,0:T(8,128)(2,1)} %mix_copies.1), calls=%async_computation.2 | async-start | bytes 917504 | tf_op jit(solution)/shard_map/all_to_all | solution.py:579
  86.5 2.3 %copy-start.7 = (bf16[24,384,256]{2,1,0:T(8,128)(2,1)S(1)}, bf16[24,384,256]{2,1,0:T(8,128)(2,1)}, u32[]{:S(2)}) copy-start(bf16[24,384,256]{2,1,0:T(8,128)(2,1)} %copy-done.6) | copy-start | bytes 14155780
  98.6 4.2 %collective-permute-start.5 = (bf16[16,112,128]{2,1,0:T(8,128)(2,1)S(1)}, bf16[16,112,128]{2,1,0:T(8,128)(2,1)S(1)}, u32[]{:S(2)}, u32[]{:S(2)}) collective-permute-start(bf16[16,112,128]{2,1,0:T(8,128)(2,1)S(1)} %all-to-all-done.2.mine), channel_id=1, source_target_pairs={{0,1},{1,0},{2,3},{3,2},{4,5},{5,4},{6,7},{7,6},{8,9},{9,8},{10,11... | collective-permute-start | bytes 1376264 | tf_op jit(solution)/shard_map/ppermute | solution.py:602

commit v9 on v8

--- a/solution.py
+++ b/solution.py
@@ -385,20 +385,17 @@
             out[chip, piece * 8:(piece + 1) * 8, :] = total
 
 
-def mix_kernel(core, mine, other, out, rows, sems):
+def mix_kernel(held, parts, *rest):
+    out, rows, sems = rest[-3:]
     copies = []
     for half in range(2):
-        for parts, held in ((mine, core[0]), (other, 1 - core[0])):
-            base = pl.multiple_of(half * (C // 2) + held * (C // 4), 8)
-            for chip in range(CHIPS):
-                for slot, row, col in tiles_of(chip):
-                    k, d = divmod(col, C // 128)
-                    piece = (half * SLOTS + slot) * 8
-                    rows[k, pl.ds(base + row * 8, 8), d * 128:(d + 1) * 128] = parts[
-                        chip, piece:piece + 8, :
-                    ].astype(F32)
-        span = pl.ds(half * (C // 2), C // 2)
-        copies.append(pltpu.make_async_copy(rows.at[:, span], out.at[:, span], sems.at[half]))
+        for chip in range(CHIPS):
+            for slot, row, col in tiles_of(chip):
+                k, d = divmod(col, C // 128)
+                piece = (half * SLOTS + slot) * 8
+                rows[half, k, row * 8:row * 8 + 8, d * 128:(d + 1) * 128] = parts[chip, piece:piece + 8, :].astype(F32)
+        base = pl.multiple_of(half * (C // 2) + held[0] * (C // 4), 8)
+        copies.append(pltpu.make_async_copy(rows.at[half], out.at[:, pl.ds(base, C // 4)], sems.at[half]))
         copies[-1].start()
     for copy in copies:
         copy.wait()
@@ -450,13 +447,16 @@
     return mark
 
 
-def tap_table(taps, offsets, counts, first_row):
+def tap_rows(taps, offsets, counts, first_row):
     slot_ids = lax.broadcasted_iota(jnp.int32, taps.shape, 3)
     live = jnp.where(slot_ids < counts[:, None, None, None], taps, 0.0).astype(BF16).astype(F32)
     shift = (R - offsets).astype(F32)[:, None]
     both = jnp.concatenate([live, shift], axis=1)
     both = jnp.pad(both, ((1, 1), (0, 0), (0, 0), (0, 0)))
-    both = lax.dynamic_slice_in_dim(both, first_row, TD + 2, 0)
+    return lax.dynamic_slice_in_dim(both, first_row, TD + 2, 0)
+
+
+def tap_table(both):
     marks = band_lanes()
     table = 0.0
     for rr in range(3):
@@ -480,8 +480,8 @@
     bottom = lax.ppermute(edge_rows[0], LAT, south)
 
     whole = pl.BlockSpec(memory_space=pltpu.VMEM)
-    taps, offsets, counts, _ = lax.optimization_barrier((taps, offsets, counts, edge_rows))
-    tab = tap_table(taps, offsets, counts, lat_pos * TD)
+    tap_part, _ = lax.optimization_barrier((tap_rows(taps, offsets, counts, lat_pos * TD), edge_rows))
+    tab = tap_table(tap_part)
     cells = TD * FD
     core = jnp.reshape(lax.axis_index(CORE), (1,)).astype(jnp.int32)
     scalar = pl.BlockSpec(memory_space=pltpu.SMEM)
@@ -600,16 +600,21 @@
     )(near(spec), near(pack), table)
     mix_mine, grad_spectra = lax.optimization_barrier((mix_mine, grad_spectra))
     mix_other = lax.ppermute(mix_mine, CORE, swap)
-    grad_mix = call(
-        mix_kernel,
-        shape((K, C, C), F32),
-        2,
-        in_specs=[scalar, whole, whole],
-        out_specs=anywhere,
-        scratch_shapes=[pltpu.VMEM((K, C, C), F32), pltpu.SemaphoreType.DMA((2,))],
-        name="mix_out",
-    )(core, near(mix_mine), near(mix_other))
-    return (grad_field.reshape(TD, FD, C), jnp.transpose(grad_spectra, (0, 2, 1, 3)), grad_mix)
+    grad_mix = ()
+    for held, parts in ((core, mix_mine), (1 - core, mix_other)):
+        grad_mix = (
+            call(
+                mix_kernel,
+                shape((K, C, C), F32),
+                1,
+                in_specs=[scalar, whole] + [anywhere] * len(grad_mix),
+                out_specs=anywhere,
+                scratch_shapes=[pltpu.VMEM((2, K, C // 4, C), F32), pltpu.SemaphoreType.DMA((2,))],
+                input_output_aliases={2: 0} if grad_mix else {},
+                name="mix_out",
+            )(held, near(parts), *grad_mix),
+        )
+    return (grad_field.reshape(TD, FD, C), jnp.transpose(grad_spectra, (0, 2, 1, 3)), grad_mix[0])
 
 
 def solution(mesh):

time: 105 us -> 103 us (0.981)
    ppermute x1, waiting for transfers between devices: 0.01 us -> 1.72 us  [on_device(): bottom = lax.ppermute(edge_rows[0], LAT, south)]
    ppermute x1, waiting for transfers between devices: 1.05 us -> 0.01 us  [on_device(): left = lax.ppermute(cotangent[:, FD - R:], LON, up)]
  transfers between devices with their start and end apart: 8 -> 8, of which waited for: 5 -> 5; matrix products, arithmetic and copies ran while one was open for 5% -> 5% of each run, Pallas kernels for 19% -> 20%
where the time goes in v9:
time: 103 us
  starting transfers between devices  29.5 us (29%)
  Pallas kernels  25.5 us (25%)
  waiting for transfers between devices  19.8 us (19%)
  blocking collectives  16.6 us (16%)
  local copies, waits for them, and re-layouts  7.39 us (7%)
  other arithmetic  3 us (3%)
    all_to_all x1, blocking collectives, on_device(): spec = lax.all_to_all(spectra, LAT, 0, 0, tiled=True)  16.6 us
    all_to_all x1, waiting for transfers between devices, on_device(): columns = lax.all_to_all(send, LON, 0, 0, tiled=True)  10.9 us
    pallas_call x1, Pallas kernels, on_device(): call(legendre_kernel, shape((MD // 2, L, 2 * HALF), BF16), 9, grid_spec=p...  9.85 us
    all_to_all x1, starting transfers between devices, on_device(): mix_mine = lax.all_to_all(mix_copies, CHIP, 0, 0, tiled=True)  7.09 us
    all_to_all x1, starting transfers between devices, on_device(): columns = lax.all_to_all(send, LON, 0, 0, tiled=True)  5.83 us
    all_to_all x1, waiting for transfers between devices, on_device(): mix_mine = lax.all_to_all(mix_copies, CHIP, 0, 0, tiled=True)  4.95 us
    ppermute x1, starting transfers between devices, on_device(): top = lax.ppermute(edge_rows[1], LAT, north)  4.81 us
    pallas_call x1, Pallas kernels, on_device(): call(synthesis_kernel, shape((2, CD, MD, L), F32), 6, grid_spec=pltpu.Pre...  4.76 us
  transfers between devices with their start and end apart: 8, of which 5 were waited for; matrix products, arithmetic and copies ran while one was open for 5% of the time, Pallas kernels for 20%

profile of v9, /device:TPU:1, one launch (start us, length us, event | category | flops | bytes accessed | tf_op | source)
XLA Modules:
  0.0 102.6 jit_solution(9584618181426967848)
XLA Ops:
  0.6 0.0 copy-start
  0.6 0.0 copy-start.2
  0.7 1.1 %fusion.8 = (bf16[24,8,384]{2,1,0:T(8,128)(2,1)S(1)}, bf16[24,8,384]{2,1,0:T(8,128)(2,1)S(1)}) fusion(bf16[24,24,384]{2,1,0:T(8,128)(2,1)} %cot.3), kind=kLoop, calls=%fused_computation.22 | loop fusion | bytes 589824 | tf_op jit(solution)/shard_map/slice | solution.py:472
  1.7 3.1 %collective-permute-start = (bf16[24,8,384]{2,1,0:T(8,128)(2,1)S(1)}, bf16[24,8,384]{2,1,0:T(8,128)(2,1)S(1)}, u32[]{:S(2)}, u32[]{:S(2)}) collective-permute-start(bf16[24,8,384]{2,1,0:T(8,128)(2,1)S(1)} %get-tuple-element.39), channel_id=1, source_target_pairs={{0,1},{1,2},{2,3},{3,4},{4,5},{5,6},{6,7},{7,8},{8,9},{9,10},{10,1... | collective-permute-start | bytes 442376 | tf_op jit(solution)/shard_map/ppermute | solution.py:472
  4.8 0.3 collective-permute-start.1
  5.2 0.7 fusion.7
  5.9 0.9 fusion.6
  6.8 0.7 convert_bitcast_fusion
  7.5 0.1 fusion.1
  7.6 0.0 collective-permute-done.left
  7.7 1.8 %collective-permute-done.1.right = bf16[24,8,384]{2,1,0:T(8,128)(2,1)S(1)} collective-permute-done((bf16[24,8,384]{2,1,0:T(8,128)(2,1)S(1)}, bf16[24,8,384]{2,1,0:T(8,128)(2,1)S(1)}, u32[]{:S(2)}, u32[]{:S(2)}) %collective-permute-start.1) | collective-permute-done | bytes 147488 | tf_op jit(solution)/shard_map/ppermute | solution.py:473
  9.4 4.8 %collective-permute-start.2 = (bf16[1,40,384]{2,1,0:T(8,128)(2,1)S(1)}, bf16[1,40,384]{2,1,0:T(8,128)(2,1)S(1)}, u32[]{:S(2)}, u32[]{:S(2)}) collective-permute-start(bf16[1,40,384]{2,1,0:T(8,128)(2,1)S(1)} %pad_maximum_fusion.1), channel_id=1, source_target_pairs={{0,32},{32,64},{64,96},{96,128},{128,160},{160,192},{192,224},{1,3... | collective-permute-start | bytes 92168 | tf_op jit(solution)/shard_map/ppermute | solution.py:479
  14.3 1.3 %collective-permute-start.3 = (bf16[1,40,384]{2,1,0:T(8,128)(2,1)S(1)}, bf16[1,40,384]{2,1,0:T(8,128)(2,1)S(1)}, u32[]{:S(2)}, u32[]{:S(2)}) collective-permute-start(bf16[1,40,384]{2,1,0:T(8,128)(2,1)S(1)} %pad_maximum_fusion), channel_id=1, source_target_pairs={{32,0},{64,32},{96,64},{128,96},{160,128},{192,160},{224,192},{33,... | collective-permute-start | bytes 92168 | tf_op jit(solution)/shard_map/ppermute | solution.py:480
  15.6 0.1 slice_bitcast_fusion.2
  15.6 0.1 copy.19
  15.7 0.1 copy.20
  15.8 0.1 copy.21
  15.8 1.2 %multiply_add_fusion.tab = f32[24,32,256]{2,1,0:T(8,128)S(1)} fusion(f32[24,256]{1,0:T(8,128)} %constant.57, f32[24,32]{1,0:T(8,128)S(1)} %copy.21, f32[24,256]{1,0:T(8,128)} %constant.56, f32[24,32]{1,0:T(8,128)S(1)} %copy.20, f32[24,256]{1,0:T(8,128)} %constant.55, f32[24,32]{1,0:T(8,128)S(1)} %copy.19), kind=kLoop, calls=%fused_computation | loop fusion | flops 983040 | bytes 869376 | tf_op jit(solution)/shard_map/add | solution.py:464
  17.0 0.0 copy-done
  17.0 0.0 copy-done.2
  17.0 1.6 %stencil_inner.1 = (bf16[384,1152]{1,0:T(8,128)(2,1)S(1)}, f32[384,1152]{1,0:T(8,128)S(1)}) custom-call(f32[24,32,256]{2,1,0:T(8,128)S(1)} %multiply_add_fusion.tab, bf16[24,24,384]{2,1,0:T(8,128)(2,1)S(1)} %copy-done, bf16[24,8,384]{2,1,0:T(8,128)(2,1)S(1)} %collective-permute-done.left, bf16[24,8,384]{2,1,0:T(8,128)(2,1)S(1)} %collective-permute-done.1.right, ...), custom_call_target="tpu_custom_call" | custom-call | flops 2200000000 | bytes 6000000 | tf_op jit(solution)/shard_map/stencil_inner/pallas_call | solution.py:493
  18.7 0.0 collective-permute-done.2.top
  18.7 1.7 %collective-permute-done.3.bottom = bf16[1,40,384]{2,1,0:T(8,128)(2,1)S(1)} collective-permute-done((bf16[1,40,384]{2,1,0:T(8,128)(2,1)S(1)}, bf16[1,40,384]{2,1,0:T(8,128)(2,1)S(1)}, u32[]{:S(2)}, u32[]{:S(2)}) %collective-permute-start.3) | collective-permute-done | bytes 30752 | tf_op jit(solution)/shard_map/ppermute | solution.py:480
  20.4 0.0 copy-start.1
  20.4 0.0 copy-start.4
  20.4 1.0 stencil_outer.1
  21.4 4.3 %collective-permute-start.4 = (bf16[192,1152]{1,0:T(8,128)(2,1)S(1)}, bf16[192,1152]{1,0:T(8,128)(2,1)S(1)}, u32[]{:S(2)}, u32[]{:S(2)}) collective-permute-start(bf16[192,1152]{1,0:T(8,128)(2,1)S(1)} %get-tuple-element.30), channel_id=1, source_target_pairs={{0,1},{1,0},{2,3},{3,2},{4,5},{5,4},{6,7},{7,6},{8,9},{9,8},{10,11... | collective-permute-start | bytes 1327112 | tf_op jit(solution)/shard_map/ppermute | solution.py:513
  25.7 0.0 copy-done.1
  25.7 0.0 copy-done.4
  25.7 3.5 %grad_field.1 = (bf16[576,384]{1,0:T(8,128)(2,1)}, bf16[32,112,128]{2,1,0:T(8,128)(2,1)}) custom-call(s32[1]{0:T(128)} %bitcast.pos, bf16[384,1152]{1,0:T(8,128)(2,1)S(1)} %get-tuple-element.21.g_inner, bf16[192,1152]{1,0:T(8,128)(2,1)S(1)} %get-tuple-element.25.g_outer, bf16[576,384]{1,0:T(8,128)(2,1)S(1)} %bitcast.14, bf16[3,384,384]{2,1,0:T(8,128)(2,1)S(1)} %copy-done.1, ...), custom_call_target="tpu_custom_call" | custom-call | flops 5500000256 | bytes 15000000 | tf_op jit(solution)/shard_map/grad_field/pallas_call | solution.py:516
  29.2 0.0 collective-permute-done.4.other
  29.2 0.9 mix_chip_sum.1
  30.1 0.0 copy-start.8
  30.2 0.0 copy-start.5
  30.2 5.8 %all-to-all-start = ((bf16[32,112,128]{2,1,0:T(8,128)(2,1)}), bf16[32,112,128]{2,1,0:T(8,128)(2,1)S(1)}, u32[]{:S(2)}, u32[]{:S(2)}) async-start(bf16[32,112,128]{2,1,0:T(8,128)(2,1)} %mix_chip_sum.1), calls=%async_computation | async-start | bytes 1835008 | tf_op jit(solution)/shard_map/all_to_all | solution.py:542
  36.0 0.8 dynamic_slice.7
  36.8 0.0 copy-done.8
  36.8 0.1 multiply_add_fusion.1.logscale
  36.9 0.0 copy-done.5
  36.9 0.0 copy-start.3
  36.9 9.8 %legendre.1.leg = bf16[24,384,256]{2,1,0:T(8,128)(2,1)S(1)} custom-call(s32[1]{0:T(128)} %bitcast.pos, f32[1,128]{1,0:T(1,128)S(1)} %copy-done.5, f32[48,128]{1,0:T(8,128)S(1)} %multiply_add_fusion.1.logscale), custom_call_target="tpu_custom_call" | custom-call | flops 9900000256 | bytes 27000000 | tf_op jit(solution)/shard_map/legendre/pallas_call | solution.py:550
  46.7 0.0 copy-start.6
  46.7 2.1 %copy-done.6 = bf16[24,384,256]{2,1,0:T(8,128)(2,1)} copy-done((bf16[24,384,256]{2,1,0:T(8,128)(2,1)}, bf16[24,384,256]{2,1,0:T(8,128)(2,1)S(1)}, u32[]{:S(2)}) %copy-start.6) | copy-done | bytes 4718616
  48.9 10.9 %all-to-all-done.columns = bf16[32,112,128]{2,1,0:T(8,128)(2,1)S(1)} async-done(((bf16[32,112,128]{2,1,0:T(8,128)(2,1)}), bf16[32,112,128]{2,1,0:T(8,128)(2,1)S(1)}, u32[]{:S(2)}, u32[]{:S(2)}) %all-to-all-start) | async-done | bytes 917536 | tf_op jit(solution)/shard_map/all_to_all | solution.py:542
  59.7 0.0 copy-done.3
  59.7 1.1 %dft.1 = bf16[8,328,128]{2,1,0:T(8,128)(2,1)S(1)} custom-call(bf16[768,1024]{1,0:T(8,128)(2,1)S(1)} %copy-done.3, bf16[32,112,128]{2,1,0:T(8,128)(2,1)S(1)} %all-to-all-done.columns), custom_call_target="tpu_custom_call" | custom-call | flops 2200000000 | bytes 6000000 | tf_op jit(solution)/shard_map/dft/pallas_call | solution.py:574
  60.8 16.6 %all_to_all.15.spec = bf16[8,328,128]{2,1,0:T(8,128)(2,1)S(1)} all-to-all(bf16[8,328,128]{2,1,0:T(8,128)(2,1)S(1)} %dft.1), channel_id=1, replica_groups=mesh['lat'=8,'chip'=16,'core'=2] {'lat'}, dimensions={0} | all-to-all | bytes 1343488 | tf_op jit(solution)/shard_map/all_to_all | solution.py:577
  77.4 0.8 mix_copies.1
  78.3 7.1 %all-to-all-start.2 = ((bf16[16,112,128]{2,1,0:T(8,128)(2,1)}), bf16[16,112,128]{2,1,0:T(8,128)(2,1)S(1)}, u32[]{:S(2)}, u32[]{:S(2)}) async-start(bf16[16,112,128]{2,1,0:T(8,128)(2,1)} %mix_copies.1), calls=%async_computation.2 | async-start | bytes 917504 | tf_op jit(solution)/shard_map/all_to_all | solution.py:579
  85.4 0.0 copy-start.7
  85.4 2.3 %copy-done.7 = bf16[24,384,256]{2,1,0:T(8,128)(2,1)S(1)} copy-done((bf16[24,384,256]{2,1,0:T(8,128)(2,1)S(1)}, bf16[24,384,256]{2,1,0:T(8,128)(2,1)}, u32[]{:S(2)}) %copy-start.7) | copy-done | bytes 4718616
  87.7 4.8 %synthesis.1 = f32[2,12,48,384]{3,2,1,0:T(8,128)} custom-call(bf16[8,328,128]{2,1,0:T(8,128)(2,1)S(1)} %all_to_all.15.spec, bf16[384,384]{1,0:T(8,128)(2,1)S(1)} %copy-done.4, bf16[24,384,256]{2,1,0:T(8,128)(2,1)S(1)} %copy-done.7), custom_call_target="tpu_custom_call" | custom-call | flops 6600000000 | bytes 18000000 | tf_op jit(solution)/shard_map/synthesis/pallas_call | solution.py:581
  92.5 5.0 %all-to-all-done.2.parts = bf16[16,112,128]{2,1,0:T(8,128)(2,1)S(1)} async-done(((bf16[16,112,128]{2,1,0:T(8,128)(2,1)}), bf16[16,112,128]{2,1,0:T(8,128)(2,1)S(1)}, u32[]{:S(2)}, u32[]{:S(2)}) %all-to-all-start.2) | async-done | bytes 458784 | tf_op jit(solution)/shard_map/all_to_all | solution.py:579
  97.4 2.8 %collective-permute-start.5 = (bf16[16,112,128]{2,1,0:T(8,128)(2,1)S(1)}, bf16[16,112,128]{2,1,0:T(8,128)(2,1)S(1)}, u32[]{:S(2)}, u32[]{:S(2)}) collective-permute-start(bf16[16,112,128]{2,1,0:T(8,128)(2,1)S(1)} %all-to-all-done.2.parts), channel_id=1, source_target_pairs={{0,1},{1,0},{2,3},{3,2},{4,5},{5,4},{6,7},{7,6},{8,9},{9,8},{10,11... | collective-permute-start | bytes 1376264 | tf_op jit(solution)/shard_map/ppermute | solution.py:602
  100.2 1.0 mix_out.2.rest_0_
  101.2 0.5 collective-permute-done.5.parts
  101.6 1.0 mix_out.3
  (5 shorter events, 0.0 us)
Async XLA Ops:
  0.6 16.4 %copy-start = (bf16[24,24,384]{2,1,0:T(8,128)(2,1)S(1)}, bf16[24,24,384]{2,1,0:T(8,128)(2,1)}, u32[]{:S(2)}) copy-start(bf16[24,24,384]{2,1,0:T(8,128)(2,1)} %cot.3) | copy-start | bytes 1327108
  0.6 16.4 %copy-start.2 = (bf16[24,24,384]{2,1,0:T(8,128)(2,1)S(1)}, bf16[24,24,384]{2,1,0:T(8,128)(2,1)}, u32[]{:S(2)}) copy-start(bf16[24,24,384]{2,1,0:T(8,128)(2,1)} %param.14) | copy-start | bytes 1327108
  1.7 5.9 %collective-permute-start = (bf16[24,8,384]{2,1,0:T(8,128)(2,1)S(1)}, bf16[24,8,384]{2,1,0:T(8,128)(2,1)S(1)}, u32[]{:S(2)}, u32[]{:S(2)}) collective-permute-start(bf16[24,8,384]{2,1,0:T(8,128)(2,1)S(1)} %get-tuple-element.39), channel_id=1, source_target_pairs={{0,1},{1,2},{2,3},{3,4},{4,5},{5,6},{6,7},{7,8},{8,9},{9,10},{10,1... | collective-permute-start | bytes 442376 | tf_op jit(solution)/shard_map/ppermute | solution.py:472
  4.8 4.6 %collective-permute-start.1 = (bf16[24,8,384]{2,1,0:T(8,128)(2,1)S(1)}, bf16[24,8,384]{2,1,0:T(8,128)(2,1)S(1)}, u32[]{:S(2)}, u32[]{:S(2)}) collective-permute-start(bf16[24,8,384]{2,1,0:T(8,128)(2,1)S(1)} %get-tuple-element.40), channel_id=1, source_target_pairs={{1,0},{2,1},{3,2},{4,3},{5,4},{6,5},{7,6},{8,7},{9,8},{10,9},{11,1... | collective-permute-start | bytes 442376 | tf_op jit(solution)/shard_map/ppermute | solution.py:473
  9.4 9.2 %collective-permute-start.2 = (bf16[1,40,384]{2,1,0:T(8,128)(2,1)S(1)}, bf16[1,40,384]{2,1,0:T(8,128)(2,1)S(1)}, u32[]{:S(2)}, u32[]{:S(2)}) collective-permute-start(bf16[1,40,384]{2,1,0:T(8,128)(2,1)S(1)} %pad_maximum_fusion.1), channel_id=1, source_target_pairs={{0,32},{32,64},{64,96},{96,128},{128,160},{160,192},{192,224},{1,3... | collective-permute-start | bytes 92168 | tf_op jit(solution)/shard_map/ppermute | solution.py:479
  14.3 6.1 %collective-permute-start.3 = (bf16[1,40,384]{2,1,0:T(8,128)(2,1)S(1)}, bf16[1,40,384]{2,1,0:T(8,128)(2,1)S(1)}, u32[]{:S(2)}, u32[]{:S(2)}) collective-permute-start(bf16[1,40,384]{2,1,0:T(8,128)(2,1)S(1)} %pad_maximum_fusion), channel_id=1, source_target_pairs={{32,0},{64,32},{96,64},{128,96},{160,128},{192,160},{224,192},{33,... | collective-permute-start | bytes 92168 | tf_op jit(solution)/shard_map/ppermute | solution.py:480
  20.4 5.3 %copy-start.1 = (bf16[3,384,384]{2,1,0:T(8,128)(2,1)S(1)}, bf16[3,384,384]{2,1,0:T(8,128)(2,1)}, u32[]{:S(2)}) copy-start(bf16[3,384,384]{2,1,0:T(8,128)(2,1)} %mix) | copy-start | bytes 2654212
  20.4 5.3 %copy-start.4 = (bf16[384,384]{1,0:T(8,128)(2,1)S(1)}, bf16[384,384]{1,0:T(8,128)(2,1)}, u32[]{:S(2)}) copy-start(bf16[384,384]{1,0:T(8,128)(2,1)} %constant.46.clone.pack) | copy-start | bytes 884740
  21.4 7.8 %collective-permute-start.4 = (bf16[192,1152]{1,0:T(8,128)(2,1)S(1)}, bf16[192,1152]{1,0:T(8,128)(2,1)S(1)}, u32[]{:S(2)}, u32[]{:S(2)}) collective-permute-start(bf16[192,1152]{1,0:T(8,128)(2,1)S(1)} %get-tuple-element.30), channel_id=1, source_target_pairs={{0,1},{1,0},{2,3},{3,2},{4,5},{5,4},{6,7},{7,6},{8,9},{9,8},{10,11... | collective-permute-start | bytes 1327112 | tf_op jit(solution)/shard_map/ppermute | solution.py:513
  30.1 6.6 %copy-start.8 = (f32[128]{0:T(128)S(1)}, f32[128]{0:T(128)}, u32[]{:S(2)}) copy-start(f32[128]{0:T(128)} %constant.58) | copy-start | bytes 1540
  30.2 6.7 %copy-start.5 = (f32[1,128]{1,0:T(1,128)S(1)}, f32[1,128]{1,0:T(1,128)}, u32[]{:S(2)}) copy-start(f32[1,128]{1,0:T(1,128)} %constant.49.clone.cosines) | copy-start | bytes 1540
  30.2 29.6 %all-to-all-start = ((bf16[32,112,128]{2,1,0:T(8,128)(2,1)}), bf16[32,112,128]{2,1,0:T(8,128)(2,1)S(1)}, u32[]{:S(2)}, u32[]{:S(2)}) async-start(bf16[32,112,128]{2,1,0:T(8,128)(2,1)} %mix_chip_sum.1), calls=%async_computation | async-start | bytes 1835008 | tf_op jit(solution)/shard_map/all_to_all | solution.py:542
  36.9 22.9 %copy-start.3 = (bf16[768,1024]{1,0:T(8,128)(2,1)S(1)}, bf16[768,1024]{1,0:T(8,128)(2,1)}, u32[]{:S(2)}) copy-start(bf16[768,1024]{1,0:T(8,128)(2,1)} %constant.50.clone.rows) | copy-start | bytes 4718596
  46.7 2.1 %copy-start.6 = (bf16[24,384,256]{2,1,0:T(8,128)(2,1)}, bf16[24,384,256]{2,1,0:T(8,128)(2,1)S(1)}, u32[]{:S(2)}) copy-start(bf16[24,384,256]{2,1,0:T(8,128)(2,1)S(1)} %legendre.1.leg) | copy-start | bytes 14155780
  78.3 19.1 %all-to-all-start.2 = ((bf16[16,112,128]{2,1,0:T(8,128)(2,1)}), bf16[16,112,128]{2,1,0:T(8,128)(2,1)S(1)}, u32[]{:S(2)}, u32[]{:S(2)}) async-start(bf16[16,112,128]{2,1,0:T(8,128)(2,1)} %mix_copies.1), calls=%async_computation.2 | async-start | bytes 917504 | tf_op jit(solution)/shard_map/all_to_all | solution.py:579
  85.4 2.3 %copy-start.7 = (bf16[24,384,256]{2,1,0:T(8,128)(2,1)S(1)}, bf16[24,384,256]{2,1,0:T(8,128)(2,1)}, u32[]{:S(2)}) copy-start(bf16[24,384,256]{2,1,0:T(8,128)(2,1)} %copy-done.6) | copy-start | bytes 14155780
  97.4 4.2 %collective-permute-start.5 = (bf16[16,112,128]{2,1,0:T(8,128)(2,1)S(1)}, bf16[16,112,128]{2,1,0:T(8,128)(2,1)S(1)}, u32[]{:S(2)}, u32[]{:S(2)}) collective-permute-start(bf16[16,112,128]{2,1,0:T(8,128)(2,1)S(1)} %all-to-all-done.2.parts), channel_id=1, source_target_pairs={{0,1},{1,0},{2,3},{3,2},{4,5},{5,4},{6,7},{7,6},{8,9},{9,8},{10,11... | collective-permute-start | bytes 1376264 | tf_op jit(solution)/shard_map/ppermute | solution.py:602

commit v10 on v9

--- a/solution.py
+++ b/solution.py
@@ -125,7 +125,16 @@
     return lax.dot_general(field, g, (((0,), (0,)), ((), ())), preferred_element_type=F32)
 
 
-def inner_kernel(tab, cot, left, right, field, g_out, mix_out, ext, band):
+def weigh(g, mix):
+    total = jnp.zeros((g.shape[0], C), F32)
+    for k in range(K):
+        total = total + lax.dot_general(
+            g[:, k * C:(k + 1) * C], mix[k], (((1,), (1,)), ((), ())), preferred_element_type=F32
+        )
+    return total
+
+
+def inner_kernel(tab, cot, left, right, field, mix, field_out, mix_out, g_out, ext, band):
     widen(ext, slice(QUAD - 1, TD - QUAD + 1), cot, left, right)
     apart = offsets_in_band()
     for n in range(INNER):
@@ -133,6 +142,7 @@
         for k in range(K):
             g_out[n * ROWS:(n + 1) * ROWS, k * C:(k + 1) * C] = got[k * ROWS:(k + 1) * ROWS]
     mix_out[...] = cells_dot(field[ROWS:(INNER + 1) * ROWS, :], g_out[...])
+    field_out[...] = weigh(g_out, mix)
 
 
 def outer_kernel(core, tab, cot, left, right, top, bottom, field, mix_inner, g_out, mine_out, other_out, ext, band):
@@ -153,18 +163,9 @@
     other_out[...] = jnp.where(first, high, low).astype(BF16)
 
 
-def field_kernel(pos, g_inner, g_outer, cot, mix, pack, gf_out, send_out, flat, turned, send):
-    inner = jnp.zeros((INNER * ROWS, C), F32)
-    outer = jnp.zeros((2 * ROWS, C), F32)
-    for k in range(K):
-        span = slice(k * C, (k + 1) * C)
-        inner = inner + lax.dot_general(
-            g_inner[:, span], mix[k], (((1,), (1,)), ((), ())), preferred_element_type=F32
-        )
-        outer = outer + lax.dot_general(
-            g_outer[:, span], mix[k], (((1,), (1,)), ((), ())), preferred_element_type=F32
-        )
-    total = cot[...].astype(F32) + jnp.concatenate([outer[:ROWS], inner, outer[ROWS:]], axis=0)
+def field_kernel(pos, inner, g_outer, cot, mix, pack, gf_out, send_out, flat, turned, send):
+    outer = weigh(g_outer, mix)
+    total = cot[...].astype(F32) + jnp.concatenate([outer[:ROWS], inner[...], outer[ROWS:]], axis=0)
     rounded = total.astype(BF16)
     gf_out[...] = rounded
     rounded = rounded.astype(F32)
@@ -490,17 +491,17 @@
     rims = (near(left), near(right))
     near_cot, near_field = near(cotangent), near(field.reshape(cells, C))
     scratch = [pltpu.VMEM((TD + 2, XW, C), F32), pltpu.VMEM((K * ROWS, 256), F32)]
-    g_inner, mix_inner = call(
+    mix_near = near(mix_weight)
+    field_inner, mix_inner = call(
         inner_kernel,
-        (near_shape((INNER * ROWS, K * C), BF16), near_shape((C, K * C), F32)),
+        (near_shape((INNER * ROWS, C), F32), near_shape((C, K * C), F32)),
         2,
-        in_specs=[whole] * 5,
-        scratch_shapes=scratch,
+        in_specs=[whole] * 6,
+        scratch_shapes=[pltpu.VMEM((INNER * ROWS, K * C), BF16)] + scratch,
         name="stencil_inner",
-    )(near(tab), near_cot, *rims, near_field)
+    )(near(tab), near_cot, *rims, near_field, mix_near)
     pack = near(jnp.asarray(packing()))
-    mix_near = near(mix_weight)
-    top, bottom, pack, mix_near = lax.optimization_barrier((top, bottom, pack, mix_near))
+    top, bottom, pack = lax.optimization_barrier((top, bottom, pack))
     g_outer, mix_mine, mix_other = call(
         outer_kernel,
         (near_shape((2 * ROWS, K * C), BF16), near_shape(half, F32), near_shape(half, BF16)),
@@ -524,7 +525,7 @@
             pltpu.VMEM((CD // 4, LONS * FD, 128), F32),
         ],
         name="grad_field",
-    )(pos, near(g_inner), near(g_outer), near(cotangent.reshape(cells, C)), near(mix_near), near(pack))
+    )(pos, near(field_inner), near(g_outer), near(cotangent.reshape(cells, C)), near(mix_near), near(pack))
     send = call(
         chip_sum_kernel,
         shape((LONS, SENT, 128), BF16),

time: 103 us -> 103 us (level)
  no operation moved by 1% of the time
where the time goes in v10:
time: 103 us; the launch traced here: 102 us
  starting transfers between devices  29.5 us (29%)
  Pallas kernels  25.4 us (25%)
  waiting for transfers between devices  19.2 us (19%)
  blocking collectives  16.6 us (16%)
  local copies, waits for them, and re-layouts  7.44 us (7%)
  other arithmetic  3 us (3%)
    all_to_all x1, blocking collectives, on_device(): spec = lax.all_to_all(spectra, LAT, 0, 0, tiled=True)  16.6 us
    all_to_all x1, waiting for transfers between devices, on_device(): columns = lax.all_to_all(send, LON, 0, 0, tiled=True)  10.9 us
    pallas_call x1, Pallas kernels, on_device(): call(legendre_kernel, shape((MD // 2, L, 2 * HALF), BF16), 9, grid_spec=p...  9.85 us
    all_to_all x1, starting transfers between devices, on_device(): mix_mine = lax.all_to_all(mix_copies, CHIP, 0, 0, tiled=True)  7.09 us
    all_to_all x1, starting transfers between devices, on_device(): columns = lax.all_to_all(send, LON, 0, 0, tiled=True)  5.8 us
    all_to_all x1, waiting for transfers between devices, on_device(): mix_mine = lax.all_to_all(mix_copies, CHIP, 0, 0, tiled=True)  4.95 us
    ppermute x1, starting transfers between devices, on_device(): top = lax.ppermute(edge_rows[1], LAT, north)  4.81 us
    pallas_call x1, Pallas kernels, on_device(): call(synthesis_kernel, shape((2, CD, MD, L), F32), 6, grid_spec=pltpu.Pre...  4.76 us
  transfers between devices with their start and end apart: 8, of which 5 were waited for; matrix products, arithmetic and copies ran while one was open for 5% of the time, Pallas kernels for 20%

profile of v10, /device:TPU:1, one launch (start us, length us, event | category | flops | bytes accessed | tf_op | source)
XLA Modules:
  0.0 102.0 jit_solution(16493031191600993247)
XLA Ops:
  0.6 0.0 copy-start
  0.6 0.0 copy-start.2
  0.7 0.0 copy-start.1
  0.7 1.1 %fusion.8 = (bf16[24,8,384]{2,1,0:T(8,128)(2,1)S(1)}, bf16[24,8,384]{2,1,0:T(8,128)(2,1)S(1)}) fusion(bf16[24,24,384]{2,1,0:T(8,128)(2,1)} %cot.3), kind=kLoop, calls=%fused_computation.22 | loop fusion | bytes 589824 | tf_op jit(solution)/shard_map/slice | solution.py:473
  1.8 3.1 %collective-permute-start = (bf16[24,8,384]{2,1,0:T(8,128)(2,1)S(1)}, bf16[24,8,384]{2,1,0:T(8,128)(2,1)S(1)}, u32[]{:S(2)}, u32[]{:S(2)}) collective-permute-start(bf16[24,8,384]{2,1,0:T(8,128)(2,1)S(1)} %get-tuple-element.37), channel_id=1, source_target_pairs={{0,1},{1,2},{2,3},{3,4},{4,5},{5,6},{6,7},{7,8},{8,9},{9,10},{10,1... | collective-permute-start | bytes 442376 | tf_op jit(solution)/shard_map/ppermute | solution.py:473
  4.9 0.3 collective-permute-start.1
  5.2 0.7 fusion.7
  6.0 0.9 fusion.6
  6.9 0.7 convert_bitcast_fusion
  7.6 0.1 fusion.1
  7.7 0.0 collective-permute-done.left
  7.7 1.8 %collective-permute-done.1.right = bf16[24,8,384]{2,1,0:T(8,128)(2,1)S(1)} collective-permute-done((bf16[24,8,384]{2,1,0:T(8,128)(2,1)S(1)}, bf16[24,8,384]{2,1,0:T(8,128)(2,1)S(1)}, u32[]{:S(2)}, u32[]{:S(2)}) %collective-permute-start.1) | collective-permute-done | bytes 147488 | tf_op jit(solution)/shard_map/ppermute | solution.py:474
  9.5 4.8 %collective-permute-start.2 = (bf16[1,40,384]{2,1,0:T(8,128)(2,1)S(1)}, bf16[1,40,384]{2,1,0:T(8,128)(2,1)S(1)}, u32[]{:S(2)}, u32[]{:S(2)}) collective-permute-start(bf16[1,40,384]{2,1,0:T(8,128)(2,1)S(1)} %pad_maximum_fusion.1), channel_id=1, source_target_pairs={{0,32},{32,64},{64,96},{96,128},{128,160},{160,192},{192,224},{1,3... | collective-permute-start | bytes 92168 | tf_op jit(solution)/shard_map/ppermute | solution.py:480
  14.3 1.3 %collective-permute-start.3 = (bf16[1,40,384]{2,1,0:T(8,128)(2,1)S(1)}, bf16[1,40,384]{2,1,0:T(8,128)(2,1)S(1)}, u32[]{:S(2)}, u32[]{:S(2)}) collective-permute-start(bf16[1,40,384]{2,1,0:T(8,128)(2,1)S(1)} %pad_maximum_fusion), channel_id=1, source_target_pairs={{32,0},{64,32},{96,64},{128,96},{160,128},{192,160},{224,192},{33,... | collective-permute-start | bytes 92168 | tf_op jit(solution)/shard_map/ppermute | solution.py:481
  15.6 0.1 slice_bitcast_fusion.2
  15.7 0.1 copy.19
  15.8 0.1 copy.20
  15.8 0.1 copy.21
  15.9 1.2 %multiply_add_fusion.tab = f32[24,32,256]{2,1,0:T(8,128)S(1)} fusion(f32[24,256]{1,0:T(8,128)} %constant.57, f32[24,32]{1,0:T(8,128)S(1)} %copy.21, f32[24,256]{1,0:T(8,128)} %constant.56, f32[24,32]{1,0:T(8,128)S(1)} %copy.20, f32[24,256]{1,0:T(8,128)} %constant.55, f32[24,32]{1,0:T(8,128)S(1)} %copy.19), kind=kLoop, calls=%fused_computation | loop fusion | flops 983040 | bytes 869376 | tf_op jit(solution)/shard_map/add | solution.py:465
  17.1 0.0 copy-done
  17.1 0.0 copy-done.2
  17.1 0.0 copy-done.1
  17.1 2.1 %stencil_inner.1 = (f32[384,384]{1,0:T(8,128)S(1)}, f32[384,1152]{1,0:T(8,128)S(1)}) custom-call(f32[24,32,256]{2,1,0:T(8,128)S(1)} %multiply_add_fusion.tab, bf16[24,24,384]{2,1,0:T(8,128)(2,1)S(1)} %copy-done, bf16[24,8,384]{2,1,0:T(8,128)(2,1)S(1)} %collective-permute-done.left, bf16[24,8,384]{2,1,0:T(8,128)(2,1)S(1)} %collective-permute-done.1.right, ...), custom_call_target="tpu_custom_call" | custom-call | flops 2200000000 | bytes 6000000 | tf_op jit(solution)/shard_map/stencil_inner/pallas_call | solution.py:495
  19.3 0.0 collective-permute-done.2.top
  19.3 1.2 %collective-permute-done.3.bottom = bf16[1,40,384]{2,1,0:T(8,128)(2,1)S(1)} collective-permute-done((bf16[1,40,384]{2,1,0:T(8,128)(2,1)S(1)}, bf16[1,40,384]{2,1,0:T(8,128)(2,1)S(1)}, u32[]{:S(2)}, u32[]{:S(2)}) %collective-permute-start.3) | collective-permute-done | bytes 30752 | tf_op jit(solution)/shard_map/ppermute | solution.py:481
  20.5 0.0 copy-start.4
  20.5 1.0 stencil_outer.1
  21.5 4.3 %collective-permute-start.4 = (bf16[192,1152]{1,0:T(8,128)(2,1)S(1)}, bf16[192,1152]{1,0:T(8,128)(2,1)S(1)}, u32[]{:S(2)}, u32[]{:S(2)}) collective-permute-start(bf16[192,1152]{1,0:T(8,128)(2,1)S(1)} %get-tuple-element.28), channel_id=1, source_target_pairs={{0,1},{1,0},{2,3},{3,2},{4,5},{5,4},{6,7},{7,6},{8,9},{9,8},{10,11... | collective-permute-start | bytes 1327112 | tf_op jit(solution)/shard_map/ppermute | solution.py:514
  25.8 0.0 copy-done.4
  25.8 3.0 %grad_field.1 = (bf16[576,384]{1,0:T(8,128)(2,1)}, bf16[32,112,128]{2,1,0:T(8,128)(2,1)}) custom-call(s32[1]{0:T(128)} %bitcast.pos, f32[384,384]{1,0:T(8,128)S(1)} %get-tuple-element.20.inner, bf16[192,1152]{1,0:T(8,128)(2,1)S(1)} %get-tuple-element.24.g_outer, bf16[576,384]{1,0:T(8,128)(2,1)S(1)} %bitcast.14, bf16[3,384,384]{2,1,0:T(8,128)(2,1)S(1)} %copy-done.1, ...), custom_call_target="tpu_custom_call" | custom-call | flops 5500000256 | bytes 15000000 | tf_op jit(solution)/shard_map/grad_field/pallas_call | solution.py:517
  28.7 0.0 collective-permute-done.4.other
  28.7 0.9 mix_chip_sum.1
  29.6 0.0 copy-start.8
  29.6 0.0 copy-start.5
  29.7 5.8 %all-to-all-start = ((bf16[32,112,128]{2,1,0:T(8,128)(2,1)}), bf16[32,112,128]{2,1,0:T(8,128)(2,1)S(1)}, u32[]{:S(2)}, u32[]{:S(2)}) async-start(bf16[32,112,128]{2,1,0:T(8,128)(2,1)} %mix_chip_sum.1), calls=%async_computation | async-start | bytes 1835008 | tf_op jit(solution)/shard_map/all_to_all | solution.py:543
  35.5 0.8 dynamic_slice.7
  36.2 0.0 copy-done.8
  36.2 0.1 multiply_add_fusion.1.logscale
  36.3 0.0 copy-done.5
  36.3 0.0 copy-start.3
  36.3 9.8 %legendre.1.leg = bf16[24,384,256]{2,1,0:T(8,128)(2,1)S(1)} custom-call(s32[1]{0:T(128)} %bitcast.pos, f32[1,128]{1,0:T(1,128)S(1)} %copy-done.5, f32[48,128]{1,0:T(8,128)S(1)} %multiply_add_fusion.1.logscale), custom_call_target="tpu_custom_call" | custom-call | flops 9900000256 | bytes 27000000 | tf_op jit(solution)/shard_map/legendre/pallas_call | solution.py:551
  46.2 0.0 copy-start.6
  46.2 2.1 %copy-done.6 = bf16[24,384,256]{2,1,0:T(8,128)(2,1)} copy-done((bf16[24,384,256]{2,1,0:T(8,128)(2,1)}, bf16[24,384,256]{2,1,0:T(8,128)(2,1)S(1)}, u32[]{:S(2)}) %copy-start.6) | copy-done | bytes 4718616
  48.3 10.9 %all-to-all-done.columns = bf16[32,112,128]{2,1,0:T(8,128)(2,1)S(1)} async-done(((bf16[32,112,128]{2,1,0:T(8,128)(2,1)}), bf16[32,112,128]{2,1,0:T(8,128)(2,1)S(1)}, u32[]{:S(2)}, u32[]{:S(2)}) %all-to-all-start) | async-done | bytes 917536 | tf_op jit(solution)/shard_map/all_to_all | solution.py:543
  59.2 0.0 copy-done.3
  59.2 1.1 %dft.1 = bf16[8,328,128]{2,1,0:T(8,128)(2,1)S(1)} custom-call(bf16[768,1024]{1,0:T(8,128)(2,1)S(1)} %copy-done.3, bf16[32,112,128]{2,1,0:T(8,128)(2,1)S(1)} %all-to-all-done.columns), custom_call_target="tpu_custom_call" | custom-call | flops 2200000000 | bytes 6000000 | tf_op jit(solution)/shard_map/dft/pallas_call | solution.py:575
  60.3 16.6 %all_to_all.15.spec = bf16[8,328,128]{2,1,0:T(8,128)(2,1)S(1)} all-to-all(bf16[8,328,128]{2,1,0:T(8,128)(2,1)S(1)} %dft.1), channel_id=1, replica_groups=mesh['lat'=8,'chip'=16,'core'=2] {'lat'}, dimensions={0} | all-to-all | bytes 1343488 | tf_op jit(solution)/shard_map/all_to_all | solution.py:578
  76.9 0.8 mix_copies.1
  77.7 7.1 %all-to-all-start.2 = ((bf16[16,112,128]{2,1,0:T(8,128)(2,1)}), bf16[16,112,128]{2,1,0:T(8,128)(2,1)S(1)}, u32[]{:S(2)}, u32[]{:S(2)}) async-start(bf16[16,112,128]{2,1,0:T(8,128)(2,1)} %mix_copies.1), calls=%async_computation.2 | async-start | bytes 917504 | tf_op jit(solution)/shard_map/all_to_all | solution.py:580
  84.8 0.0 copy-start.7
  84.8 2.3 %copy-done.7 = bf16[24,384,256]{2,1,0:T(8,128)(2,1)S(1)} copy-done((bf16[24,384,256]{2,1,0:T(8,128)(2,1)S(1)}, bf16[24,384,256]{2,1,0:T(8,128)(2,1)}, u32[]{:S(2)}) %copy-start.7) | copy-done | bytes 4718616
  87.1 4.8 %synthesis.1 = f32[2,12,48,384]{3,2,1,0:T(8,128)} custom-call(bf16[8,328,128]{2,1,0:T(8,128)(2,1)S(1)} %all_to_all.15.spec, bf16[384,384]{1,0:T(8,128)(2,1)S(1)} %copy-done.4, bf16[24,384,256]{2,1,0:T(8,128)(2,1)S(1)} %copy-done.7), custom_call_target="tpu_custom_call" | custom-call | flops 6600000000 | bytes 18000000 | tf_op jit(solution)/shard_map/synthesis/pallas_call | solution.py:582
  91.9 5.0 %all-to-all-done.2.parts = bf16[16,112,128]{2,1,0:T(8,128)(2,1)S(1)} async-done(((bf16[16,112,128]{2,1,0:T(8,128)(2,1)}), bf16[16,112,128]{2,1,0:T(8,128)(2,1)S(1)}, u32[]{:S(2)}, u32[]{:S(2)}) %all-to-all-start.2) | async-done | bytes 458784 | tf_op jit(solution)/shard_map/all_to_all | solution.py:580
  96.9 2.8 %collective-permute-start.5 = (bf16[16,112,128]{2,1,0:T(8,128)(2,1)S(1)}, bf16[16,112,128]{2,1,0:T(8,128)(2,1)S(1)}, u32[]{:S(2)}, u32[]{:S(2)}) collective-permute-start(bf16[16,112,128]{2,1,0:T(8,128)(2,1)S(1)} %all-to-all-done.2.parts), channel_id=1, source_target_pairs={{0,1},{1,0},{2,3},{3,2},{4,5},{5,4},{6,7},{7,6},{8,9},{9,8},{10,11... | collective-permute-start | bytes 1376264 | tf_op jit(solution)/shard_map/ppermute | solution.py:603
  99.6 1.0 mix_out.2.rest_0_
  100.6 0.5 collective-permute-done.5.parts
  101.1 1.0 mix_out.3
  (5 shorter events, 0.0 us)
Async XLA Ops:
  0.6 16.5 %copy-start = (bf16[24,24,384]{2,1,0:T(8,128)(2,1)S(1)}, bf16[24,24,384]{2,1,0:T(8,128)(2,1)}, u32[]{:S(2)}) copy-start(bf16[24,24,384]{2,1,0:T(8,128)(2,1)} %cot.3) | copy-start | bytes 1327108
  0.6 16.5 %copy-start.2 = (bf16[24,24,384]{2,1,0:T(8,128)(2,1)S(1)}, bf16[24,24,384]{2,1,0:T(8,128)(2,1)}, u32[]{:S(2)}) copy-start(bf16[24,24,384]{2,1,0:T(8,128)(2,1)} %param.14) | copy-start | bytes 1327108
  0.7 16.5 %copy-start.1 = (bf16[3,384,384]{2,1,0:T(8,128)(2,1)S(1)}, bf16[3,384,384]{2,1,0:T(8,128)(2,1)}, u32[]{:S(2)}) copy-start(bf16[3,384,384]{2,1,0:T(8,128)(2,1)} %mix.3) | copy-start | bytes 2654212
  1.8 5.9 %collective-permute-start = (bf16[24,8,384]{2,1,0:T(8,128)(2,1)S(1)}, bf16[24,8,384]{2,1,0:T(8,128)(2,1)S(1)}, u32[]{:S(2)}, u32[]{:S(2)}) collective-permute-start(bf16[24,8,384]{2,1,0:T(8,128)(2,1)S(1)} %get-tuple-element.37), channel_id=1, source_target_pairs={{0,1},{1,2},{2,3},{3,4},{4,5},{5,6},{6,7},{7,8},{8,9},{9,10},{10,1... | collective-permute-start | bytes 442376 | tf_op jit(solution)/shard_map/ppermute | solution.py:473
  4.9 4.6 %collective-permute-start.1 = (bf16[24,8,384]{2,1,0:T(8,128)(2,1)S(1)}, bf16[24,8,384]{2,1,0:T(8,128)(2,1)S(1)}, u32[]{:S(2)}, u32[]{:S(2)}) collective-permute-start(bf16[24,8,384]{2,1,0:T(8,128)(2,1)S(1)} %get-tuple-element.38), channel_id=1, source_target_pairs={{1,0},{2,1},{3,2},{4,3},{5,4},{6,5},{7,6},{8,7},{9,8},{10,9},{11,1... | collective-permute-start | bytes 442376 | tf_op jit(solution)/shard_map/ppermute | solution.py:474
  9.5 9.8 %collective-permute-start.2 = (bf16[1,40,384]{2,1,0:T(8,128)(2,1)S(1)}, bf16[1,40,384]{2,1,0:T(8,128)(2,1)S(1)}, u32[]{:S(2)}, u32[]{:S(2)}) collective-permute-start(bf16[1,40,384]{2,1,0:T(8,128)(2,1)S(1)} %pad_maximum_fusion.1), channel_id=1, source_target_pairs={{0,32},{32,64},{64,96},{96,128},{128,160},{160,192},{192,224},{1,3... | collective-permute-start | bytes 92168 | tf_op jit(solution)/shard_map/ppermute | solution.py:480
  14.3 6.1 %collective-permute-start.3 = (bf16[1,40,384]{2,1,0:T(8,128)(2,1)S(1)}, bf16[1,40,384]{2,1,0:T(8,128)(2,1)S(1)}, u32[]{:S(2)}, u32[]{:S(2)}) collective-permute-start(bf16[1,40,384]{2,1,0:T(8,128)(2,1)S(1)} %pad_maximum_fusion), channel_id=1, source_target_pairs={{32,0},{64,32},{96,64},{128,96},{160,128},{192,160},{224,192},{33,... | collective-permute-start | bytes 92168 | tf_op jit(solution)/shard_map/ppermute | solution.py:481
  20.5 5.3 %copy-start.4 = (bf16[384,384]{1,0:T(8,128)(2,1)S(1)}, bf16[384,384]{1,0:T(8,128)(2,1)}, u32[]{:S(2)}) copy-start(bf16[384,384]{1,0:T(8,128)(2,1)} %constant.46.clone.pack) | copy-start | bytes 884740
  21.5 7.3 %collective-permute-start.4 = (bf16[192,1152]{1,0:T(8,128)(2,1)S(1)}, bf16[192,1152]{1,0:T(8,128)(2,1)S(1)}, u32[]{:S(2)}, u32[]{:S(2)}) collective-permute-start(bf16[192,1152]{1,0:T(8,128)(2,1)S(1)} %get-tuple-element.28), channel_id=1, source_target_pairs={{0,1},{1,0},{2,3},{3,2},{4,5},{5,4},{6,7},{7,6},{8,9},{9,8},{10,11... | collective-permute-start | bytes 1327112 | tf_op jit(solution)/shard_map/ppermute | solution.py:514
  29.6 6.6 %copy-start.8 = (f32[128]{0:T(128)S(1)}, f32[128]{0:T(128)}, u32[]{:S(2)}) copy-start(f32[128]{0:T(128)} %constant.58) | copy-start | bytes 1540
  29.6 6.7 %copy-start.5 = (f32[1,128]{1,0:T(1,128)S(1)}, f32[1,128]{1,0:T(1,128)}, u32[]{:S(2)}) copy-start(f32[1,128]{1,0:T(1,128)} %constant.49.clone.cosines) | copy-start | bytes 1540
  29.7 29.5 %all-to-all-start = ((bf16[32,112,128]{2,1,0:T(8,128)(2,1)}), bf16[32,112,128]{2,1,0:T(8,128)(2,1)S(1)}, u32[]{:S(2)}, u32[]{:S(2)}) async-start(bf16[32,112,128]{2,1,0:T(8,128)(2,1)} %mix_chip_sum.1), calls=%async_computation | async-start | bytes 1835008 | tf_op jit(solution)/shard_map/all_to_all | solution.py:543
  36.3 22.9 %copy-start.3 = (bf16[768,1024]{1,0:T(8,128)(2,1)S(1)}, bf16[768,1024]{1,0:T(8,128)(2,1)}, u32[]{:S(2)}) copy-start(bf16[768,1024]{1,0:T(8,128)(2,1)} %constant.50.clone.rows) | copy-start | bytes 4718596
  46.2 2.1 %copy-start.6 = (bf16[24,384,256]{2,1,0:T(8,128)(2,1)}, bf16[24,384,256]{2,1,0:T(8,128)(2,1)S(1)}, u32[]{:S(2)}) copy-start(bf16[24,384,256]{2,1,0:T(8,128)(2,1)S(1)} %legendre.1.leg) | copy-start | bytes 14155780
  77.7 19.1 %all-to-all-start.2 = ((bf16[16,112,128]{2,1,0:T(8,128)(2,1)}), bf16[16,112,128]{2,1,0:T(8,128)(2,1)S(1)}, u32[]{:S(2)}, u32[]{:S(2)}) async-start(bf16[16,112,128]{2,1,0:T(8,128)(2,1)} %mix_copies.1), calls=%async_computation.2 | async-start | bytes 917504 | tf_op jit(solution)/shard_map/all_to_all | solution.py:580
  84.8 2.3 %copy-start.7 = (bf16[24,384,256]{2,1,0:T(8,128)(2,1)S(1)}, bf16[24,384,256]{2,1,0:T(8,128)(2,1)}, u32[]{:S(2)}) copy-start(bf16[24,384,256]{2,1,0:T(8,128)(2,1)} %copy-done.6) | copy-start | bytes 14155780
  96.9 4.2 %collective-permute-start.5 = (bf16[16,112,128]{2,1,0:T(8,128)(2,1)S(1)}, bf16[16,112,128]{2,1,0:T(8,128)(2,1)S(1)}, u32[]{:S(2)}, u32[]{:S(2)}) collective-permute-start(bf16[16,112,128]{2,1,0:T(8,128)(2,1)S(1)} %all-to-all-done.2.parts), channel_id=1, source_target_pairs={{0,1},{1,0},{2,3},{3,2},{4,5},{5,4},{6,7},{7,6},{8,9},{9,8},{10,11... | collective-permute-start | bytes 1376264 | tf_op jit(solution)/shard_map/ppermute | solution.py:603

commit v11 on v10

--- a/solution.py
+++ b/solution.py
@@ -96,6 +96,12 @@
     ext[there, R + FD:XW, :] = right[rows].astype(F32)
 
 
+def edge_kernel(cot, left, right, first, last):
+    for row, out in ((0, first), (TD - 1, last)):
+        pieces = [part[row:row + 1].astype(F32) for part in (left, cot, right)]
+        out[...] = jnp.concatenate(pieces, axis=1).astype(BF16)
+
+
 def offsets_in_band():
     lane = lax.broadcasted_iota(jnp.int32, (FD, 256), 1)
     column = lane
@@ -472,15 +478,21 @@
     down = [(j, i) for i, j in up]
     left = lax.ppermute(cotangent[:, FD - R:], LON, up)
     right = lax.ppermute(cotangent[:, :R], LON, down)
-    edge_rows = [
-        jnp.concatenate([left[t:t + 1], cotangent[t:t + 1], right[t:t + 1]], axis=1) for t in (0, TD - 1)
-    ]
+    whole = pl.BlockSpec(memory_space=pltpu.VMEM)
+    near_cot, rims = near(cotangent), (near(left), near(right))
+    edge = (1, XW, C)
+    edge_rows = call(
+        edge_kernel,
+        (near_shape(edge, BF16), near_shape(edge, BF16)),
+        1,
+        in_specs=[whole] * 3,
+        name="edge_rows",
+    )(near_cot, *rims)
     north = [(i, i + 1) for i in range(LATS - 1)]
     south = [(j, i) for i, j in north]
     top = lax.ppermute(edge_rows[1], LAT, north)
     bottom = lax.ppermute(edge_rows[0], LAT, south)
 
-    whole = pl.BlockSpec(memory_space=pltpu.VMEM)
     tap_part, _ = lax.optimization_barrier((tap_rows(taps, offsets, counts, lat_pos * TD), edge_rows))
     tab = tap_table(tap_part)
     cells = TD * FD
@@ -488,8 +500,7 @@
     scalar = pl.BlockSpec(memory_space=pltpu.SMEM)
     anywhere = pl.BlockSpec(memory_space=pl.ANY)
     half = (C // 2, K * C)
-    rims = (near(left), near(right))
-    near_cot, near_field = near(cotangent), near(field.reshape(cells, C))
+    near_field = near(field.reshape(cells, C))
     scratch = [pltpu.VMEM((TD + 2, XW, C), F32), pltpu.VMEM((K * ROWS, 256), F32)]
     mix_near = near(mix_weight)
     field_inner, mix_inner = call(

time: 103 us -> 104 us (level)
  waiting for transfers between devices: 19.2 us -> 20.7 us
    unnamed x18 -> x26, local copies, waits for them, and re-layouts: 4.51 us -> 5.55 us
  transfers between devices with their start and end apart: 8 -> 8, of which waited for: 5 -> 5; matrix products, arithmetic and copies ran while one was open for 5% -> 3% of each run, Pallas kernels for 20% -> 20%
where the time goes in v11:
time: 104 us; the launch traced here: 103 us
  starting transfers between devices  29.6 us (28%)
  Pallas kernels  25.4 us (24%)
  waiting for transfers between devices  20.7 us (20%)
  blocking collectives  16.6 us (16%)
  local copies, waits for them, and re-layouts  7.6 us (7%)
  other arithmetic  2.21 us (2%)
    all_to_all x1, blocking collectives, on_device(): spec = lax.all_to_all(spectra, LAT, 0, 0, tiled=True)  16.6 us
    all_to_all x1, waiting for transfers between devices, on_device(): columns = lax.all_to_all(send, LON, 0, 0, tiled=True)  10.9 us
    pallas_call x1, Pallas kernels, on_device(): call(legendre_kernel, shape((MD // 2, L, 2 * HALF), BF16), 9, grid_spec=p...  9.85 us
    all_to_all x1, starting transfers between devices, on_device(): mix_mine = lax.all_to_all(mix_copies, CHIP, 0, 0, tiled=True)  7.09 us
    all_to_all x1, starting transfers between devices, on_device(): columns = lax.all_to_all(send, LON, 0, 0, tiled=True)  5.8 us
    unnamed x26, local copies, waits for them, and re-layouts  5.55 us
    all_to_all x1, waiting for transfers between devices, on_device(): mix_mine = lax.all_to_all(mix_copies, CHIP, 0, 0, tiled=True)  4.95 us
    ppermute x1, starting transfers between devices, on_device(): top = lax.ppermute(edge_rows[1], LAT, north)  4.95 us
  transfers between devices with their start and end apart: 8, of which 5 were waited for; matrix products, arithmetic and copies ran while one was open for 3% of the time, Pallas kernels for 20%

profile of v11, /device:TPU:1, one launch (start us, length us, event | category | flops | bytes accessed | tf_op | source)
XLA Modules:
  0.0 103.0 jit_solution(16681026499270641865)
XLA Ops:
  0.6 1.0 fusion.7
  1.6 3.1 %collective-permute-start = (bf16[24,8,384]{2,1,0:T(8,128)(2,1)S(1)}, bf16[24,8,384]{2,1,0:T(8,128)(2,1)S(1)}, u32[]{:S(2)}, u32[]{:S(2)}) collective-permute-start(bf16[24,8,384]{2,1,0:T(8,128)(2,1)S(1)} %get-tuple-element.40), channel_id=1, source_target_pairs={{0,1},{1,2},{2,3},{3,4},{4,5},{5,6},{6,7},{7,8},{8,9},{9,10},{10,1... | collective-permute-start | bytes 442376 | tf_op jit(solution)/shard_map/ppermute | solution.py:479
  4.8 0.3 collective-permute-start.1
  5.1 0.9 fusion.6
  6.0 0.7 convert_bitcast_fusion
  6.7 0.0 copy-start.9
  6.7 0.0 copy-start.10
  6.7 0.0 copy-start.11
  6.7 0.1 fusion.1
  6.8 0.0 collective-permute-done.left
  6.9 2.5 %collective-permute-done.1.right = bf16[24,8,384]{2,1,0:T(8,128)(2,1)S(1)} collective-permute-done((bf16[24,8,384]{2,1,0:T(8,128)(2,1)S(1)}, bf16[24,8,384]{2,1,0:T(8,128)(2,1)S(1)}, u32[]{:S(2)}, u32[]{:S(2)}) %collective-permute-start.1) | collective-permute-done | bytes 147488 | tf_op jit(solution)/shard_map/ppermute | solution.py:480
  9.3 0.0 copy-start
  9.3 1.0 copy-done
  10.3 0.0 copy-start.1
  10.3 0.0 copy-start.2
  10.3 0.0 copy-start.3
  10.4 5.0 %collective-permute-start.2 = (bf16[1,40,384]{2,1,0:T(8,128)(2,1)S(1)}, bf16[1,40,384]{2,1,0:T(8,128)(2,1)S(1)}, u32[]{:S(2)}, u32[]{:S(2)}) collective-permute-start(bf16[1,40,384]{2,1,0:T(8,128)(2,1)S(1)} %get-tuple-element.22), channel_id=1, source_target_pairs={{0,32},{32,64},{64,96},{96,128},{128,160},{160,192},{192,224},{1,3... | collective-permute-start | bytes 92168 | tf_op jit(solution)/shard_map/ppermute | solution.py:493
  15.3 1.3 %collective-permute-start.3 = (bf16[1,40,384]{2,1,0:T(8,128)(2,1)S(1)}, bf16[1,40,384]{2,1,0:T(8,128)(2,1)S(1)}, u32[]{:S(2)}, u32[]{:S(2)}) collective-permute-start(bf16[1,40,384]{2,1,0:T(8,128)(2,1)S(1)} %get-tuple-element.21), channel_id=1, source_target_pairs={{32,0},{64,32},{96,64},{128,96},{160,128},{192,160},{224,192},{33,... | collective-permute-start | bytes 92168 | tf_op jit(solution)/shard_map/ppermute | solution.py:494
  16.6 0.1 slice_bitcast_fusion.2
  16.7 0.1 copy.19
  16.8 0.1 copy.20
  16.8 0.1 copy.21
  16.9 0.0 copy-done.9
  16.9 0.0 copy-done.10
  16.9 0.0 copy-done.11
  16.9 0.4 multiply_add_fusion.tab
  17.3 0.0 copy-done.1
  17.3 0.0 copy-done.2
  17.3 0.0 copy-done.3
  17.4 2.1 %stencil_inner.1 = (f32[384,384]{1,0:T(8,128)S(1)}, f32[384,1152]{1,0:T(8,128)S(1)}) custom-call(f32[24,32,256]{2,1,0:T(8,128)S(1)} %multiply_add_fusion.tab, bf16[24,24,384]{2,1,0:T(8,128)(2,1)S(1)} %copy-done.1, bf16[24,8,384]{2,1,0:T(8,128)(2,1)S(1)} %collective-permute-done.left, bf16[24,8,384]{2,1,0:T(8,128)(2,1)S(1)} %collective-permute-done.1.right, ...), custom_call_target="tpu_custom_call" | custom-call | flops 2200000000 | bytes 6000000 | tf_op jit(solution)/shard_map/stencil_inner/pallas_call | solution.py:506
  19.5 0.0 collective-permute-done.2.top
  19.5 1.9 %collective-permute-done.3.bottom = bf16[1,40,384]{2,1,0:T(8,128)(2,1)S(1)} collective-permute-done((bf16[1,40,384]{2,1,0:T(8,128)(2,1)S(1)}, bf16[1,40,384]{2,1,0:T(8,128)(2,1)S(1)}, u32[]{:S(2)}, u32[]{:S(2)}) %collective-permute-start.3) | collective-permute-done | bytes 30752 | tf_op jit(solution)/shard_map/ppermute | solution.py:494
  21.5 0.0 copy-start.5
  21.5 1.0 stencil_outer.1
  22.5 4.3 %collective-permute-start.4 = (bf16[192,1152]{1,0:T(8,128)(2,1)S(1)}, bf16[192,1152]{1,0:T(8,128)(2,1)S(1)}, u32[]{:S(2)}, u32[]{:S(2)}) collective-permute-start(bf16[192,1152]{1,0:T(8,128)(2,1)S(1)} %get-tuple-element.32), channel_id=1, source_target_pairs={{0,1},{1,0},{2,3},{3,2},{4,5},{5,4},{6,7},{7,6},{8,9},{9,8},{10,11... | collective-permute-start | bytes 1327112 | tf_op jit(solution)/shard_map/ppermute | solution.py:525
  26.7 0.0 copy-done.5
  26.7 3.0 %grad_field.1 = (bf16[576,384]{1,0:T(8,128)(2,1)}, bf16[32,112,128]{2,1,0:T(8,128)(2,1)}) custom-call(s32[1]{0:T(128)} %bitcast.pos, f32[384,384]{1,0:T(8,128)S(1)} %get-tuple-element.24.inner, bf16[192,1152]{1,0:T(8,128)(2,1)S(1)} %get-tuple-element.28.g_outer, bf16[576,384]{1,0:T(8,128)(2,1)S(1)} %bitcast.14, bf16[3,384,384]{2,1,0:T(8,128)(2,1)S(1)} %copy-done.2, ...), custom_call_target="tpu_custom_call" | custom-call | flops 5500000256 | bytes 15000000 | tf_op jit(solution)/shard_map/grad_field/pallas_call | solution.py:528
  29.7 0.0 collective-permute-done.4.other
  29.7 0.9 mix_chip_sum.1
  30.6 0.0 copy-start.12
  30.6 0.0 copy-start.6
  30.6 5.8 %all-to-all-start = ((bf16[32,112,128]{2,1,0:T(8,128)(2,1)}), bf16[32,112,128]{2,1,0:T(8,128)(2,1)S(1)}, u32[]{:S(2)}, u32[]{:S(2)}) async-start(bf16[32,112,128]{2,1,0:T(8,128)(2,1)} %mix_chip_sum.1), calls=%async_computation | async-start | bytes 1835008 | tf_op jit(solution)/shard_map/all_to_all | solution.py:554
  36.4 0.8 dynamic_slice.7
  37.2 0.0 copy-done.12
  37.2 0.1 multiply_add_fusion.1.logscale
  37.3 0.0 copy-done.6
  37.3 0.0 copy-start.4
  37.3 9.8 %legendre.1.leg = bf16[24,384,256]{2,1,0:T(8,128)(2,1)S(1)} custom-call(s32[1]{0:T(128)} %bitcast.pos, f32[1,128]{1,0:T(1,128)S(1)} %copy-done.6, f32[48,128]{1,0:T(8,128)S(1)} %multiply_add_fusion.1.logscale), custom_call_target="tpu_custom_call" | custom-call | flops 9900000256 | bytes 27000000 | tf_op jit(solution)/shard_map/legendre/pallas_call | solution.py:562
  47.1 0.0 copy-start.7
  47.2 2.1 %copy-done.7 = bf16[24,384,256]{2,1,0:T(8,128)(2,1)} copy-done((bf16[24,384,256]{2,1,0:T(8,128)(2,1)}, bf16[24,384,256]{2,1,0:T(8,128)(2,1)S(1)}, u32[]{:S(2)}) %copy-start.7) | copy-done | bytes 4718616
  49.3 10.9 %all-to-all-done.columns = bf16[32,112,128]{2,1,0:T(8,128)(2,1)S(1)} async-done(((bf16[32,112,128]{2,1,0:T(8,128)(2,1)}), bf16[32,112,128]{2,1,0:T(8,128)(2,1)S(1)}, u32[]{:S(2)}, u32[]{:S(2)}) %all-to-all-start) | async-done | bytes 917536 | tf_op jit(solution)/shard_map/all_to_all | solution.py:554
  60.2 0.0 copy-done.4
  60.2 1.1 %dft.1 = bf16[8,328,128]{2,1,0:T(8,128)(2,1)S(1)} custom-call(bf16[768,1024]{1,0:T(8,128)(2,1)S(1)} %copy-done.4, bf16[32,112,128]{2,1,0:T(8,128)(2,1)S(1)} %all-to-all-done.columns), custom_call_target="tpu_custom_call" | custom-call | flops 2200000000 | bytes 6000000 | tf_op jit(solution)/shard_map/dft/pallas_call | solution.py:586
  61.3 16.6 %all_to_all.15.spec = bf16[8,328,128]{2,1,0:T(8,128)(2,1)S(1)} all-to-all(bf16[8,328,128]{2,1,0:T(8,128)(2,1)S(1)} %dft.1), channel_id=1, replica_groups=mesh['lat'=8,'chip'=16,'core'=2] {'lat'}, dimensions={0} | all-to-all | bytes 1343488 | tf_op jit(solution)/shard_map/all_to_all | solution.py:589
  77.9 0.8 mix_copies.1
  78.7 7.1 %all-to-all-start.2 = ((bf16[16,112,128]{2,1,0:T(8,128)(2,1)}), bf16[16,112,128]{2,1,0:T(8,128)(2,1)S(1)}, u32[]{:S(2)}, u32[]{:S(2)}) async-start(bf16[16,112,128]{2,1,0:T(8,128)(2,1)} %mix_copies.1), calls=%async_computation.2 | async-start | bytes 917504 | tf_op jit(solution)/shard_map/all_to_all | solution.py:591
  85.8 0.0 copy-start.8
  85.8 2.3 %copy-done.8 = bf16[24,384,256]{2,1,0:T(8,128)(2,1)S(1)} copy-done((bf16[24,384,256]{2,1,0:T(8,128)(2,1)S(1)}, bf16[24,384,256]{2,1,0:T(8,128)(2,1)}, u32[]{:S(2)}) %copy-start.8) | copy-done | bytes 4718616
  88.1 4.8 %synthesis.1 = f32[2,12,48,384]{3,2,1,0:T(8,128)} custom-call(bf16[8,328,128]{2,1,0:T(8,128)(2,1)S(1)} %all_to_all.15.spec, bf16[384,384]{1,0:T(8,128)(2,1)S(1)} %copy-done.5, bf16[24,384,256]{2,1,0:T(8,128)(2,1)S(1)} %copy-done.8), custom_call_target="tpu_custom_call" | custom-call | flops 6600000000 | bytes 18000000 | tf_op jit(solution)/shard_map/synthesis/pallas_call | solution.py:593
  92.9 5.0 %all-to-all-done.2.parts = bf16[16,112,128]{2,1,0:T(8,128)(2,1)S(1)} async-done(((bf16[16,112,128]{2,1,0:T(8,128)(2,1)}), bf16[16,112,128]{2,1,0:T(8,128)(2,1)S(1)}, u32[]{:S(2)}, u32[]{:S(2)}) %all-to-all-start.2) | async-done | bytes 458784 | tf_op jit(solution)/shard_map/all_to_all | solution.py:591
  97.8 2.8 %collective-permute-start.5 = (bf16[16,112,128]{2,1,0:T(8,128)(2,1)S(1)}, bf16[16,112,128]{2,1,0:T(8,128)(2,1)S(1)}, u32[]{:S(2)}, u32[]{:S(2)}) collective-permute-start(bf16[16,112,128]{2,1,0:T(8,128)(2,1)S(1)} %all-to-all-done.2.parts), channel_id=1, source_target_pairs={{0,1},{1,0},{2,3},{3,2},{4,5},{5,4},{6,7},{7,6},{8,9},{9,8},{10,11... | collective-permute-start | bytes 1376264 | tf_op jit(solution)/shard_map/ppermute | solution.py:614
  100.6 1.0 mix_out.2.rest_0_
  101.6 0.5 collective-permute-done.5.parts
  102.1 1.0 mix_out.3
  (2 shorter events, 0.0 us)
Async XLA Ops:
  1.6 5.2 %collective-permute-start = (bf16[24,8,384]{2,1,0:T(8,128)(2,1)S(1)}, bf16[24,8,384]{2,1,0:T(8,128)(2,1)S(1)}, u32[]{:S(2)}, u32[]{:S(2)}) collective-permute-start(bf16[24,8,384]{2,1,0:T(8,128)(2,1)S(1)} %get-tuple-element.40), channel_id=1, source_target_pairs={{0,1},{1,2},{2,3},{3,4},{4,5},{5,6},{6,7},{7,8},{8,9},{9,10},{10,1... | collective-permute-start | bytes 442376 | tf_op jit(solution)/shard_map/ppermute | solution.py:479
  4.8 4.6 %collective-permute-start.1 = (bf16[24,8,384]{2,1,0:T(8,128)(2,1)S(1)}, bf16[24,8,384]{2,1,0:T(8,128)(2,1)S(1)}, u32[]{:S(2)}, u32[]{:S(2)}) collective-permute-start(bf16[24,8,384]{2,1,0:T(8,128)(2,1)S(1)} %get-tuple-element.39), channel_id=1, source_target_pairs={{1,0},{2,1},{3,2},{4,3},{5,4},{6,5},{7,6},{8,7},{9,8},{10,9},{11,1... | collective-permute-start | bytes 442376 | tf_op jit(solution)/shard_map/ppermute | solution.py:480
  6.7 10.2 %copy-start.9 = (f32[24,256]{1,0:T(8,128)S(1)}, f32[24,256]{1,0:T(8,128)}, u32[]{:S(2)}) copy-start(f32[24,256]{1,0:T(8,128)} %constant.55) | copy-start | bytes 73732
  6.7 10.2 %copy-start.10 = (f32[24,256]{1,0:T(8,128)S(1)}, f32[24,256]{1,0:T(8,128)}, u32[]{:S(2)}) copy-start(f32[24,256]{1,0:T(8,128)} %constant.56) | copy-start | bytes 73732
  6.7 10.2 %copy-start.11 = (f32[24,256]{1,0:T(8,128)S(1)}, f32[24,256]{1,0:T(8,128)}, u32[]{:S(2)}) copy-start(f32[24,256]{1,0:T(8,128)} %constant.57) | copy-start | bytes 73732
  9.3 1.0 copy-start
  10.3 7.0 %copy-start.1 = (bf16[24,24,384]{2,1,0:T(8,128)(2,1)S(1)}, bf16[24,24,384]{2,1,0:T(8,128)(2,1)}, u32[]{:S(2)}) copy-start(bf16[24,24,384]{2,1,0:T(8,128)(2,1)} %cot.5) | copy-start | bytes 1327108
  10.3 7.0 %copy-start.2 = (bf16[3,384,384]{2,1,0:T(8,128)(2,1)S(1)}, bf16[3,384,384]{2,1,0:T(8,128)(2,1)}, u32[]{:S(2)}) copy-start(bf16[3,384,384]{2,1,0:T(8,128)(2,1)} %mix.3) | copy-start | bytes 2654212
  10.3 7.0 %copy-start.3 = (bf16[24,24,384]{2,1,0:T(8,128)(2,1)S(1)}, bf16[24,24,384]{2,1,0:T(8,128)(2,1)}, u32[]{:S(2)}) copy-start(bf16[24,24,384]{2,1,0:T(8,128)(2,1)} %param.14) | copy-start | bytes 1327108
  10.4 9.2 %collective-permute-start.2 = (bf16[1,40,384]{2,1,0:T(8,128)(2,1)S(1)}, bf16[1,40,384]{2,1,0:T(8,128)(2,1)S(1)}, u32[]{:S(2)}, u32[]{:S(2)}) collective-permute-start(bf16[1,40,384]{2,1,0:T(8,128)(2,1)S(1)} %get-tuple-element.22), channel_id=1, source_target_pairs={{0,32},{32,64},{64,96},{96,128},{128,160},{160,192},{192,224},{1,3... | collective-permute-start | bytes 92168 | tf_op jit(solution)/shard_map/ppermute | solution.py:493
  15.3 6.1 %collective-permute-start.3 = (bf16[1,40,384]{2,1,0:T(8,128)(2,1)S(1)}, bf16[1,40,384]{2,1,0:T(8,128)(2,1)S(1)}, u32[]{:S(2)}, u32[]{:S(2)}) collective-permute-start(bf16[1,40,384]{2,1,0:T(8,128)(2,1)S(1)} %get-tuple-element.21), channel_id=1, source_target_pairs={{32,0},{64,32},{96,64},{128,96},{160,128},{192,160},{224,192},{33,... | collective-permute-start | bytes 92168 | tf_op jit(solution)/shard_map/ppermute | solution.py:494
  21.5 5.3 %copy-start.5 = (bf16[384,384]{1,0:T(8,128)(2,1)S(1)}, bf16[384,384]{1,0:T(8,128)(2,1)}, u32[]{:S(2)}) copy-start(bf16[384,384]{1,0:T(8,128)(2,1)} %constant.46.clone.pack) | copy-start | bytes 884740
  22.5 7.3 %collective-permute-start.4 = (bf16[192,1152]{1,0:T(8,128)(2,1)S(1)}, bf16[192,1152]{1,0:T(8,128)(2,1)S(1)}, u32[]{:S(2)}, u32[]{:S(2)}) collective-permute-start(bf16[192,1152]{1,0:T(8,128)(2,1)S(1)} %get-tuple-element.32), channel_id=1, source_target_pairs={{0,1},{1,0},{2,3},{3,2},{4,5},{5,4},{6,7},{7,6},{8,9},{9,8},{10,11... | collective-permute-start | bytes 1327112 | tf_op jit(solution)/shard_map/ppermute | solution.py:525
  30.6 6.6 %copy-start.12 = (f32[128]{0:T(128)S(1)}, f32[128]{0:T(128)}, u32[]{:S(2)}) copy-start(f32[128]{0:T(128)} %constant.58) | copy-start | bytes 1540
  30.6 6.7 %copy-start.6 = (f32[1,128]{1,0:T(1,128)S(1)}, f32[1,128]{1,0:T(1,128)}, u32[]{:S(2)}) copy-start(f32[1,128]{1,0:T(1,128)} %constant.49.clone.cosines) | copy-start | bytes 1540
  30.6 29.5 %all-to-all-start = ((bf16[32,112,128]{2,1,0:T(8,128)(2,1)}), bf16[32,112,128]{2,1,0:T(8,128)(2,1)S(1)}, u32[]{:S(2)}, u32[]{:S(2)}) async-start(bf16[32,112,128]{2,1,0:T(8,128)(2,1)} %mix_chip_sum.1), calls=%async_computation | async-start | bytes 1835008 | tf_op jit(solution)/shard_map/all_to_all | solution.py:554
  37.3 22.9 %copy-start.4 = (bf16[768,1024]{1,0:T(8,128)(2,1)S(1)}, bf16[768,1024]{1,0:T(8,128)(2,1)}, u32[]{:S(2)}) copy-start(bf16[768,1024]{1,0:T(8,128)(2,1)} %constant.50.clone.rows) | copy-start | bytes 4718596
  47.1 2.2 %copy-start.7 = (bf16[24,384,256]{2,1,0:T(8,128)(2,1)}, bf16[24,384,256]{2,1,0:T(8,128)(2,1)S(1)}, u32[]{:S(2)}) copy-start(bf16[24,384,256]{2,1,0:T(8,128)(2,1)S(1)} %legendre.1.leg) | copy-start | bytes 14155780
  78.7 19.1 %all-to-all-start.2 = ((bf16[16,112,128]{2,1,0:T(8,128)(2,1)}), bf16[16,112,128]{2,1,0:T(8,128)(2,1)S(1)}, u32[]{:S(2)}, u32[]{:S(2)}) async-start(bf16[16,112,128]{2,1,0:T(8,128)(2,1)} %mix_copies.1), calls=%async_computation.2 | async-start | bytes 917504 | tf_op jit(solution)/shard_map/all_to_all | solution.py:591
  85.8 2.3 %copy-start.8 = (bf16[24,384,256]{2,1,0:T(8,128)(2,1)S(1)}, bf16[24,384,256]{2,1,0:T(8,128)(2,1)}, u32[]{:S(2)}) copy-start(bf16[24,384,256]{2,1,0:T(8,128)(2,1)} %copy-done.7) | copy-start | bytes 14155780
  97.8 4.2 %collective-permute-start.5 = (bf16[16,112,128]{2,1,0:T(8,128)(2,1)S(1)}, bf16[16,112,128]{2,1,0:T(8,128)(2,1)S(1)}, u32[]{:S(2)}, u32[]{:S(2)}) collective-permute-start(bf16[16,112,128]{2,1,0:T(8,128)(2,1)S(1)} %all-to-all-done.2.parts), channel_id=1, source_target_pairs={{0,1},{1,0},{2,3},{3,2},{4,5},{5,4},{6,7},{7,6},{8,9},{9,8},{10,11... | collective-permute-start | bytes 1376264 | tf_op jit(solution)/shard_map/ppermute | solution.py:614

commit v12 on v11

--- a/solution.py
+++ b/solution.py
@@ -96,9 +96,9 @@
     ext[there, R + FD:XW, :] = right[rows].astype(F32)
 
 
-def edge_kernel(cot, left, right, first, last):
-    for row, out in ((0, first), (TD - 1, last)):
-        pieces = [part[row:row + 1].astype(F32) for part in (left, cot, right)]
+def edge_kernel(top, bottom, left, right, first, last):
+    for row, own, out in ((0, top, first), (TD - 1, bottom, last)):
+        pieces = [part.astype(F32) for part in (left[row:row + 1], own[...], right[row:row + 1])]
         out[...] = jnp.concatenate(pieces, axis=1).astype(BF16)
 
 
@@ -485,9 +485,9 @@
         edge_kernel,
         (near_shape(edge, BF16), near_shape(edge, BF16)),
         1,
-        in_specs=[whole] * 3,
+        in_specs=[whole] * 4,
         name="edge_rows",
-    )(near_cot, *rims)
+    )(near(cotangent[:1]), near(cotangent[TD - 1:]), *rims)
     north = [(i, i + 1) for i in range(LATS - 1)]
     south = [(j, i) for i, j in north]
     top = lax.ppermute(edge_rows[1], LAT, north)

time: 104 us -> 103 us (level)
    unnamed x26 -> x24, local copies, waits for them, and re-layouts: 5.55 us -> 4.54 us
  transfers between devices with their start and end apart: 8 -> 8, of which waited for: 5 -> 5; matrix products, arithmetic and copies ran while one was open for 3% -> 4% of each run, Pallas kernels for 20% -> 20%
where the time goes in v12:
time: 103 us; the launch traced here: 102 us
  starting transfers between devices  29.6 us (29%)
  Pallas kernels  25.5 us (25%)
  waiting for transfers between devices  20 us (19%)
  blocking collectives  16.6 us (16%)
  local copies, waits for them, and re-layouts  7.34 us (7%)
  other arithmetic  2.21 us (2%)
    all_to_all x1, blocking collectives, on_device(): spec = lax.all_to_all(spectra, LAT, 0, 0, tiled=True)  16.6 us
    all_to_all x1, waiting for transfers between devices, on_device(): columns = lax.all_to_all(send, LON, 0, 0, tiled=True)  10.9 us
    pallas_call x1, Pallas kernels, on_device(): call(legendre_kernel, shape((MD // 2, L, 2 * HALF), BF16), 9, grid_spec=p...  9.85 us
    all_to_all x1, starting transfers between devices, on_device(): mix_mine = lax.all_to_all(mix_copies, CHIP, 0, 0, tiled=True)  7.09 us
    all_to_all x1, starting transfers between devices, on_device(): columns = lax.all_to_all(send, LON, 0, 0, tiled=True)  5.8 us
    all_to_all x1, waiting for transfers between devices, on_device(): mix_mine = lax.all_to_all(mix_copies, CHIP, 0, 0, tiled=True)  4.95 us
    ppermute x1, starting transfers between devices, on_device(): top = lax.ppermute(edge_rows[1], LAT, north)  4.95 us
    pallas_call x1, Pallas kernels, on_device(): call(synthesis_kernel, shape((2, CD, MD, L), F32), 6, grid_spec=pltpu.Pre...  4.76 us
  transfers between devices with their start and end apart: 8, of which 5 were waited for; matrix products, arithmetic and copies ran while one was open for 4% of the time, Pallas kernels for 20%

profile of v12, /device:TPU:1, one launch (start us, length us, event | category | flops | bytes accessed | tf_op | source)
XLA Modules:
  0.0 102.1 jit_solution(9488988151141856833)
XLA Ops:
  0.6 1.0 fusion.7
  1.6 3.1 %collective-permute-start = (bf16[24,8,384]{2,1,0:T(8,128)(2,1)S(1)}, bf16[24,8,384]{2,1,0:T(8,128)(2,1)S(1)}, u32[]{:S(2)}, u32[]{:S(2)}) collective-permute-start(bf16[24,8,384]{2,1,0:T(8,128)(2,1)S(1)} %get-tuple-element.40), channel_id=1, source_target_pairs={{0,1},{1,2},{2,3},{3,4},{4,5},{5,6},{6,7},{7,8},{8,9},{9,10},{10,1... | collective-permute-start | bytes 442376 | tf_op jit(solution)/shard_map/ppermute | solution.py:479
  4.8 0.3 collective-permute-start.1
  5.1 0.7 fusion.8
  5.8 0.9 fusion.6
  6.7 0.7 convert_bitcast_fusion
  7.4 0.1 fusion.1
  7.5 0.0 collective-permute-done.left
  7.6 1.8 %collective-permute-done.1.right = bf16[24,8,384]{2,1,0:T(8,128)(2,1)S(1)} collective-permute-done((bf16[24,8,384]{2,1,0:T(8,128)(2,1)S(1)}, bf16[24,8,384]{2,1,0:T(8,128)(2,1)S(1)}, u32[]{:S(2)}, u32[]{:S(2)}) %collective-permute-start.1) | collective-permute-done | bytes 147488 | tf_op jit(solution)/shard_map/ppermute | solution.py:480
  9.3 0.0 copy-start.8
  9.3 0.0 copy-start.9
  9.3 0.0 copy-start.10
  9.3 0.0 copy-start
  9.3 0.0 copy-start.1
  9.3 0.0 copy-start.2
  9.4 5.0 %collective-permute-start.2 = (bf16[1,40,384]{2,1,0:T(8,128)(2,1)S(1)}, bf16[1,40,384]{2,1,0:T(8,128)(2,1)S(1)}, u32[]{:S(2)}, u32[]{:S(2)}) collective-permute-start(bf16[1,40,384]{2,1,0:T(8,128)(2,1)S(1)} %get-tuple-element.22), channel_id=1, source_target_pairs={{0,32},{32,64},{64,96},{96,128},{128,160},{160,192},{192,224},{1,3... | collective-permute-start | bytes 92168 | tf_op jit(solution)/shard_map/ppermute | solution.py:493
  14.3 1.3 %collective-permute-start.3 = (bf16[1,40,384]{2,1,0:T(8,128)(2,1)S(1)}, bf16[1,40,384]{2,1,0:T(8,128)(2,1)S(1)}, u32[]{:S(2)}, u32[]{:S(2)}) collective-permute-start(bf16[1,40,384]{2,1,0:T(8,128)(2,1)S(1)} %get-tuple-element.21), channel_id=1, source_target_pairs={{32,0},{64,32},{96,64},{128,96},{160,128},{192,160},{224,192},{33,... | collective-permute-start | bytes 92168 | tf_op jit(solution)/shard_map/ppermute | solution.py:494
  15.6 0.1 slice_bitcast_fusion.2
  15.7 0.1 copy.19
  15.8 0.1 copy.20
  15.8 0.1 copy.21
  15.9 0.0 copy-done.8
  15.9 0.0 copy-done.9
  15.9 0.0 copy-done.10
  15.9 0.4 multiply_add_fusion.tab
  16.4 0.0 copy-done
  16.4 0.0 copy-done.1
  16.4 0.0 copy-done.2
  16.4 2.2 %stencil_inner.1 = (f32[384,384]{1,0:T(8,128)S(1)}, f32[384,1152]{1,0:T(8,128)S(1)}) custom-call(f32[24,32,256]{2,1,0:T(8,128)S(1)} %multiply_add_fusion.tab, bf16[24,24,384]{2,1,0:T(8,128)(2,1)S(1)} %copy-done, bf16[24,8,384]{2,1,0:T(8,128)(2,1)S(1)} %collective-permute-done.left, bf16[24,8,384]{2,1,0:T(8,128)(2,1)S(1)} %collective-permute-done.1.right, ...), custom_call_target="tpu_custom_call" | custom-call | flops 2200000000 | bytes 6000000 | tf_op jit(solution)/shard_map/stencil_inner/pallas_call | solution.py:506
  18.5 0.0 collective-permute-done.2.top
  18.6 1.9 %collective-permute-done.3.bottom = bf16[1,40,384]{2,1,0:T(8,128)(2,1)S(1)} collective-permute-done((bf16[1,40,384]{2,1,0:T(8,128)(2,1)S(1)}, bf16[1,40,384]{2,1,0:T(8,128)(2,1)S(1)}, u32[]{:S(2)}, u32[]{:S(2)}) %collective-permute-start.3) | collective-permute-done | bytes 30752 | tf_op jit(solution)/shard_map/ppermute | solution.py:494
  20.5 0.0 copy-start.4
  20.5 1.0 stencil_outer.1
  21.5 4.3 %collective-permute-start.4 = (bf16[192,1152]{1,0:T(8,128)(2,1)S(1)}, bf16[192,1152]{1,0:T(8,128)(2,1)S(1)}, u32[]{:S(2)}, u32[]{:S(2)}) collective-permute-start(bf16[192,1152]{1,0:T(8,128)(2,1)S(1)} %get-tuple-element.32), channel_id=1, source_target_pairs={{0,1},{1,0},{2,3},{3,2},{4,5},{5,4},{6,7},{7,6},{8,9},{9,8},{10,11... | collective-permute-start | bytes 1327112 | tf_op jit(solution)/shard_map/ppermute | solution.py:525
  25.8 0.0 copy-done.4
  25.8 3.0 %grad_field.1 = (bf16[576,384]{1,0:T(8,128)(2,1)}, bf16[32,112,128]{2,1,0:T(8,128)(2,1)}) custom-call(s32[1]{0:T(128)} %bitcast.pos, f32[384,384]{1,0:T(8,128)S(1)} %get-tuple-element.24.inner, bf16[192,1152]{1,0:T(8,128)(2,1)S(1)} %get-tuple-element.28.g_outer, bf16[576,384]{1,0:T(8,128)(2,1)S(1)} %bitcast.14, bf16[3,384,384]{2,1,0:T(8,128)(2,1)S(1)} %copy-done.1, ...), custom_call_target="tpu_custom_call" | custom-call | flops 5500000256 | bytes 15000000 | tf_op jit(solution)/shard_map/grad_field/pallas_call | solution.py:528
  28.8 0.0 collective-permute-done.4.other
  28.8 0.9 mix_chip_sum.1
  29.6 0.0 copy-start.11
  29.7 0.0 copy-start.5
  29.7 5.8 %all-to-all-start = ((bf16[32,112,128]{2,1,0:T(8,128)(2,1)}), bf16[32,112,128]{2,1,0:T(8,128)(2,1)S(1)}, u32[]{:S(2)}, u32[]{:S(2)}) async-start(bf16[32,112,128]{2,1,0:T(8,128)(2,1)} %mix_chip_sum.1), calls=%async_computation | async-start | bytes 1835008 | tf_op jit(solution)/shard_map/all_to_all | solution.py:554
  35.5 0.8 dynamic_slice.7
  36.2 0.0 copy-done.11
  36.2 0.1 multiply_add_fusion.1.logscale
  36.3 0.0 copy-done.5
  36.3 0.0 copy-start.3
  36.3 9.8 %legendre.1.leg = bf16[24,384,256]{2,1,0:T(8,128)(2,1)S(1)} custom-call(s32[1]{0:T(128)} %bitcast.pos, f32[1,128]{1,0:T(1,128)S(1)} %copy-done.5, f32[48,128]{1,0:T(8,128)S(1)} %multiply_add_fusion.1.logscale), custom_call_target="tpu_custom_call" | custom-call | flops 9900000256 | bytes 27000000 | tf_op jit(solution)/shard_map/legendre/pallas_call | solution.py:562
  46.2 0.0 copy-start.6
  46.2 2.1 %copy-done.6 = bf16[24,384,256]{2,1,0:T(8,128)(2,1)} copy-done((bf16[24,384,256]{2,1,0:T(8,128)(2,1)}, bf16[24,384,256]{2,1,0:T(8,128)(2,1)S(1)}, u32[]{:S(2)}) %copy-start.6) | copy-done | bytes 4718616
  48.4 10.9 %all-to-all-done.columns = bf16[32,112,128]{2,1,0:T(8,128)(2,1)S(1)} async-done(((bf16[32,112,128]{2,1,0:T(8,128)(2,1)}), bf16[32,112,128]{2,1,0:T(8,128)(2,1)S(1)}, u32[]{:S(2)}, u32[]{:S(2)}) %all-to-all-start) | async-done | bytes 917536 | tf_op jit(solution)/shard_map/all_to_all | solution.py:554
  59.2 0.0 copy-done.3
  59.2 1.1 %dft.1 = bf16[8,328,128]{2,1,0:T(8,128)(2,1)S(1)} custom-call(bf16[768,1024]{1,0:T(8,128)(2,1)S(1)} %copy-done.3, bf16[32,112,128]{2,1,0:T(8,128)(2,1)S(1)} %all-to-all-done.columns), custom_call_target="tpu_custom_call" | custom-call | flops 2200000000 | bytes 6000000 | tf_op jit(solution)/shard_map/dft/pallas_call | solution.py:586
  60.3 16.6 %all_to_all.15.spec = bf16[8,328,128]{2,1,0:T(8,128)(2,1)S(1)} all-to-all(bf16[8,328,128]{2,1,0:T(8,128)(2,1)S(1)} %dft.1), channel_id=1, replica_groups=mesh['lat'=8,'chip'=16,'core'=2] {'lat'}, dimensions={0} | all-to-all | bytes 1343488 | tf_op jit(solution)/shard_map/all_to_all | solution.py:589
  76.9 0.8 mix_copies.1
  77.7 7.1 %all-to-all-start.2 = ((bf16[16,112,128]{2,1,0:T(8,128)(2,1)}), bf16[16,112,128]{2,1,0:T(8,128)(2,1)S(1)}, u32[]{:S(2)}, u32[]{:S(2)}) async-start(bf16[16,112,128]{2,1,0:T(8,128)(2,1)} %mix_copies.1), calls=%async_computation.2 | async-start | bytes 917504 | tf_op jit(solution)/shard_map/all_to_all | solution.py:591
  84.8 0.0 copy-start.7
  84.8 2.3 %copy-done.7 = bf16[24,384,256]{2,1,0:T(8,128)(2,1)S(1)} copy-done((bf16[24,384,256]{2,1,0:T(8,128)(2,1)S(1)}, bf16[24,384,256]{2,1,0:T(8,128)(2,1)}, u32[]{:S(2)}) %copy-start.7) | copy-done | bytes 4718616
  87.2 4.8 %synthesis.1 = f32[2,12,48,384]{3,2,1,0:T(8,128)} custom-call(bf16[8,328,128]{2,1,0:T(8,128)(2,1)S(1)} %all_to_all.15.spec, bf16[384,384]{1,0:T(8,128)(2,1)S(1)} %copy-done.4, bf16[24,384,256]{2,1,0:T(8,128)(2,1)S(1)} %copy-done.7), custom_call_target="tpu_custom_call" | custom-call | flops 6600000000 | bytes 18000000 | tf_op jit(solution)/shard_map/synthesis/pallas_call | solution.py:593
  91.9 5.0 %all-to-all-done.2.parts = bf16[16,112,128]{2,1,0:T(8,128)(2,1)S(1)} async-done(((bf16[16,112,128]{2,1,0:T(8,128)(2,1)}), bf16[16,112,128]{2,1,0:T(8,128)(2,1)S(1)}, u32[]{:S(2)}, u32[]{:S(2)}) %all-to-all-start.2) | async-done | bytes 458784 | tf_op jit(solution)/shard_map/all_to_all | solution.py:591
  96.9 2.8 %collective-permute-start.5 = (bf16[16,112,128]{2,1,0:T(8,128)(2,1)S(1)}, bf16[16,112,128]{2,1,0:T(8,128)(2,1)S(1)}, u32[]{:S(2)}, u32[]{:S(2)}) collective-permute-start(bf16[16,112,128]{2,1,0:T(8,128)(2,1)S(1)} %all-to-all-done.2.parts), channel_id=1, source_target_pairs={{0,1},{1,0},{2,3},{3,2},{4,5},{5,4},{6,7},{7,6},{8,9},{9,8},{10,11... | collective-permute-start | bytes 1376264 | tf_op jit(solution)/shard_map/ppermute | solution.py:614
  99.7 1.0 mix_out.2.rest_0_
  100.6 0.5 collective-permute-done.5.parts
  101.1 1.0 mix_out.3
  (2 shorter events, 0.0 us)
Async XLA Ops:
  1.6 5.9 %collective-permute-start = (bf16[24,8,384]{2,1,0:T(8,128)(2,1)S(1)}, bf16[24,8,384]{2,1,0:T(8,128)(2,1)S(1)}, u32[]{:S(2)}, u32[]{:S(2)}) collective-permute-start(bf16[24,8,384]{2,1,0:T(8,128)(2,1)S(1)} %get-tuple-element.40), channel_id=1, source_target_pairs={{0,1},{1,2},{2,3},{3,4},{4,5},{5,6},{6,7},{7,8},{8,9},{9,10},{10,1... | collective-permute-start | bytes 442376 | tf_op jit(solution)/shard_map/ppermute | solution.py:479
  4.8 4.6 %collective-permute-start.1 = (bf16[24,8,384]{2,1,0:T(8,128)(2,1)S(1)}, bf16[24,8,384]{2,1,0:T(8,128)(2,1)S(1)}, u32[]{:S(2)}, u32[]{:S(2)}) collective-permute-start(bf16[24,8,384]{2,1,0:T(8,128)(2,1)S(1)} %get-tuple-element.39), channel_id=1, source_target_pairs={{1,0},{2,1},{3,2},{4,3},{5,4},{6,5},{7,6},{8,7},{9,8},{10,9},{11,1... | collective-permute-start | bytes 442376 | tf_op jit(solution)/shard_map/ppermute | solution.py:480
  9.3 6.6 %copy-start.8 = (f32[24,256]{1,0:T(8,128)S(1)}, f32[24,256]{1,0:T(8,128)}, u32[]{:S(2)}) copy-start(f32[24,256]{1,0:T(8,128)} %constant.55) | copy-start | bytes 73732
  9.3 6.6 %copy-start.9 = (f32[24,256]{1,0:T(8,128)S(1)}, f32[24,256]{1,0:T(8,128)}, u32[]{:S(2)}) copy-start(f32[24,256]{1,0:T(8,128)} %constant.56) | copy-start | bytes 73732
  9.3 6.6 %copy-start.10 = (f32[24,256]{1,0:T(8,128)S(1)}, f32[24,256]{1,0:T(8,128)}, u32[]{:S(2)}) copy-start(f32[24,256]{1,0:T(8,128)} %constant.57) | copy-start | bytes 73732
  9.3 7.0 %copy-start = (bf16[24,24,384]{2,1,0:T(8,128)(2,1)S(1)}, bf16[24,24,384]{2,1,0:T(8,128)(2,1)}, u32[]{:S(2)}) copy-start(bf16[24,24,384]{2,1,0:T(8,128)(2,1)} %cot.3) | copy-start | bytes 1327108
  9.3 7.0 %copy-start.1 = (bf16[3,384,384]{2,1,0:T(8,128)(2,1)S(1)}, bf16[3,384,384]{2,1,0:T(8,128)(2,1)}, u32[]{:S(2)}) copy-start(bf16[3,384,384]{2,1,0:T(8,128)(2,1)} %mix.3) | copy-start | bytes 2654212
  9.3 7.0 %copy-start.2 = (bf16[24,24,384]{2,1,0:T(8,128)(2,1)S(1)}, bf16[24,24,384]{2,1,0:T(8,128)(2,1)}, u32[]{:S(2)}) copy-start(bf16[24,24,384]{2,1,0:T(8,128)(2,1)} %param.14) | copy-start | bytes 1327108
  9.4 9.2 %collective-permute-start.2 = (bf16[1,40,384]{2,1,0:T(8,128)(2,1)S(1)}, bf16[1,40,384]{2,1,0:T(8,128)(2,1)S(1)}, u32[]{:S(2)}, u32[]{:S(2)}) collective-permute-start(bf16[1,40,384]{2,1,0:T(8,128)(2,1)S(1)} %get-tuple-element.22), channel_id=1, source_target_pairs={{0,32},{32,64},{64,96},{96,128},{128,160},{160,192},{192,224},{1,3... | collective-permute-start | bytes 92168 | tf_op jit(solution)/shard_map/ppermute | solution.py:493
  14.3 6.1 %collective-permute-start.3 = (bf16[1,40,384]{2,1,0:T(8,128)(2,1)S(1)}, bf16[1,40,384]{2,1,0:T(8,128)(2,1)S(1)}, u32[]{:S(2)}, u32[]{:S(2)}) collective-permute-start(bf16[1,40,384]{2,1,0:T(8,128)(2,1)S(1)} %get-tuple-element.21), channel_id=1, source_target_pairs={{32,0},{64,32},{96,64},{128,96},{160,128},{192,160},{224,192},{33,... | collective-permute-start | bytes 92168 | tf_op jit(solution)/shard_map/ppermute | solution.py:494
  20.5 5.3 %copy-start.4 = (bf16[384,384]{1,0:T(8,128)(2,1)S(1)}, bf16[384,384]{1,0:T(8,128)(2,1)}, u32[]{:S(2)}) copy-start(bf16[384,384]{1,0:T(8,128)(2,1)} %constant.46.clone.pack) | copy-start | bytes 884740
  21.5 7.3 %collective-permute-start.4 = (bf16[192,1152]{1,0:T(8,128)(2,1)S(1)}, bf16[192,1152]{1,0:T(8,128)(2,1)S(1)}, u32[]{:S(2)}, u32[]{:S(2)}) collective-permute-start(bf16[192,1152]{1,0:T(8,128)(2,1)S(1)} %get-tuple-element.32), channel_id=1, source_target_pairs={{0,1},{1,0},{2,3},{3,2},{4,5},{5,4},{6,7},{7,6},{8,9},{9,8},{10,11... | collective-permute-start | bytes 1327112 | tf_op jit(solution)/shard_map/ppermute | solution.py:525
  29.6 6.6 %copy-start.11 = (f32[128]{0:T(128)S(1)}, f32[128]{0:T(128)}, u32[]{:S(2)}) copy-start(f32[128]{0:T(128)} %constant.58) | copy-start | bytes 1540
  29.7 6.7 %copy-start.5 = (f32[1,128]{1,0:T(1,128)S(1)}, f32[1,128]{1,0:T(1,128)}, u32[]{:S(2)}) copy-start(f32[1,128]{1,0:T(1,128)} %constant.49.clone.cosines) | copy-start | bytes 1540
  29.7 29.5 %all-to-all-start = ((bf16[32,112,128]{2,1,0:T(8,128)(2,1)}), bf16[32,112,128]{2,1,0:T(8,128)(2,1)S(1)}, u32[]{:S(2)}, u32[]{:S(2)}) async-start(bf16[32,112,128]{2,1,0:T(8,128)(2,1)} %mix_chip_sum.1), calls=%async_computation | async-start | bytes 1835008 | tf_op jit(solution)/shard_map/all_to_all | solution.py:554
  36.3 22.9 %copy-start.3 = (bf16[768,1024]{1,0:T(8,128)(2,1)S(1)}, bf16[768,1024]{1,0:T(8,128)(2,1)}, u32[]{:S(2)}) copy-start(bf16[768,1024]{1,0:T(8,128)(2,1)} %constant.50.clone.rows) | copy-start | bytes 4718596
  46.2 2.2 %copy-start.6 = (bf16[24,384,256]{2,1,0:T(8,128)(2,1)}, bf16[24,384,256]{2,1,0:T(8,128)(2,1)S(1)}, u32[]{:S(2)}) copy-start(bf16[24,384,256]{2,1,0:T(8,128)(2,1)S(1)} %legendre.1.leg) | copy-start | bytes 14155780
  77.7 19.1 %all-to-all-start.2 = ((bf16[16,112,128]{2,1,0:T(8,128)(2,1)}), bf16[16,112,128]{2,1,0:T(8,128)(2,1)S(1)}, u32[]{:S(2)}, u32[]{:S(2)}) async-start(bf16[16,112,128]{2,1,0:T(8,128)(2,1)} %mix_copies.1), calls=%async_computation.2 | async-start | bytes 917504 | tf_op jit(solution)/shard_map/all_to_all | solution.py:591
  84.8 2.3 %copy-start.7 = (bf16[24,384,256]{2,1,0:T(8,128)(2,1)S(1)}, bf16[24,384,256]{2,1,0:T(8,128)(2,1)}, u32[]{:S(2)}) copy-start(bf16[24,384,256]{2,1,0:T(8,128)(2,1)} %copy-done.6) | copy-start | bytes 14155780
  96.9 4.2 %collective-permute-start.5 = (bf16[16,112,128]{2,1,0:T(8,128)(2,1)S(1)}, bf16[16,112,128]{2,1,0:T(8,128)(2,1)S(1)}, u32[]{:S(2)}, u32[]{:S(2)}) collective-permute-start(bf16[16,112,128]{2,1,0:T(8,128)(2,1)S(1)} %all-to-all-done.2.parts), channel_id=1, source_target_pairs={{0,1},{1,0},{2,3},{3,2},{4,5},{5,4},{6,7},{7,6},{8,9},{9,8},{10,11... | collective-permute-start | bytes 1376264 | tf_op jit(solution)/shard_map/ppermute | solution.py:614
